TPU v7x, 32 devices: a whole 2x2x4 slice. The times are simulated.
32 devices in a mesh: dp: 8 (over z, x), expert: 4 (over y, core).
Axes of the slice: x: 2, y: 2, z: 4, core: 2. Of those that a mesh axis runs over, the one named last changes fastest.
Arguments:
- tokens: bfloat16 [20480, 1024], P(('dp', 'expert')), may hold values from -6 to 6
- cotangent: bfloat16 [20480, 1024], P(('dp', 'expert')), may hold values from -6 to 6
- expert_ids: int32 [20480, 8], P(('dp', 'expert')), may hold values from 0 to 31, all different within a row; in each aligned block of 320 rows (0 to 319, 320 to 639, ...) at most 100 rows name the same one
- norm_attn: float32 [1024], replicated, may hold values from 0.5 to 1.5
- w_qkv: bfloat16 [1024, 2048], replicated, may hold values from -0.75 to 0.75
- w_out: bfloat16 [1024, 1024], replicated, may hold values from -0.8984375 to 0.8984375
- norm_moe: float32 [1024], replicated, may hold values from 0.5 to 1.5
- w_router: bfloat16 [1024, 32], replicated, may hold values from -0.095703125 to 0.095703125
- w_gate_up: bfloat16 [32, 1024, 1024], P('expert'), may hold values from -0.1875 to 0.1875
- w_down: bfloat16 [32, 512, 1024], P('expert'), may hold values from -5.375 to 5.375
Outputs:
- output: bfloat16 [20480, 1024], P(('dp', 'expert'))
- grad_tokens: bfloat16 [20480, 1024], P(('dp', 'expert'))
- grad_norm_attn: float32 [1024], replicated
- grad_qkv: float32 [1024, 2048], replicated
- grad_out: float32 [1024, 1024], replicated
- grad_norm_moe: float32 [1024], replicated
- grad_router: float32 [1024, 32], replicated
- grad_gate_up: float32 [32, 1024, 1024], P('expert', 'dp')
- grad_down: float32 [32, 512, 1024], P('expert', 'dp')
Inputs may be any that keep to these rules, and one draw needn't show every extreme that they name: `expert_ids`: each row names 8 different experts. In each aligned block of 320 rows no expert is named by more than 100 rows, a bound that some block reaches.
All inputs are finite; a program needn't handle non-finite values.
Results may differ from a plain program's by a relative error of at most 0.018.
The roundings to bfloat16 on the way count: a program that leaves them out, or rounds other values in their place, can miss the bound.
Values may be sent and summed in bfloat16 or wider, within the bound.
No kernel may reach another device: no remote copies, remote signals or barrier semaphores. Data moves between devices by JAX's collectives and lax.ppermute only.
A program may use at most 320 MiB of HBM per device.

v0:
```python
import jax
import jax.numpy as jnp
from jax import lax
from jax.sharding import PartitionSpec as P

D = 1024
HEADS = 16
KV_HEADS = 8
HEAD_DIM = 64
FF = 512
EXPERTS = 32
TOP = 8
PROMPT_DEV = 64
MICRO = 2
CAP = 100


epsilon = 1e-06
score_scale = 1.0 / 64.0
branch_scale = 0.22
masked_score = -1e30


def normalize(values, gain_vec):
    return (
        values * lax.rsqrt(jnp.mean(values * values, axis=-1, keepdims=True) + epsilon) * gain_vec
    )


def rotary_tables(positions):
    half_dim = HEAD_DIM // 2
    inverse = 10000.0 ** (-2.0 * jnp.arange(half_dim, dtype=jnp.float32) / HEAD_DIM)
    angles = positions[:, None] * inverse[None, :]
    cosine = jnp.concatenate([jnp.cos(angles), jnp.cos(angles)], axis=-1)
    sine_table = jnp.concatenate([jnp.sin(angles), jnp.sin(angles)], axis=-1)
    return (cosine, sine_table)


def rotate(vectors, cosine, sine_table):
    half_dim = HEAD_DIM // 2
    turned = jnp.concatenate([-vectors[..., half_dim:], vectors[..., :half_dim]], axis=-1)
    return vectors * cosine[:, None, :] + turned * sine_table[:, None, :]


def swiglu(gate_up):
    return jax.nn.silu(gate_up[..., :FF]) * gate_up[..., FF:]


def gate_softmax(chosen):
    return jax.nn.softmax(chosen, axis=-1)


def head_scores(queries, key_rows, allowed):
    scores = (
        jnp.einsum("qgd,kd->gqk", queries, key_rows, preferred_element_type=jnp.float32)
        * score_scale
    )
    return jnp.where(allowed[None], scores, masked_score)


def attend_forward(allowed):

    def per_head(pieces):
        queries, key_rows, value_rows = pieces
        scores = head_scores(queries, key_rows, allowed)
        largest = jnp.max(scores, axis=-1, keepdims=True)
        raised = jnp.exp(scores - largest)
        total = jnp.sum(raised, axis=-1, keepdims=True)
        weights = (raised / total).astype(jnp.bfloat16)
        mixed_rows = jnp.einsum(
            "gqk,kd->qgd", weights, value_rows, preferred_element_type=jnp.float32
        )
        return (mixed_rows, largest + jnp.log(total))

    return per_head


def attend_backward(allowed):

    def per_head(pieces):
        queries, key_rows, value_rows, log_total, grad_rows = pieces
        scores = head_scores(queries, key_rows, allowed)
        probs = jnp.exp(scores - log_total)
        grad_probs = jnp.einsum(
            "qgd,kd->gqk", grad_rows, value_rows, preferred_element_type=jnp.float32
        )
        centre = jnp.sum(probs * grad_probs, axis=-1, keepdims=True)
        grad_scores = (probs * (grad_probs - centre)).astype(jnp.bfloat16)
        grad_values = jnp.einsum(
            "gqk,qgd->kd", probs.astype(jnp.bfloat16), grad_rows, preferred_element_type=jnp.float32
        )
        grad_queries = (
            jnp.einsum("gqk,kd->qgd", grad_scores, key_rows, preferred_element_type=jnp.float32)
            * score_scale
        )
        grad_keys = (
            jnp.einsum("gqk,qgd->kd", grad_scores, queries, preferred_element_type=jnp.float32)
            * score_scale
        )
        return (grad_queries, grad_keys, grad_values)

    return per_head


def local(
    tokens, cotangent, expert_ids, norm_attn, w_qkv, w_out, norm_moe, w_router, w_gate_up, w_down
):
    groups = lax.axis_size("expert")
    member = lax.axis_index("expert")
    tok_rows = tokens.shape[0] // MICRO
    local_experts = w_gate_up.shape[0]
    prompt_len = PROMPT_DEV * groups
    query_width = HEADS * HEAD_DIM
    key_width = KV_HEADS * HEAD_DIM
    share = HEADS // KV_HEADS
    local_index = jnp.arange(tok_rows, dtype=jnp.int32)
    positions = jnp.where(
        local_index < PROMPT_DEV,
        member * PROMPT_DEV + local_index,
        prompt_len + local_index - PROMPT_DEV,
    )
    cosine, sine_table = rotary_tables(positions.astype(jnp.float32))
    zero_row = jnp.zeros((1, D), jnp.bfloat16)

    def place_heads(query_cols, key_cols):
        return (
            rotate(query_cols.reshape(tok_rows, HEADS, HEAD_DIM), cosine, sine_table),
            rotate(key_cols.reshape(tok_rows, KV_HEADS, HEAD_DIM), cosine, sine_table),
        )

    output_blocks = []
    grad_token_blocks = []
    dense_sums = None
    expert_sums = None
    for micro in range(MICRO):
        row_start = micro * tok_rows
        inputs = tokens[row_start : row_start + tok_rows].astype(jnp.float32)
        block_cot = cotangent[row_start : row_start + tok_rows]
        block_ids = expert_ids[row_start : row_start + tok_rows]
        normed, attn_norm_back = jax.vjp(normalize, inputs, norm_attn)
        normed_low = normed.astype(jnp.bfloat16)
        projected = jnp.dot(normed_low, w_qkv, preferred_element_type=jnp.float32)
        (turned_queries, turned_keys), rotary_back = jax.vjp(
            place_heads,
            projected[:, :query_width],
            projected[:, query_width : query_width + key_width],
        )
        query_low = turned_queries.astype(jnp.bfloat16)
        key_low = turned_keys.astype(jnp.bfloat16).reshape(tok_rows, key_width)
        value_low = projected[:, query_width + key_width :].astype(jnp.bfloat16)
        prompt_keys, prompt_values = (
            lax.all_gather(key_low[:PROMPT_DEV], "expert", axis=0, tiled=True),
            lax.all_gather(value_low[:PROMPT_DEV], "expert", axis=0, tiled=True),
        )
        all_keys = jnp.concatenate([prompt_keys, key_low[PROMPT_DEV:]], axis=0)
        all_values = jnp.concatenate([prompt_values, value_low[PROMPT_DEV:]], axis=0)
        key_count = all_keys.shape[0]
        allowed = jnp.arange(key_count, dtype=jnp.int32)[None, :] <= positions[:, None]
        head_queries = query_low.reshape(tok_rows, KV_HEADS, share, HEAD_DIM).transpose(1, 0, 2, 3)
        head_keys = all_keys.reshape(key_count, KV_HEADS, HEAD_DIM).transpose(1, 0, 2)
        head_values = all_values.reshape(key_count, KV_HEADS, HEAD_DIM).transpose(1, 0, 2)
        head_mixed, log_total = lax.map(
            attend_forward(allowed), (head_queries, head_keys, head_values)
        )
        attended_low = (
            head_mixed.transpose(1, 0, 2, 3).reshape(tok_rows, query_width).astype(jnp.bfloat16)
        )
        hidden = inputs + branch_scale * jnp.dot(
            attended_low, w_out, preferred_element_type=jnp.float32
        )
        normed_moe, moe_norm_back = jax.vjp(normalize, hidden, norm_moe)
        moe_low = normed_moe.astype(jnp.bfloat16)
        logits = jnp.dot(moe_low, w_router, preferred_element_type=jnp.float32)
        flat_ids = block_ids.reshape(-1)
        routed = flat_ids.shape[0]
        one_hot = (flat_ids[:, None] == jnp.arange(EXPERTS, dtype=jnp.int32)[None, :]).astype(
            jnp.int32
        )
        slot_rank = jnp.sum(jnp.cumsum(one_hot, axis=0) * one_hot, axis=1) - 1
        owner = flat_ids // local_experts
        places = (flat_ids % local_experts * groups + owner) * CAP + slot_rank
        slot_table = (
            jnp.full((local_experts * groups * CAP,), routed, dtype=jnp.int32)
            .at[places]
            .set(jnp.arange(routed, dtype=jnp.int32))
        )
        send_rows = jnp.concatenate([moe_low, zero_row], axis=0)[slot_table // TOP].reshape(
            local_experts, groups, CAP, D
        )
        received = lax.all_to_all(
            send_rows, "expert", split_axis=1, concat_axis=1, tiled=True
        ).reshape(local_experts, groups * CAP, D)
        gate_up = jnp.einsum(
            "erd,edf->erf", received, w_gate_up, preferred_element_type=jnp.float32
        )
        middle, swiglu_back = jax.vjp(swiglu, gate_up)
        middle_low = middle.astype(jnp.bfloat16)
        expert_out = jnp.einsum(
            "erf,efd->erd", middle_low, w_down, preferred_element_type=jnp.float32
        ).astype(jnp.bfloat16)
        returned = lax.all_to_all(
            expert_out.reshape(local_experts, groups, CAP, D),
            "expert",
            split_axis=1,
            concat_axis=1,
            tiled=True,
        ).reshape(-1, D)
        picked = returned[places].reshape(tok_rows, TOP, D)
        chosen = jnp.take_along_axis(logits, block_ids, axis=1)
        gate_weights, gate_back = jax.vjp(gate_softmax, chosen)
        mixture = jnp.sum(gate_weights[:, :, None] * picked, axis=1)
        output_blocks.append((hidden + branch_scale * mixture).astype(jnp.bfloat16))
        grad_out_rows = block_cot.astype(jnp.float32)
        grad_mixture = branch_scale * grad_out_rows
        grad_gates = jnp.sum(picked * grad_mixture[:, None, :], axis=-1)
        grad_routed = (
            (gate_weights[:, :, None] * grad_mixture[:, None, :])
            .astype(jnp.bfloat16)
            .reshape(routed, D)
        )
        send_grads = jnp.concatenate([grad_routed, zero_row], axis=0)[slot_table].reshape(
            local_experts, groups, CAP, D
        )
        grads_in = lax.all_to_all(send_grads, "expert", split_axis=1, concat_axis=1, tiled=True)
        grads_in = grads_in.reshape(local_experts, groups * CAP, D)
        grad_middle = jnp.einsum(
            "erd,efd->erf", grads_in, w_down, preferred_element_type=jnp.float32
        )
        grad_down_local = jnp.einsum(
            "erf,erd->efd", middle_low, grads_in, preferred_element_type=jnp.float32
        )
        grad_gate_act = swiglu_back(grad_middle)[0].astype(jnp.bfloat16)
        grad_gate_up_local = jnp.einsum(
            "erd,erf->edf", received, grad_gate_act, preferred_element_type=jnp.float32
        )
        grad_rows = jnp.einsum(
            "erf,edf->erd", grad_gate_act, w_gate_up, preferred_element_type=jnp.float32
        )
        grad_rows = grad_rows.astype(jnp.bfloat16).reshape(local_experts, groups, CAP, D)
        grad_back = lax.all_to_all(
            grad_rows, "expert", split_axis=1, concat_axis=1, tiled=True
        ).reshape(-1, D)
        if expert_sums is None:
            expert_sums = (grad_gate_up_local, grad_down_local)
        else:
            expert_sums = (expert_sums[0] + grad_gate_up_local, expert_sums[1] + grad_down_local)
        grad_chosen = gate_back(grad_gates)[0]
        column_hits = (
            block_ids[:, :, None] == jnp.arange(EXPERTS, dtype=jnp.int32)[None, None, :]
        ).astype(jnp.float32)
        grad_logits = jnp.sum(grad_chosen[:, :, None] * column_hits, axis=1).astype(jnp.bfloat16)
        grad_router = jnp.einsum(
            "rd,re->de", moe_low, grad_logits, preferred_element_type=jnp.float32
        )
        gathered_back = grad_back[places].reshape(tok_rows, TOP, D).astype(jnp.float32)
        grad_normed_moe = jnp.sum(gathered_back, axis=1) + jnp.dot(
            grad_logits, w_router.T, preferred_element_type=jnp.float32
        )
        grad_hidden_norm, grad_norm_moe = moe_norm_back(grad_normed_moe)
        grad_hidden = grad_out_rows + grad_hidden_norm
        grad_branch = (branch_scale * grad_hidden).astype(jnp.bfloat16)
        grad_out = jnp.einsum(
            "rd,re->de", attended_low, grad_branch, preferred_element_type=jnp.float32
        )
        grad_attended = jnp.dot(grad_branch, w_out.T, preferred_element_type=jnp.float32).astype(
            jnp.bfloat16
        )
        head_grads = grad_attended.reshape(tok_rows, KV_HEADS, share, HEAD_DIM).transpose(
            1, 0, 2, 3
        )
        grad_queries, grad_keys, grad_values = lax.map(
            attend_backward(allowed), (head_queries, head_keys, head_values, log_total, head_grads)
        )
        keys_flat = grad_keys.transpose(1, 0, 2).reshape(key_count, key_width)
        values_flat = grad_values.transpose(1, 0, 2).reshape(key_count, key_width)
        prompt_key_grads, prompt_value_grads = (
            lax.psum_scatter(keys_flat[:prompt_len], "expert", scatter_dimension=0, tiled=True),
            lax.psum_scatter(values_flat[:prompt_len], "expert", scatter_dimension=0, tiled=True),
        )
        own_key_grads = jnp.concatenate([prompt_key_grads, keys_flat[prompt_len:]], axis=0)
        own_value_grads = jnp.concatenate([prompt_value_grads, values_flat[prompt_len:]], axis=0)
        queries_flat = grad_queries.transpose(1, 0, 2, 3).reshape(tok_rows, HEADS, HEAD_DIM)
        grad_query_cols, grad_key_cols = rotary_back(
            (queries_flat, own_key_grads.reshape(tok_rows, KV_HEADS, HEAD_DIM))
        )
        grad_projected = jnp.concatenate(
            [grad_query_cols, grad_key_cols, own_value_grads], axis=1
        ).astype(jnp.bfloat16)
        grad_qkv = jnp.einsum(
            "rd,rf->df", normed_low, grad_projected, preferred_element_type=jnp.float32
        )
        grad_normed = jnp.dot(grad_projected, w_qkv.T, preferred_element_type=jnp.float32)
        grad_inputs, grad_norm_attn = attn_norm_back(grad_normed)
        grad_token_blocks.append((grad_hidden + grad_inputs).astype(jnp.bfloat16))
        block_dense = (grad_qkv, grad_out, grad_router, grad_norm_attn, grad_norm_moe)
        if dense_sums is None:
            dense_sums = block_dense
        else:
            dense_sums = tuple((left + right for left, right in zip(dense_sums, block_dense)))
    grad_qkv, grad_out, grad_router, grad_norm_attn, grad_norm_moe = lax.psum(
        (dense_sums[0], dense_sums[1], dense_sums[2], dense_sums[3], dense_sums[4]),
        ("dp", "expert"),
    )
    grad_gate_up_part, grad_down_part = (
        lax.psum_scatter(
            expert_sums[0].astype(jnp.bfloat16), "dp", scatter_dimension=1, tiled=True
        ).astype(jnp.float32),
        lax.psum_scatter(
            expert_sums[1].astype(jnp.bfloat16), "dp", scatter_dimension=1, tiled=True
        ).astype(jnp.float32),
    )
    output = jnp.concatenate(output_blocks, axis=0)
    grad_tokens = jnp.concatenate(grad_token_blocks, axis=0)
    return (
        output,
        grad_tokens,
        grad_norm_attn,
        grad_qkv,
        grad_out,
        grad_norm_moe,
        grad_router,
        grad_gate_up_part,
        grad_down_part,
    )


def solution(mesh):
    in_specs = (
        P(("dp", "expert"), None),
        P(("dp", "expert"), None),
        P(("dp", "expert"), None),
        P(),
        P(),
        P(),
        P(),
        P(),
        P("expert", None, None),
        P("expert", None, None),
    )
    out_specs = (
        P(("dp", "expert"), None),
        P(("dp", "expert"), None),
        P(),
        P(),
        P(),
        P(),
        P(),
        P("expert", "dp", None),
        P("expert", "dp", None),
    )
    return jax.shard_map(local, mesh=mesh, in_specs=in_specs, out_specs=out_specs, check_vma=False)
```

profile of v0, /device:TPU:0, one launch (start us, length us, event | category | flops | bytes accessed | tf_op | source)
XLA Modules:
  0.0 1952.6 jit_solution(5401249178789708607)
XLA Ops:
  47.3 17.9 reduce-window.16
  73.8 10.1 scatter_custom_fusion.1
  143.2 32.5 %while.56 = (s32[]{:T(128)}, bf16[8,320,2,64]{1,3,2,0:T(8,128)(2,1)}, f32[8,2,320,1]{2,1,3,0:T(2,128)S(1)}, bf16[8,512,64]{1,2,0:T(8,128)(2,1)}, bf16[8,512,64]{...) while((s32[]{:T(128)}, ...), condition=%wide.region_4.5_spmd.clone, body=%wide.region_1.4_spmd.clone.sunk | while | flops 86670720 | bytes 4711265 | solution.py:162
  177.6 32.5 %while.57 = (s32[]{:T(128)}, bf16[8,320,2,64]{1,3,2,0:T(8,128)(2,1)}, f32[8,2,320,1]{2,1,3,0:T(2,128)S(1)}, bf16[8,512,64]{1,2,0:T(8,128)(2,1)}, bf16[8,512,64]{...) while((s32[]{:T(128)}, ...), condition=%wide.region_17.19_spmd.clone, body=%wide.region_14.18_spmd.clone.sunk | while | flops 86670720 | bytes 4711265 | solution.py:162
  215.8 20.9 %gather_fusion.9 = f32[2560]{0:T(1024)S(1)} fusion(f32[320,32]{0,1:T(8,128)S(1)} %fusion.227, s32[2560]{0:T(1024)S(1)} %reshape.834), kind=kCustom, calls=%fused_computation.1.clone | custom fusion | bytes 40960 | tf_op jit(solution)/shard_map/jit(take_along_axis)/gather | solution.py:209
  236.9 20.9 %gather_fusion.8 = f32[2560]{0:T(1024)S(1)} fusion(f32[320,32]{0,1:T(8,128)S(1)} %fusion.226, s32[2560]{0:T(1024)S(1)} %reshape.829), kind=kCustom, calls=%fused_computation.clone | custom fusion | bytes 40960 | tf_op jit(solution)/shard_map/jit(take_along_axis)/gather | solution.py:209
  267.2 18.4 gather_fusion.6
  285.6 8.7 reshape.709
  294.3 9.3 copy.258
  313.0 17.9 reduce-window.14
  342.2 9.9 scatter_custom_fusion
  352.2 18.6 gather_fusion.4
  379.1 9.4 copy.250
  394.1 11.0 gather_fusion
  413.4 9.4 copy.227
  422.8 44.7 %all-to-all-done.4 = bf16[8,4,100,1024]{3,0,2,1:T(8,128)(2,1)} async-done(((bf16[8,4,100,1024]{3,0,2,1:T(8,128)(2,1)}), bf16[8,4,100,1024]{3,0,2,1:T(8,128)(2,1)}, u32[]{:S(2)}, u32[]{:S(2)}) %all-to-all-start.4) | async-done | bytes 6553632 | tf_op jit(solution)/shard_map/all_to_all | solution.py:224
  472.9 11.0 gather_fusion.2
  492.2 9.3 copy.245
  501.5 44.7 %all-to-all-done = bf16[8,4,100,1024]{3,0,2,1:T(8,128)(2,1)} async-done(((bf16[8,4,100,1024]{3,0,2,1:T(8,128)(2,1)}), bf16[8,4,100,1024]{3,0,2,1:T(8,128)(2,1)}, u32[]{:S(2)}, u32[]{:S(2)}) %all-to-all-start) | async-done | bytes 6553632 | tf_op jit(solution)/shard_map/all_to_all | solution.py:190
  552.0 23.4 %fusion.118 = f32[8,400,1024]{2,1,0:T(8,128)} fusion(bf16[8,1024,1024]{2,1,0:T(8,128)(2,1)} %param.28, bf16[8,400,1024]{2,0,1:T(8,128)(2,1)} %bitcast.17), kind=kOutput, calls=%fused_computation.178 | convolution fusion | flops 6710886400 | bytes 36438016 | tf_op jit(solution)/shard_map/erd,edf->erf/dot_general | solution.py:193
  575.4 21.7 %fusion.152 = (f32[8,400,512]{2,1,0:T(8,128)}, f32[8,400,512]{2,1,0:T(8,128)}, bf16[8,400,512]{2,1,0:T(8,128)(2,1)}) fusion(f32[8,400,1024]{2,1,0:T(8,128)} %fusion.118, bf16[8,512,1024]{2,1,0:T(8,128)(2,1)} %param.29, bf16[8,400,1024]{2,0,1:T(8,128)(2,1)} %bitcast.41), kind=kOutput, calls=%fused_computation.271 | convolution fusion | flops 3378380800 | bytes 44433408 | tf_op jit(solution)/shard_map/erd,efd->erf/dot_general | solution.py:226
  597.0 19.7 %convolution_convert_fusion.1 = bf16[8,400,1024]{2,1,0:T(8,128)(2,1)} fusion(bf16[8,1024,1024]{2,1,0:T(8,128)(2,1)} %param.28, f32[8,400,512]{2,1,0:T(8,128)} %get-tuple-element.386, f32[8,400,512]{2,1,0:T(8,128)} %get-tuple-element.385), kind=kOutput, calls=%fused_computation.163 | convolution fusion | flops 6720716800 | bytes 36438016 | tf_op jit(solution)/shard_map/erf,edf->erd/dot_general | solution.py:236
  616.8 9.2 copy.252
  645.6 59.2 %all-to-all-done.5 = bf16[8,4,100,1024]{3,0,2,1:T(8,128)(2,1)} async-done(((bf16[8,4,100,1024]{3,0,2,1:T(8,128)(2,1)}), bf16[8,4,100,1024]{3,0,2,1:T(8,128)(2,1)}, u32[]{:S(2)}, u32[]{:S(2)}) %all-to-all-start.5) | async-done | bytes 6553632 | tf_op jit(solution)/shard_map/all_to_all | solution.py:240
  710.4 23.4 %fusion.114 = f32[8,400,1024]{2,1,0:T(8,128)} fusion(bf16[8,1024,1024]{2,1,0:T(8,128)(2,1)} %param.28, bf16[8,400,1024]{2,0,1:T(8,128)(2,1)} %bitcast.37), kind=kOutput, calls=%fused_computation.174 | convolution fusion | flops 6710886400 | bytes 36438016 | tf_op jit(solution)/shard_map/erd,edf->erf/dot_general | solution.py:193
  733.8 21.7 %fusion.153 = (f32[8,400,512]{2,1,0:T(8,128)}, f32[8,400,512]{2,1,0:T(8,128)}, bf16[8,400,512]{2,1,0:T(8,128)(2,1)}) fusion(f32[8,400,1024]{2,1,0:T(8,128)} %fusion.114, bf16[8,512,1024]{2,1,0:T(8,128)(2,1)} %param.29, bf16[8,400,1024]{2,0,1:T(8,128)(2,1)} %bitcast.60), kind=kOutput, calls=%fused_computation.272 | convolution fusion | flops 3378380800 | bytes 44433408 | tf_op jit(solution)/shard_map/erd,efd->erf/dot_general | solution.py:226
  755.5 19.7 %convolution_convert_fusion = bf16[8,400,1024]{2,1,0:T(8,128)(2,1)} fusion(bf16[8,1024,1024]{2,1,0:T(8,128)(2,1)} %param.28, f32[8,400,512]{2,1,0:T(8,128)} %get-tuple-element.388, f32[8,400,512]{2,1,0:T(8,128)} %get-tuple-element.387), kind=kOutput, calls=%fused_computation.162 | convolution fusion | flops 6720716800 | bytes 36438016 | tf_op jit(solution)/shard_map/erf,edf->erd/dot_general | solution.py:236
  775.2 9.2 copy.260
  804.2 59.1 %all-to-all-done.7 = bf16[8,4,100,1024]{3,0,2,1:T(8,128)(2,1)} async-done(((bf16[8,4,100,1024]{3,0,2,1:T(8,128)(2,1)}), bf16[8,4,100,1024]{3,0,2,1:T(8,128)(2,1)}, u32[]{:S(2)}, u32[]{:S(2)}) %all-to-all-start.7) | async-done | bytes 6553632 | tf_op jit(solution)/shard_map/all_to_all | solution.py:240
  868.9 9.4 copy.253
  878.4 8.8 reshape.704
  887.1 9.4 copy.230
  896.6 8.4 reshape.690
  905.0 15.8 gather_fusion.5
  920.8 15.9 gather_fusion.1
  945.6 9.4 copy.261
  963.4 15.9 gather_fusion.7
  992.5 9.6 copy.248
  1010.5 15.9 gather_fusion.3
  1048.5 70.3 %while.58 = (s32[]{:T(128)}, f32[8,320,2,64]{1,3,2,0:T(8,128)}, f32[8,512,64]{1,2,0:T(8,128)S(1)}, f32[8,512,64]{1,2,0:T(8,128)}, bf16[8,512,64]{1,2,0:T(8,128)(...) while((s32[]{:T(128)}, f32[8,320,2,64]{1,3,2,0:T(8,128)}, ...), condition=%wide.region_33.35_spmd.clone, body=%wide.region_31.34_spmd.clone.sunk | while | flops 212901248 | bytes 11225977 | solution.py:271
  1133.7 76.0 %while.59 = (s32[]{:T(128)}, f32[8,320,2,64]{1,3,2,0:T(8,128)}, f32[8,512,64]{1,2,0:T(8,128)}, f32[8,512,64]{1,2,0:T(8,128)}, bf16[8,512,64]{1,2,0:T(8,128)(2,1)...) while((s32[]{:T(128)}, f32[8,320,2,64]{1,3,2,0:T(8,128)}, ...), condition=%wide.region_44.46_spmd.clone, body=%wide.region_42.45_spmd.clone.sunk | while | flops 212901248 | bytes 11225977 | solution.py:271
  1214.0 18.4 fusion.109
  1235.4 24.4 %add_convert_fusion.1 = bf16[8,512,1024]{2,1,0:T(8,128)(2,1)} fusion(f32[8,512,1024]{2,1,0:T(8,128)} %fusion.109, bf16[8,400,512]{2,1,0:T(8,128)(2,1)} %get-tuple-element.390, bf16[8,400,1024]{2,0,1:T(8,128)(2,1)} %bitcast.60), kind=kOutput, calls=%fused_computation.133 | convolution fusion | flops 3363831808 | bytes 34996224 | tf_op jit(solution)/shard_map/erf,erd->efd/dot_general | solution.py:229
  1259.8 21.6 %fusion.116 = f32[8,1024,1024]{2,1,0:T(8,128)} fusion(bf16[8,400,1024]{2,0,1:T(8,128)(2,1)} %bitcast.17, f32[8,400,512]{2,1,0:T(8,128)} %get-tuple-element.386, f32[8,400,512]{2,1,0:T(8,128)} %get-tuple-element.385), kind=kOutput, calls=%fused_computation.176 | convolution fusion | flops 6717440000 | bytes 53215232 | tf_op jit(solution)/shard_map/erd,erf->edf/dot_general | solution.py:233
  1281.4 29.3 %add_convert_fusion = bf16[8,1024,1024]{2,1,0:T(8,128)(2,1)} fusion(f32[8,1024,1024]{2,1,0:T(8,128)} %fusion.116, bf16[8,400,1024]{2,0,1:T(8,128)(2,1)} %bitcast.37, f32[8,400,512]{2,1,0:T(8,128)} %get-tuple-element.388, f32[8,400,512]{2,1,0:T(8,128)} %get-tuple-element.387), kind=kOutput, calls=%fused_computation.132 | convolution fusion | flops 6734217216 | bytes 69992448 | tf_op jit(solution)/shard_map/erd,erf->edf/dot_general | solution.py:233
  1359.1 43.7 %all-reduce.16 = (f32[1024]{0:T(1024)}, f32[1024]{0:T(1024)}) all-reduce(f32[1024]{0:T(1024)S(1)} %add.411, f32[1024]{0:T(1024)S(1)} %add.414), channel_id=1, replica_groups=mesh['dp'=8,'expert'=4] {'dp','expert'}, use_global_device_ids=true, to_apply=%region_50.52 | all-reduce | flops 2048 | bytes 16384 | tf_op jit(solution)/shard_map/psum | solution.py:300
  1416.3 279.3 %reduce-scatter.15.cloned.1.call-done = bf16[8,128,1024]{2,1,0:T(8,128)(2,1)} async-done(((bf16[8,1024,1024]{2,1,0:T(8,128)(2,1)}), bf16[8,128,1024]{2,1,0:T(8,128)(2,1)}) %reduce-scatter.15.cloned.1.call-update) | async-done | bytes 2097168 | tf_op jit(solution)/shard_map/reduce_scatter | solution.py:305
  1699.7 234.9 %all-reduce.20.cloned.1.call-done = (f32[1024,2048]{1,0:T(8,128)}, f32[1024,1024]{1,0:T(8,128)}, f32[1024,32]{0,1:T(8,128)}) async-done(((f32[1024,2048]{1,0:T(8,128)}, f32[1024,1024]{1,0:T(8,128)}, f32[1024,32]{0,1:T(8,128)}), (f32[1024,2048]{1,0:T(8,128)}, f32[1024,1024]{1,0:T(8,128)}, f32[1024,32]{0,1:T(8,128)})) %all-reduce.20.cloned.1.call-update) | async-done | bytes 12714000 | tf_op jit(solution)/shard_map/psum | solution.py:300
  (680 shorter events, 606.5 us)
Async XLA Ops:
  7.2 202.9 %copy-start = (bf16[1024,1024]{1,0:T(8,128)(2,1)S(1)}, bf16[1024,1024]{1,0:T(8,128)(2,1)}, u32[]{:S(2)}) copy-start(bf16[1024,1024]{1,0:T(8,128)(2,1)} %param.25) | copy-start | bytes 6291460
  7.2 9.3 copy-start.1
  9.6 7.3 copy-start.83
  16.9 7.3 copy-start.115
  29.5 110.6 %copy-start.47 = (f32[320,64]{0,1:T(8,128)}, f32[320,64]{0,1:T(8,128)S(1)}, u32[]{:S(2)}) copy-start(f32[320,64]{0,1:T(8,128)S(1)} %pad_maximum_fusion.6) | copy-start | bytes 245764
  84.5 10.4 copy-start.65
  100.7 8.5 copy-start.66
  236.9 22.7 %copy-start.79 = (s32[640,8]{0,1:T(8,128)S(1)}, s32[640,8]{0,1:T(8,128)}, u32[]{:S(2)}) copy-start(s32[640,8]{0,1:T(8,128)} %param.22) | copy-start | bytes 61444
  236.9 25.2 %copy-start.17 = (f32[320,1024]{1,0:T(8,128)S(1)}, f32[320,1024]{1,0:T(8,128)}, u32[]{:S(2)}) copy-start(f32[320,1024]{1,0:T(8,128)} %get-tuple-element.408) | copy-start | bytes 3932164
  259.7 74.5 %copy-start.77 = (f32[320,8]{0,1:T(8,128)}, f32[320,8]{0,1:T(8,128)S(1)}, u32[]{:S(2)}) copy-start(f32[320,8]{0,1:T(8,128)S(1)} %get-tuple-element.374) | copy-start | bytes 30724
  259.7 74.5 %copy-start.94 = (f32[320]{0:T(512)}, f32[320]{0:T(512)S(1)}, u32[]{:S(2)}) copy-start(f32[320]{0:T(512)S(1)} %get-tuple-element.373) | copy-start | bytes 3844
  303.7 84.8 %all-to-all-start.6 = ((bf16[8,4,100,1024]{3,0,2,1:T(8,128)(2,1)}), bf16[8,4,100,1024]{3,0,2,1:T(8,128)(2,1)}, u32[]{:S(2)}, u32[]{:S(2)}) async-start(bf16[8,4,100,1024]{3,0,2,1:T(8,128)(2,1)} %copy.258), calls=%async_computation.6 | async-start | bytes 13107200 | tf_op jit(solution)/shard_map/all_to_all | solution.py:224
  310.1 26.1 %copy-start.19 = (f32[320,1024]{1,0:T(8,128)S(1)}, f32[320,1024]{1,0:T(8,128)}, u32[]{:S(2)}) copy-start(f32[320,1024]{1,0:T(8,128)} %get-tuple-element.407) | copy-start | bytes 3932164
  388.5 79.0 %all-to-all-start.4 = ((bf16[8,4,100,1024]{3,0,2,1:T(8,128)(2,1)}), bf16[8,4,100,1024]{3,0,2,1:T(8,128)(2,1)}, u32[]{:S(2)}, u32[]{:S(2)}) async-start(bf16[8,4,100,1024]{3,0,2,1:T(8,128)(2,1)} %copy.250), calls=%async_computation.4 | async-start | bytes 13107200 | tf_op jit(solution)/shard_map/all_to_all | solution.py:224
  422.8 50.0 %copy-start.25 = (bf16[320,1024]{1,0:T(8,128)(2,1)S(1)}, bf16[320,1024]{1,0:T(8,128)(2,1)}, u32[]{:S(2)}) copy-start(bf16[320,1024]{1,0:T(8,128)(2,1)} %copy-done.24) | copy-start | bytes 1966084
  422.8 50.0 %copy-start.89 = (s32[3200]{0:T(1024)S(1)}, s32[3200]{0:T(1024)}, u32[]{:S(2)}) copy-start(s32[3200]{0:T(1024)} %get-tuple-element.442) | copy-start | bytes 38404
  467.5 78.8 %all-to-all-start = ((bf16[8,4,100,1024]{3,0,2,1:T(8,128)(2,1)}), bf16[8,4,100,1024]{3,0,2,1:T(8,128)(2,1)}, u32[]{:S(2)}, u32[]{:S(2)}) async-start(bf16[8,4,100,1024]{3,0,2,1:T(8,128)(2,1)} %copy.227), calls=%async_computation | async-start | bytes 13107200 | tf_op jit(solution)/shard_map/all_to_all | solution.py:190
  546.3 79.7 %all-to-all-start.2 = ((bf16[8,4,100,1024]{3,0,2,1:T(8,128)(2,1)}), bf16[8,4,100,1024]{3,0,2,1:T(8,128)(2,1)}, u32[]{:S(2)}, u32[]{:S(2)}) async-start(bf16[8,4,100,1024]{3,0,2,1:T(8,128)(2,1)} %copy.245), calls=%async_computation.2 | async-start | bytes 13107200 | tf_op jit(solution)/shard_map/all_to_all | solution.py:190
  625.9 78.8 %all-to-all-start.5 = ((bf16[8,4,100,1024]{3,0,2,1:T(8,128)(2,1)}), bf16[8,4,100,1024]{3,0,2,1:T(8,128)(2,1)}, u32[]{:S(2)}, u32[]{:S(2)}) async-start(bf16[8,4,100,1024]{3,0,2,1:T(8,128)(2,1)} %bitcast.448), calls=%async_computation.5 | async-start | bytes 13107200 | tf_op jit(solution)/shard_map/all_to_all | solution.py:240
  704.7 79.7 %all-to-all-start.1 = ((bf16[8,4,100,1024]{3,0,2,1:T(8,128)(2,1)}), bf16[8,4,100,1024]{3,0,2,1:T(8,128)(2,1)}, u32[]{:S(2)}, u32[]{:S(2)}) async-start(bf16[8,4,100,1024]{3,0,2,1:T(8,128)(2,1)} %bitcast.447), calls=%async_computation.1 | async-start | bytes 13107200 | tf_op jit(solution)/shard_map/all_to_all | solution.py:201
  784.4 78.9 %all-to-all-start.7 = ((bf16[8,4,100,1024]{3,0,2,1:T(8,128)(2,1)}), bf16[8,4,100,1024]{3,0,2,1:T(8,128)(2,1)}, u32[]{:S(2)}, u32[]{:S(2)}) async-start(bf16[8,4,100,1024]{3,0,2,1:T(8,128)(2,1)} %bitcast.449), calls=%async_computation.7 | async-start | bytes 13107200 | tf_op jit(solution)/shard_map/all_to_all | solution.py:240
  863.3 129.2 %all-to-all-start.3 = ((bf16[8,4,100,1024]{3,0,2,1:T(8,128)(2,1)}), bf16[8,4,100,1024]{3,0,2,1:T(8,128)(2,1)}, u32[]{:S(2)}, u32[]{:S(2)}) async-start(bf16[8,4,100,1024]{3,0,2,1:T(8,128)(2,1)} %bitcast.446), calls=%async_computation.3 | async-start | bytes 13107200 | tf_op jit(solution)/shard_map/all_to_all | solution.py:201
  868.8 459.0 %reduce-scatter.19.cloned.1.call-start = ((), (), s32[]{:S(2)}) async-start(), calls=%async_computation.16 | async-start | bytes 655360
  920.8 15.9 copy-start.20
  936.7 8.9 copy-start.78
  936.7 8.9 copy-start.95
  963.4 16.0 copy-start.86
  979.5 7.9 copy-start.7
  1010.5 15.9 copy-start.18
  1026.4 9.0 copy-start.76
  1026.4 9.0 copy-start.93
  1026.4 9.1 copy-start.84
  1026.4 9.2 copy-start.62
  1122.0 206.9 %reduce-scatter.21.cloned.1.call-start = ((), (), s32[]{:S(2)}) async-start(), calls=%async_computation.17 | async-start | bytes 655360
  1130.1 200.6 %reduce-scatter.23.cloned.1.call-start = ((), (), s32[]{:S(2)}) async-start(), calls=%async_computation.18 | async-start | bytes 655360
  1214.0 118.4 %reduce-scatter.25.cloned.1.call-start = ((), (), s32[]{:S(2)}) async-start(), calls=%async_computation.19 | async-start | bytes 655360
  1214.0 18.4 copy-start.40
  1235.3 178.2 %reduce-scatter.17.cloned.1.call-start = ((), (), s32[]{:S(2)}) async-start(), calls=%async_computation.15 | async-start | bytes 9437184 | tf_op jit(solution)/shard_map/reduce_scatter | solution.py:308
  1259.7 435.9 %reduce-scatter.15.cloned.1.call-start = ((), (), s32[]{:S(2)}) async-start(), calls=%async_computation.14 | async-start | bytes 18874368 | tf_op jit(solution)/shard_map/reduce_scatter | solution.py:305
  1310.8 7.3 copy-start.50
  1310.8 623.8 %all-reduce.20.cloned.1.call-start = ((), (), s32[]{:S(2)}) async-start(), calls=%async_computation.20 | async-start | bytes 25427968 | tf_op jit(solution)/shard_map/psum | solution.py:300
  1311.1 7.0 copy-start.15
  1327.8 6.3 copy-start.34
  1327.8 6.3 copy-start.36
  1328.9 6.7 copy-start.51
  1355.5 47.3 %copy-start.116 = (f32[320]{0:T(512)S(1)}, f32[320]{0:T(512)}, u32[]{:S(2)}) copy-start(f32[320]{0:T(512)} %copy-done.115) | copy-start | bytes 3844
  1355.6 47.3 %copy-start.118 = (f32[320]{0:T(512)S(1)}, f32[320]{0:T(512)}, u32[]{:S(2)}) copy-start(f32[320]{0:T(512)} %copy-done.117) | copy-start | bytes 3844
  1934.6 8.0 copy-start.38
  (88 other events, 228.9 us)
Sparse Core Ops, SparseCore 0:
  1122.1 23.2 reduce-scatter.18
  1147.9 21.6 reduce-scatter.20
  1214.1 23.3 reduce-scatter.22
  1239.8 21.6 reduce-scatter.24
  1265.0 148.4 reduce-scatter.16
  1417.2 278.4 reduce-scatter.14
  1702.6 231.9 all-reduce.19
where the time goes:
time: 1970 us; the launch traced here: 1950 us
  waiting for transfers between devices  728 us (37%)
  local copies, waits for them, and re-layouts  490 us (25%)
  matrix products  465 us (24%)
  other arithmetic  136 us (7%)
  blocking collectives  71.5 us (4%)
  starting transfers between devices  44.3 us (2%)
    reduce_scatter x1, waiting for transfers between devices, local(): lax.psum_scatter(expert_sums[0].astype(jnp.bfloat16), 'dp', scatter_dimen...  279 us
    psum x1, waiting for transfers between devices, local(): lax.psum((dense_sums[0], dense_sums[1], dense_sums[2], dense_sums[3], den...  235 us
    all_to_all x2, waiting for transfers between devices, local(): lax.all_to_all(grad_rows, 'expert', split_axis=1, concat_axis=1, tiled=True)  118 us
    dot_general x2, matrix products, local(): jnp.einsum('erd,erf->edf', received, grad_gate_act, preferred_element_typ...  51 us
    dot_general x32, matrix products, head_scores(): jnp.einsum('qgd,kd->gqk', queries, key_rows, preferred_element_type=jnp.f...  49.7 us
    gather x10, local copies, waits for them, and re-layouts, local(): chosen = jnp.take_along_axis(logits, block_ids, axis=1)  47.4 us
    dot_general x2, matrix products, local(): jnp.einsum('erd,edf->erf', received, w_gate_up, preferred_element_type=jn...  46.7 us
    all_to_all x2, waiting for transfers between devices, local(): lax.all_to_all(send_rows, 'expert', split_axis=1, concat_axis=1, tiled=True)  44.7 us
  transfers between devices with their start and end apart: 15, of which 7 were waited for; matrix products, arithmetic and copies ran while one was open for 35% of the time, Pallas kernels for 0%

commit v1 on v0

v1 whole, which is shorter than its diff:
```python
import functools

import jax
import jax.numpy as jnp
from jax import lax
from jax.experimental import pallas as pl
from jax.experimental.pallas import tpu as pltpu
from jax.sharding import PartitionSpec as P

D = 1024
HEADS = 16
KV_HEADS = 8
HEAD_DIM = 64
FF = 512
EXPERTS = 32
TOP = 8
PROMPT_DEV = 64
MICRO = 2
CAP = 100
SLOTS = 112
CHUNKS = (2, 2, 2, 1, 1)


epsilon = 1e-06
score_scale = 1.0 / 64.0
branch_scale = 0.22
masked_score = -1e30

f32 = jnp.float32
bf16 = jnp.bfloat16
vmem_limit = 60 * 1024 * 1024


def params():
    return pltpu.CompilerParams(
        vmem_limit_bytes=vmem_limit, dimension_semantics=("arbitrary",)
    )


def mm(left, right, dims):
    return lax.dot_general(left, right, (dims, ((), ())), preferred_element_type=f32)


def fill_one_hot(slot_rows, onehot_ref):
    experts, rows = slot_rows.shape
    place = lax.broadcasted_iota(jnp.int32, (SLOTS, rows), 0)
    for e in range(experts):
        hit = place == slot_rows[e : e + 1, :]
        onehot_ref[e * SLOTS : (e + 1) * SLOTS, :] = jnp.where(hit, 1.0, 0.0).astype(bf16)


def chosen_of(ids, count):
    rows = ids.shape[1]
    label = lax.broadcasted_iota(jnp.int32, (count, rows), 0)
    hit = ids[0:1, :] == label
    for k in range(1, ids.shape[0]):
        hit = hit | (ids[k : k + 1, :] == label)
    return hit


def select_block(row_refs, rows_ref):
    b = pl.program_id(0)
    at = 0
    for ref in row_refs:
        for i in range(ref.shape[0]):

            @pl.when(b == at)
            def _(ref=ref, i=i):
                rows_ref[...] = ref[i]

            at += 1


def store_picked(onehot_ref, rows_ref, out_ref):
    picked = mm(onehot_ref[...], rows_ref[...], ((1,), (0,))).astype(bf16)
    for e in range(out_ref.shape[0]):
        out_ref[e, 0] = picked[e * SLOTS : (e + 1) * SLOTS]


def pick_grad_body(*refs, pieces):
    ids_ref = refs[0]
    row_refs = refs[1 : 1 + pieces]
    out_ref, slot_ref, onehot_ref, rows_ref, earlier_ref = refs[1 + pieces :]
    experts, rows = slot_ref.shape[1], slot_ref.shape[2]

    @pl.when(pl.program_id(0) == 0)
    def _():
        first = lax.broadcasted_iota(jnp.int32, (rows, rows), 0)
        second = lax.broadcasted_iota(jnp.int32, (rows, rows), 1)
        earlier_ref[...] = jnp.where(first < second, 1.0, 0.0).astype(bf16)

    select_block(row_refs, rows_ref)
    hit = chosen_of(ids_ref[0], 8)
    rank = mm(jnp.where(hit, 1.0, 0.0).astype(bf16), earlier_ref[...], ((1,), (0,)))
    slots = jnp.where(hit, rank, -1.0).astype(jnp.int32)[:experts]
    slot_ref[0] = slots
    fill_one_hot(slots, onehot_ref)
    store_picked(onehot_ref, rows_ref, out_ref)


def full_spec(array):
    zeros = (0,) * array.ndim
    return pl.BlockSpec(array.shape, lambda *_: zeros)


def pick_grads(ids, pieces, experts):
    blocks, top, tok = ids.shape
    return pl.pallas_call(
        functools.partial(pick_grad_body, pieces=len(pieces)),
        grid=(blocks,),
        in_specs=[pl.BlockSpec((1, top, tok), lambda b: (b, 0, 0))]
        + [full_spec(piece) for piece in pieces],
        out_specs=[
            pl.BlockSpec((experts, 1, SLOTS, D), lambda b: (0, b, 0, 0)),
            pl.BlockSpec((1, experts, tok), lambda b: (b, 0, 0)),
        ],
        out_shape=[
            jax.ShapeDtypeStruct((experts, blocks, SLOTS, D), bf16),
            jax.ShapeDtypeStruct((blocks, experts, tok), jnp.int32),
        ],
        scratch_shapes=[
            pltpu.VMEM((experts * SLOTS, tok), bf16),
            pltpu.VMEM((tok, D), bf16),
            pltpu.VMEM((tok, tok), bf16),
        ],
        compiler_params=params(),
    )(ids, *pieces)


def pick_token_body(*refs, pieces):
    ids_ref, slot_ref, router_ref = refs[:3]
    row_refs = refs[3 : 3 + pieces]
    out_ref, slot_gate_ref, gate_ref, onehot_ref, rows_ref = refs[3 + pieces :]
    experts, rows = slot_ref.shape[1], slot_ref.shape[2]
    select_block(row_refs, rows_ref)
    logits = mm(router_ref[...], rows_ref[...], ((0,), (1,)))
    hit = chosen_of(ids_ref[0], EXPERTS)
    masked = jnp.where(hit, logits, masked_score)
    raised = jnp.where(hit, jnp.exp(masked - jnp.max(masked, axis=0, keepdims=True)), 0.0)
    gates = raised / jnp.sum(raised, axis=0, keepdims=True)
    gate_ref[0] = gates
    fill_one_hot(slot_ref[0], onehot_ref)
    store_picked(onehot_ref, rows_ref, out_ref)
    place = lax.broadcasted_iota(jnp.int32, (SLOTS, rows), 0)
    for e in range(experts):
        here = place == slot_ref[0, e : e + 1, :]
        gate = jnp.sum(jnp.where(here, gates[e : e + 1, :], 0.0), axis=1, keepdims=True)
        slot_gate_ref[e, 0] = jnp.broadcast_to(gate, (SLOTS, 128))


def pick_tokens(ids, slots, w_router, pieces):
    blocks, experts, tok = slots.shape
    return pl.pallas_call(
        functools.partial(pick_token_body, pieces=len(pieces)),
        grid=(blocks,),
        in_specs=[
            pl.BlockSpec((1, ids.shape[1], tok), lambda b: (b, 0, 0)),
            pl.BlockSpec((1, experts, tok), lambda b: (b, 0, 0)),
            full_spec(w_router),
        ]
        + [full_spec(piece) for piece in pieces],
        out_specs=[
            pl.BlockSpec((experts, 1, SLOTS, D), lambda b: (0, b, 0, 0)),
            pl.BlockSpec((experts, 1, SLOTS, 128), lambda b: (0, b, 0, 0)),
            pl.BlockSpec((1, EXPERTS, tok), lambda b: (b, 0, 0)),
        ],
        out_shape=[
            jax.ShapeDtypeStruct((experts, blocks, SLOTS, D), bf16),
            jax.ShapeDtypeStruct((experts, blocks, SLOTS, 128), f32),
            jax.ShapeDtypeStruct((blocks, EXPERTS, tok), f32),
        ],
        scratch_shapes=[pltpu.VMEM((experts * SLOTS, tok), bf16), pltpu.VMEM((tok, D), bf16)],
        compiler_params=params(),
    )(ids, slots, w_router, *pieces)


def sum_rows_body(*refs, chunks, with_dots):
    slot_ref = refs[0]
    row_refs = refs[1 : 1 + chunks]
    refs = refs[1 + chunks :]
    if with_dots:
        dot_refs, refs = refs[:chunks], refs[chunks:]
        out_ref, back_ref, onehot_ref, flat_ref = refs
    else:
        out_ref, onehot_ref, flat_ref = refs
    fill_one_hot(slot_ref[0], onehot_ref)
    e = 0
    for ref in row_refs:
        for i in range(ref.shape[0]):
            flat_ref[e * SLOTS : (e + 1) * SLOTS, :] = ref[i, 0]
            e += 1
    out_ref[0] = mm(onehot_ref[...], flat_ref[...], ((0,), (0,))).astype(bf16)
    if with_dots:
        place = lax.broadcasted_iota(jnp.int32, (SLOTS, slot_ref.shape[2]), 0)
        e = 0
        for ref in dot_refs:
            for i in range(ref.shape[0]):
                hit = place == slot_ref[0, e : e + 1, :]
                back_ref[0, e : e + 1, :] = jnp.sum(
                    jnp.where(hit, ref[i, 0, :, 0:1], 0.0), axis=0, keepdims=True
                )
                e += 1


def sum_rows(slots, rows, dots=None):
    blocks, experts, tok = slots.shape

    def chunk_spec(chunk):
        return pl.BlockSpec((chunk.shape[0], 1) + chunk.shape[2:], lambda b: (0, b, 0, 0))

    in_specs = [pl.BlockSpec((1, experts, tok), lambda b: (b, 0, 0))]
    in_specs += [chunk_spec(chunk) for chunk in rows]
    args = [slots] + rows
    out_shape = [jax.ShapeDtypeStruct((blocks, tok, D), bf16)]
    out_specs = [pl.BlockSpec((1, tok, D), lambda b: (b, 0, 0))]
    if dots is not None:
        in_specs += [chunk_spec(chunk) for chunk in dots]
        args += dots
        out_shape.append(jax.ShapeDtypeStruct((blocks, experts, tok), f32))
        out_specs.append(pl.BlockSpec((1, experts, tok), lambda b: (b, 0, 0)))
    return pl.pallas_call(
        functools.partial(sum_rows_body, chunks=len(rows), with_dots=dots is not None),
        grid=(blocks,),
        in_specs=in_specs,
        out_specs=out_specs,
        out_shape=out_shape,
        scratch_shapes=[
            pltpu.VMEM((experts * SLOTS, tok), bf16),
            pltpu.VMEM((experts * SLOTS, D), bf16),
        ],
        compiler_params=params(),
    )(*args)


def expert_body(
    parity_ref,
    x_ref,
    d_ref,
    gate_ref,
    wgu_ref,
    wd_ref,
    out_ref,
    back_ref,
    dots_ref,
    *part_refs,
    tile,
):
    mid_ref, grad_ref, act_ref, gu_ref, down_ref = part_refs[-5:]
    part_refs = part_refs[:-5]
    rows = x_ref.shape[1]

    def step(i, carry):
        span = pl.ds(pl.multiple_of(i * tile, tile), tile)
        hidden = mm(x_ref[0, span, :], wgu_ref[0], ((1,), (0,)))
        gate, up = hidden[:, :FF], hidden[:, FF:]
        sig = 1.0 / (1.0 + jnp.exp(-gate))
        silu = gate * sig
        middle = (silu * up).astype(bf16)
        mid_ref[span, :] = middle
        out = mm(middle, wd_ref[0], ((1,), (0,))).astype(bf16).astype(f32)
        weight = gate_ref[0, span, 0:1]
        scaled = branch_scale * d_ref[0, span, :].astype(f32)
        dots_ref[0, span, :] = jnp.broadcast_to(
            jnp.sum(scaled * out, axis=1, keepdims=True), (tile, 128)
        )
        out_ref[0, span, :] = (weight * out).astype(bf16)
        grad = (weight * scaled).astype(bf16)
        grad_ref[span, :] = grad
        grad_mid = mm(grad, wd_ref[0], ((1,), (1,)))
        act_ref[span, :FF] = (grad_mid * up * sig * (1.0 + gate * (1.0 - sig))).astype(bf16)
        act_ref[span, FF:] = (grad_mid * silu).astype(bf16)
        back_ref[0, span, :] = mm(act_ref[span, :], wgu_ref[0], ((1,), (1,))).astype(bf16)
        return carry

    lax.fori_loop(0, rows // tile, step, 0)
    gu_ref[...] = mm(x_ref[0], act_ref[...], ((0,), (0,))).astype(bf16)
    down_ref[...] = mm(mid_ref[...], grad_ref[...], ((0,), (0,))).astype(bf16)
    parity = parity_ref[0]
    pairs = part_refs[0].shape[1]
    half = (gu_ref.shape[0] + down_ref.shape[0]) // (2 * pairs)
    keep_ref, send_ref = part_refs[0], part_refs[-1]
    shift = half if len(part_refs) == 1 else 0
    start = 0
    for full in (gu_ref, down_ref):
        piece = full.shape[0] // (2 * pairs)
        for j in range(pairs):
            mine = pl.multiple_of((2 * j + parity) * piece, piece)
            other = pl.multiple_of((2 * j + 1 - parity) * piece, piece)
            keep_ref[0, j, start : start + piece, :] = full[pl.ds(mine, piece), :]
            send_ref[0, j, shift + start : shift + start + piece, :] = full[pl.ds(other, piece), :]
        start += piece


def expert_chunk(parity, first, count, pairs, split, x_rows, d_rows, slot_gate, w_gate_up, w_down):
    rows = x_rows.shape[1]
    tile = 2 * SLOTS
    mode = pl.Buffered(1 if rows > 1024 else 2)
    row_spec = pl.BlockSpec((1, rows, D), lambda e, p: (e + first, 0, 0), pipeline_mode=mode)
    col_spec = pl.BlockSpec((1, rows, 128), lambda e, p: (e + first, 0, 0))
    parts = 2 if split else 1
    piece = (D + FF) // (parts * pairs)
    part_spec = pl.BlockSpec((1, pairs, piece, D), lambda e, p: (e, 0, 0, 0))
    part_shape = jax.ShapeDtypeStruct((count, pairs, piece, D), bf16)
    out_row = pl.BlockSpec((1, rows, D), lambda e, p: (e, 0, 0))
    grid_spec = pltpu.PrefetchScalarGridSpec(
        num_scalar_prefetch=1,
        grid=(count,),
        in_specs=[
            row_spec,
            row_spec,
            col_spec,
            pl.BlockSpec((1, D, 2 * FF), lambda e, p: (e + first, 0, 0)),
            pl.BlockSpec((1, FF, D), lambda e, p: (e + first, 0, 0)),
        ],
        out_specs=[
            out_row,
            out_row,
            pl.BlockSpec((1, rows, 128), lambda e, p: (e, 0, 0)),
        ]
        + [part_spec] * parts,
        scratch_shapes=[
            pltpu.VMEM((rows, FF), bf16),
            pltpu.VMEM((rows, D), bf16),
            pltpu.VMEM((rows, 2 * FF), bf16),
            pltpu.VMEM((D, 2 * FF), bf16),
            pltpu.VMEM((FF, D), bf16),
        ],
    )
    return pl.pallas_call(
        functools.partial(expert_body, tile=tile),
        grid_spec=grid_spec,
        out_shape=[
            jax.ShapeDtypeStruct((count, rows, D), bf16),
            jax.ShapeDtypeStruct((count, rows, D), bf16),
            jax.ShapeDtypeStruct((count, rows, 128), f32),
        ]
        + [part_shape] * parts,
        compiler_params=params(),
    )(parity, x_rows, d_rows, slot_gate, w_gate_up, w_down)


def core_swap(value, groups):
    return lax.ppermute(value, "expert", [(m, m ^ 1) for m in range(groups)])


def from_row(value, groups, shift):
    count = groups // 2
    pairs = [((((y + shift) % count) * 2 + c), y * 2 + c) for y in range(count) for c in range(2)]
    return lax.ppermute(value, "expert", pairs)


def to_row(value, groups, shift):
    count = groups // 2
    pairs = [(y * 2 + c, ((y + shift) % count) * 2 + c) for y in range(count) for c in range(2)]
    return lax.ppermute(value, "expert", pairs)


def gather_members(value, groups):
    column = [value] + [from_row(value, groups, s) for s in range(1, groups // 2)]
    result = []
    for piece in column:
        result += [piece, core_swap(piece, groups)]
    return result


def return_members(pieces, groups):
    swapped = [core_swap(pieces[2 * s + 1], groups) for s in range(groups // 2)]
    terms = [pieces[0], swapped[0]]
    for s in range(1, groups // 2):
        both = (pieces[2 * s].astype(f32) + swapped[s].astype(f32)).astype(bf16)
        terms.append(to_row(both, groups, s))
    return terms


def exchange_members(pieces, groups):
    count = groups // 2
    result = []
    for s in range(count):
        for c in range(2):
            if s == 0 and c == 0:
                result.append(pieces[0])
                continue
            pairs = [
                (((y - s) % count) * 2 + (core ^ c), y * 2 + core)
                for y in range(count)
                for core in range(2)
            ]
            result.append(lax.ppermute(pieces[2 * s + c], "expert", pairs))
    return result


def lane(shape):
    return lax.broadcasted_iota(jnp.int32, shape, len(shape) - 1)


def turn(value, cosine, sine, sign):
    first = lax.rem(lane(value.shape), HEAD_DIM) < HEAD_DIM // 2
    other = jnp.where(
        first, pltpu.roll(value, 128 - HEAD_DIM // 2, 1), pltpu.roll(value, HEAD_DIM // 2, 1)
    )
    return value * cosine + sign * other * sine


def project_body(x_ref, gain_ref, w_ref, cos_ref, sin_ref, normed_ref, q_ref, kv_ref):
    x = x_ref[0].astype(f32)
    scale = lax.rsqrt(jnp.mean(x * x, axis=1, keepdims=True) + epsilon)
    normed = (x * scale * gain_ref[...]).astype(bf16)
    normed_ref[0] = normed
    cosine, sine = cos_ref[...], sin_ref[...]
    q_width, k_width = HEADS * HEAD_DIM, KV_HEADS * HEAD_DIM
    for start in range(0, q_width + 2 * k_width, 512):
        part = mm(normed, w_ref[:, start : start + 512], ((1,), (0,)))
        for inner in range(0, 512, 128):
            at = start + inner
            value = part[:, inner : inner + 128]
            if at < q_width:
                q_ref[0, :, at : at + 128] = turn(value, cosine, sine, 1.0).astype(bf16)
            elif at < q_width + k_width:
                at -= q_width
                kv_ref[0, :, at : at + 128] = turn(value, cosine, sine, 1.0).astype(bf16)
            else:
                at -= q_width
                kv_ref[0, :, at : at + 128] = value.astype(bf16)


def project(tokens, gain, w_qkv, cosine, sine):
    micro, rows, _ = tokens.shape
    block = pl.BlockSpec((1, rows, D), lambda m: (m, 0, 0))
    table = pl.BlockSpec((rows, 128), lambda m: (0, 0))
    shape = jax.ShapeDtypeStruct((micro, rows, D), bf16)
    return pl.pallas_call(
        project_body,
        grid=(micro,),
        in_specs=[
            block,
            pl.BlockSpec((1, D), lambda m: (0, 0)),
            pl.BlockSpec(w_qkv.shape, lambda m: (0, 0)),
            table,
            table,
        ],
        out_specs=[block, block, block],
        out_shape=[shape, shape, shape],
        compiler_params=params(),
    )(tokens, gain, w_qkv, cosine, sine)


def stack_heads(block, scale):
    wide = block.astype(f32) * scale
    result = []
    for p in range(2):
        part = wide[:, p * 128 : (p + 1) * 128]
        half = (lane(part.shape) >= HEAD_DIM) == (p == 1)
        for h in range(2):
            moved = part if h == p else pltpu.roll(part, HEAD_DIM, 1)
            result.append(jnp.where(half, moved, 0.0).astype(bf16))
    return jnp.concatenate(result, axis=0)


def unstack_heads(stacked, rows):
    result = []
    for p in range(2):
        pieces = []
        for h in range(2):
            i = 2 * p + h
            part = stacked[i * rows : (i + 1) * rows]
            pieces.append(part if h == p else pltpu.roll(part, HEAD_DIM, 1))
        result.append(jnp.where(lane(pieces[0].shape) < HEAD_DIM, pieces[0], pieces[1]))
    return result


def attend_body(
    q_ref, pk_ref, pv_ref, ok_ref, ov_ref, bias_ref, x_ref, w_ref, gain_ref,
    att_ref, lse_ref, hidden_ref, low_ref, all_ref,
):
    j = pl.program_id(0)
    rows = q_ref.shape[1]
    q = stack_heads(q_ref[0], score_scale)
    k = jnp.concatenate([pk_ref[0], ok_ref[0, PROMPT_DEV:, :]], axis=0)
    v = jnp.concatenate([pv_ref[0], ov_ref[0, PROMPT_DEV:, :]], axis=0)
    scores = mm(k, q, ((1,), (1,))) + bias_ref[...]
    largest = jnp.max(scores, axis=0, keepdims=True)
    raised = jnp.exp(scores - largest)
    total = jnp.sum(raised, axis=0, keepdims=True)
    weights = (raised * (1.0 / total)).astype(bf16)
    lse_ref[0] = largest + jnp.log(total)
    mixed = mm(v, weights, ((0,), (0,))).T
    for p, part in enumerate(unstack_heads(mixed, rows)):
        at = pl.multiple_of(j * 256 + p * 128, 128)
        att_ref[0, :, p * 128 : (p + 1) * 128] = part.astype(bf16)
        all_ref[:, pl.ds(at, 128)] = part.astype(bf16)

    @pl.when(j == pl.num_programs(0) - 1)
    def _():
        branch = mm(all_ref[...], w_ref[...], ((1,), (0,)))
        hidden = x_ref[0].astype(f32) + branch_scale * branch
        hidden_ref[0] = hidden
        scale = lax.rsqrt(jnp.mean(hidden * hidden, axis=1, keepdims=True) + epsilon)
        low_ref[0] = (hidden * scale * gain_ref[...]).astype(bf16)


def attend(micro, q, kv, prompt, bias, tokens, w_out, gain):
    rows, prompt_rows = q.shape[1], prompt.shape[1]
    steps = KV_HEADS // 2
    full = pl.BlockSpec((1, rows, D), lambda j: (micro, 0, 0))
    one = pl.BlockSpec((1, rows, D), lambda j: (0, 0, 0))
    return pl.pallas_call(
        attend_body,
        grid=(steps,),
        in_specs=[
            pl.BlockSpec((1, rows, 256), lambda j: (micro, 0, j)),
            pl.BlockSpec((1, prompt_rows, 128), lambda j: (micro, 0, j)),
            pl.BlockSpec((1, prompt_rows, 128), lambda j: (micro, 0, j + steps)),
            pl.BlockSpec((1, rows, 128), lambda j: (micro, 0, j)),
            pl.BlockSpec((1, rows, 128), lambda j: (micro, 0, j + steps)),
            pl.BlockSpec(bias.shape, lambda j: (0, 0)),
            full,
            pl.BlockSpec(w_out.shape, lambda j: (0, 0)),
            pl.BlockSpec((1, D), lambda j: (0, 0)),
        ],
        out_specs=[
            pl.BlockSpec((1, rows, 256), lambda j: (0, 0, j)),
            pl.BlockSpec((1, 1, 4 * rows), lambda j: (j, 0, 0)),
            one,
            one,
        ],
        out_shape=[
            jax.ShapeDtypeStruct((1, rows, D), bf16),
            jax.ShapeDtypeStruct((steps, 1, 4 * rows), f32),
            jax.ShapeDtypeStruct((1, rows, D), f32),
            jax.ShapeDtypeStruct((1, rows, D), bf16),
        ],
        scratch_shapes=[pltpu.VMEM((rows, D), bf16)],
        compiler_params=params(),
    )(q, prompt, prompt, kv, kv, bias, tokens, w_out, gain)


def norm_back(value, gain, grad):
    scale = lax.rsqrt(jnp.mean(value * value, axis=1, keepdims=True) + epsilon)
    scaled = grad * gain
    inner = jnp.mean(scaled * value, axis=1, keepdims=True)
    back = scale * scaled - value * (scale * scale * scale * inner)
    return back, jnp.sum(grad * value * scale, axis=0, keepdims=True)


def middle_body(*refs, terms):
    term_refs = refs[:terms]
    (logit_ref, router_ref, hidden_ref, gain_ref, cot_ref, w_ref) = refs[terms : terms + 6]
    grad_hidden_ref, branch_ref, att_ref, gain_out_ref = refs[terms + 6 :]
    total = mm(logit_ref[0], router_ref[...], ((0,), (1,)))
    for ref in term_refs:
        total = total + ref[0].astype(f32)
    back, gain_grad = norm_back(hidden_ref[0], gain_ref[...], total)
    grad_hidden = cot_ref[0].astype(f32) + back
    grad_hidden_ref[0] = grad_hidden
    branch = (branch_scale * grad_hidden).astype(bf16)
    branch_ref[0] = branch
    att_ref[0] = mm(branch, w_ref[...], ((1,), (1,))).astype(bf16)

    @pl.when(pl.program_id(0) == 0)
    def _():
        gain_out_ref[...] = gain_grad

    @pl.when(pl.program_id(0) != 0)
    def _():
        gain_out_ref[...] += gain_grad


def middle_back(terms, grad_logits, w_router, hidden, gain, cotangent, w_out):
    micro, rows, _ = hidden.shape
    block = pl.BlockSpec((1, rows, D), lambda m: (m, 0, 0))
    row = pl.BlockSpec((1, D), lambda m: (0, 0))
    return pl.pallas_call(
        functools.partial(middle_body, terms=len(terms)),
        grid=(micro,),
        in_specs=[block] * len(terms)
        + [
            pl.BlockSpec((1, EXPERTS, rows), lambda m: (m, 0, 0)),
            pl.BlockSpec(w_router.shape, lambda m: (0, 0)),
            block,
            row,
            block,
            pl.BlockSpec(w_out.shape, lambda m: (0, 0)),
        ],
        out_specs=[block, block, block, row],
        out_shape=[
            jax.ShapeDtypeStruct((micro, rows, D), f32),
            jax.ShapeDtypeStruct((micro, rows, D), bf16),
            jax.ShapeDtypeStruct((micro, rows, D), bf16),
            jax.ShapeDtypeStruct((1, D), f32),
        ],
        compiler_params=params(),
    )(*terms, grad_logits, w_router, hidden, gain, cotangent, w_out)


def attend_back_body(
    q_ref, pk_ref, pv_ref, ok_ref, ov_ref, bias_ref, lse_ref, grad_ref, cos_ref, sin_ref,
    gq_ref, gpk_ref, gpv_ref, gok_ref, gov_ref,
):
    rows, prompt_rows = q_ref.shape[1], pk_ref.shape[1]
    q = stack_heads(q_ref[0], score_scale)
    grad = stack_heads(grad_ref[0], 1.0)
    k = jnp.concatenate([pk_ref[0], ok_ref[0, PROMPT_DEV:, :]], axis=0)
    v = jnp.concatenate([pv_ref[0], ov_ref[0, PROMPT_DEV:, :]], axis=0)
    probs = jnp.exp(mm(k, q, ((1,), (1,))) + bias_ref[...] - lse_ref[0, 0])
    grad_probs = mm(v, grad, ((1,), (1,)))
    centre = jnp.sum(probs * grad_probs, axis=0, keepdims=True)
    grad_scores = (probs * (grad_probs - centre)).astype(bf16)
    grad_v = mm(probs.astype(bf16), grad, ((1,), (0,)))
    grad_k = mm(grad_scores, q, ((1,), (0,)))
    grad_q = mm(k, grad_scores, ((0,), (0,))).T * score_scale
    cosine, sine = cos_ref[...], sin_ref[...]
    for p, part in enumerate(unstack_heads(grad_q, rows)):
        gq_ref[0, :, p * 128 : (p + 1) * 128] = turn(part, cosine, sine, -1.0).astype(bf16)
    gpk_ref[0] = grad_k[:prompt_rows].astype(bf16)
    gpv_ref[0] = grad_v[:prompt_rows].astype(bf16)
    gok_ref[0] = turn(
        grad_k[prompt_rows:], cosine[PROMPT_DEV:], sine[PROMPT_DEV:], -1.0
    ).astype(bf16)
    gov_ref[0] = grad_v[prompt_rows:].astype(bf16)


def attend_back(q, kv, prompt, bias, lse, grad, cosine, sine):
    micro, rows, _ = q.shape
    prompt_rows = prompt.shape[1]
    own_rows = rows - PROMPT_DEV
    steps = KV_HEADS // 2
    wide = pl.BlockSpec((1, rows, 256), lambda m, j: (m, 0, j))
    table = pl.BlockSpec((rows, 128), lambda m, j: (0, 0))
    prompt_spec = pl.BlockSpec((1, prompt_rows, 128), lambda m, j: (m, 0, j))
    own_spec = pl.BlockSpec((1, own_rows, 128), lambda m, j: (m, 0, j))
    k_width = KV_HEADS * HEAD_DIM
    return pl.pallas_call(
        attend_back_body,
        grid=(micro, steps),
        in_specs=[
            wide,
            prompt_spec,
            pl.BlockSpec((1, prompt_rows, 128), lambda m, j: (m, 0, j + steps)),
            pl.BlockSpec((1, rows, 128), lambda m, j: (m, 0, j)),
            pl.BlockSpec((1, rows, 128), lambda m, j: (m, 0, j + steps)),
            pl.BlockSpec(bias.shape, lambda m, j: (0, 0)),
            pl.BlockSpec((1, 1, 1, 4 * rows), lambda m, j: (m, j, 0, 0)),
            wide,
            table,
            table,
        ],
        out_specs=[wide, prompt_spec, prompt_spec, own_spec, own_spec],
        out_shape=[
            jax.ShapeDtypeStruct((micro, rows, D), bf16),
            jax.ShapeDtypeStruct((micro, prompt_rows, k_width), bf16),
            jax.ShapeDtypeStruct((micro, prompt_rows, k_width), bf16),
            jax.ShapeDtypeStruct((micro, own_rows, k_width), bf16),
            jax.ShapeDtypeStruct((micro, own_rows, k_width), bf16),
        ],
        compiler_params=pltpu.CompilerParams(
            vmem_limit_bytes=vmem_limit, dimension_semantics=("arbitrary", "arbitrary")
        ),
    )(q, prompt, prompt, kv, kv, bias, lse, grad, cosine, sine)


def weight_body(*refs, terms):
    normed_ref, gq_ref, gok_ref, gov_ref = refs[:4]
    k_terms, v_terms = refs[4 : 4 + terms], refs[4 + terms : 4 + 2 * terms]
    cos_ref, sin_ref, gp_ref, out_ref, acc_ref = refs[4 + 2 * terms :]
    q_width, k_width = HEADS * HEAD_DIM, KV_HEADS * HEAD_DIM
    gp_ref[0, :, :q_width] = gq_ref[0]
    gp_ref[0, PROMPT_DEV:, q_width : q_width + k_width] = gok_ref[0]
    gp_ref[0, PROMPT_DEV:, q_width + k_width :] = gov_ref[0]
    prompt_k, prompt_v = [sum(ref[0].astype(f32) for ref in group) for group in (k_terms, v_terms)]
    cosine, sine = cos_ref[:PROMPT_DEV, :], sin_ref[:PROMPT_DEV, :]
    for at in range(0, k_width, 128):
        turned = turn(prompt_k[:, at : at + 128], cosine, sine, -1.0)
        gp_ref[0, :PROMPT_DEV, q_width + at : q_width + at + 128] = turned.astype(bf16)
    gp_ref[0, :PROMPT_DEV, q_width + k_width :] = prompt_v.astype(bf16)
    part = mm(normed_ref[0], gp_ref[0], ((0,), (0,)))
    m = pl.program_id(0)

    @pl.when(m == 0)
    def _():
        acc_ref[...] = part

    @pl.when(m != 0)
    def _():
        acc_ref[...] += part

    @pl.when(m == pl.num_programs(0) - 1)
    def _():
        out_ref[...] = acc_ref[...].astype(bf16)


def weight_back(normed, gq, gok, gov, k_terms, v_terms, cosine, sine):
    micro, rows, _ = normed.shape
    k_width = KV_HEADS * HEAD_DIM
    wide = pl.BlockSpec((1, rows, D), lambda m: (m, 0, 0))
    own = pl.BlockSpec((1, rows - PROMPT_DEV, k_width), lambda m: (m, 0, 0))
    term = pl.BlockSpec((1, PROMPT_DEV, k_width), lambda m: (m, 0, 0))
    table = pl.BlockSpec((rows, 128), lambda m: (0, 0))
    return pl.pallas_call(
        functools.partial(weight_body, terms=len(k_terms)),
        grid=(micro,),
        in_specs=[wide, wide, own, own] + [term] * (2 * len(k_terms)) + [table, table],
        out_specs=[
            pl.BlockSpec((1, rows, 2 * D), lambda m: (m, 0, 0)),
            pl.BlockSpec((D, 2 * D), lambda m: (0, 0)),
        ],
        out_shape=[
            jax.ShapeDtypeStruct((micro, rows, 2 * D), bf16),
            jax.ShapeDtypeStruct((D, 2 * D), bf16),
        ],
        scratch_shapes=[pltpu.VMEM((D, 2 * D), f32)],
        compiler_params=params(),
    )(normed, gq, gok, gov, *k_terms, *v_terms, cosine, sine)


def token_body(gp_ref, w_ref, x_ref, gain_ref, hidden_ref, out_ref, gain_out_ref):
    grad = mm(gp_ref[0], w_ref[...], ((1,), (1,)))
    back, gain_grad = norm_back(x_ref[0].astype(f32), gain_ref[...], grad)
    out_ref[0] = (hidden_ref[0] + back).astype(bf16)

    @pl.when(pl.program_id(0) == 0)
    def _():
        gain_out_ref[...] = gain_grad

    @pl.when(pl.program_id(0) != 0)
    def _():
        gain_out_ref[...] += gain_grad


def token_back(gp, w_qkv, tokens, gain, grad_hidden):
    micro, rows, _ = tokens.shape
    block = pl.BlockSpec((1, rows, D), lambda m: (m, 0, 0))
    row = pl.BlockSpec((1, D), lambda m: (0, 0))
    return pl.pallas_call(
        token_body,
        grid=(micro,),
        in_specs=[
            pl.BlockSpec((1, rows, 2 * D), lambda m: (m, 0, 0)),
            pl.BlockSpec(w_qkv.shape, lambda m: (0, 0)),
            block,
            row,
            block,
        ],
        out_specs=[block, row],
        out_shape=[
            jax.ShapeDtypeStruct((micro, rows, D), bf16),
            jax.ShapeDtypeStruct((1, D), f32),
        ],
        compiler_params=params(),
    )(gp, w_qkv, tokens, gain, grad_hidden)


def after(value, *others):
    return lax.optimization_barrier((value,) + others)[0]


def local(
    tokens, cotangent, expert_ids, norm_attn, w_qkv, w_out, norm_moe, w_router, w_gate_up, w_down
):
    groups = lax.axis_size("expert")
    dp_size = lax.axis_size("dp")
    member = lax.axis_index("expert")
    dp_index = lax.axis_index("dp")
    rows_all = tokens.shape[0]
    tok_rows = rows_all // MICRO
    local_experts = w_gate_up.shape[0]
    prompt_len = PROMPT_DEV * groups
    k_width = KV_HEADS * HEAD_DIM
    pairs = dp_size // 2
    blocks = groups * MICRO
    attn_gain = norm_attn.reshape(1, D)
    moe_gain = norm_moe.reshape(1, D)
    token_rows = tokens.reshape(MICRO, tok_rows, D)
    cot_rows = cotangent.reshape(MICRO, tok_rows, D)

    local_index = jnp.arange(tok_rows, dtype=jnp.int32)
    positions = jnp.where(
        local_index < PROMPT_DEV,
        member * PROMPT_DEV + local_index,
        prompt_len + local_index - PROMPT_DEV,
    )
    half_dim = HEAD_DIM // 2
    inverse = 10000.0 ** (-2.0 * jnp.arange(half_dim, dtype=f32) / HEAD_DIM)
    angles = positions.astype(f32)[:, None] * inverse[None, :]
    cosine = jnp.tile(jnp.cos(angles), (1, 128 // half_dim))
    sine = jnp.tile(jnp.sin(angles), (1, 128 // half_dim))
    sine = jnp.where(jnp.arange(128)[None, :] % HEAD_DIM < half_dim, -sine, sine)
    rows_of = []
    for s in range(groups // 2):
        for c in range(2):
            place = lax.rem(member // 2 + s, groups // 2) * 2 + lax.rem(member + c, 2)
            rows_of.append(place * PROMPT_DEV + jnp.arange(PROMPT_DEV, dtype=jnp.int32))
    key_positions = jnp.concatenate(
        rows_of + [prompt_len + jnp.arange(tok_rows - PROMPT_DEV, dtype=jnp.int32)]
    )
    bias = jnp.where(
        key_positions[:, None] <= jnp.tile(positions, HEADS // (KV_HEADS // 2))[None, :],
        0.0,
        masked_score,
    )

    normed, queries, key_value = project(token_rows, attn_gain, w_qkv, cosine, sine)
    prompt = jnp.concatenate(gather_members(key_value[:, :PROMPT_DEV], groups), axis=1)

    first_expert = member * local_experts
    ids_t = gather_members(expert_ids.reshape(MICRO, tok_rows, TOP).transpose(0, 2, 1), groups)
    ids_all = lax.rem(jnp.concatenate(ids_t, axis=0) + (EXPERTS - first_expert), EXPERTS)
    cot_pieces = gather_members(cot_rows, groups)
    router = lax.dynamic_slice_in_dim(
        jnp.concatenate([w_router, w_router], axis=1), first_expert, EXPERTS, 1
    )

    attended, lse, hidden, moe_pieces, moe_low = [], [], [], [], []
    for m in range(MICRO):
        mask = bias if m == 0 else after(bias, *cot_pieces)
        att, log_total, hid, low = attend(
            m, queries, key_value, prompt, mask, token_rows, w_out, moe_gain
        )
        attended.append(att)
        lse.append(log_total[None])
        hidden.append(hid)
        moe_low.append(low)
        moe_pieces.append(gather_members(low, groups))
    d_rows, slots = pick_grads(ids_all, cot_pieces, local_experts)
    attended = jnp.concatenate(attended, axis=0)
    lse = jnp.concatenate(lse, axis=0)
    hidden = jnp.concatenate(hidden, axis=0)
    moe_low = jnp.concatenate(moe_low, axis=0)

    x_rows, slot_gate, gates = pick_tokens(
        ids_all, slots, router, [moe_pieces[m][g] for g in range(groups) for m in range(MICRO)]
    )
    slot_rows = blocks * SLOTS
    x_rows = x_rows.reshape(local_experts, slot_rows, D)
    d_rows = d_rows.reshape(local_experts, slot_rows, D)
    slot_gate = slot_gate.reshape(local_experts, slot_rows, 128)
    parity = lax.rem(dp_index, 2).astype(jnp.int32).reshape(1)
    swap_x = [(d, d ^ 1) for d in range(dp_size)]
    z_groups = [[d for d in range(dp_size) if d % 2 == r] for r in range(2)]
    piece = (D + FF) // (2 * pairs)

    def sum_z(value):
        count, _, height, _ = value.shape
        return lax.psum_scatter(
            value.reshape(count, pairs * height, D),
            "dp",
            scatter_dimension=1,
            axis_index_groups=z_groups,
            tiled=True,
        )

    outs, backs, dots, parts, pending = [], [], [], [], []
    first = 0
    for count in CHUNKS if sum(CHUNKS) == local_experts else (1,) * local_experts:
        split = first > 0
        out, back, dot, *sums = expert_chunk(
            parity, first, count, pairs, split, x_rows, d_rows, slot_gate, w_gate_up, w_down
        )
        shape = (count, blocks, SLOTS)
        outs.append(out.reshape(shape + (D,)))
        backs.append(back.reshape(shape + (D,)))
        dots.append(dot.reshape(shape + (128,)))
        if split:
            pending.append((sums[0], lax.ppermute(sums[1], "dp", swap_x)))
        else:
            whole = sum_z(sums[0])
        first += count

    def reduce_next():
        keep, got = pending.pop(0)
        half = (keep.astype(f32) + got.astype(f32)).astype(bf16)
        parts.append(sum_z(half))
        return half

    back_sum, back_dots = sum_rows(after(slots, reduce_next()), backs, dots)

    def pieces_of(value):
        return [value[j * MICRO : (j + 1) * MICRO] for j in range(groups)]

    back_terms = return_members(pieces_of(back_sum), groups)
    dot_pieces = exchange_members(pieces_of(back_dots), groups)
    token_dots = jnp.zeros((MICRO, EXPERTS, tok_rows), f32)
    for s in range(groups // 2):
        for c in range(2):
            place = lax.rem(member // 2 + groups // 2 - s, groups // 2) * 2 + lax.rem(
                member + c, 2
            )
            label = lax.rem(place + groups - member, groups) * local_experts
            token_dots = lax.dynamic_update_slice_in_dim(
                token_dots, dot_pieces[2 * s + c], label, 1
            )
    own_gates = gates[:MICRO]
    centre = jnp.sum(own_gates * token_dots, axis=1, keepdims=True)
    grad_logits = (own_gates * (token_dots - centre)).astype(bf16)
    (mixed,) = sum_rows(after(slots, back_sum), outs)
    mix_terms = return_members(pieces_of(mixed), groups)

    grad_hidden, grad_branch, grad_attended, grad_norm_moe = middle_back(
        back_terms, grad_logits, router, hidden, moe_gain, after(cot_rows, mixed), w_out
    )
    grad_router = jnp.einsum("btd,bet->de", moe_low, grad_logits, preferred_element_type=f32)
    grad_out = jnp.einsum("brd,bre->de", attended, grad_branch, preferred_element_type=f32)
    gq, gpk, gpv, gok, gov = attend_back(
        queries, key_value, prompt, bias, lse, grad_attended, cosine, sine
    )
    def prompt_terms(value):
        return return_members(
            [value[:, j * PROMPT_DEV : (j + 1) * PROMPT_DEV] for j in range(groups)], groups
        )

    gp, grad_qkv = weight_back(
        after(normed, reduce_next()), gq, gok, gov, prompt_terms(gpk), prompt_terms(gpv), cosine, sine
    )
    grad_tokens, grad_norm_attn = token_back(gp, w_qkv, token_rows, attn_gain, grad_hidden)
    while pending:
        reduce_next()
    swapped = lax.ppermute(whole[:, piece:], "dp", swap_x)
    whole = (whole[:, :piece].astype(f32) + swapped.astype(f32)).astype(bf16)
    parts.insert(0, whole)
    grad_router = lax.dynamic_slice_in_dim(
        jnp.concatenate([grad_router, grad_router], axis=1), EXPERTS - first_expert, EXPERTS, 1
    )
    mixture = sum(term.astype(f32) for term in mix_terms)
    output = (hidden + branch_scale * mixture).astype(bf16)

    small = jnp.concatenate(
        [
            grad_router,
            grad_norm_attn.reshape(D, 1),
            grad_norm_moe.reshape(D, 1),
            jnp.zeros((D, 128 - EXPERTS - 2), f32),
        ],
        axis=1,
    )
    wide = jnp.concatenate([grad_qkv, grad_out.astype(bf16), small.astype(bf16)], axis=1)
    wide = lax.psum(wide, ("dp", "expert")).astype(f32)
    experts_sum = jnp.concatenate(parts, axis=0).astype(f32)
    gu_piece = D // (2 * pairs)
    return (
        output.reshape(rows_all, D),
        grad_tokens.reshape(rows_all, D),
        wide[:, 3 * D + EXPERTS],
        wide[:, : 2 * D],
        wide[:, 2 * D : 3 * D],
        wide[:, 3 * D + EXPERTS + 1],
        wide[:, 3 * D : 3 * D + EXPERTS],
        experts_sum[:, :gu_piece],
        experts_sum[:, gu_piece:],
    )


def solution(mesh):
    in_specs = (
        P(("dp", "expert"), None),
        P(("dp", "expert"), None),
        P(("dp", "expert"), None),
        P(),
        P(),
        P(),
        P(),
        P(),
        P("expert", None, None),
        P("expert", None, None),
    )
    out_specs = (
        P(("dp", "expert"), None),
        P(("dp", "expert"), None),
        P(),
        P(),
        P(),
        P(),
        P(),
        P("expert", "dp", None),
        P("expert", "dp", None),
    )
    return jax.shard_map(local, mesh=mesh, in_specs=in_specs, out_specs=out_specs, check_vma=False)
```

time: 1970 us -> 784 us (0.40)
  matrix products: 465 us -> 4.22 us
  local copies, waits for them, and re-layouts: 490 us -> 49.9 us
  waiting for transfers between devices: 728 us -> 374 us
  Pallas kernels: 0 us -> 260 us
  other arithmetic: 136 us -> 43.1 us
  blocking collectives: 71.5 us -> 0 us
    dot_general x142 -> x2, matrix products: 465 us -> 4.22 us  [the longest x1 3.56 us: local(): jnp.einsum('brd,bre->de', attended, grad_branch, preferred_element_type=f32)]
    reduce_scatter x2 -> x5, waiting for transfers between devices: 286 us -> 0.09 us  [sum_z(): lax.psum_scatter(value.reshape(count, pairs * height, D), 'dp', scatter_d...]
    pallas_call x0 -> x16, Pallas kernels: none -> 260 us  [the longest x5 123 us: expert_chunk(): pl.pallas_call(functools.partial(expert_body, tile=tile), grid_spec=grid_...]
    ppermute x0 -> x35, waiting for transfers between devices: none -> 215 us  [the longest x4 117 us: local(): pending.append((sums[0], lax.ppermute(sums[1], 'dp', swap_x)))]
    all_to_all x8 -> x0, waiting for transfers between devices: 208 us -> none  [the longest x2 118 us: local(): lax.all_to_all(grad_rows, 'expert', split_axis=1, concat_axis=1, tiled=True)]
    gather x18 -> x0, local copies, waits for them, and re-layouts: 170 us -> none  [the longest x10 47.4 us: local(): chosen = jnp.take_along_axis(logits, block_ids, axis=1)]
    reshape x14 -> x4, local copies, waits for them, and re-layouts: 107 us -> 0.5 us  [the longest x1 0.21 us: local(): grad_norm_moe.reshape(D, 1)]
    psum x1, waiting for transfers between devices: 235 us -> 157 us  [local(): wide = lax.psum(wide, ('dp', 'expert')).astype(f32)]
  transfers between devices with their start and end apart: 15 -> 41, of which waited for: 7 -> 15; matrix products, arithmetic and copies ran while one was open for 35% -> 12% of each run, Pallas kernels for 0% -> 28%
where the time goes in v1:
time: 784 us; the launch traced here: 774 us
  waiting for transfers between devices  374 us (48%)
  Pallas kernels  260 us (33%)
  local copies, waits for them, and re-layouts  49.9 us (6%)
  other arithmetic  43.1 us (5%)
  starting transfers between devices  26.1 us (3%)
  between operations  16.3 us (2%)
    psum x1, waiting for transfers between devices, local(): wide = lax.psum(wide, ('dp', 'expert')).astype(f32)  157 us
    pallas_call x5, Pallas kernels, expert_chunk(): pl.pallas_call(functools.partial(expert_body, tile=tile), grid_spec=grid_...  123 us
    ppermute x4, waiting for transfers between devices, local(): pending.append((sums[0], lax.ppermute(sums[1], 'dp', swap_x)))  117 us
    ppermute x5, waiting for transfers between devices, from_row(): return lax.ppermute(value, 'expert', pairs)  54.4 us
    ppermute x4, waiting for transfers between devices, to_row(): return lax.ppermute(value, 'expert', pairs)  43.1 us
    pallas_call x2, Pallas kernels, sum_rows(): pl.pallas_call(functools.partial(sum_rows_body, chunks=len(rows), with_do...  25.8 us
    pallas_call x2, Pallas kernels, attend(): pl.pallas_call(attend_body, grid=(steps,), in_specs=[pl.BlockSpec((1, row...  23 us
    pallas_call x1, Pallas kernels, attend_back(): pl.pallas_call(attend_back_body, grid=(micro, steps), in_specs=[wide, pro...  22.8 us
  transfers between devices with their start and end apart: 41, of which 15 were waited for; matrix products, arithmetic and copies ran while one was open for 12% of the time, Pallas kernels for 28%

profile of v1, /device:TPU:0, one launch (start us, length us, event | category | flops | bytes accessed | tf_op | source)
XLA Modules:
  0.0 774.0 jit_solution(10095714712556608208)
XLA Ops:
  8.1 3.1 collective-permute-start.4
  11.4 28.7 %collective-permute-done.4.refs_3_ = bf16[2,320,1024]{2,1,0:T(8,128)(2,1)S(1)} collective-permute-done((bf16[2,320,1024]{2,1,0:T(8,128)(2,1)}, bf16[2,320,1024]{2,1,0:T(8,128)(2,1)S(1)}, u32[]{:S(2)}, u32[]{:S(2)}) %collective-permute-start.4) | collective-permute-done | bytes 1310752 | tf_op jit(solution)/shard_map/ppermute | solution.py:349
  41.9 6.7 shard_map.169
  51.6 6.6 collective-permute-done.1
  61.0 11.3 %shard_map.170 = (bf16[1,320,1024]{2,1,0:T(8,128)(2,1)}, f32[4,1,1280]{2,1,0:T(1,128)}, f32[1,320,1024]{2,1,0:T(8,128)}, bf16[1,320,1024]{2,1,0:T(8,128)(2,1)}) custom-call(bf16[2,320,1024]{2,1,0:T(8,128)(2,1)} %get-tuple-element.69.q_ref, bf16[2,256,1024]{2,1,0:T(8,128)(2,1)} %pad_maximum_fusion.pk_ref.pv_ref, ...), custom_call_target="tpu_custom_call" | custom-call | tf_op jit(solution)/shard_map/pallas_call | solution.py:506
  74.2 11.7 %shard_map.171 = (bf16[1,320,1024]{2,1,0:T(8,128)(2,1)}, f32[4,1,1280]{2,1,0:T(1,128)}, f32[1,320,1024]{2,1,0:T(8,128)}, bf16[1,320,1024]{2,1,0:T(8,128)(2,1)}) custom-call(bf16[2,320,1024]{2,1,0:T(8,128)(2,1)} %get-tuple-element.69.q_ref, bf16[2,256,1024]{2,1,0:T(8,128)(2,1)} %pad_maximum_fusion.pk_ref.pv_ref, ...), custom_call_target="tpu_custom_call" | custom-call | tf_op jit(solution)/shard_map/pallas_call | solution.py:506
  86.3 4.1 collective-permute-done.11.refs_7_
  90.9 13.0 %collective-permute-done.12.refs_8_ = bf16[1,320,1024]{2,1,0:T(8,128)(2,1)S(1)} collective-permute-done((bf16[1,320,1024]{2,1,0:T(8,128)(2,1)}, bf16[1,320,1024]{2,1,0:T(8,128)(2,1)S(1)}, u32[]{:S(2)}, u32[]{:S(2)}) %collective-permute-start.12) | collective-permute-done | bytes 655392 | tf_op jit(solution)/shard_map/ppermute | solution.py:349
  105.7 2.1 collective-permute-done.7
  110.9 14.9 %shard_map.172 = (bf16[8,8,112,1024]{3,2,1,0:T(8,128)(2,1)}, s32[8,8,320]{2,1,0:T(8,128)}) custom-call(s32[8,8,320]{2,1,0:T(8,128)} %negate_select_fusion.1.refs_0_, bf16[2,320,1024]{2,1,0:T(8,128)(2,1)} %bitcast.79, bf16[2,320,1024]{2,1,0:T(8,128)(2,1)} %copy-done.8, bf16[2,320,1024]{2,1,0:T(8,128)(2,1)} %copy-done.7, ...), custom_call_target="tpu_custom_call" | custom-call | tf_op jit(solution)/shard_map/pallas_call | solution.py:108
  126.9 16.8 %shard_map.173 = (bf16[8,8,112,1024]{3,2,1,0:T(8,128)(2,1)}, f32[8,8,112,128]{3,2,1,0:T(8,128)}, f32[8,32,320]{2,1,0:T(8,128)}) custom-call(s32[8,8,320]{2,1,0:T(8,128)} %negate_select_fusion.1.refs_0_, s32[8,8,320]{2,1,0:T(8,128)} %get-tuple-element.94.refs_1_.refs_0_, bf16[1024,32]{1,0:T(8,128)(2,1)} %dynamic-slice_maximum_fusion.1.refs_2_.refs_4_, ...), custom_call_target="tpu_custom_call" | custom-call | tf_op jit(solution)/shard_map/pallas_call | solution.py:153
  143.6 29.5 %shard_map.175 = (bf16[2,896,1024]{2,1,0:T(8,128)(2,1)}, bf16[2,896,1024]{2,1,0:T(8,128)(2,1)}, f32[2,896,128]{2,1,0:T(8,128)}, bf16[2,4,384,1024]{3,2,1,0:T(8,128)(2,1)}) custom-call(s32[1]{0:T(128)} %bitcast.7.parity_ref, bf16[8,896,1024]{2,1,0:T(8,128)(2,1)} %bitcast.56, bf16[8,896,1024]{2,1,0:T(8,128)(2,1)} %bitcast.51, f32[8,896,128]{2,1,0:T(8,128)} %bitcast.61, ...), custom_call_target="tpu_custom_call" | custom-call | tf_op jit(solution)/shard_map/pallas_call | solution.py:329
  173.2 29.4 %shard_map.174 = (bf16[2,896,1024]{2,1,0:T(8,128)(2,1)}, bf16[2,896,1024]{2,1,0:T(8,128)(2,1)}, f32[2,896,128]{2,1,0:T(8,128)}, bf16[2,4,192,1024]{3,2,1,0:T(8,128)(2,1)}, bf16[2,4,192,1024]{3,2,1,0:T(8,128)(2,1)}) custom-call(s32[1]{0:T(128)} %bitcast.7.parity_ref, bf16[8,896,1024]{2,1,0:T(8,128)(2,1)} %bitcast.57, bf16[8,896,1024]{2,1,0:T(8,128)(2,1)} %bitcast.52, ...), custom_call_target="tpu_custom_call" | custom-call | tf_op jit(solution)/shard_map/pallas_call | solution.py:329
  204.3 29.3 %shard_map.176 = (bf16[2,896,1024]{2,1,0:T(8,128)(2,1)}, bf16[2,896,1024]{2,1,0:T(8,128)(2,1)}, f32[2,896,128]{2,1,0:T(8,128)}, bf16[2,4,192,1024]{3,2,1,0:T(8,128)(2,1)}, bf16[2,4,192,1024]{3,2,1,0:T(8,128)(2,1)}) custom-call(s32[1]{0:T(128)} %bitcast.7.parity_ref, bf16[8,896,1024]{2,1,0:T(8,128)(2,1)} %bitcast.58, bf16[8,896,1024]{2,1,0:T(8,128)(2,1)} %bitcast.53, ...), custom_call_target="tpu_custom_call" | custom-call | tf_op jit(solution)/shard_map/pallas_call | solution.py:329
  233.8 17.5 %shard_map.178 = (bf16[1,896,1024]{2,1,0:T(8,128)(2,1)}, bf16[1,896,1024]{2,1,0:T(8,128)(2,1)}, f32[1,896,128]{2,1,0:T(8,128)}, bf16[1,4,192,1024]{3,2,1,0:T(8,128)(2,1)}, bf16[1,4,192,1024]{3,2,1,0:T(8,128)(2,1)}) custom-call(s32[1]{0:T(128)} %bitcast.7.parity_ref, bf16[8,896,1024]{2,1,0:T(8,128)(2,1)} %bitcast.59, bf16[8,896,1024]{2,1,0:T(8,128)(2,1)} %bitcast.54, ...), custom_call_target="tpu_custom_call" | custom-call | tf_op jit(solution)/shard_map/pallas_call | solution.py:329
  251.3 17.1 %shard_map.177 = (bf16[1,896,1024]{2,1,0:T(8,128)(2,1)}, bf16[1,896,1024]{2,1,0:T(8,128)(2,1)}, f32[1,896,128]{2,1,0:T(8,128)}, bf16[1,4,192,1024]{3,2,1,0:T(8,128)(2,1)}, bf16[1,4,192,1024]{3,2,1,0:T(8,128)(2,1)}) custom-call(s32[1]{0:T(128)} %bitcast.7.parity_ref, bf16[8,896,1024]{2,1,0:T(8,128)(2,1)} %bitcast.60, bf16[8,896,1024]{2,1,0:T(8,128)(2,1)} %bitcast.55, ...), custom_call_target="tpu_custom_call" | custom-call | tf_op jit(solution)/shard_map/pallas_call | solution.py:329
  268.4 5.4 collective-permute-done.15
  273.9 6.1 add_convert_fusion.1
  280.0 13.3 %shard_map.179 = (bf16[8,320,1024]{2,1,0:T(8,128)(2,1)}, f32[8,8,320]{2,1,0:T(8,128)}) custom-call(s32[8,8,320]{2,1,0:T(8,128)} %get-tuple-element.94.refs_1_.refs_0_, bf16[2,8,112,1024]{3,2,1,0:T(8,128)(2,1)} %bitcast.84, bf16[2,8,112,1024]{3,2,1,0:T(8,128)(2,1)} %bitcast.85, bf16[2,8,112,1024]{3,2,1,0:T(8,128)(2,1)} %bitcast.86, ...), custom_call_target="tpu_custom_call" | custom-call | tf_op jit(solution)/shard_map/pallas_call | solution.py:221
  293.3 4.2 fusion.17
  302.7 3.3 add_convert_fusion.4
  306.0 34.5 %collective-permute-done.19 = bf16[2,4,192,1024]{3,2,1,0:T(8,128)(2,1)S(1)} collective-permute-done((bf16[2,4,192,1024]{3,2,1,0:T(8,128)(2,1)}, bf16[2,4,192,1024]{3,2,1,0:T(8,128)(2,1)S(1)}, u32[]{:S(2)}, u32[]{:S(2)}) %collective-permute-start.19) | collective-permute-done | bytes 3145760 | tf_op jit(solution)/shard_map/ppermute | solution.py:863
  342.2 3.3 add_convert_fusion
  345.6 12.5 %shard_map.180 = bf16[8,320,1024]{2,1,0:T(8,128)(2,1)} custom-call(s32[8,8,320]{2,1,0:T(8,128)} %get-tuple-element.94.refs_1_.refs_0_, bf16[2,8,112,1024]{3,2,1,0:T(8,128)(2,1)} %bitcast.81, bf16[2,8,112,1024]{3,2,1,0:T(8,128)(2,1)} %bitcast.82, bf16[2,8,112,1024]{3,2,1,0:T(8,128)(2,1)} %bitcast.83, bf16[1,8,112,1024]{3,2,1,0:T(8,128)(2,1)} %bitcast.88, ...), custom_call_target="tpu_custom_call" | custom-call | tf_op jit(solution)/shard_map/pallas_call | solution.py:221
  359.3 11.7 %collective-permute-done.22.refs_2_ = bf16[2,320,1024]{2,1,0:T(8,128)(2,1)} collective-permute-done((bf16[2,320,1024]{2,1,0:T(8,128)(2,1)}, bf16[2,320,1024]{2,1,0:T(8,128)(2,1)}, u32[]{:S(2)}, u32[]{:S(2)}) %collective-permute-start.22) | collective-permute-done | bytes 1310752 | tf_op jit(solution)/shard_map/ppermute | solution.py:355
  371.0 8.1 %shard_map.181 = (f32[2,320,1024]{2,1,0:T(8,128)}, bf16[2,320,1024]{2,1,0:T(8,128)(2,1)}, bf16[2,320,1024]{2,1,0:T(8,128)(2,1)}, f32[1,1024]{1,0:T(1,128)}) custom-call(bf16[2,320,1024]{2,1,0:T(8,128)(2,1)} %get-tuple-element.151.refs_0_, bf16[2,320,1024]{2,1,0:T(8,128)(2,1)} %collective-permute-done.20.refs_1_, ...), custom_call_target="tpu_custom_call" | custom-call | tf_op jit(solution)/shard_map/pallas_call | solution.py:572
  379.1 22.8 %shard_map.182 = (bf16[2,320,1024]{2,1,0:T(8,128)(2,1)}, bf16[2,256,512]{2,1,0:T(8,128)(2,1)}, bf16[2,256,512]{2,1,0:T(8,128)(2,1)}, bf16[2,256,512]{2,1,0:T(8,128)(2,1)}, bf16[2,256,512]{2,1,0:T(8,128)(2,1)}) custom-call(bf16[2,320,1024]{2,1,0:T(8,128)(2,1)} %get-tuple-element.69.q_ref, bf16[2,256,1024]{2,1,0:T(8,128)(2,1)} %pad_maximum_fusion.pk_ref.pv_ref, ...), custom_call_target="tpu_custom_call" | custom-call | tf_op jit(solution)/shard_map/pallas_call | solution.py:632
  406.4 3.6 bitcast_convert_fusion
  414.2 2.5 collective-permute-done.31.refs_9_
  416.7 2.4 collective-permute-done.28.refs_6_
  419.8 11.2 %shard_map.183 = (bf16[2,320,2048]{2,1,0:T(8,128)(2,1)}, bf16[1024,2048]{1,0:T(8,128)(2,1)}) custom-call(bf16[2,320,1024]{2,1,0:T(8,128)(2,1)} %get-tuple-element.103.refs_0_, bf16[2,320,1024]{2,1,0:T(8,128)(2,1)} %get-tuple-element.110.refs_1_, bf16[2,256,512]{2,1,0:T(8,128)(2,1)} %get-tuple-element.111.refs_2_, ...), custom_call_target="tpu_custom_call" | custom-call | tf_op jit(solution)/shard_map/pallas_call | solution.py:698
  431.0 8.2 %shard_map.184 = (bf16[2,320,1024]{2,1,0:T(8,128)(2,1)}, f32[1,1024]{1,0:T(1,128)}) custom-call(bf16[2,320,2048]{2,1,0:T(8,128)(2,1)} %get-tuple-element.115.gp_ref, bf16[1024,2048]{1,0:T(8,128)(2,1)} %w_ref.7, bf16[2,320,1024]{2,1,0:T(8,128)(2,1)} %bitcast.71, f32[1,1024]{1,0:T(1,128)} %bitcast.108, f32[2,320,1024]{2,1,0:T(8,128)} %get-tuple-element.116.hidden_ref), custom_call_target="tpu_custom_call" | custom-call | tf_op jit(solution)/shard_map/pallas_call | solution.py:733
  440.2 10.4 %concatenate.45 = bf16[1024,3200]{1,0:T(8,128)(2,1)} concatenate(bf16[1024,2048]{1,0:T(8,128)(2,1)} %get-tuple-element.118, bf16[1024,1024]{1,0:T(8,128)(2,1)S(1)} %bitcast_convert_fusion, bf16[1024,32]{1,0:T(8,128)(2,1)S(1)} %fusion.11, bf16[1024,1]{1,0:T(8,128)(2,1)S(1)} %copy.36, bf16[1024,1]{1,0:T(8,128)(2,1)S(1)} %copy.37, bf16[1024,94]{1,0:T(8,128)(2,1)S(1)} %broadcast_in_dim.39), dimensions={1} | concatenate | bytes 13107200 | tf_op jit(solution)/shard_map/concatenate | solution.py:934
  453.9 42.7 %collective-permute-done.33 = bf16[1,4,192,1024]{3,2,1,0:T(8,128)(2,1)S(1)} collective-permute-done((bf16[1,4,192,1024]{3,2,1,0:T(8,128)(2,1)S(1)}, bf16[1,4,192,1024]{3,2,1,0:T(8,128)(2,1)S(1)}, u32[]{:S(2)}, u32[]{:S(2)}) %collective-permute-start.33) | collective-permute-done | bytes 1572896 | tf_op jit(solution)/shard_map/ppermute | solution.py:863
  496.6 1.8 add_convert_fusion.3
  500.6 3.5 fusion.18
  504.1 34.1 %collective-permute-done.34 = bf16[1,4,192,1024]{3,2,1,0:T(8,128)(2,1)S(1)} collective-permute-done((bf16[1,4,192,1024]{3,2,1,0:T(8,128)(2,1)S(1)}, bf16[1,4,192,1024]{3,2,1,0:T(8,128)(2,1)S(1)}, u32[]{:S(2)}, u32[]{:S(2)}) %collective-permute-start.34) | collective-permute-done | bytes 1572896 | tf_op jit(solution)/shard_map/ppermute | solution.py:863
  538.2 1.8 add_convert_fusion.2
  540.1 3.5 add_convert_fusion.6
  544.9 2.1 slice.134
  548.5 26.5 %collective-permute-done.18 = bf16[2,320,1024]{2,1,0:T(8,128)(2,1)} collective-permute-done((bf16[2,320,1024]{2,1,0:T(8,128)(2,1)}, bf16[2,320,1024]{2,1,0:T(8,128)(2,1)}, u32[]{:S(2)}, u32[]{:S(2)}) %collective-permute-start.18) | collective-permute-done | bytes 1310752 | tf_op jit(solution)/shard_map/ppermute | solution.py:355
  574.9 4.2 add_convert_fusion.5
  579.1 157.4 %all-reduce.2.cloned.1.call-done = bf16[1024,3200]{1,0:T(8,128)(2,1)} async-done(((bf16[1024,3200]{1,0:T(8,128)(2,1)}), bf16[1024,3200]{1,0:T(8,128)(2,1)}) %all-reduce.2.cloned.1.call-update) | async-done | bytes 6553616 | tf_op jit(solution)/shard_map/psum | solution.py:935
  738.3 8.6 %convert_element_type.138 = f32[1024,3200]{1,0:T(8,128)} convert(bf16[1024,3200]{1,0:T(8,128)(2,1)} %all-reduce.2.cloned.1.call-done) | non-fusion elementwise | flops 3276800 | bytes 19660800 | tf_op jit(solution)/shard_map/convert_element_type | solution.py:935
  746.9 4.5 slice.129
  751.4 2.6 slice.130
  754.0 2.4 slice_reduce_fusion
  762.4 2.5 slice.135
  (188 shorter events, 54.5 us)
Async XLA Ops:
  8.0 536.9 %reduce-scatter.6.cloned.1.call-start = ((), (), s32[]{:S(2)}) async-start(), calls=%async_computation.6 | async-start | bytes 7864320 | tf_op jit(solution)/shard_map/reduce_scatter | solution.py:843
  8.1 32.0 %collective-permute-start.4 = (bf16[2,320,1024]{2,1,0:T(8,128)(2,1)}, bf16[2,320,1024]{2,1,0:T(8,128)(2,1)S(1)}, u32[]{:S(2)}, u32[]{:S(2)}) collective-permute-start(bf16[2,320,1024]{2,1,0:T(8,128)(2,1)} %bitcast.77), channel_id=1, source_target_pairs={{2,0},{3,1},{0,2},{1,3},{6,4},{7,5},{4,6},{5,7},{10,8},{11,9},{8,1... | collective-permute-start | bytes 3932168 | tf_op jit(solution)/shard_map/ppermute | solution.py:349
  11.1 63.0 %collective-permute-start.3 = (bf16[2,320,1024]{2,1,0:T(8,128)(2,1)}, bf16[2,320,1024]{2,1,0:T(8,128)(2,1)S(1)}, u32[]{:S(2)}, u32[]{:S(2)}) collective-permute-start(bf16[2,320,1024]{2,1,0:T(8,128)(2,1)} %bitcast.78), channel_id=1, source_target_pairs={{0,1},{1,0},{2,3},{3,2},{4,5},{5,4},{6,7},{7,6},{8,9},{9,8},{10,11... | collective-permute-start | bytes 3932168 | tf_op jit(solution)/shard_map/ppermute | solution.py:343
  40.1 34.1 %collective-permute-start.5 = (bf16[2,320,1024]{2,1,0:T(8,128)(2,1)S(1)}, bf16[2,320,1024]{2,1,0:T(8,128)(2,1)}, u32[]{:S(2)}, u32[]{:S(2)}) collective-permute-start(bf16[2,320,1024]{2,1,0:T(8,128)(2,1)S(1)} %collective-permute-done.4.refs_3_), channel_id=1, source_target_pairs={{0,1},{1,0},{2,3},{3,2},{4,5},{5,4},{6,7},{7,6},{8,9},{9,8},{10,11... | collective-permute-start | bytes 3932168 | tf_op jit(solution)/shard_map/ppermute | solution.py:343
  49.5 8.6 %collective-permute-start.1 = (bf16[2,64,1024]{2,1,0:T(8,128)(2,1)S(1)}, bf16[2,64,1024]{2,1,0:T(8,128)(2,1)S(1)}, u32[]{:S(2)}, u32[]{:S(2)}) collective-permute-start(bf16[2,64,1024]{2,1,0:T(8,128)(2,1)S(1)} %slice.93), channel_id=1, source_target_pairs={{2,0},{3,1},{0,2},{1,3},{6,4},{7,5},{4,6},{5,7},{10,8},{11,9},{8,1... | collective-permute-start | bytes 786440 | tf_op jit(solution)/shard_map/ppermute | solution.py:349
  51.3 8.6 %collective-permute-start = (bf16[2,64,1024]{2,1,0:T(8,128)(2,1)S(1)}, bf16[2,64,1024]{2,1,0:T(8,128)(2,1)S(1)}, u32[]{:S(2)}, u32[]{:S(2)}) collective-permute-start(bf16[2,64,1024]{2,1,0:T(8,128)(2,1)S(1)} %slice.93), channel_id=1, source_target_pairs={{0,1},{1,0},{2,3},{3,2},{4,5},{5,4},{6,7},{7,6},{8,9},{9,8},{10,11... | collective-permute-start | bytes 786440 | tf_op jit(solution)/shard_map/ppermute | solution.py:343
  58.1 1.8 collective-permute-start.2
  72.3 31.5 %copy-start.25 = (s32[640,8]{0,1:T(8,128)S(1)}, s32[640,8]{0,1:T(8,128)}, u32[]{:S(2)}) copy-start(s32[640,8]{0,1:T(8,128)} %param.12) | copy-start | bytes 61444
  72.3 35.5 %copy-start.22 = (bf16[1024,32]{0,1:T(8,128)(2,1)S(1)}, bf16[1024,32]{0,1:T(8,128)(2,1)}, u32[]{:S(2)}) copy-start(bf16[1024,32]{0,1:T(8,128)(2,1)} %param.17) | copy-start | bytes 196612
  72.4 18.0 %collective-permute-start.11 = (bf16[1,320,1024]{2,1,0:T(8,128)(2,1)}, bf16[1,320,1024]{2,1,0:T(8,128)(2,1)}, u32[]{:S(2)}, u32[]{:S(2)}) collective-permute-start(bf16[1,320,1024]{2,1,0:T(8,128)(2,1)} %get-tuple-element.75.refs_3_), channel_id=1, source_target_pairs={{2,0},{3,1},{0,2},{1,3},{6,4},{7,5},{4,6},{5,7},{10,8},{11,9},{8,1... | collective-permute-start | bytes 1966088 | tf_op jit(solution)/shard_map/ppermute | solution.py:349
  85.9 18.0 %collective-permute-start.12 = (bf16[1,320,1024]{2,1,0:T(8,128)(2,1)}, bf16[1,320,1024]{2,1,0:T(8,128)(2,1)S(1)}, u32[]{:S(2)}, u32[]{:S(2)}) collective-permute-start(bf16[1,320,1024]{2,1,0:T(8,128)(2,1)} %get-tuple-element.76.refs_4_), channel_id=1, source_target_pairs={{2,0},{3,1},{0,2},{1,3},{6,4},{7,5},{4,6},{5,7},{10,8},{11,9},{8,1... | collective-permute-start | bytes 1966088 | tf_op jit(solution)/shard_map/ppermute | solution.py:349
  86.2 39.6 %collective-permute-start.9 = (bf16[1,320,1024]{2,1,0:T(8,128)(2,1)S(1)}, bf16[1,320,1024]{2,1,0:T(8,128)(2,1)S(1)}, u32[]{:S(2)}, u32[]{:S(2)}) collective-permute-start(bf16[1,320,1024]{2,1,0:T(8,128)(2,1)S(1)} %copy-done.9), channel_id=1, source_target_pairs={{0,1},{1,0},{2,3},{3,2},{4,5},{5,4},{6,7},{7,6},{8,9},{9,8},{10,11... | collective-permute-start | bytes 1966088 | tf_op jit(solution)/shard_map/ppermute | solution.py:343
  90.3 35.5 %collective-permute-start.13 = (bf16[1,320,1024]{2,1,0:T(8,128)(2,1)}, bf16[1,320,1024]{2,1,0:T(8,128)(2,1)S(1)}, u32[]{:S(2)}, u32[]{:S(2)}) collective-permute-start(bf16[1,320,1024]{2,1,0:T(8,128)(2,1)} %collective-permute-done.11.refs_7_), channel_id=1, source_target_pairs={{0,1},{1,0},{2,3},{3,2},{4,5},{5,4},{6,7},{7,6},{8,9},{9,8},{10,11... | collective-permute-start | bytes 1966088 | tf_op jit(solution)/shard_map/ppermute | solution.py:343
  90.3 35.5 %collective-permute-start.10 = (bf16[1,320,1024]{2,1,0:T(8,128)(2,1)}, bf16[1,320,1024]{2,1,0:T(8,128)(2,1)}, u32[]{:S(2)}, u32[]{:S(2)}) collective-permute-start(bf16[1,320,1024]{2,1,0:T(8,128)(2,1)} %get-tuple-element.76.refs_4_), channel_id=1, source_target_pairs={{0,1},{1,0},{2,3},{3,2},{4,5},{5,4},{6,7},{7,6},{8,9},{9,8},{10,11... | collective-permute-start | bytes 1966088 | tf_op jit(solution)/shard_map/ppermute | solution.py:343
  103.8 22.0 %collective-permute-start.14 = (bf16[1,320,1024]{2,1,0:T(8,128)(2,1)S(1)}, bf16[1,320,1024]{2,1,0:T(8,128)(2,1)}, u32[]{:S(2)}, u32[]{:S(2)}) collective-permute-start(bf16[1,320,1024]{2,1,0:T(8,128)(2,1)S(1)} %collective-permute-done.12.refs_8_), channel_id=1, source_target_pairs={{0,1},{1,0},{2,3},{3,2},{4,5},{5,4},{6,7},{7,6},{8,9},{9,8},{10,11... | collective-permute-start | bytes 1966088 | tf_op jit(solution)/shard_map/ppermute | solution.py:343
  103.9 3.9 collective-permute-start.7
  107.8 1.2 collective-permute-start.6
  109.0 1.2 collective-permute-start.8
  173.2 563.3 %all-reduce.2.cloned.1.call-start = ((), (), s32[]{:S(2)}) async-start(), calls=%async_computation.5 | async-start | bytes 13107200 | tf_op jit(solution)/shard_map/psum | solution.py:935
  202.6 71.3 %collective-permute-start.15 = (bf16[2,4,192,1024]{3,2,1,0:T(8,128)(2,1)}, bf16[2,4,192,1024]{3,2,1,0:T(8,128)(2,1)}, u32[]{:S(2)}, u32[]{:S(2)}) collective-permute-start(bf16[2,4,192,1024]{3,2,1,0:T(8,128)(2,1)} %get-tuple-element.81), channel_id=1, source_target_pairs={{0,4},{4,0},{8,12},{12,8},{16,20},{20,16},{24,28},{28,24},{1,5},{5... | collective-permute-start | bytes 9437192 | tf_op jit(solution)/shard_map/ppermute | solution.py:863
  233.6 106.9 %collective-permute-start.19 = (bf16[2,4,192,1024]{3,2,1,0:T(8,128)(2,1)}, bf16[2,4,192,1024]{3,2,1,0:T(8,128)(2,1)S(1)}, u32[]{:S(2)}, u32[]{:S(2)}) collective-permute-start(bf16[2,4,192,1024]{3,2,1,0:T(8,128)(2,1)} %get-tuple-element.102), channel_id=1, source_target_pairs={{0,4},{4,0},{8,12},{12,8},{16,20},{20,16},{24,28},{28,24},{1,5},{5... | collective-permute-start | bytes 9437192 | tf_op jit(solution)/shard_map/ppermute | solution.py:863
  297.5 4.9 collective-permute-start.21
  299.3 46.3 %copy-start = (f32[2,320,1024]{2,1,0:T(8,128)}, f32[2,320,1024]{2,1,0:T(8,128)S(1)}, u32[]{:S(2)}) copy-start(f32[2,320,1024]{2,1,0:T(8,128)S(1)} %constant_dynamic-update-slice_fusion.refs_5_) | copy-start | bytes 7864324
  299.3 42.9 %copy-start.2 = (bf16[2,4,192,1024]{3,2,1,0:T(8,128)(2,1)S(1)}, bf16[2,4,192,1024]{3,2,1,0:T(8,128)(2,1)}, u32[]{:S(2)}) copy-start(bf16[2,4,192,1024]{3,2,1,0:T(8,128)(2,1)} %get-tuple-element.101) | copy-start | bytes 9437188
  300.0 58.1 %collective-permute-start.23 = (f32[2,8,320]{2,1,0:T(8,128)S(1)}, f32[2,8,320]{2,1,0:T(8,128)S(1)}, u32[]{:S(2)}, u32[]{:S(2)}) collective-permute-start(f32[2,8,320]{2,1,0:T(8,128)S(1)} %get-tuple-element.162), channel_id=1, source_target_pairs={{1,0},{0,1},{3,2},{2,3},{5,4},{4,5},{7,6},{6,7},{9,8},{8,9},{11,10... | collective-permute-start | bytes 61448 | tf_op jit(solution)/shard_map/ppermute | solution.py:388
  300.6 57.5 %collective-permute-start.24 = (f32[2,8,320]{2,1,0:T(8,128)S(1)}, f32[2,8,320]{2,1,0:T(8,128)S(1)}, u32[]{:S(2)}, u32[]{:S(2)}) collective-permute-start(f32[2,8,320]{2,1,0:T(8,128)S(1)} %get-tuple-element.161), channel_id=1, source_target_pairs={{2,0},{3,1},{0,2},{1,3},{6,4},{7,5},{4,6},{5,7},{10,8},{11,9},{8,1... | collective-permute-start | bytes 61448 | tf_op jit(solution)/shard_map/ppermute | solution.py:388
  302.4 55.8 %collective-permute-start.25 = (f32[2,8,320]{2,1,0:T(8,128)S(1)}, f32[2,8,320]{2,1,0:T(8,128)S(1)}, u32[]{:S(2)}, u32[]{:S(2)}) collective-permute-start(f32[2,8,320]{2,1,0:T(8,128)S(1)} %get-tuple-element.160), channel_id=1, source_target_pairs={{3,0},{2,1},{1,2},{0,3},{7,4},{6,5},{5,6},{4,7},{11,8},{10,9},{9,1... | collective-permute-start | bytes 61448 | tf_op jit(solution)/shard_map/ppermute | solution.py:388
  302.4 56.9 %collective-permute-start.20 = (bf16[2,320,1024]{2,1,0:T(8,128)(2,1)}, bf16[2,320,1024]{2,1,0:T(8,128)(2,1)}, u32[]{:S(2)}, u32[]{:S(2)}) collective-permute-start(bf16[2,320,1024]{2,1,0:T(8,128)(2,1)} %get-tuple-element.150), channel_id=1, source_target_pairs={{0,1},{1,0},{2,3},{3,2},{4,5},{5,4},{6,7},{7,6},{8,9},{9,8},{10,11... | collective-permute-start | bytes 3932168 | tf_op jit(solution)/shard_map/ppermute | solution.py:343
  340.5 30.5 %collective-permute-start.22 = (bf16[2,320,1024]{2,1,0:T(8,128)(2,1)}, bf16[2,320,1024]{2,1,0:T(8,128)(2,1)}, u32[]{:S(2)}, u32[]{:S(2)}) collective-permute-start(bf16[2,320,1024]{2,1,0:T(8,128)(2,1)} %add_convert_fusion.4), channel_id=1, source_target_pairs={{0,2},{1,3},{2,0},{3,1},{4,6},{5,7},{6,4},{7,5},{8,10},{9,11},{10,... | collective-permute-start | bytes 3932168 | tf_op jit(solution)/shard_map/ppermute | solution.py:355
  403.6 6.4 collective-permute-start.30
  405.3 7.3 collective-permute-start.27
  405.8 8.4 %collective-permute-start.26 = (bf16[2,64,512]{2,1,0:T(8,128)(2,1)}, bf16[2,64,512]{2,1,0:T(8,128)(2,1)S(1)}, u32[]{:S(2)}, u32[]{:S(2)}) collective-permute-start(bf16[2,64,512]{2,1,0:T(8,128)(2,1)} %get-tuple-element.158), channel_id=1, source_target_pairs={{0,1},{1,0},{2,3},{3,2},{4,5},{5,4},{6,7},{7,6},{8,9},{9,8},{10,11... | collective-permute-start | bytes 393224 | tf_op jit(solution)/shard_map/ppermute | solution.py:343
  405.8 8.4 %collective-permute-start.29 = (bf16[2,64,512]{2,1,0:T(8,128)(2,1)S(1)}, bf16[2,64,512]{2,1,0:T(8,128)(2,1)S(1)}, u32[]{:S(2)}, u32[]{:S(2)}) collective-permute-start(bf16[2,64,512]{2,1,0:T(8,128)(2,1)S(1)} %get-tuple-element.155), channel_id=1, source_target_pairs={{0,1},{1,0},{2,3},{3,2},{4,5},{5,4},{6,7},{7,6},{8,9},{9,8},{10,11... | collective-permute-start | bytes 393224 | tf_op jit(solution)/shard_map/ppermute | solution.py:343
  410.9 5.8 collective-permute-start.31
  413.6 5.6 collective-permute-start.28
  450.6 307.3 %reduce-scatter.8.cloned.1.call-start = ((), (), s32[]{:S(2)}) async-start(), calls=%async_computation.7 | async-start | bytes 3932160 | tf_op jit(solution)/shard_map/reduce_scatter | solution.py:843
  450.6 46.0 %copy-start.5 = (bf16[1,4,192,1024]{3,2,1,0:T(8,128)(2,1)S(1)}, bf16[1,4,192,1024]{3,2,1,0:T(8,128)(2,1)}, u32[]{:S(2)}) copy-start(bf16[1,4,192,1024]{3,2,1,0:T(8,128)(2,1)} %get-tuple-element.125) | copy-start | bytes 4718596
  451.3 307.8 %reduce-scatter.10.cloned.1.call-start = ((), (), s32[]{:S(2)}) async-start(), calls=%async_computation.8 | async-start | bytes 3932160 | tf_op jit(solution)/shard_map/reduce_scatter | solution.py:843
  452.1 308.2 %reduce-scatter.12.cloned.1.call-start = ((), (), s32[]{:S(2)}) async-start(), calls=%async_computation.9 | async-start | bytes 1966080 | tf_op jit(solution)/shard_map/reduce_scatter | solution.py:843
  452.1 44.5 %collective-permute-start.33 = (bf16[1,4,192,1024]{3,2,1,0:T(8,128)(2,1)S(1)}, bf16[1,4,192,1024]{3,2,1,0:T(8,128)(2,1)S(1)}, u32[]{:S(2)}, u32[]{:S(2)}) collective-permute-start(bf16[1,4,192,1024]{3,2,1,0:T(8,128)(2,1)S(1)} %copy-done.28), channel_id=1, source_target_pairs={{0,4},{4,0},{8,12},{12,8},{16,20},{20,16},{24,28},{28,24},{1,5},{5... | collective-permute-start | bytes 4718600 | tf_op jit(solution)/shard_map/ppermute | solution.py:863
  498.5 262.9 %reduce-scatter.14.cloned.1.call-start = ((), (), s32[]{:S(2)}) async-start(), calls=%async_computation.10 | async-start | bytes 1966080 | tf_op jit(solution)/shard_map/reduce_scatter | solution.py:843
  498.8 39.4 %copy-start.4 = (bf16[1,4,192,1024]{3,2,1,0:T(8,128)(2,1)S(1)}, bf16[1,4,192,1024]{3,2,1,0:T(8,128)(2,1)}, u32[]{:S(2)}) copy-start(bf16[1,4,192,1024]{3,2,1,0:T(8,128)(2,1)} %get-tuple-element.127) | copy-start | bytes 4718596
  498.8 39.4 %collective-permute-start.34 = (bf16[1,4,192,1024]{3,2,1,0:T(8,128)(2,1)S(1)}, bf16[1,4,192,1024]{3,2,1,0:T(8,128)(2,1)S(1)}, u32[]{:S(2)}, u32[]{:S(2)}) collective-permute-start(bf16[1,4,192,1024]{3,2,1,0:T(8,128)(2,1)S(1)} %copy-done.27), channel_id=1, source_target_pairs={{0,4},{4,0},{8,12},{12,8},{16,20},{20,16},{24,28},{28,24},{1,5},{5... | collective-permute-start | bytes 4718600 | tf_op jit(solution)/shard_map/ppermute | solution.py:863
  504.1 36.0 %collective-permute-start.17 = (bf16[2,320,1024]{2,1,0:T(8,128)(2,1)}, bf16[2,320,1024]{2,1,0:T(8,128)(2,1)}, u32[]{:S(2)}, u32[]{:S(2)}) collective-permute-start(bf16[2,320,1024]{2,1,0:T(8,128)(2,1)} %get-tuple-element.153), channel_id=1, source_target_pairs={{0,1},{1,0},{2,3},{3,2},{4,5},{5,4},{6,7},{7,6},{8,9},{9,8},{10,11... | collective-permute-start | bytes 3932168 | tf_op jit(solution)/shard_map/ppermute | solution.py:343
  540.0 34.9 %copy-start.1 = (f32[2,320,1024]{2,1,0:T(8,128)S(1)}, f32[2,320,1024]{2,1,0:T(8,128)}, u32[]{:S(2)}) copy-start(f32[2,320,1024]{2,1,0:T(8,128)} %copy-done) | copy-start | bytes 7864324
  540.0 8.4 %collective-permute-start.16 = (bf16[2,320,1024]{2,1,0:T(8,128)(2,1)}, bf16[2,320,1024]{2,1,0:T(8,128)(2,1)}, u32[]{:S(2)}, u32[]{:S(2)}) collective-permute-start(bf16[2,320,1024]{2,1,0:T(8,128)(2,1)} %get-tuple-element.152), channel_id=1, source_target_pairs={{0,1},{1,0},{2,3},{3,2},{4,5},{5,4},{6,7},{7,6},{8,9},{9,8},{10,11... | collective-permute-start | bytes 3932168 | tf_op jit(solution)/shard_map/ppermute | solution.py:343
  543.6 31.3 %collective-permute-start.18 = (bf16[2,320,1024]{2,1,0:T(8,128)(2,1)}, bf16[2,320,1024]{2,1,0:T(8,128)(2,1)}, u32[]{:S(2)}, u32[]{:S(2)}) collective-permute-start(bf16[2,320,1024]{2,1,0:T(8,128)(2,1)} %add_convert_fusion.6), channel_id=1, source_target_pairs={{0,2},{1,3},{2,0},{3,1},{4,6},{5,7},{6,4},{7,5},{8,10},{9,11},{10,... | collective-permute-start | bytes 3932168 | tf_op jit(solution)/shard_map/ppermute | solution.py:355
  546.9 209.5 %collective-permute-start.32 = (bf16[2,192,1024]{2,1,0:T(8,128)(2,1)}, bf16[2,192,1024]{2,1,0:T(8,128)(2,1)}, u32[]{:S(2)}, u32[]{:S(2)}) collective-permute-start(bf16[2,192,1024]{2,1,0:T(8,128)(2,1)} %slice.134), channel_id=1, source_target_pairs={{0,4},{4,0},{8,12},{12,8},{16,20},{20,16},{24,28},{28,24},{1,5},{5... | collective-permute-start | bytes 2359304 | tf_op jit(solution)/shard_map/ppermute | solution.py:916
  (24 other events, 163.8 us)
Sparse Core Ops, SparseCore 0:
  173.3 112.2 reduce-scatter.5
  453.7 71.5 reduce-scatter.7
  527.6 66.2 reduce-scatter.9
  596.7 38.5 reduce-scatter.11
  638.0 37.8 reduce-scatter.13
Sparse Core Ops, SparseCore 1:
  450.7 285.7 all-reduce.1

commit v2 on v1

--- a/solution.py
+++ b/solution.py
@@ -18,7 +18,7 @@
 MICRO = 2
 CAP = 100
 SLOTS = 112
-CHUNKS = (2, 2, 2, 1, 1)
+CHUNKS = ((1, True), (1, False), (2, False), (2, False), (1, True), (1, False))
 
 
 epsilon = 1e-06
@@ -35,6 +35,10 @@
     return pltpu.CompilerParams(
         vmem_limit_bytes=vmem_limit, dimension_semantics=("arbitrary",)
     )
+
+
+def cost(micros):
+    return pl.CostEstimate(flops=int(micros * 1.15e9), bytes_accessed=0, transcendentals=0)
 
 
 def mm(left, right, dims):
@@ -123,6 +127,7 @@
             pltpu.VMEM((tok, D), bf16),
             pltpu.VMEM((tok, tok), bf16),
         ],
+        cost_estimate=cost(15),
         compiler_params=params(),
     )(ids, *pieces)
 
@@ -170,6 +175,7 @@
             jax.ShapeDtypeStruct((blocks, EXPERTS, tok), f32),
         ],
         scratch_shapes=[pltpu.VMEM((experts * SLOTS, tok), bf16), pltpu.VMEM((tok, D), bf16)],
+        cost_estimate=cost(17),
         compiler_params=params(),
     )(ids, slots, w_router, *pieces)
 
@@ -228,6 +234,7 @@
             pltpu.VMEM((experts * SLOTS, tok), bf16),
             pltpu.VMEM((experts * SLOTS, D), bf16),
         ],
+        cost_estimate=cost(15),
         compiler_params=params(),
     )(*args)
 
@@ -335,6 +342,7 @@
             jax.ShapeDtypeStruct((count, rows, 128), f32),
         ]
         + [part_shape] * parts,
+        cost_estimate=cost(15 * count),
         compiler_params=params(),
     )(parity, x_rows, d_rows, slot_gate, w_gate_up, w_down)
 
@@ -440,6 +448,7 @@
         ],
         out_specs=[block, block, block],
         out_shape=[shape, shape, shape],
+        cost_estimate=cost(7),
         compiler_params=params(),
     )(tokens, gain, w_qkv, cosine, sine)
 
@@ -530,6 +539,7 @@
             jax.ShapeDtypeStruct((1, rows, D), bf16),
         ],
         scratch_shapes=[pltpu.VMEM((rows, D), bf16)],
+        cost_estimate=cost(12),
         compiler_params=params(),
     )(q, prompt, prompt, kv, kv, bias, tokens, w_out, gain)
 
@@ -588,6 +598,7 @@
             jax.ShapeDtypeStruct((micro, rows, D), bf16),
             jax.ShapeDtypeStruct((1, D), f32),
         ],
+        cost_estimate=cost(8),
         compiler_params=params(),
     )(*terms, grad_logits, w_router, hidden, gain, cotangent, w_out)
 
@@ -652,6 +663,7 @@
             jax.ShapeDtypeStruct((micro, own_rows, k_width), bf16),
             jax.ShapeDtypeStruct((micro, own_rows, k_width), bf16),
         ],
+        cost_estimate=cost(23),
         compiler_params=pltpu.CompilerParams(
             vmem_limit_bytes=vmem_limit, dimension_semantics=("arbitrary", "arbitrary")
         ),
@@ -708,6 +720,7 @@
             jax.ShapeDtypeStruct((D, 2 * D), bf16),
         ],
         scratch_shapes=[pltpu.VMEM((D, 2 * D), f32)],
+        cost_estimate=cost(11),
         compiler_params=params(),
     )(normed, gq, gok, gov, *k_terms, *v_terms, cosine, sine)
 
@@ -745,8 +758,55 @@
             jax.ShapeDtypeStruct((micro, rows, D), bf16),
             jax.ShapeDtypeStruct((1, D), f32),
         ],
+        cost_estimate=cost(8),
         compiler_params=params(),
     )(gp, w_qkv, tokens, gain, grad_hidden)
+
+
+def halve(value, axis, swap, bit):
+    rows = value.shape[0] // 2
+    keep = lax.dynamic_slice_in_dim(value, bit * rows, rows, 0)
+    send = lax.dynamic_slice_in_dim(value, (1 - bit) * rows, rows, 0)
+    got = lax.ppermute(send, axis, swap)
+    return (keep.astype(f32) + got.astype(f32)).astype(bf16)
+
+
+def finish_dense_body(table_ref, *refs, pieces):
+    first_refs, second_refs = refs[:pieces], refs[pieces : 2 * pieces]
+    qkv_ref, out_ref = refs[2 * pieces :]
+    width = first_refs[0].shape[1]
+    rest = qkv_ref.shape[1] - width
+    for i in range(pieces):
+
+        @pl.when(pl.program_id(0) == i)
+        def _(i=i):
+            qkv_ref[:, :width] = first_refs[i][...].astype(f32)
+            qkv_ref[:, width:] = second_refs[i][:, :rest].astype(f32)
+            out_ref[...] = second_refs[i][:, rest:].astype(f32)
+
+
+def finish_dense(table, first, second):
+    pieces = len(first)
+    height = first[0].shape[0]
+    grid_spec = pltpu.PrefetchScalarGridSpec(
+        num_scalar_prefetch=1,
+        grid=(pieces,),
+        in_specs=[full_spec(piece) for piece in first + second],
+        out_specs=[
+            pl.BlockSpec((height, 2 * D), lambda i, t: (t[i], 0)),
+            pl.BlockSpec((height, D), lambda i, t: (t[i], 0)),
+        ],
+    )
+    return pl.pallas_call(
+        functools.partial(finish_dense_body, pieces=pieces),
+        grid_spec=grid_spec,
+        out_shape=[
+            jax.ShapeDtypeStruct((pieces * height, 2 * D), f32),
+            jax.ShapeDtypeStruct((pieces * height, D), f32),
+        ],
+        cost_estimate=cost(9),
+        compiler_params=params(),
+    )(table, *first, *second)
 
 
 def after(value, *others):
@@ -798,20 +858,24 @@
         masked_score,
     )
 
-    normed, queries, key_value = project(token_rows, attn_gain, w_qkv, cosine, sine)
-    prompt = jnp.concatenate(gather_members(key_value[:, :PROMPT_DEV], groups), axis=1)
-
     first_expert = member * local_experts
     ids_t = gather_members(expert_ids.reshape(MICRO, tok_rows, TOP).transpose(0, 2, 1), groups)
     ids_all = lax.rem(jnp.concatenate(ids_t, axis=0) + (EXPERTS - first_expert), EXPERTS)
-    cot_pieces = gather_members(cot_rows, groups)
+    cot_pieces = [gather_members(cot_rows[:1], groups)]
+    normed, queries, key_value = project(token_rows, attn_gain, w_qkv, cosine, sine)
+    prompt_pieces = gather_members(key_value[:, :PROMPT_DEV], groups)
+    prompt = jnp.concatenate(prompt_pieces, axis=1)
+    cot_pieces += [
+        gather_members(after(cot_rows[m : m + 1], prompt_pieces[2]), groups)
+        for m in range(1, MICRO)
+    ]
     router = lax.dynamic_slice_in_dim(
         jnp.concatenate([w_router, w_router], axis=1), first_expert, EXPERTS, 1
     )
 
     attended, lse, hidden, moe_pieces, moe_low = [], [], [], [], []
     for m in range(MICRO):
-        mask = bias if m == 0 else after(bias, *cot_pieces)
+        mask = bias if m == 0 else after(bias, moe_low[-1])
         att, log_total, hid, low = attend(
             m, queries, key_value, prompt, mask, token_rows, w_out, moe_gain
         )
@@ -820,21 +884,25 @@
         hidden.append(hid)
         moe_low.append(low)
         moe_pieces.append(gather_members(low, groups))
-    d_rows, slots = pick_grads(ids_all, cot_pieces, local_experts)
+
+    def by_block(pieces):
+        return [pieces[m][g] for g in range(groups) for m in range(MICRO)]
+
+    d_rows, slots = pick_grads(after(ids_all, moe_low[-1]), by_block(cot_pieces), local_experts)
     attended = jnp.concatenate(attended, axis=0)
     lse = jnp.concatenate(lse, axis=0)
     hidden = jnp.concatenate(hidden, axis=0)
     moe_low = jnp.concatenate(moe_low, axis=0)
 
-    x_rows, slot_gate, gates = pick_tokens(
-        ids_all, slots, router, [moe_pieces[m][g] for g in range(groups) for m in range(MICRO)]
-    )
+    x_rows, slot_gate, gates = pick_tokens(ids_all, slots, router, by_block(moe_pieces))
     slot_rows = blocks * SLOTS
     x_rows = x_rows.reshape(local_experts, slot_rows, D)
     d_rows = d_rows.reshape(local_experts, slot_rows, D)
     slot_gate = slot_gate.reshape(local_experts, slot_rows, 128)
-    parity = lax.rem(dp_index, 2).astype(jnp.int32).reshape(1)
+    parity = lax.rem(dp_index, 2).astype(jnp.int32)
     swap_x = [(d, d ^ 1) for d in range(dp_size)]
+    swap_y = [(m, m ^ 2) for m in range(groups)]
+    swap_core = [(m, m ^ 1) for m in range(groups)]
     z_groups = [[d for d in range(dp_size) if d % 2 == r] for r in range(2)]
     piece = (D + FF) // (2 * pairs)
 
@@ -848,30 +916,45 @@
             tiled=True,
         )
 
-    outs, backs, dots, parts, pending = [], [], [], [], []
+    plan = CHUNKS
+    if sum(count for count, _ in plan) != local_experts:
+        plan = tuple((1, e == 0) for e in range(local_experts))
+    outs, backs, dots, halves, parts = [], [], [], {}, {}
+
+    def add_x(i, *before):
+        keep, got = halves.pop(i)
+        got = after(got, *before)
+        half = (keep.astype(f32) + got.astype(f32)).astype(bf16)
+        parts[i] = sum_z(half)
+        return half
+
     first = 0
-    for count in CHUNKS if sum(CHUNKS) == local_experts else (1,) * local_experts:
-        split = first > 0
+    order = parity.reshape(1)
+    for i, (count, whole) in enumerate(plan):
+        if i:
+            order = after(order, outs[-1])
+        if i == 4:
+            order = after(order, add_x(1, outs[-1]), parts[0])
         out, back, dot, *sums = expert_chunk(
-            parity, first, count, pairs, split, x_rows, d_rows, slot_gate, w_gate_up, w_down
+            order, first, count, pairs, not whole, x_rows, d_rows, slot_gate, w_gate_up, w_down
         )
         shape = (count, blocks, SLOTS)
         outs.append(out.reshape(shape + (D,)))
         backs.append(back.reshape(shape + (D,)))
         dots.append(dot.reshape(shape + (128,)))
-        if split:
-            pending.append((sums[0], lax.ppermute(sums[1], "dp", swap_x)))
+        if whole:
+            parts[i] = sum_z(sums[0])
         else:
-            whole = sum_z(sums[0])
+            halves[i] = (sums[0], lax.ppermute(sums[1], "dp", swap_x))
         first += count
 
-    def reduce_next():
-        keep, got = pending.pop(0)
-        half = (keep.astype(f32) + got.astype(f32)).astype(bf16)
-        parts.append(sum_z(half))
-        return half
-
-    back_sum, back_dots = sum_rows(after(slots, reduce_next()), backs, dots)
+    def left(i, *before):
+        return [add_x(i, *before)] if i in halves else []
+
+    def sent(i):
+        return [parts[i]] if i in parts else []
+
+    back_sum, back_dots = sum_rows(slots, backs, dots)
 
     def pieces_of(value):
         return [value[j * MICRO : (j + 1) * MICRO] for j in range(groups)]
@@ -891,58 +974,109 @@
     own_gates = gates[:MICRO]
     centre = jnp.sum(own_gates * token_dots, axis=1, keepdims=True)
     grad_logits = (own_gates * (token_dots - centre)).astype(bf16)
-    (mixed,) = sum_rows(after(slots, back_sum), outs)
+    (mixed,) = sum_rows(after(slots, back_sum, *sent(1)), outs)
     mix_terms = return_members(pieces_of(mixed), groups)
 
     grad_hidden, grad_branch, grad_attended, grad_norm_moe = middle_back(
-        back_terms, grad_logits, router, hidden, moe_gain, after(cot_rows, mixed), w_out
-    )
-    grad_router = jnp.einsum("btd,bet->de", moe_low, grad_logits, preferred_element_type=f32)
-    grad_out = jnp.einsum("brd,bre->de", attended, grad_branch, preferred_element_type=f32)
+        back_terms, grad_logits, router, hidden, moe_gain, after(cot_rows, mixed, *left(2, mixed)), w_out
+    )
+    grad_router = jnp.einsum("bet,btd->ed", grad_logits, moe_low, preferred_element_type=f32)
+    grad_out = jnp.einsum(
+        "brd,bre->de", attended, grad_branch, preferred_element_type=f32
+    ).astype(bf16)
     gq, gpk, gpv, gok, gov = attend_back(
-        queries, key_value, prompt, bias, lse, grad_attended, cosine, sine
-    )
+        queries,
+        key_value,
+        prompt,
+        after(bias, grad_out, *sent(4)),
+        lse,
+        grad_attended,
+        cosine,
+        sine,
+    )
+
     def prompt_terms(value):
         return return_members(
             [value[:, j * PROMPT_DEV : (j + 1) * PROMPT_DEV] for j in range(groups)], groups
         )
 
-    gp, grad_qkv = weight_back(
-        after(normed, reduce_next()), gq, gok, gov, prompt_terms(gpk), prompt_terms(gpv), cosine, sine
-    )
-    grad_tokens, grad_norm_attn = token_back(gp, w_qkv, token_rows, attn_gain, grad_hidden)
-    while pending:
-        reduce_next()
-    swapped = lax.ppermute(whole[:, piece:], "dp", swap_x)
-    whole = (whole[:, :piece].astype(f32) + swapped.astype(f32)).astype(bf16)
-    parts.insert(0, whole)
-    grad_router = lax.dynamic_slice_in_dim(
-        jnp.concatenate([grad_router, grad_router], axis=1), EXPERTS - first_expert, EXPERTS, 1
-    )
     mixture = sum(term.astype(f32) for term in mix_terms)
     output = (hidden + branch_scale * mixture).astype(bf16)
+    core_bit, row_bit = lax.rem(member, 2), lax.rem(member // 2, 2)
+    grad_out = halve(halve(grad_out, "expert", swap_core, core_bit), "expert", swap_y, row_bit)
+    gp, grad_qkv = weight_back(
+        after(normed, output, *left(3, gq)),
+        gq,
+        gok,
+        gov,
+        prompt_terms(gpk),
+        prompt_terms(gpv),
+        cosine,
+        sine,
+    )
+    grad_tokens, grad_norm_attn = token_back(
+        after(gp, grad_qkv, *sent(2)), w_qkv, token_rows, attn_gain, grad_hidden
+    )
+    grad_qkv = halve(grad_qkv, "expert", swap_core, core_bit)
+    last = [add_x(i, gp) for i in list(halves)]
+    grad_qkv = after(grad_qkv, *last)
+    grad_qkv = halve(grad_qkv, "expert", swap_y, row_bit)
+
+    whole_sums = [parts[i] for i, (_, whole) in enumerate(plan) if whole]
+    whole_sums = jnp.concatenate(whole_sums, axis=0)
+    swapped = lax.ppermute(after(whole_sums[:, piece:], *last), "dp", swap_x)
+    whole_sums = (whole_sums[:, :piece].astype(f32) + swapped.astype(f32)).astype(bf16)
+    pieces, at = [], 0
+    for i, (count, whole) in enumerate(plan):
+        pieces.append(whole_sums[at : at + count] if whole else parts[i])
+        at += count if whole else 0
 
     small = jnp.concatenate(
         [
-            grad_router,
-            grad_norm_attn.reshape(D, 1),
-            grad_norm_moe.reshape(D, 1),
-            jnp.zeros((D, 128 - EXPERTS - 2), f32),
-        ],
-        axis=1,
-    )
-    wide = jnp.concatenate([grad_qkv, grad_out.astype(bf16), small.astype(bf16)], axis=1)
-    wide = lax.psum(wide, ("dp", "expert")).astype(f32)
-    experts_sum = jnp.concatenate(parts, axis=0).astype(f32)
+            lax.dynamic_slice_in_dim(
+                jnp.concatenate([grad_router, grad_router], axis=0),
+                EXPERTS - first_expert,
+                EXPERTS,
+                0,
+            ),
+            grad_norm_attn,
+            grad_norm_moe,
+            jnp.zeros((6, D), f32),
+        ],
+        axis=0,
+    )
+    small = lax.psum(small, ("dp", "expert"))
+    dense = after(jnp.concatenate([grad_qkv, grad_out], axis=1), *sent(3))
+    dense = halve(dense, "dp", swap_x, parity)
+    dense = lax.psum(dense, "dp", axis_index_groups=z_groups)
+    if groups > 4:
+        rest = [[m for m in range(groups) if m % 4 == r] for r in range(4)]
+        dense = lax.psum(dense, "expert", axis_index_groups=rest)
+    width = dense.shape[1] // 2
+    left_own, right_own = dense[:, :width], dense[:, width:]
+    left_x = lax.ppermute(left_own, "dp", swap_x)
+    right_y = lax.ppermute(right_own, "expert", swap_y)
+    left_four = [left_own, left_x] + [
+        lax.ppermute(value, "expert", swap_y) for value in (left_own, left_x)
+    ]
+    right_x = [lax.ppermute(value, "dp", swap_x) for value in (right_own, right_y)]
+    right_four = [right_own, right_x[0], right_y, right_x[1]]
+    left_all = left_four + [core_swap(value, groups) for value in left_four]
+    right_all = right_four + [core_swap(value, groups) for value in right_four]
+    base = core_bit * 4 + row_bit * 2 + parity
+    table = jnp.bitwise_xor(base, jnp.arange(8, dtype=jnp.int32)).astype(jnp.int32)
+    full_qkv, full_out = finish_dense(table, left_all, right_all)
+
+    experts_sum = jnp.concatenate(pieces, axis=0).astype(f32)
     gu_piece = D // (2 * pairs)
     return (
         output.reshape(rows_all, D),
         grad_tokens.reshape(rows_all, D),
-        wide[:, 3 * D + EXPERTS],
-        wide[:, : 2 * D],
-        wide[:, 2 * D : 3 * D],
-        wide[:, 3 * D + EXPERTS + 1],
-        wide[:, 3 * D : 3 * D + EXPERTS],
+        small[EXPERTS],
+        full_qkv,
+        full_out,
+        small[EXPERTS + 1],
+        small[:EXPERTS].T,
         experts_sum[:, :gu_piece],
         experts_sum[:, gu_piece:],
     )

time: 784 us -> 760 us (0.969)
  waiting for transfers between devices: 374 us -> 342 us
  local copies, waits for them, and re-layouts: 49.9 us -> 35.4 us
  Pallas kernels: 260 us -> 274 us
    ppermute x3, waiting for transfers between devices: 0.01 us -> 27.2 us  [exchange_members(): result.append(lax.ppermute(pieces[2 * s + c], 'expert', pairs))]
    ppermute x4, waiting for transfers between devices: 43.1 us -> 16.2 us  [to_row(): return lax.ppermute(value, 'expert', pairs)]
    ppermute x5 -> x6, waiting for transfers between devices: 54.4 us -> 32.5 us  [from_row(): return lax.ppermute(value, 'expert', pairs)]
    ppermute x5 -> x16, waiting for transfers between devices: 117 us -> 101 us  [the longest x5 39.4 us: halve(): got = lax.ppermute(send, axis, swap)]
    concatenate x2 -> x3, local copies, waits for them, and re-layouts: 11.4 us -> 1.15 us  [the longest x1 1.02 us: local(): experts_sum = jnp.concatenate(pieces, axis=0).astype(f32)]
    slice x6 -> x5, local copies, waits for them, and re-layouts: 13.5 us -> 3.72 us  [the longest x1 1.44 us: local(): small[EXPERTS + 1]]
    pallas_call x0 -> x1, Pallas kernels: none -> 8.96 us  [finish_dense(): pl.pallas_call(functools.partial(finish_dense_body, pieces=pieces), grid_...]
    pallas_call x5 -> x6, Pallas kernels: 123 us -> 128 us  [expert_chunk(): pl.pallas_call(functools.partial(expert_body, tile=tile), grid_spec=grid_...]
  transfers between devices with their start and end apart: 41 -> 65, of which waited for: 15 -> 18; matrix products, arithmetic and copies ran while one was open for 12% -> 11% of each run, Pallas kernels for 28% -> 31%
where the time goes in v2:
time: 760 us; the launch traced here: 750 us
  waiting for transfers between devices  342 us (45%)
  Pallas kernels  274 us (36%)
  other arithmetic  44 us (6%)
  local copies, waits for them, and re-layouts  35.4 us (5%)
  starting transfers between devices  32.7 us (4%)
  between operations  15.6 us (2%)
    pallas_call x6, Pallas kernels, expert_chunk(): pl.pallas_call(functools.partial(expert_body, tile=tile), grid_spec=grid_...  128 us
    psum x1, waiting for transfers between devices, local(): small = lax.psum(small, ('dp', 'expert'))  113 us
    psum x1, waiting for transfers between devices, local(): dense = lax.psum(dense, 'dp', axis_index_groups=z_groups)  47.4 us
    ppermute x5, waiting for transfers between devices, halve(): got = lax.ppermute(send, axis, swap)  39.4 us
    ppermute x4, waiting for transfers between devices, local(): halves[i] = (sums[0], lax.ppermute(sums[1], 'dp', swap_x))  38.5 us
    ppermute x6, waiting for transfers between devices, from_row(): return lax.ppermute(value, 'expert', pairs)  32.5 us
    ppermute x3, waiting for transfers between devices, exchange_members(): result.append(lax.ppermute(pieces[2 * s + c], 'expert', pairs))  27.2 us
    pallas_call x2, Pallas kernels, sum_rows(): pl.pallas_call(functools.partial(sum_rows_body, chunks=len(rows), with_do...  25.9 us
  transfers between devices with their start and end apart: 65, of which 18 were waited for; matrix products, arithmetic and copies ran while one was open for 11% of the time, Pallas kernels for 31%

profile of v2, /device:TPU:0, one launch (start us, length us, event | category | flops | bytes accessed | tf_op | source)
XLA Modules:
  0.0 750.1 jit_solution(10173580561024152902)
XLA Ops:
  8.0 3.1 collective-permute-start.4
  13.0 6.8 shard_map.169
  23.4 6.6 collective-permute-done.1
  33.5 11.2 %shard_map.170 = (bf16[1,320,1024]{2,1,0:T(8,128)(2,1)}, f32[4,1,1280]{2,1,0:T(1,128)}, f32[1,320,1024]{2,1,0:T(8,128)}, bf16[1,320,1024]{2,1,0:T(8,128)(2,1)}) custom-call(bf16[2,320,1024]{2,1,0:T(8,128)(2,1)} %get-tuple-element.91.q_ref, bf16[2,256,1024]{2,1,0:T(8,128)(2,1)} %pad_maximum_fusion.1.pk_ref.pv_ref, ...), custom_call_target="tpu_custom_call" | custom-call | flops 13799999488 | tf_op jit(solution)/shard_map/pallas_call | solution.py:515
  44.7 11.3 %shard_map.171 = (bf16[1,320,1024]{2,1,0:T(8,128)(2,1)}, f32[4,1,1280]{2,1,0:T(1,128)}, f32[1,320,1024]{2,1,0:T(8,128)}, bf16[1,320,1024]{2,1,0:T(8,128)(2,1)}) custom-call(bf16[2,320,1024]{2,1,0:T(8,128)(2,1)} %get-tuple-element.91.q_ref, bf16[2,256,1024]{2,1,0:T(8,128)(2,1)} %pad_maximum_fusion.1.pk_ref.pv_ref, ...), custom_call_target="tpu_custom_call" | custom-call | flops 13799999488 | tf_op jit(solution)/shard_map/pallas_call | solution.py:515
  61.7 12.5 %collective-permute-done.14.refs_7_ = bf16[1,320,1024]{2,1,0:T(8,128)(2,1)} collective-permute-done((bf16[1,320,1024]{2,1,0:T(8,128)(2,1)S(1)}, bf16[1,320,1024]{2,1,0:T(8,128)(2,1)}, u32[]{:S(2)}, u32[]{:S(2)}) %collective-permute-start.14) | collective-permute-done | bytes 655392 | tf_op jit(solution)/shard_map/ppermute | solution.py:357
  74.2 13.4 %collective-permute-done.15.refs_8_ = bf16[1,320,1024]{2,1,0:T(8,128)(2,1)} collective-permute-done((bf16[1,320,1024]{2,1,0:T(8,128)(2,1)}, bf16[1,320,1024]{2,1,0:T(8,128)(2,1)}, u32[]{:S(2)}, u32[]{:S(2)}) %collective-permute-start.15) | collective-permute-done | bytes 655392 | tf_op jit(solution)/shard_map/ppermute | solution.py:357
  88.4 15.0 %shard_map.172 = (bf16[8,8,112,1024]{3,2,1,0:T(8,128)(2,1)}, s32[8,8,320]{2,1,0:T(8,128)}) custom-call(s32[8,8,320]{2,1,0:T(8,128)} %negate_select_fusion.1.refs_0_, bf16[1,320,1024]{2,1,0:T(8,128)(2,1)} %copy-done.16, bf16[1,320,1024]{2,1,0:T(8,128)(2,1)} %copy-done.15, bf16[1,320,1024]{2,1,0:T(8,128)(2,1)} %copy-done.28, ...), custom_call_target="tpu_custom_call" | custom-call | flops 17250000896 | tf_op jit(solution)/shard_map/pallas_call | solution.py:112
  104.8 16.8 %shard_map.173 = (bf16[8,8,112,1024]{3,2,1,0:T(8,128)(2,1)}, f32[8,8,112,128]{3,2,1,0:T(8,128)}, f32[8,32,320]{2,1,0:T(8,128)}) custom-call(s32[8,8,320]{2,1,0:T(8,128)} %negate_select_fusion.1.refs_0_, s32[8,8,320]{2,1,0:T(8,128)} %get-tuple-element.132.refs_1_.refs_0_, bf16[1024,32]{1,0:T(8,128)(2,1)} %dynamic-slice_maximum_fusion.refs_2_.refs_4_, ...), custom_call_target="tpu_custom_call" | custom-call | flops 19549999104 | tf_op jit(solution)/shard_map/pallas_call | solution.py:158
  121.5 17.1 %shard_map.174 = (bf16[1,896,1024]{2,1,0:T(8,128)(2,1)}, bf16[1,896,1024]{2,1,0:T(8,128)(2,1)}, f32[1,896,128]{2,1,0:T(8,128)}, bf16[1,4,384,1024]{3,2,1,0:T(8,128)(2,1)}) custom-call(s32[1]{0:T(128)} %bitcast.8.parity_ref, bf16[8,896,1024]{2,1,0:T(8,128)(2,1)} %bitcast.89, bf16[8,896,1024]{2,1,0:T(8,128)(2,1)} %bitcast.83, f32[8,896,128]{2,1,0:T(8,128)} %bitcast.95, ...), custom_call_target="tpu_custom_call" | custom-call | flops 17250000896 | tf_op jit(solution)/shard_map/pallas_call | solution.py:336
  138.7 17.1 %shard_map.175 = (bf16[1,896,1024]{2,1,0:T(8,128)(2,1)}, bf16[1,896,1024]{2,1,0:T(8,128)(2,1)}, f32[1,896,128]{2,1,0:T(8,128)}, bf16[1,4,192,1024]{3,2,1,0:T(8,128)(2,1)}, bf16[1,4,192,1024]{3,2,1,0:T(8,128)(2,1)}) custom-call(s32[1]{0:T(128)} %bitcast.8.parity_ref, bf16[8,896,1024]{2,1,0:T(8,128)(2,1)} %bitcast.90, bf16[8,896,1024]{2,1,0:T(8,128)(2,1)} %bitcast.84, ...), custom_call_target="tpu_custom_call" | custom-call | flops 17250000896 | tf_op jit(solution)/shard_map/pallas_call | solution.py:336
  157.5 29.4 %shard_map.176 = (bf16[2,896,1024]{2,1,0:T(8,128)(2,1)}, bf16[2,896,1024]{2,1,0:T(8,128)(2,1)}, f32[2,896,128]{2,1,0:T(8,128)}, bf16[2,4,192,1024]{3,2,1,0:T(8,128)(2,1)}, bf16[2,4,192,1024]{3,2,1,0:T(8,128)(2,1)}) custom-call(s32[1]{0:T(128)} %bitcast.8.parity_ref, bf16[8,896,1024]{2,1,0:T(8,128)(2,1)} %bitcast.91, bf16[8,896,1024]{2,1,0:T(8,128)(2,1)} %bitcast.85, ...), custom_call_target="tpu_custom_call" | custom-call | flops 34500001792 | tf_op jit(solution)/shard_map/pallas_call | solution.py:336
  186.9 29.7 %shard_map.177 = (bf16[2,896,1024]{2,1,0:T(8,128)(2,1)}, bf16[2,896,1024]{2,1,0:T(8,128)(2,1)}, f32[2,896,128]{2,1,0:T(8,128)}, bf16[2,4,192,1024]{3,2,1,0:T(8,128)(2,1)}, bf16[2,4,192,1024]{3,2,1,0:T(8,128)(2,1)}) custom-call(s32[1]{0:T(128)} %bitcast.8.parity_ref, bf16[8,896,1024]{2,1,0:T(8,128)(2,1)} %bitcast.92, bf16[8,896,1024]{2,1,0:T(8,128)(2,1)} %bitcast.86, ...), custom_call_target="tpu_custom_call" | custom-call | flops 34500001792 | tf_op jit(solution)/shard_map/pallas_call | solution.py:336
  224.3 17.1 %shard_map.178 = (bf16[1,896,1024]{2,1,0:T(8,128)(2,1)}, bf16[1,896,1024]{2,1,0:T(8,128)(2,1)}, f32[1,896,128]{2,1,0:T(8,128)}, bf16[1,4,384,1024]{3,2,1,0:T(8,128)(2,1)}) custom-call(s32[1]{0:T(128)} %bitcast.8.parity_ref, bf16[8,896,1024]{2,1,0:T(8,128)(2,1)} %bitcast.93, bf16[8,896,1024]{2,1,0:T(8,128)(2,1)} %bitcast.87, f32[8,896,128]{2,1,0:T(8,128)} %bitcast.99, ...), custom_call_target="tpu_custom_call" | custom-call | flops 17250000896 | tf_op jit(solution)/shard_map/pallas_call | solution.py:336
  241.4 17.4 %shard_map.179 = (bf16[1,896,1024]{2,1,0:T(8,128)(2,1)}, bf16[1,896,1024]{2,1,0:T(8,128)(2,1)}, f32[1,896,128]{2,1,0:T(8,128)}, bf16[1,4,192,1024]{3,2,1,0:T(8,128)(2,1)}, bf16[1,4,192,1024]{3,2,1,0:T(8,128)(2,1)}) custom-call(s32[1]{0:T(128)} %bitcast.8.parity_ref, bf16[8,896,1024]{2,1,0:T(8,128)(2,1)} %bitcast.94, bf16[8,896,1024]{2,1,0:T(8,128)(2,1)} %bitcast.88, ...), custom_call_target="tpu_custom_call" | custom-call | flops 17250000896 | tf_op jit(solution)/shard_map/pallas_call | solution.py:336
  258.8 13.4 %shard_map.180 = (bf16[8,320,1024]{2,1,0:T(8,128)(2,1)}, f32[8,8,320]{2,1,0:T(8,128)}) custom-call(s32[8,8,320]{2,1,0:T(8,128)} %get-tuple-element.132.refs_1_.refs_0_, bf16[1,8,112,1024]{3,2,1,0:T(8,128)(2,1)} %bitcast.107, bf16[1,8,112,1024]{3,2,1,0:T(8,128)(2,1)} %bitcast.108, bf16[2,8,112,1024]{3,2,1,0:T(8,128)(2,1)} %bitcast.103, ...), custom_call_target="tpu_custom_call" | custom-call | flops 17250000896 | tf_op jit(solution)/shard_map/pallas_call | solution.py:227
  272.2 4.2 fusion.16
  276.4 12.5 %shard_map.181 = bf16[8,320,1024]{2,1,0:T(8,128)(2,1)} custom-call(s32[8,8,320]{2,1,0:T(8,128)} %get-tuple-element.132.refs_1_.refs_0_, bf16[1,8,112,1024]{3,2,1,0:T(8,128)(2,1)} %bitcast.105, bf16[1,8,112,1024]{3,2,1,0:T(8,128)(2,1)} %bitcast.106, bf16[2,8,112,1024]{3,2,1,0:T(8,128)(2,1)} %bitcast.101, bf16[2,8,112,1024]{3,2,1,0:T(8,128)(2,1)} %bitcast.102, ...), custom_call_target="tpu_custom_call" | custom-call | flops 17250000896 | tf_op jit(solution)/shard_map/pallas_call | solution.py:227
  291.5 2.1 collective-permute-done.29
  294.0 3.3 add_convert_fusion.5
  298.9 5.1 add_convert_fusion.1
  304.6 24.1 %collective-permute-done.27 = f32[2,8,320]{2,1,0:T(8,128)S(1)} collective-permute-done((f32[2,8,320]{2,1,0:T(8,128)S(1)}, f32[2,8,320]{2,1,0:T(8,128)S(1)}, u32[]{:S(2)}, u32[]{:S(2)}) %collective-permute-start.27) | collective-permute-done | bytes 20512 | tf_op jit(solution)/shard_map/ppermute | solution.py:396
  329.1 3.1 collective-permute-done.28
  332.5 2.3 add_convert_fusion.7
  336.6 8.3 %shard_map.182 = (f32[2,320,1024]{2,1,0:T(8,128)}, bf16[2,320,1024]{2,1,0:T(8,128)(2,1)}, bf16[2,320,1024]{2,1,0:T(8,128)(2,1)}, f32[1,1024]{1,0:T(1,128)}) custom-call(bf16[2,320,1024]{2,1,0:T(8,128)(2,1)} %get-tuple-element.175.refs_0_, bf16[2,320,1024]{2,1,0:T(8,128)(2,1)} %collective-permute-done.23.refs_1_, ...), custom_call_target="tpu_custom_call" | custom-call | flops 9200000000 | tf_op jit(solution)/shard_map/pallas_call | solution.py:582
  344.9 4.8 bitcast_convert_fusion
  349.7 16.1 %collective-permute-done.21 = bf16[2,320,1024]{2,1,0:T(8,128)(2,1)} collective-permute-done((bf16[2,320,1024]{2,1,0:T(8,128)(2,1)S(1)}, bf16[2,320,1024]{2,1,0:T(8,128)(2,1)}, u32[]{:S(2)}, u32[]{:S(2)}) %collective-permute-start.21) | collective-permute-done | bytes 1310752 | tf_op jit(solution)/shard_map/ppermute | solution.py:363
  365.9 4.2 add_convert_fusion.6
  370.1 22.9 %shard_map.183 = (bf16[2,320,1024]{2,1,0:T(8,128)(2,1)}, bf16[2,256,512]{2,1,0:T(8,128)(2,1)}, bf16[2,256,512]{2,1,0:T(8,128)(2,1)}, bf16[2,256,512]{2,1,0:T(8,128)(2,1)}, bf16[2,256,512]{2,1,0:T(8,128)(2,1)}) custom-call(bf16[2,320,1024]{2,1,0:T(8,128)(2,1)} %get-tuple-element.91.q_ref, bf16[2,256,1024]{2,1,0:T(8,128)(2,1)} %pad_maximum_fusion.1.pk_ref.pv_ref, ...), custom_call_target="tpu_custom_call" | custom-call | flops 26449999872 | tf_op jit(solution)/shard_map/pallas_call | solution.py:643
  401.5 5.2 add_convert_fusion
  407.5 11.3 %shard_map.184 = (bf16[2,320,2048]{2,1,0:T(8,128)(2,1)}, bf16[1024,2048]{1,0:T(8,128)(2,1)}) custom-call(bf16[2,320,1024]{2,1,0:T(8,128)(2,1)} %get-tuple-element.153.refs_0_, bf16[2,320,1024]{2,1,0:T(8,128)(2,1)} %get-tuple-element.151.refs_1_, bf16[2,256,512]{2,1,0:T(8,128)(2,1)} %get-tuple-element.154.refs_2_, ...), custom_call_target="tpu_custom_call" | custom-call | flops 12650000384 | tf_op jit(solution)/shard_map/pallas_call | solution.py:710
  418.8 3.4 constant_dynamic-slice_fusion.4
  422.8 36.5 %collective-permute-done.37 = bf16[1,4,192,1024]{3,2,1,0:T(8,128)(2,1)} collective-permute-done((bf16[1,4,192,1024]{3,2,1,0:T(8,128)(2,1)}, bf16[1,4,192,1024]{3,2,1,0:T(8,128)(2,1)}, u32[]{:S(2)}, u32[]{:S(2)}) %collective-permute-start.37) | collective-permute-done | bytes 1572896 | tf_op jit(solution)/shard_map/ppermute | solution.py:948
  459.3 3.4 add_convert_fusion.3
  462.7 2.4 add_convert_fusion.2
  471.4 31.0 %collective-permute-done.40 = bf16[256,1024]{1,0:T(8,128)(2,1)} collective-permute-done((bf16[256,1024]{1,0:T(8,128)(2,1)}, bf16[256,1024]{1,0:T(8,128)(2,1)}, u32[]{:S(2)}, u32[]{:S(2)}) %collective-permute-start.40) | collective-permute-done | bytes 524320 | tf_op jit(solution)/shard_map/ppermute | solution.py:770
  502.4 2.0 add_convert_fusion.12
  507.6 8.2 %shard_map.185 = (bf16[2,320,1024]{2,1,0:T(8,128)(2,1)}, f32[1,1024]{1,0:T(1,128)}) custom-call(bf16[2,320,2048]{2,1,0:T(8,128)(2,1)} %get-tuple-element.160.gp_ref, bf16[1024,2048]{1,0:T(8,128)(2,1)} %w_ref.7, bf16[2,320,1024]{2,1,0:T(8,128)(2,1)} %bitcast.77, f32[1,1024]{1,0:T(1,128)} %bitcast.82, f32[2,320,1024]{2,1,0:T(8,128)} %get-tuple-element.161.hidden_ref), custom_call_target="tpu_custom_call" | custom-call | flops 9200000000 | tf_op jit(solution)/shard_map/pallas_call | solution.py:746
  517.3 8.4 %collective-permute-done.41 = bf16[128,3072]{1,0:T(8,128)(2,1)S(1)} collective-permute-done((bf16[128,3072]{1,0:T(8,128)(2,1)}, bf16[128,3072]{1,0:T(8,128)(2,1)S(1)}, u32[]{:S(2)}, u32[]{:S(2)}) %collective-permute-start.41) | collective-permute-done | bytes 786464 | tf_op jit(solution)/shard_map/ppermute | solution.py:770
  528.7 113.3 %all-reduce.3.cloned.1.call-done = f32[40,1024]{1,0:T(8,128)} async-done(((f32[40,1024]{1,0:T(8,128)}), f32[40,1024]{1,0:T(8,128)}) %all-reduce.3.cloned.1.call-update) | async-done | bytes 163856 | tf_op jit(solution)/shard_map/psum | solution.py:1048
  643.6 47.4 %all-reduce.5.cloned.1.call-done = bf16[128,3072]{1,0:T(8,128)(2,1)} async-done(((bf16[128,3072]{1,0:T(8,128)(2,1)}), bf16[128,3072]{1,0:T(8,128)(2,1)}) %all-reduce.5.cloned.1.call-update) | async-done | bytes 786448 | tf_op jit(solution)/shard_map/psum | solution.py:1051
  698.3 6.0 collective-permute-done.50.refs_10_
  707.3 7.0 collective-permute-done.42.refs_1_
  715.7 6.2 collective-permute-done.51.refs_11_
  721.9 2.2 collective-permute-done.44.refs_3_
  724.2 3.7 reduce-scatter.17.cloned.1.call-done
  730.5 2.5 slice.161
  733.8 9.0 %shard_map.186 = (f32[1024,2048]{1,0:T(8,128)}, f32[1024,1024]{1,0:T(8,128)}) custom-call(s32[8]{0:T(128)} %iota_xor_fusion.table_ref, bf16[128,1536]{1,0:T(8,128)(2,1)} %copy-done.19, bf16[128,1536]{1,0:T(8,128)(2,1)} %collective-permute-done.42.refs_1_, bf16[128,1536]{1,0:T(8,128)(2,1)} %collective-permute-done.43.refs_2_, ...), custom_call_target="tpu_custom_call" | custom-call | flops 10350000128 | tf_op jit(solution)/shard_map/pallas_call | solution.py:800
  (272 shorter events, 75.0 us)
Async XLA Ops:
  7.2 217.1 %reduce-scatter.7.cloned.1.call-start = ((), (), s32[]{:S(2)}) async-start(), calls=%async_computation.6 | async-start | bytes 3932160 | tf_op jit(solution)/shard_map/reduce_scatter | solution.py:911
  8.0 23.7 %collective-permute-start.4 = (s32[2,8,320]{2,1,0:T(8,128)S(1)}, s32[2,8,320]{2,1,0:T(8,128)S(1)}, u32[]{:S(2)}, u32[]{:S(2)}) collective-permute-start(s32[2,8,320]{2,1,0:T(8,128)S(1)} %bitcast.67), channel_id=1, source_target_pairs={{2,0},{3,1},{0,2},{1,3},{6,4},{7,5},{4,6},{5,7},{10,8},{11,9},{8,1... | collective-permute-start | bytes 61448 | tf_op jit(solution)/shard_map/ppermute | solution.py:357
  11.1 44.9 %collective-permute-start.3 = (s32[2,8,320]{2,1,0:T(8,128)S(1)}, s32[2,8,320]{2,1,0:T(8,128)S(1)}, u32[]{:S(2)}, u32[]{:S(2)}) collective-permute-start(s32[2,8,320]{2,1,0:T(8,128)S(1)} %bitcast.68), channel_id=1, source_target_pairs={{0,1},{1,0},{2,3},{3,2},{4,5},{5,4},{6,7},{7,6},{8,9},{9,8},{10,11... | collective-permute-start | bytes 61448 | tf_op jit(solution)/shard_map/ppermute | solution.py:351
  21.5 36.7 %collective-permute-start.8 = (bf16[1,320,1024]{2,1,0:T(8,128)(2,1)S(1)}, bf16[1,320,1024]{2,1,0:T(8,128)(2,1)}, u32[]{:S(2)}, u32[]{:S(2)}) collective-permute-start(bf16[1,320,1024]{2,1,0:T(8,128)(2,1)S(1)} %get-tuple-element.179.refs_1_), channel_id=1, source_target_pairs={{2,0},{3,1},{0,2},{1,3},{6,4},{7,5},{4,6},{5,7},{10,8},{11,9},{8,1... | collective-permute-start | bytes 1966088 | tf_op jit(solution)/shard_map/ppermute | solution.py:357
  31.7 26.8 %collective-permute-start.6 = (bf16[1,320,1024]{2,1,0:T(8,128)(2,1)S(1)}, bf16[1,320,1024]{2,1,0:T(8,128)(2,1)S(1)}, u32[]{:S(2)}, u32[]{:S(2)}) collective-permute-start(bf16[1,320,1024]{2,1,0:T(8,128)(2,1)S(1)} %get-tuple-element.179.refs_1_), channel_id=1, source_target_pairs={{0,1},{1,0},{2,3},{3,2},{4,5},{5,4},{6,7},{7,6},{8,9},{9,8},{10,11... | collective-permute-start | bytes 1966088 | tf_op jit(solution)/shard_map/ppermute | solution.py:351
  32.2 24.2 %collective-permute-start.5 = (s32[2,8,320]{2,1,0:T(8,128)S(1)}, s32[2,8,320]{2,1,0:T(8,128)S(1)}, u32[]{:S(2)}, u32[]{:S(2)}) collective-permute-start(s32[2,8,320]{2,1,0:T(8,128)S(1)} %collective-permute-done.4), channel_id=1, source_target_pairs={{0,1},{1,0},{2,3},{3,2},{4,5},{5,4},{6,7},{7,6},{8,9},{9,8},{10,11... | collective-permute-start | bytes 61448 | tf_op jit(solution)/shard_map/ppermute | solution.py:351
  32.3 26.2 %collective-permute-start.9 = (bf16[1,320,1024]{2,1,0:T(8,128)(2,1)S(1)}, bf16[1,320,1024]{2,1,0:T(8,128)(2,1)}, u32[]{:S(2)}, u32[]{:S(2)}) collective-permute-start(bf16[1,320,1024]{2,1,0:T(8,128)(2,1)S(1)} %get-tuple-element.99.refs_2_), channel_id=1, source_target_pairs={{2,0},{3,1},{0,2},{1,3},{6,4},{7,5},{4,6},{5,7},{10,8},{11,9},{8,1... | collective-permute-start | bytes 1966088 | tf_op jit(solution)/shard_map/ppermute | solution.py:357
  56.5 17.7 %collective-permute-start.14 = (bf16[1,320,1024]{2,1,0:T(8,128)(2,1)S(1)}, bf16[1,320,1024]{2,1,0:T(8,128)(2,1)}, u32[]{:S(2)}, u32[]{:S(2)}) collective-permute-start(bf16[1,320,1024]{2,1,0:T(8,128)(2,1)S(1)} %copy-done.27), channel_id=1, source_target_pairs={{2,0},{3,1},{0,2},{1,3},{6,4},{7,5},{4,6},{5,7},{10,8},{11,9},{8,1... | collective-permute-start | bytes 1966088 | tf_op jit(solution)/shard_map/ppermute | solution.py:357
  58.2 29.4 %collective-permute-start.15 = (bf16[1,320,1024]{2,1,0:T(8,128)(2,1)}, bf16[1,320,1024]{2,1,0:T(8,128)(2,1)}, u32[]{:S(2)}, u32[]{:S(2)}) collective-permute-start(bf16[1,320,1024]{2,1,0:T(8,128)(2,1)} %get-tuple-element.97.refs_4_), channel_id=1, source_target_pairs={{2,0},{3,1},{0,2},{1,3},{6,4},{7,5},{4,6},{5,7},{10,8},{11,9},{8,1... | collective-permute-start | bytes 1966088 | tf_op jit(solution)/shard_map/ppermute | solution.py:357
  58.5 29.1 %collective-permute-start.10 = (bf16[1,320,1024]{2,1,0:T(8,128)(2,1)}, bf16[1,320,1024]{2,1,0:T(8,128)(2,1)S(1)}, u32[]{:S(2)}, u32[]{:S(2)}) collective-permute-start(bf16[1,320,1024]{2,1,0:T(8,128)(2,1)} %collective-permute-done.8.refs_5_), channel_id=1, source_target_pairs={{0,1},{1,0},{2,3},{3,2},{4,5},{5,4},{6,7},{7,6},{8,9},{9,8},{10,11... | collective-permute-start | bytes 1966088 | tf_op jit(solution)/shard_map/ppermute | solution.py:351
  59.3 28.8 %collective-permute-start.11 = (bf16[1,320,1024]{2,1,0:T(8,128)(2,1)}, bf16[1,320,1024]{2,1,0:T(8,128)(2,1)}, u32[]{:S(2)}, u32[]{:S(2)}) collective-permute-start(bf16[1,320,1024]{2,1,0:T(8,128)(2,1)} %collective-permute-done.9.refs_6_), channel_id=1, source_target_pairs={{0,1},{1,0},{2,3},{3,2},{4,5},{5,4},{6,7},{7,6},{8,9},{9,8},{10,11... | collective-permute-start | bytes 1966088 | tf_op jit(solution)/shard_map/ppermute | solution.py:351
  61.2 42.3 %collective-permute-start.12 = (bf16[1,320,1024]{2,1,0:T(8,128)(2,1)S(1)}, bf16[1,320,1024]{2,1,0:T(8,128)(2,1)S(1)}, u32[]{:S(2)}, u32[]{:S(2)}) collective-permute-start(bf16[1,320,1024]{2,1,0:T(8,128)(2,1)S(1)} %copy-done.27), channel_id=1, source_target_pairs={{0,1},{1,0},{2,3},{3,2},{4,5},{5,4},{6,7},{7,6},{8,9},{9,8},{10,11... | collective-permute-start | bytes 1966088 | tf_op jit(solution)/shard_map/ppermute | solution.py:351
  74.2 29.3 %collective-permute-start.13 = (bf16[1,320,1024]{2,1,0:T(8,128)(2,1)}, bf16[1,320,1024]{2,1,0:T(8,128)(2,1)S(1)}, u32[]{:S(2)}, u32[]{:S(2)}) collective-permute-start(bf16[1,320,1024]{2,1,0:T(8,128)(2,1)} %get-tuple-element.97.refs_4_), channel_id=1, source_target_pairs={{0,1},{1,0},{2,3},{3,2},{4,5},{5,4},{6,7},{7,6},{8,9},{9,8},{10,11... | collective-permute-start | bytes 1966088 | tf_op jit(solution)/shard_map/ppermute | solution.py:351
  87.6 15.9 %collective-permute-start.16 = (bf16[1,320,1024]{2,1,0:T(8,128)(2,1)}, bf16[1,320,1024]{2,1,0:T(8,128)(2,1)S(1)}, u32[]{:S(2)}, u32[]{:S(2)}) collective-permute-start(bf16[1,320,1024]{2,1,0:T(8,128)(2,1)} %collective-permute-done.14.refs_7_), channel_id=1, source_target_pairs={{0,1},{1,0},{2,3},{3,2},{4,5},{5,4},{6,7},{7,6},{8,9},{9,8},{10,11... | collective-permute-start | bytes 1966088 | tf_op jit(solution)/shard_map/ppermute | solution.py:351
  87.6 15.9 %collective-permute-start.17 = (bf16[1,320,1024]{2,1,0:T(8,128)(2,1)}, bf16[1,320,1024]{2,1,0:T(8,128)(2,1)}, u32[]{:S(2)}, u32[]{:S(2)}) collective-permute-start(bf16[1,320,1024]{2,1,0:T(8,128)(2,1)} %collective-permute-done.15.refs_8_), channel_id=1, source_target_pairs={{0,1},{1,0},{2,3},{3,2},{4,5},{5,4},{6,7},{7,6},{8,9},{9,8},{10,11... | collective-permute-start | bytes 1966088 | tf_op jit(solution)/shard_map/ppermute | solution.py:351
  138.6 133.6 %reduce-scatter.9.cloned.1.call-start = ((), (), s32[]{:S(2)}) async-start(), calls=%async_computation.7 | async-start | bytes 1966080 | tf_op jit(solution)/shard_map/reduce_scatter | solution.py:911
  155.8 60.8 %collective-permute-start.18 = (bf16[1,4,192,1024]{3,2,1,0:T(8,128)(2,1)}, bf16[1,4,192,1024]{3,2,1,0:T(8,128)(2,1)S(1)}, u32[]{:S(2)}, u32[]{:S(2)}) collective-permute-start(bf16[1,4,192,1024]{3,2,1,0:T(8,128)(2,1)} %get-tuple-element.117), channel_id=1, source_target_pairs={{0,4},{4,0},{8,12},{12,8},{16,20},{20,16},{24,28},{28,24},{1,5},{5... | collective-permute-start | bytes 4718600 | tf_op jit(solution)/shard_map/ppermute | solution.py:948
  218.5 151.6 %reduce-scatter.11.cloned.1.call-start = ((), (), s32[]{:S(2)}) async-start(), calls=%async_computation.8 | async-start | bytes 3932160 | tf_op jit(solution)/shard_map/reduce_scatter | solution.py:911
  222.2 71.3 %collective-permute-start.29 = (bf16[2,4,192,1024]{3,2,1,0:T(8,128)(2,1)}, bf16[2,4,192,1024]{3,2,1,0:T(8,128)(2,1)}, u32[]{:S(2)}, u32[]{:S(2)}) collective-permute-start(bf16[2,4,192,1024]{3,2,1,0:T(8,128)(2,1)} %get-tuple-element.142), channel_id=1, source_target_pairs={{0,4},{4,0},{8,12},{12,8},{16,20},{20,16},{24,28},{28,24},{1,5},{5... | collective-permute-start | bytes 9437192 | tf_op jit(solution)/shard_map/ppermute | solution.py:948
  222.6 170.4 %collective-permute-start.22 = (bf16[2,4,192,1024]{3,2,1,0:T(8,128)(2,1)}, bf16[2,4,192,1024]{3,2,1,0:T(8,128)(2,1)}, u32[]{:S(2)}, u32[]{:S(2)}) collective-permute-start(bf16[2,4,192,1024]{3,2,1,0:T(8,128)(2,1)} %get-tuple-element.136), channel_id=1, source_target_pairs={{0,4},{4,0},{8,12},{12,8},{16,20},{20,16},{24,28},{28,24},{1,5},{5... | collective-permute-start | bytes 9437192 | tf_op jit(solution)/shard_map/ppermute | solution.py:948
  241.3 263.1 %reduce-scatter.13.cloned.1.call-start = ((), (), s32[]{:S(2)}) async-start(), calls=%async_computation.9 | async-start | bytes 3932160 | tf_op jit(solution)/shard_map/reduce_scatter | solution.py:911
  276.4 17.7 %collective-permute-start.24 = (bf16[2,320,1024]{2,1,0:T(8,128)(2,1)}, bf16[2,320,1024]{2,1,0:T(8,128)(2,1)}, u32[]{:S(2)}, u32[]{:S(2)}) collective-permute-start(bf16[2,320,1024]{2,1,0:T(8,128)(2,1)} %get-tuple-element.173), channel_id=1, source_target_pairs={{0,1},{1,0},{2,3},{3,2},{4,5},{5,4},{6,7},{7,6},{8,9},{9,8},{10,11... | collective-permute-start | bytes 3932168 | tf_op jit(solution)/shard_map/ppermute | solution.py:351
  290.9 41.6 %collective-permute-start.20 = (bf16[2,320,1024]{2,1,0:T(8,128)(2,1)S(1)}, bf16[2,320,1024]{2,1,0:T(8,128)(2,1)}, u32[]{:S(2)}, u32[]{:S(2)}) collective-permute-start(bf16[2,320,1024]{2,1,0:T(8,128)(2,1)S(1)} %get-tuple-element.177), channel_id=1, source_target_pairs={{0,1},{1,0},{2,3},{3,2},{4,5},{5,4},{6,7},{7,6},{8,9},{9,8},{10,11... | collective-permute-start | bytes 3932168 | tf_op jit(solution)/shard_map/ppermute | solution.py:351
  293.5 43.1 %collective-permute-start.23 = (bf16[2,320,1024]{2,1,0:T(8,128)(2,1)}, bf16[2,320,1024]{2,1,0:T(8,128)(2,1)}, u32[]{:S(2)}, u32[]{:S(2)}) collective-permute-start(bf16[2,320,1024]{2,1,0:T(8,128)(2,1)} %get-tuple-element.174), channel_id=1, source_target_pairs={{0,1},{1,0},{2,3},{3,2},{4,5},{5,4},{6,7},{7,6},{8,9},{9,8},{10,11... | collective-permute-start | bytes 3932168 | tf_op jit(solution)/shard_map/ppermute | solution.py:351
  297.3 39.2 %collective-permute-start.25 = (bf16[2,320,1024]{2,1,0:T(8,128)(2,1)}, bf16[2,320,1024]{2,1,0:T(8,128)(2,1)}, u32[]{:S(2)}, u32[]{:S(2)}) collective-permute-start(bf16[2,320,1024]{2,1,0:T(8,128)(2,1)} %add_convert_fusion.5), channel_id=1, source_target_pairs={{0,2},{1,3},{2,0},{3,1},{4,6},{5,7},{6,4},{7,5},{8,10},{9,11},{10,... | collective-permute-start | bytes 3932168 | tf_op jit(solution)/shard_map/ppermute | solution.py:363
  304.0 202.3 %reduce-scatter.15.cloned.1.call-start = ((), (), s32[]{:S(2)}) async-start(), calls=%async_computation.11 | async-start | bytes 3932160 | tf_op jit(solution)/shard_map/reduce_scatter | solution.py:911
  304.0 24.7 %collective-permute-start.27 = (f32[2,8,320]{2,1,0:T(8,128)S(1)}, f32[2,8,320]{2,1,0:T(8,128)S(1)}, u32[]{:S(2)}, u32[]{:S(2)}) collective-permute-start(f32[2,8,320]{2,1,0:T(8,128)S(1)} %get-tuple-element.191), channel_id=1, source_target_pairs={{2,0},{3,1},{0,2},{1,3},{6,4},{7,5},{4,6},{5,7},{10,8},{11,9},{8,1... | collective-permute-start | bytes 61448 | tf_op jit(solution)/shard_map/ppermute | solution.py:396
  332.2 17.5 %collective-permute-start.19 = (bf16[2,320,1024]{2,1,0:T(8,128)(2,1)S(1)}, bf16[2,320,1024]{2,1,0:T(8,128)(2,1)}, u32[]{:S(2)}, u32[]{:S(2)}) collective-permute-start(bf16[2,320,1024]{2,1,0:T(8,128)(2,1)S(1)} %get-tuple-element.176), channel_id=1, source_target_pairs={{0,1},{1,0},{2,3},{3,2},{4,5},{5,4},{6,7},{7,6},{8,9},{9,8},{10,11... | collective-permute-start | bytes 3932168 | tf_op jit(solution)/shard_map/ppermute | solution.py:351
  334.8 31.1 %collective-permute-start.21 = (bf16[2,320,1024]{2,1,0:T(8,128)(2,1)S(1)}, bf16[2,320,1024]{2,1,0:T(8,128)(2,1)}, u32[]{:S(2)}, u32[]{:S(2)}) collective-permute-start(bf16[2,320,1024]{2,1,0:T(8,128)(2,1)S(1)} %add_convert_fusion.7), channel_id=1, source_target_pairs={{0,2},{1,3},{2,0},{3,1},{4,6},{5,7},{6,4},{7,5},{8,10},{9,11},{10,... | collective-permute-start | bytes 3932168 | tf_op jit(solution)/shard_map/ppermute | solution.py:363
  394.7 12.1 %collective-permute-start.30 = (bf16[2,64,512]{2,1,0:T(8,128)(2,1)S(1)}, bf16[2,64,512]{2,1,0:T(8,128)(2,1)S(1)}, u32[]{:S(2)}, u32[]{:S(2)}) collective-permute-start(bf16[2,64,512]{2,1,0:T(8,128)(2,1)S(1)} %get-tuple-element.186), channel_id=1, source_target_pairs={{0,1},{1,0},{2,3},{3,2},{4,5},{5,4},{6,7},{7,6},{8,9},{9,8},{10,11... | collective-permute-start | bytes 393224 | tf_op jit(solution)/shard_map/ppermute | solution.py:351
  406.7 235.3 %all-reduce.3.cloned.1.call-start = ((), (), s32[]{:S(2)}) async-start(), calls=%async_computation.10 | async-start | bytes 327680 | tf_op jit(solution)/shard_map/psum | solution.py:1048
  422.2 40.6 %collective-permute-start.36 = (bf16[512,2048]{1,0:T(8,128)(2,1)}, bf16[512,2048]{1,0:T(8,128)(2,1)}, u32[]{:S(2)}, u32[]{:S(2)}) collective-permute-start(bf16[512,2048]{1,0:T(8,128)(2,1)} %constant_dynamic-slice_fusion.4), channel_id=1, source_target_pairs={{0,1},{1,0},{2,3},{3,2},{4,5},{5,4},{6,7},{7,6},{8,9},{9,8},{10,11... | collective-permute-start | bytes 6291464 | tf_op jit(solution)/shard_map/ppermute | solution.py:770
  422.2 37.1 %collective-permute-start.37 = (bf16[1,4,192,1024]{3,2,1,0:T(8,128)(2,1)}, bf16[1,4,192,1024]{3,2,1,0:T(8,128)(2,1)}, u32[]{:S(2)}, u32[]{:S(2)}) collective-permute-start(bf16[1,4,192,1024]{3,2,1,0:T(8,128)(2,1)} %get-tuple-element.166), channel_id=1, source_target_pairs={{0,4},{4,0},{8,12},{12,8},{16,20},{20,16},{24,28},{28,24},{1,5},{5... | collective-permute-start | bytes 4718600 | tf_op jit(solution)/shard_map/ppermute | solution.py:948
  422.5 45.1 %collective-permute-start.39 = (bf16[512,1024]{1,0:T(8,128)(2,1)S(1)}, bf16[512,1024]{1,0:T(8,128)(2,1)S(1)}, u32[]{:S(2)}, u32[]{:S(2)}) collective-permute-start(bf16[512,1024]{1,0:T(8,128)(2,1)S(1)} %constant_dynamic-slice_fusion.2), channel_id=1, source_target_pairs={{0,1},{1,0},{2,3},{3,2},{4,5},{5,4},{6,7},{7,6},{8,9},{9,8},{10,11... | collective-permute-start | bytes 3145736 | tf_op jit(solution)/shard_map/ppermute | solution.py:770
  466.2 38.3 %collective-permute-start.38 = (bf16[256,2048]{1,0:T(8,128)(2,1)}, bf16[256,2048]{1,0:T(8,128)(2,1)}, u32[]{:S(2)}, u32[]{:S(2)}) collective-permute-start(bf16[256,2048]{1,0:T(8,128)(2,1)} %constant_dynamic-slice_fusion.3), channel_id=1, source_target_pairs={{0,2},{1,3},{2,0},{3,1},{4,6},{5,7},{6,4},{7,5},{8,10},{9,11},{10,... | collective-permute-start | bytes 3145736 | tf_op jit(solution)/shard_map/ppermute | solution.py:770
  468.8 33.6 %collective-permute-start.40 = (bf16[256,1024]{1,0:T(8,128)(2,1)}, bf16[256,1024]{1,0:T(8,128)(2,1)}, u32[]{:S(2)}, u32[]{:S(2)}) collective-permute-start(bf16[256,1024]{1,0:T(8,128)(2,1)} %constant_dynamic-slice_fusion.1), channel_id=1, source_target_pairs={{0,2},{1,3},{2,0},{3,1},{4,6},{5,7},{6,4},{7,5},{8,10},{9,11},{10,... | collective-permute-start | bytes 1572872 | tf_op jit(solution)/shard_map/ppermute | solution.py:770
  507.2 18.4 %collective-permute-start.41 = (bf16[128,3072]{1,0:T(8,128)(2,1)}, bf16[128,3072]{1,0:T(8,128)(2,1)S(1)}, u32[]{:S(2)}, u32[]{:S(2)}) collective-permute-start(bf16[128,3072]{1,0:T(8,128)(2,1)} %constant_dynamic-slice_fusion), channel_id=1, source_target_pairs={{0,4},{4,0},{8,12},{12,8},{16,20},{20,16},{24,28},{28,24},{1,5},{5... | collective-permute-start | bytes 2359304 | tf_op jit(solution)/shard_map/ppermute | solution.py:770
  517.2 173.7 %all-reduce.5.cloned.1.call-start = ((), (), s32[]{:S(2)}) async-start(), calls=%async_computation.12 | async-start | bytes 1572864 | tf_op jit(solution)/shard_map/psum | solution.py:1051
  526.8 201.2 %reduce-scatter.17.cloned.1.call-start = ((), (), s32[]{:S(2)}) async-start(), calls=%async_computation.13 | async-start | bytes 1966080 | tf_op jit(solution)/shard_map/reduce_scatter | solution.py:911
  528.3 169.0 %collective-permute-start.56 = (bf16[2,192,1024]{2,1,0:T(8,128)(2,1)S(1)}, bf16[2,192,1024]{2,1,0:T(8,128)(2,1)S(1)}, u32[]{:S(2)}, u32[]{:S(2)}) collective-permute-start(bf16[2,192,1024]{2,1,0:T(8,128)(2,1)S(1)} %slice.158), channel_id=1, source_target_pairs={{0,4},{4,0},{8,12},{12,8},{16,20},{20,16},{24,28},{28,24},{1,5},{5... | collective-permute-start | bytes 2359304 | tf_op jit(solution)/shard_map/ppermute | solution.py:1027
  693.8 12.1 %collective-permute-start.49 = (bf16[128,1536]{1,0:T(8,128)(2,1)S(1)}, bf16[128,1536]{1,0:T(8,128)(2,1)}, u32[]{:S(2)}, u32[]{:S(2)}) collective-permute-start(bf16[128,1536]{1,0:T(8,128)(2,1)S(1)} %get-tuple-element.180.refs_8_), channel_id=1, source_target_pairs={{0,4},{4,0},{8,12},{12,8},{16,20},{20,16},{24,28},{28,24},{1,5},{5... | collective-permute-start | bytes 1179656 | tf_op jit(solution)/shard_map/ppermute | solution.py:1062
  695.2 19.1 %collective-permute-start.42 = (bf16[128,1536]{1,0:T(8,128)(2,1)S(1)}, bf16[128,1536]{1,0:T(8,128)(2,1)}, u32[]{:S(2)}, u32[]{:S(2)}) collective-permute-start(bf16[128,1536]{1,0:T(8,128)(2,1)S(1)} %get-tuple-element.181.refs_0_), channel_id=1, source_target_pairs={{0,4},{4,0},{8,12},{12,8},{16,20},{20,16},{24,28},{28,24},{1,5},{5... | collective-permute-start | bytes 1179656 | tf_op jit(solution)/shard_map/ppermute | solution.py:1057
  697.6 17.4 %collective-permute-start.45 = (bf16[128,1536]{1,0:T(8,128)(2,1)S(1)}, bf16[128,1536]{1,0:T(8,128)(2,1)S(1)}, u32[]{:S(2)}, u32[]{:S(2)}) collective-permute-start(bf16[128,1536]{1,0:T(8,128)(2,1)S(1)} %get-tuple-element.181.refs_0_), channel_id=1, source_target_pairs={{0,1},{1,0},{2,3},{3,2},{4,5},{5,4},{6,7},{7,6},{8,9},{9,8},{10,11... | collective-permute-start | bytes 1179656 | tf_op jit(solution)/shard_map/ppermute | solution.py:351
  697.7 17.4 %collective-permute-start.43 = (bf16[128,1536]{1,0:T(8,128)(2,1)S(1)}, bf16[128,1536]{1,0:T(8,128)(2,1)}, u32[]{:S(2)}, u32[]{:S(2)}) collective-permute-start(bf16[128,1536]{1,0:T(8,128)(2,1)S(1)} %get-tuple-element.181.refs_0_), channel_id=1, source_target_pairs={{0,2},{1,3},{2,0},{3,1},{4,6},{5,7},{6,4},{7,5},{8,10},{9,11},{10,... | collective-permute-start | bytes 1179656 | tf_op jit(solution)/shard_map/ppermute | solution.py:1060
  705.9 16.0 %collective-permute-start.51 = (bf16[128,1536]{1,0:T(8,128)(2,1)S(1)}, bf16[128,1536]{1,0:T(8,128)(2,1)}, u32[]{:S(2)}, u32[]{:S(2)}) collective-permute-start(bf16[128,1536]{1,0:T(8,128)(2,1)S(1)} %collective-permute-done.50.refs_10_), channel_id=1, source_target_pairs={{0,4},{4,0},{8,12},{12,8},{16,20},{20,16},{24,28},{28,24},{1,5},{5... | collective-permute-start | bytes 1179656 | tf_op jit(solution)/shard_map/ppermute | solution.py:1062
  715.0 18.0 %collective-permute-start.46 = (bf16[128,1536]{1,0:T(8,128)(2,1)}, bf16[128,1536]{1,0:T(8,128)(2,1)S(1)}, u32[]{:S(2)}, u32[]{:S(2)}) collective-permute-start(bf16[128,1536]{1,0:T(8,128)(2,1)} %collective-permute-done.42.refs_1_), channel_id=1, source_target_pairs={{0,1},{1,0},{2,3},{3,2},{4,5},{5,4},{6,7},{7,6},{8,9},{9,8},{10,11... | collective-permute-start | bytes 1179656 | tf_op jit(solution)/shard_map/ppermute | solution.py:351
  715.1 17.9 %collective-permute-start.53 = (bf16[128,1536]{1,0:T(8,128)(2,1)}, bf16[128,1536]{1,0:T(8,128)(2,1)}, u32[]{:S(2)}, u32[]{:S(2)}) collective-permute-start(bf16[128,1536]{1,0:T(8,128)(2,1)} %collective-permute-done.49.refs_9_), channel_id=1, source_target_pairs={{0,1},{1,0},{2,3},{3,2},{4,5},{5,4},{6,7},{7,6},{8,9},{9,8},{10,11... | collective-permute-start | bytes 1179656 | tf_op jit(solution)/shard_map/ppermute | solution.py:351
  715.6 17.4 %collective-permute-start.47 = (bf16[128,1536]{1,0:T(8,128)(2,1)}, bf16[128,1536]{1,0:T(8,128)(2,1)}, u32[]{:S(2)}, u32[]{:S(2)}) collective-permute-start(bf16[128,1536]{1,0:T(8,128)(2,1)} %collective-permute-done.43.refs_2_), channel_id=1, source_target_pairs={{0,1},{1,0},{2,3},{3,2},{4,5},{5,4},{6,7},{7,6},{8,9},{9,8},{10,11... | collective-permute-start | bytes 1179656 | tf_op jit(solution)/shard_map/ppermute | solution.py:351
  (59 other events, 676.8 us)
Sparse Core Ops, SparseCore 0:
  138.7 62.0 reduce-scatter.6
  218.6 35.6 reduce-scatter.8
  256.6 59.2 reduce-scatter.10
  318.7 60.2 reduce-scatter.12
  406.8 60.4 reduce-scatter.14
  517.3 124.6 all-reduce.2
  644.9 45.9 all-reduce.4
  693.2 34.6 reduce-scatter.16

commit v3 on v2

--- a/solution.py
+++ b/solution.py
@@ -363,19 +363,32 @@
     return lax.ppermute(value, "expert", pairs)
 
 
-def gather_members(value, groups):
-    column = [value] + [from_row(value, groups, s) for s in range(1, groups // 2)]
-    result = []
-    for piece in column:
+def after(value, *others):
+    return lax.optimization_barrier((value,) + others)[0]
+
+
+def gather_column(value, groups):
+    return [value] + [from_row(value, groups, s) for s in range(1, groups // 2)]
+
+
+def gather_cores(column, groups, *before):
+    result = [column[0], core_swap(column[0], groups)]
+    for piece in column[1:]:
+        piece = after(piece, *before)
         result += [piece, core_swap(piece, groups)]
     return result
 
 
-def return_members(pieces, groups):
+def gather_members(value, groups):
+    return gather_cores(gather_column(value, groups), groups)
+
+
+def return_members(pieces, groups, *before):
     swapped = [core_swap(pieces[2 * s + 1], groups) for s in range(groups // 2)]
     terms = [pieces[0], swapped[0]]
     for s in range(1, groups // 2):
-        both = (pieces[2 * s].astype(f32) + swapped[s].astype(f32)).astype(bf16)
+        mine = after(pieces[2 * s], *before)
+        both = (mine.astype(f32) + swapped[s].astype(f32)).astype(bf16)
         terms.append(to_row(both, groups, s))
     return terms
 
@@ -809,10 +822,6 @@
     )(table, *first, *second)
 
 
-def after(value, *others):
-    return lax.optimization_barrier((value,) + others)[0]
-
-
 def local(
     tokens, cotangent, expert_ids, norm_attn, w_qkv, w_out, norm_moe, w_router, w_gate_up, w_down
 ):
@@ -875,7 +884,7 @@
 
     attended, lse, hidden, moe_pieces, moe_low = [], [], [], [], []
     for m in range(MICRO):
-        mask = bias if m == 0 else after(bias, moe_low[-1])
+        mask = after(bias, cot_pieces[0][2] if m == 0 else moe_low[-1])
         att, log_total, hid, low = attend(
             m, queries, key_value, prompt, mask, token_rows, w_out, moe_gain
         )
@@ -883,12 +892,13 @@
         lse.append(log_total[None])
         hidden.append(hid)
         moe_low.append(low)
-        moe_pieces.append(gather_members(low, groups))
+        moe_pieces.append(gather_column(low, groups))
 
     def by_block(pieces):
         return [pieces[m][g] for g in range(groups) for m in range(MICRO)]
 
     d_rows, slots = pick_grads(after(ids_all, moe_low[-1]), by_block(cot_pieces), local_experts)
+    moe_pieces = [gather_cores(column, groups, slots) for column in moe_pieces]
     attended = jnp.concatenate(attended, axis=0)
     lse = jnp.concatenate(lse, axis=0)
     hidden = jnp.concatenate(hidden, axis=0)
@@ -933,8 +943,10 @@
     for i, (count, whole) in enumerate(plan):
         if i:
             order = after(order, outs[-1])
+        if i == 3:
+            order = after(order, add_x(1, outs[-1]))
         if i == 4:
-            order = after(order, add_x(1, outs[-1]), parts[0])
+            order = after(order, parts[0])
         out, back, dot, *sums = expert_chunk(
             order, first, count, pairs, not whole, x_rows, d_rows, slot_gate, w_gate_up, w_down
         )
@@ -959,8 +971,8 @@
     def pieces_of(value):
         return [value[j * MICRO : (j + 1) * MICRO] for j in range(groups)]
 
-    back_terms = return_members(pieces_of(back_sum), groups)
     dot_pieces = exchange_members(pieces_of(back_dots), groups)
+    back_terms = return_members(pieces_of(back_sum), groups, *dot_pieces)
     token_dots = jnp.zeros((MICRO, EXPERTS, tok_rows), f32)
     for s in range(groups // 2):
         for c in range(2):
@@ -974,11 +986,11 @@
     own_gates = gates[:MICRO]
     centre = jnp.sum(own_gates * token_dots, axis=1, keepdims=True)
     grad_logits = (own_gates * (token_dots - centre)).astype(bf16)
-    (mixed,) = sum_rows(after(slots, back_sum, *sent(1)), outs)
+    (mixed,) = sum_rows(after(slots, back_sum, *sent(1), *left(2, back_sum)), outs)
     mix_terms = return_members(pieces_of(mixed), groups)
 
     grad_hidden, grad_branch, grad_attended, grad_norm_moe = middle_back(
-        back_terms, grad_logits, router, hidden, moe_gain, after(cot_rows, mixed, *left(2, mixed)), w_out
+        back_terms, grad_logits, router, hidden, moe_gain, after(cot_rows, mixed, *sent(4)), w_out
     )
     grad_router = jnp.einsum("bet,btd->ed", grad_logits, moe_low, preferred_element_type=f32)
     grad_out = jnp.einsum(
@@ -988,7 +1000,7 @@
         queries,
         key_value,
         prompt,
-        after(bias, grad_out, *sent(4)),
+        after(bias, grad_out),
         lse,
         grad_attended,
         cosine,
@@ -1000,12 +1012,12 @@
             [value[:, j * PROMPT_DEV : (j + 1) * PROMPT_DEV] for j in range(groups)], groups
         )
 
-    mixture = sum(term.astype(f32) for term in mix_terms)
+    mixture = sum(after(term, gq).astype(f32) for term in mix_terms)
     output = (hidden + branch_scale * mixture).astype(bf16)
     core_bit, row_bit = lax.rem(member, 2), lax.rem(member // 2, 2)
     grad_out = halve(halve(grad_out, "expert", swap_core, core_bit), "expert", swap_y, row_bit)
     gp, grad_qkv = weight_back(
-        after(normed, output, *left(3, gq)),
+        after(normed, output, grad_out, *left(3, gq)),
         gq,
         gok,
         gov,
@@ -1015,11 +1027,10 @@
         sine,
     )
     grad_tokens, grad_norm_attn = token_back(
-        after(gp, grad_qkv, *sent(2)), w_qkv, token_rows, attn_gain, grad_hidden
-    )
+        after(gp, grad_qkv), w_qkv, token_rows, attn_gain, grad_hidden
+    )
+    last = [add_x(i, grad_norm_attn) for i in list(halves)]
     grad_qkv = halve(grad_qkv, "expert", swap_core, core_bit)
-    last = [add_x(i, gp) for i in list(halves)]
-    grad_qkv = after(grad_qkv, *last)
     grad_qkv = halve(grad_qkv, "expert", swap_y, row_bit)
 
     whole_sums = [parts[i] for i, (_, whole) in enumerate(plan) if whole]
@@ -1041,17 +1052,23 @@
             ),
             grad_norm_attn,
             grad_norm_moe,
-            jnp.zeros((6, D), f32),
+            jnp.zeros((14, D), f32),
         ],
         axis=0,
     )
-    small = lax.psum(small, ("dp", "expert"))
-    dense = after(jnp.concatenate([grad_qkv, grad_out], axis=1), *sent(3))
-    dense = halve(dense, "dp", swap_x, parity)
+    small = after(small, *last)
+    for axis, swap in (("expert", swap_core), ("expert", swap_y), ("dp", swap_x)):
+        small = small + lax.ppermute(small, axis, swap)
+    dense = jnp.concatenate([grad_qkv, grad_out], axis=1)
+    dense = after(halve(dense, "dp", swap_x, parity), *sent(2), *sent(3))
+    dense_rows = dense.shape[0]
+    dense = jnp.concatenate([dense, small.reshape(-1, 3 * D).astype(bf16)], axis=0)
     dense = lax.psum(dense, "dp", axis_index_groups=z_groups)
     if groups > 4:
         rest = [[m for m in range(groups) if m % 4 == r] for r in range(4)]
         dense = lax.psum(dense, "expert", axis_index_groups=rest)
+    small = dense[dense_rows:].reshape(-1, D).astype(f32)
+    dense = dense[:dense_rows]
     width = dense.shape[1] // 2
     left_own, right_own = dense[:, :width], dense[:, width:]
     left_x = lax.ppermute(left_own, "dp", swap_x)

time: 760 us -> 620 us (0.82)
  waiting for transfers between devices: 342 us -> 197 us
    psum x1 -> x0, waiting for transfers between devices: 113 us -> none  [local(): small = lax.psum(small, ('dp', 'expert'))]
    ppermute x5, waiting for transfers between devices: 39.4 us -> 8.8 us  [halve(): got = lax.ppermute(send, axis, swap)]
    reduce_scatter x6, waiting for transfers between devices: 3.77 us -> 31.8 us  [sum_z(): lax.psum_scatter(value.reshape(count, pairs * height, D), 'dp', scatter_d...]
    ppermute x3, waiting for transfers between devices: 27.2 us -> 0.01 us  [exchange_members(): result.append(lax.ppermute(pieces[2 * s + c], 'expert', pairs))]
    psum x1, waiting for transfers between devices: 47.4 us -> 25 us  [local(): dense = lax.psum(dense, 'dp', axis_index_groups=z_groups)]
    ppermute x0 -> x3, waiting for transfers between devices: none -> 20.8 us  [local(): small = small + lax.ppermute(small, axis, swap)]
    ppermute x1, waiting for transfers between devices: 0.01 us -> 16.9 us  [local(): swapped = lax.ppermute(after(whole_sums[:, piece:], *last), 'dp', swap_x)]
    ppermute x6, waiting for transfers between devices: 32.5 us -> 19.8 us  [from_row(): return lax.ppermute(value, 'expert', pairs)]
  transfers between devices with their start and end apart: 65 -> 67, of which waited for: 18 -> 23; matrix products, arithmetic and copies ran while one was open for 11% -> 13% of each run, Pallas kernels for 31% -> 38%
where the time goes in v3:
time: 620 us; the launch traced here: 611 us
  Pallas kernels  274 us (44%)
  waiting for transfers between devices  197 us (32%)
  other arithmetic  45.3 us (7%)
  local copies, waits for them, and re-layouts  37.8 us (6%)
  starting transfers between devices  35.7 us (6%)
  between operations  15.5 us (2%)
    pallas_call x6, Pallas kernels, expert_chunk(): pl.pallas_call(functools.partial(expert_body, tile=tile), grid_spec=grid_...  127 us
    reduce_scatter x6, waiting for transfers between devices, sum_z(): lax.psum_scatter(value.reshape(count, pairs * height, D), 'dp', scatter_d...  31.8 us
    ppermute x4, waiting for transfers between devices, local(): halves[i] = (sums[0], lax.ppermute(sums[1], 'dp', swap_x))  29.6 us
    ppermute x4, waiting for transfers between devices, to_row(): return lax.ppermute(value, 'expert', pairs)  27.1 us
    pallas_call x2, Pallas kernels, sum_rows(): pl.pallas_call(functools.partial(sum_rows_body, chunks=len(rows), with_do...  25.9 us
    psum x1, waiting for transfers between devices, local(): dense = lax.psum(dense, 'dp', axis_index_groups=z_groups)  25 us
    pallas_call x1, Pallas kernels, attend_back(): pl.pallas_call(attend_back_body, grid=(micro, steps), in_specs=[wide, pro...  22.9 us
    pallas_call x2, Pallas kernels, attend(): pl.pallas_call(attend_body, grid=(steps,), in_specs=[pl.BlockSpec((1, row...  22.5 us
  transfers between devices with their start and end apart: 67, of which 23 were waited for; matrix products, arithmetic and copies ran while one was open for 13% of the time, Pallas kernels for 38%

profile of v3, /device:TPU:0, one launch (start us, length us, event | category | flops | bytes accessed | tf_op | source)
XLA Modules:
  0.0 610.6 jit_solution(17893243426595379169)
XLA Ops:
  8.0 3.1 collective-permute-start.5
  13.0 6.8 %shard_map.169 = (bf16[2,320,1024]{2,1,0:T(8,128)(2,1)}, bf16[2,320,1024]{2,1,0:T(8,128)(2,1)}, bf16[2,320,1024]{2,1,0:T(8,128)(2,1)}) custom-call(bf16[2,320,1024]{2,1,0:T(8,128)(2,1)} %bitcast.74, f32[1,1024]{1,0:T(1,128)} %bitcast.81, bf16[1024,2048]{1,0:T(8,128)(2,1)} %w_ref.7, f32[320,128]{1,0:T(8,128)} %copy.24.cos_ref.refs_10_, ...), custom_call_target="tpu_custom_call" | custom-call | flops 8049999872 | tf_op jit(solution)/shard_map/pallas_call | solution.py:452
  23.5 6.5 %collective-permute-done.1 = bf16[2,64,1024]{2,1,0:T(8,128)(2,1)S(1)} collective-permute-done((bf16[2,64,1024]{2,1,0:T(8,128)(2,1)S(1)}, bf16[2,64,1024]{2,1,0:T(8,128)(2,1)S(1)}, u32[]{:S(2)}, u32[]{:S(2)}) %collective-permute-start.1) | collective-permute-done | bytes 262176 | tf_op jit(solution)/shard_map/ppermute | solution.py:357
  34.2 10.0 %collective-permute-done.3.refs_5_ = bf16[1,320,1024]{2,1,0:T(8,128)(2,1)} collective-permute-done((bf16[1,320,1024]{2,1,0:T(8,128)(2,1)S(1)}, bf16[1,320,1024]{2,1,0:T(8,128)(2,1)}, u32[]{:S(2)}, u32[]{:S(2)}) %collective-permute-start.3) | collective-permute-done | bytes 655392 | tf_op jit(solution)/shard_map/ppermute | solution.py:357
  44.2 11.2 %shard_map.170 = (bf16[1,320,1024]{2,1,0:T(8,128)(2,1)}, f32[4,1,1280]{2,1,0:T(1,128)}, f32[1,320,1024]{2,1,0:T(8,128)}, bf16[1,320,1024]{2,1,0:T(8,128)(2,1)}) custom-call(bf16[2,320,1024]{2,1,0:T(8,128)(2,1)} %get-tuple-element.99.q_ref, bf16[2,256,1024]{2,1,0:T(8,128)(2,1)} %pad_maximum_fusion.pk_ref.pv_ref, ...), custom_call_target="tpu_custom_call" | custom-call | flops 13799999488 | tf_op jit(solution)/shard_map/pallas_call | solution.py:528
  55.6 2.2 collective-permute-done.9.refs_6_
  57.8 11.3 %shard_map.171 = (bf16[1,320,1024]{2,1,0:T(8,128)(2,1)}, f32[4,1,1280]{2,1,0:T(1,128)}, f32[1,320,1024]{2,1,0:T(8,128)}, bf16[1,320,1024]{2,1,0:T(8,128)(2,1)}) custom-call(bf16[2,320,1024]{2,1,0:T(8,128)(2,1)} %get-tuple-element.99.q_ref, bf16[2,256,1024]{2,1,0:T(8,128)(2,1)} %pad_maximum_fusion.pk_ref.pv_ref, ...), custom_call_target="tpu_custom_call" | custom-call | flops 13799999488 | tf_op jit(solution)/shard_map/pallas_call | solution.py:528
  70.8 15.0 %shard_map.172 = (bf16[8,8,112,1024]{3,2,1,0:T(8,128)(2,1)}, s32[8,8,320]{2,1,0:T(8,128)}) custom-call(s32[8,8,320]{2,1,0:T(8,128)} %negate_select_fusion.1.refs_0_, bf16[1,320,1024]{2,1,0:T(8,128)(2,1)} %copy-done.22, bf16[1,320,1024]{2,1,0:T(8,128)(2,1)} %copy-done.21, bf16[1,320,1024]{2,1,0:T(8,128)(2,1)} %collective-permute-done.7.refs_3_, ...), custom_call_target="tpu_custom_call" | custom-call | flops 17250000896 | tf_op jit(solution)/shard_map/pallas_call | solution.py:112
  90.1 16.8 %shard_map.173 = (bf16[8,8,112,1024]{3,2,1,0:T(8,128)(2,1)}, f32[8,8,112,128]{3,2,1,0:T(8,128)}, f32[8,32,320]{2,1,0:T(8,128)}) custom-call(s32[8,8,320]{2,1,0:T(8,128)} %negate_select_fusion.1.refs_0_, s32[8,8,320]{2,1,0:T(8,128)} %get-tuple-element.147.refs_1_.refs_0_, bf16[1024,32]{1,0:T(8,128)(2,1)} %dynamic-slice_maximum_fusion.refs_2_.refs_4_, ...), custom_call_target="tpu_custom_call" | custom-call | flops 19549999104 | tf_op jit(solution)/shard_map/pallas_call | solution.py:158
  106.9 17.0 %shard_map.174 = (bf16[1,896,1024]{2,1,0:T(8,128)(2,1)}, bf16[1,896,1024]{2,1,0:T(8,128)(2,1)}, f32[1,896,128]{2,1,0:T(8,128)}, bf16[1,4,384,1024]{3,2,1,0:T(8,128)(2,1)}) custom-call(s32[1]{0:T(128)} %bitcast.8.parity_ref, bf16[8,896,1024]{2,1,0:T(8,128)(2,1)} %bitcast.89, bf16[8,896,1024]{2,1,0:T(8,128)(2,1)} %bitcast.83, f32[8,896,128]{2,1,0:T(8,128)} %bitcast.95, ...), custom_call_target="tpu_custom_call" | custom-call | flops 17250000896 | tf_op jit(solution)/shard_map/pallas_call | solution.py:336
  126.4 17.1 %shard_map.175 = (bf16[1,896,1024]{2,1,0:T(8,128)(2,1)}, bf16[1,896,1024]{2,1,0:T(8,128)(2,1)}, f32[1,896,128]{2,1,0:T(8,128)}, bf16[1,4,192,1024]{3,2,1,0:T(8,128)(2,1)}, bf16[1,4,192,1024]{3,2,1,0:T(8,128)(2,1)}) custom-call(s32[1]{0:T(128)} %bitcast.8.parity_ref, bf16[8,896,1024]{2,1,0:T(8,128)(2,1)} %bitcast.90, bf16[8,896,1024]{2,1,0:T(8,128)(2,1)} %bitcast.84, ...), custom_call_target="tpu_custom_call" | custom-call | flops 17250000896 | tf_op jit(solution)/shard_map/pallas_call | solution.py:336
  145.0 29.4 %shard_map.176 = (bf16[2,896,1024]{2,1,0:T(8,128)(2,1)}, bf16[2,896,1024]{2,1,0:T(8,128)(2,1)}, f32[2,896,128]{2,1,0:T(8,128)}, bf16[2,4,192,1024]{3,2,1,0:T(8,128)(2,1)}, bf16[2,4,192,1024]{3,2,1,0:T(8,128)(2,1)}) custom-call(s32[1]{0:T(128)} %bitcast.8.parity_ref, bf16[8,896,1024]{2,1,0:T(8,128)(2,1)} %bitcast.91, bf16[8,896,1024]{2,1,0:T(8,128)(2,1)} %bitcast.85, ...), custom_call_target="tpu_custom_call" | custom-call | flops 34500001792 | tf_op jit(solution)/shard_map/pallas_call | solution.py:336
  174.9 6.1 collective-permute-done.18
  181.0 1.9 add_convert_fusion.4
  182.9 29.8 %shard_map.177 = (bf16[2,896,1024]{2,1,0:T(8,128)(2,1)}, bf16[2,896,1024]{2,1,0:T(8,128)(2,1)}, f32[2,896,128]{2,1,0:T(8,128)}, bf16[2,4,192,1024]{3,2,1,0:T(8,128)(2,1)}, bf16[2,4,192,1024]{3,2,1,0:T(8,128)(2,1)}) custom-call(s32[1]{0:T(128)} %bitcast.8.parity_ref, bf16[8,896,1024]{2,1,0:T(8,128)(2,1)} %bitcast.92, bf16[8,896,1024]{2,1,0:T(8,128)(2,1)} %bitcast.86, ...), custom_call_target="tpu_custom_call" | custom-call | flops 34500001792 | tf_op jit(solution)/shard_map/pallas_call | solution.py:336
  212.7 16.8 %shard_map.178 = (bf16[1,896,1024]{2,1,0:T(8,128)(2,1)}, bf16[1,896,1024]{2,1,0:T(8,128)(2,1)}, f32[1,896,128]{2,1,0:T(8,128)}, bf16[1,4,384,1024]{3,2,1,0:T(8,128)(2,1)}) custom-call(s32[1]{0:T(128)} %bitcast.8.parity_ref, bf16[8,896,1024]{2,1,0:T(8,128)(2,1)} %bitcast.93, bf16[8,896,1024]{2,1,0:T(8,128)(2,1)} %bitcast.87, f32[8,896,128]{2,1,0:T(8,128)} %bitcast.99, ...), custom_call_target="tpu_custom_call" | custom-call | flops 17250000896 | tf_op jit(solution)/shard_map/pallas_call | solution.py:336
  229.5 17.3 %shard_map.179 = (bf16[1,896,1024]{2,1,0:T(8,128)(2,1)}, bf16[1,896,1024]{2,1,0:T(8,128)(2,1)}, f32[1,896,128]{2,1,0:T(8,128)}, bf16[1,4,192,1024]{3,2,1,0:T(8,128)(2,1)}, bf16[1,4,192,1024]{3,2,1,0:T(8,128)(2,1)}) custom-call(s32[1]{0:T(128)} %bitcast.8.parity_ref, bf16[8,896,1024]{2,1,0:T(8,128)(2,1)} %bitcast.94, bf16[8,896,1024]{2,1,0:T(8,128)(2,1)} %bitcast.88, ...), custom_call_target="tpu_custom_call" | custom-call | flops 17250000896 | tf_op jit(solution)/shard_map/pallas_call | solution.py:336
  246.9 13.4 %shard_map.180 = (bf16[8,320,1024]{2,1,0:T(8,128)(2,1)}, f32[8,8,320]{2,1,0:T(8,128)}) custom-call(s32[8,8,320]{2,1,0:T(8,128)} %get-tuple-element.147.refs_1_.refs_0_, bf16[1,8,112,1024]{3,2,1,0:T(8,128)(2,1)} %bitcast.106, bf16[1,8,112,1024]{3,2,1,0:T(8,128)(2,1)} %bitcast.109, bf16[2,8,112,1024]{3,2,1,0:T(8,128)(2,1)} %bitcast.103, ...), custom_call_target="tpu_custom_call" | custom-call | flops 17250000896 | tf_op jit(solution)/shard_map/pallas_call | solution.py:227
  260.4 5.3 add_convert_fusion.1
  267.6 5.3 fusion.19
  272.9 12.5 %shard_map.181 = bf16[8,320,1024]{2,1,0:T(8,128)(2,1)} custom-call(s32[8,8,320]{2,1,0:T(8,128)} %get-tuple-element.147.refs_1_.refs_0_, bf16[1,8,112,1024]{3,2,1,0:T(8,128)(2,1)} %bitcast.105, bf16[1,8,112,1024]{3,2,1,0:T(8,128)(2,1)} %bitcast.107, bf16[2,8,112,1024]{3,2,1,0:T(8,128)(2,1)} %bitcast.101, bf16[2,8,112,1024]{3,2,1,0:T(8,128)(2,1)} %bitcast.102, ...), custom_call_target="tpu_custom_call" | custom-call | flops 17250000896 | tf_op jit(solution)/shard_map/pallas_call | solution.py:227
  285.4 5.4 fusion.18
  291.4 3.2 add_convert_fusion.7
  298.4 3.3 add_convert_fusion.6
  303.0 23.5 %collective-permute-done.25.refs_2_ = bf16[2,320,1024]{2,1,0:T(8,128)(2,1)} collective-permute-done((bf16[2,320,1024]{2,1,0:T(8,128)(2,1)}, bf16[2,320,1024]{2,1,0:T(8,128)(2,1)}, u32[]{:S(2)}, u32[]{:S(2)}) %collective-permute-start.25) | collective-permute-done | bytes 1310752 | tf_op jit(solution)/shard_map/ppermute | solution.py:363
  326.6 8.4 %shard_map.182 = (f32[2,320,1024]{2,1,0:T(8,128)}, bf16[2,320,1024]{2,1,0:T(8,128)(2,1)}, bf16[2,320,1024]{2,1,0:T(8,128)(2,1)}, f32[1,1024]{1,0:T(1,128)}) custom-call(bf16[2,320,1024]{2,1,0:T(8,128)(2,1)} %get-tuple-element.195.refs_0_, bf16[2,320,1024]{2,1,0:T(8,128)(2,1)} %collective-permute-done.20.refs_1_, ...), custom_call_target="tpu_custom_call" | custom-call | flops 9200000000 | tf_op jit(solution)/shard_map/pallas_call | solution.py:595
  335.0 3.2 bitcast_convert_fusion
  339.8 22.9 %shard_map.183 = (bf16[2,320,1024]{2,1,0:T(8,128)(2,1)}, bf16[2,256,512]{2,1,0:T(8,128)(2,1)}, bf16[2,256,512]{2,1,0:T(8,128)(2,1)}, bf16[2,256,512]{2,1,0:T(8,128)(2,1)}, bf16[2,256,512]{2,1,0:T(8,128)(2,1)}) custom-call(bf16[2,320,1024]{2,1,0:T(8,128)(2,1)} %get-tuple-element.99.q_ref, bf16[2,256,1024]{2,1,0:T(8,128)(2,1)} %pad_maximum_fusion.pk_ref.pv_ref, ...), custom_call_target="tpu_custom_call" | custom-call | flops 26449999872 | tf_op jit(solution)/shard_map/pallas_call | solution.py:656
  362.7 4.0 collective-permute-done.31
  371.3 5.4 add_convert_fusion
  379.8 3.8 add_convert_fusion.5
  385.8 7.6 %collective-permute-done.30 = bf16[256,1024]{1,0:T(8,128)(2,1)S(1)} collective-permute-done((bf16[256,1024]{1,0:T(8,128)(2,1)S(1)}, bf16[256,1024]{1,0:T(8,128)(2,1)S(1)}, u32[]{:S(2)}, u32[]{:S(2)}) %collective-permute-start.30) | collective-permute-done | bytes 524320 | tf_op jit(solution)/shard_map/ppermute | solution.py:783
  396.2 1.8 collective-permute-done.37.refs_9_
  398.7 11.3 %shard_map.184 = (bf16[2,320,2048]{2,1,0:T(8,128)(2,1)}, bf16[1024,2048]{1,0:T(8,128)(2,1)}) custom-call(bf16[2,320,1024]{2,1,0:T(8,128)(2,1)} %get-tuple-element.169.refs_0_, bf16[2,320,1024]{2,1,0:T(8,128)(2,1)} %get-tuple-element.161.refs_1_, bf16[2,256,512]{2,1,0:T(8,128)(2,1)} %get-tuple-element.170.refs_2_, ...), custom_call_target="tpu_custom_call" | custom-call | flops 12650000384 | tf_op jit(solution)/shard_map/pallas_call | solution.py:723
  416.1 3.0 add_convert_fusion.2
  421.3 8.3 %shard_map.185 = (bf16[2,320,1024]{2,1,0:T(8,128)(2,1)}, f32[1,1024]{1,0:T(1,128)}) custom-call(bf16[2,320,2048]{2,1,0:T(8,128)(2,1)} %get-tuple-element.174.gp_ref, bf16[1024,2048]{1,0:T(8,128)(2,1)} %w_ref.7, bf16[2,320,1024]{2,1,0:T(8,128)(2,1)} %bitcast.77, f32[1,1024]{1,0:T(1,128)} %bitcast.82, f32[2,320,1024]{2,1,0:T(8,128)} %get-tuple-element.175.hidden_ref), custom_call_target="tpu_custom_call" | custom-call | flops 9200000000 | tf_op jit(solution)/shard_map/pallas_call | solution.py:759
  429.6 19.5 %collective-permute-done.41 = bf16[1,4,192,1024]{3,2,1,0:T(8,128)(2,1)} collective-permute-done((bf16[1,4,192,1024]{3,2,1,0:T(8,128)(2,1)}, bf16[1,4,192,1024]{3,2,1,0:T(8,128)(2,1)}, u32[]{:S(2)}, u32[]{:S(2)}) %collective-permute-start.41) | collective-permute-done | bytes 1572896 | tf_op jit(solution)/shard_map/ppermute | solution.py:960
  449.9 3.2 add_convert_fusion.3
  457.8 5.8 collective-permute-done.43
  464.2 15.0 %collective-permute-done.44 = f32[48,1024]{1,0:T(8,128)} collective-permute-done((f32[48,1024]{1,0:T(8,128)S(1)}, f32[48,1024]{1,0:T(8,128)}, u32[]{:S(2)}, u32[]{:S(2)}) %collective-permute-start.44) | collective-permute-done | bytes 196640 | tf_op jit(solution)/shard_map/ppermute | solution.py:1061
  485.0 16.9 %collective-permute-done.59 = bf16[2,192,1024]{2,1,0:T(8,128)(2,1)S(1)} collective-permute-done((bf16[2,192,1024]{2,1,0:T(8,128)(2,1)S(1)}, bf16[2,192,1024]{2,1,0:T(8,128)(2,1)S(1)}, u32[]{:S(2)}, u32[]{:S(2)}) %collective-permute-start.59) | collective-permute-done | bytes 786464 | tf_op jit(solution)/shard_map/ppermute | solution.py:1038
  504.3 25.0 %all-reduce.2.cloned.1.call-done = bf16[144,3072]{1,0:T(8,128)(2,1)} async-done(((bf16[144,3072]{1,0:T(8,128)(2,1)}), bf16[144,3072]{1,0:T(8,128)(2,1)}) %all-reduce.2.cloned.1.call-update) | async-done | bytes 884752 | tf_op jit(solution)/shard_map/psum | solution.py:1066
  529.2 2.0 fusion.20
  534.9 31.8 %reduce-scatter.17.cloned.1.call-done = bf16[1,192,1024]{2,1,0:T(8,128)(2,1)} async-done(((bf16[1,768,1024]{2,1,0:T(8,128)(2,1)}), bf16[1,192,1024]{2,1,0:T(8,128)(2,1)}) %reduce-scatter.17.cloned.1.call-update) | async-done | bytes 393232 | tf_op jit(solution)/shard_map/reduce_scatter | solution.py:921
  569.2 2.5 slice.169
  576.5 7.4 %collective-permute-done.46.refs_2_ = bf16[128,1536]{1,0:T(8,128)(2,1)S(1)} collective-permute-done((bf16[128,1536]{1,0:T(8,128)(2,1)}, bf16[128,1536]{1,0:T(8,128)(2,1)S(1)}, u32[]{:S(2)}, u32[]{:S(2)}) %collective-permute-start.46) | collective-permute-done | bytes 393248 | tf_op jit(solution)/shard_map/ppermute | solution.py:1077
  584.9 6.9 %collective-permute-done.47.refs_3_ = bf16[128,1536]{1,0:T(8,128)(2,1)S(1)} collective-permute-done((bf16[128,1536]{1,0:T(8,128)(2,1)}, bf16[128,1536]{1,0:T(8,128)(2,1)S(1)}, u32[]{:S(2)}, u32[]{:S(2)}) %collective-permute-start.47) | collective-permute-done | bytes 393248 | tf_op jit(solution)/shard_map/ppermute | solution.py:1077
  594.4 9.0 %shard_map.186 = (f32[1024,2048]{1,0:T(8,128)}, f32[1024,1024]{1,0:T(8,128)}) custom-call(s32[8]{0:T(128)} %iota_xor_fusion.table_ref, bf16[128,1536]{1,0:T(8,128)(2,1)} %get-tuple-element.199.refs_0_, bf16[128,1536]{1,0:T(8,128)(2,1)} %collective-permute-done.45.refs_1_, bf16[128,1536]{1,0:T(8,128)(2,1)} %copy-done.39, bf16[128,1536]{1,0:T(8,128)(2,1)} %copy-done.42, ...), custom_call_target="tpu_custom_call" | custom-call | flops 10350000128 | tf_op jit(solution)/shard_map/pallas_call | solution.py:813
  (303 shorter events, 80.3 us)
Async XLA Ops:
  7.2 205.5 %reduce-scatter.7.cloned.1.call-start = ((), (), s32[]{:S(2)}) async-start(), calls=%async_computation.6 | async-start | bytes 3932160 | tf_op jit(solution)/shard_map/reduce_scatter | solution.py:921
  8.0 15.4 %collective-permute-start.5 = (s32[2,8,320]{2,1,0:T(8,128)S(1)}, s32[2,8,320]{2,1,0:T(8,128)S(1)}, u32[]{:S(2)}, u32[]{:S(2)}) collective-permute-start(s32[2,8,320]{2,1,0:T(8,128)S(1)} %bitcast.67), channel_id=1, source_target_pairs={{2,0},{3,1},{0,2},{1,3},{6,4},{7,5},{4,6},{5,7},{10,8},{11,9},{8,1... | collective-permute-start | bytes 61448 | tf_op jit(solution)/shard_map/ppermute | solution.py:357
  11.1 20.7 %collective-permute-start.4 = (s32[2,8,320]{2,1,0:T(8,128)S(1)}, s32[2,8,320]{2,1,0:T(8,128)S(1)}, u32[]{:S(2)}, u32[]{:S(2)}) collective-permute-start(s32[2,8,320]{2,1,0:T(8,128)S(1)} %bitcast.68), channel_id=1, source_target_pairs={{0,1},{1,0},{2,3},{3,2},{4,5},{5,4},{6,7},{7,6},{8,9},{9,8},{10,11... | collective-permute-start | bytes 61448 | tf_op jit(solution)/shard_map/ppermute | solution.py:351
  21.5 22.6 %collective-permute-start.3 = (bf16[1,320,1024]{2,1,0:T(8,128)(2,1)S(1)}, bf16[1,320,1024]{2,1,0:T(8,128)(2,1)}, u32[]{:S(2)}, u32[]{:S(2)}) collective-permute-start(bf16[1,320,1024]{2,1,0:T(8,128)(2,1)S(1)} %get-tuple-element.197.refs_1_), channel_id=1, source_target_pairs={{2,0},{3,1},{0,2},{1,3},{6,4},{7,5},{4,6},{5,7},{10,8},{11,9},{8,1... | collective-permute-start | bytes 1966088 | tf_op jit(solution)/shard_map/ppermute | solution.py:357
  31.9 37.2 %collective-permute-start.7 = (bf16[1,320,1024]{2,1,0:T(8,128)(2,1)S(1)}, bf16[1,320,1024]{2,1,0:T(8,128)(2,1)}, u32[]{:S(2)}, u32[]{:S(2)}) collective-permute-start(bf16[1,320,1024]{2,1,0:T(8,128)(2,1)S(1)} %get-tuple-element.197.refs_1_), channel_id=1, source_target_pairs={{0,1},{1,0},{2,3},{3,2},{4,5},{5,4},{6,7},{7,6},{8,9},{9,8},{10,11... | collective-permute-start | bytes 1966088 | tf_op jit(solution)/shard_map/ppermute | solution.py:351
  33.0 24.7 %collective-permute-start.9 = (bf16[1,320,1024]{2,1,0:T(8,128)(2,1)S(1)}, bf16[1,320,1024]{2,1,0:T(8,128)(2,1)}, u32[]{:S(2)}, u32[]{:S(2)}) collective-permute-start(bf16[1,320,1024]{2,1,0:T(8,128)(2,1)S(1)} %get-tuple-element.108.refs_2_), channel_id=1, source_target_pairs={{2,0},{3,1},{0,2},{1,3},{6,4},{7,5},{4,6},{5,7},{10,8},{11,9},{8,1... | collective-permute-start | bytes 1966088 | tf_op jit(solution)/shard_map/ppermute | solution.py:357
  33.1 36.5 %collective-permute-start.8 = (bf16[1,320,1024]{2,1,0:T(8,128)(2,1)S(1)}, bf16[1,320,1024]{2,1,0:T(8,128)(2,1)}, u32[]{:S(2)}, u32[]{:S(2)}) collective-permute-start(bf16[1,320,1024]{2,1,0:T(8,128)(2,1)S(1)} %get-tuple-element.108.refs_2_), channel_id=1, source_target_pairs={{0,1},{1,0},{2,3},{3,2},{4,5},{5,4},{6,7},{7,6},{8,9},{9,8},{10,11... | collective-permute-start | bytes 1966088 | tf_op jit(solution)/shard_map/ppermute | solution.py:351
  44.2 25.8 %collective-permute-start.10 = (bf16[1,320,1024]{2,1,0:T(8,128)(2,1)}, bf16[1,320,1024]{2,1,0:T(8,128)(2,1)S(1)}, u32[]{:S(2)}, u32[]{:S(2)}) collective-permute-start(bf16[1,320,1024]{2,1,0:T(8,128)(2,1)} %collective-permute-done.3.refs_5_), channel_id=1, source_target_pairs={{0,1},{1,0},{2,3},{3,2},{4,5},{5,4},{6,7},{7,6},{8,9},{9,8},{10,11... | collective-permute-start | bytes 1966088 | tf_op jit(solution)/shard_map/ppermute | solution.py:351
  55.4 31.5 %collective-permute-start.14 = (bf16[1,320,1024]{2,1,0:T(8,128)(2,1)}, bf16[1,320,1024]{2,1,0:T(8,128)(2,1)S(1)}, u32[]{:S(2)}, u32[]{:S(2)}) collective-permute-start(bf16[1,320,1024]{2,1,0:T(8,128)(2,1)} %get-tuple-element.103.refs_3_), channel_id=1, source_target_pairs={{2,0},{3,1},{0,2},{1,3},{6,4},{7,5},{4,6},{5,7},{10,8},{11,9},{8,1... | collective-permute-start | bytes 1966088 | tf_op jit(solution)/shard_map/ppermute | solution.py:357
  57.7 12.2 %collective-permute-start.11 = (bf16[1,320,1024]{2,1,0:T(8,128)(2,1)}, bf16[1,320,1024]{2,1,0:T(8,128)(2,1)}, u32[]{:S(2)}, u32[]{:S(2)}) collective-permute-start(bf16[1,320,1024]{2,1,0:T(8,128)(2,1)} %collective-permute-done.9.refs_6_), channel_id=1, source_target_pairs={{0,1},{1,0},{2,3},{3,2},{4,5},{5,4},{6,7},{7,6},{8,9},{9,8},{10,11... | collective-permute-start | bytes 1966088 | tf_op jit(solution)/shard_map/ppermute | solution.py:351
  69.1 19.6 %collective-permute-start.12 = (bf16[1,320,1024]{2,1,0:T(8,128)(2,1)S(1)}, bf16[1,320,1024]{2,1,0:T(8,128)(2,1)S(1)}, u32[]{:S(2)}, u32[]{:S(2)}) collective-permute-start(bf16[1,320,1024]{2,1,0:T(8,128)(2,1)S(1)} %copy-done.32), channel_id=1, source_target_pairs={{0,1},{1,0},{2,3},{3,2},{4,5},{5,4},{6,7},{7,6},{8,9},{9,8},{10,11... | collective-permute-start | bytes 1966088 | tf_op jit(solution)/shard_map/ppermute | solution.py:351
  69.6 17.2 %collective-permute-start.15 = (bf16[1,320,1024]{2,1,0:T(8,128)(2,1)}, bf16[1,320,1024]{2,1,0:T(8,128)(2,1)S(1)}, u32[]{:S(2)}, u32[]{:S(2)}) collective-permute-start(bf16[1,320,1024]{2,1,0:T(8,128)(2,1)} %get-tuple-element.106.refs_4_), channel_id=1, source_target_pairs={{2,0},{3,1},{0,2},{1,3},{6,4},{7,5},{4,6},{5,7},{10,8},{11,9},{8,1... | collective-permute-start | bytes 1966088 | tf_op jit(solution)/shard_map/ppermute | solution.py:357
  69.9 18.7 %collective-permute-start.13 = (bf16[1,320,1024]{2,1,0:T(8,128)(2,1)}, bf16[1,320,1024]{2,1,0:T(8,128)(2,1)}, u32[]{:S(2)}, u32[]{:S(2)}) collective-permute-start(bf16[1,320,1024]{2,1,0:T(8,128)(2,1)} %get-tuple-element.106.refs_4_), channel_id=1, source_target_pairs={{0,1},{1,0},{2,3},{3,2},{4,5},{5,4},{6,7},{7,6},{8,9},{9,8},{10,11... | collective-permute-start | bytes 1966088 | tf_op jit(solution)/shard_map/ppermute | solution.py:351
  124.0 141.7 %reduce-scatter.9.cloned.1.call-start = ((), (), s32[]{:S(2)}) async-start(), calls=%async_computation.7 | async-start | bytes 1966080 | tf_op jit(solution)/shard_map/reduce_scatter | solution.py:921
  143.5 37.5 %collective-permute-start.18 = (bf16[1,4,192,1024]{3,2,1,0:T(8,128)(2,1)}, bf16[1,4,192,1024]{3,2,1,0:T(8,128)(2,1)S(1)}, u32[]{:S(2)}, u32[]{:S(2)}) collective-permute-start(bf16[1,4,192,1024]{3,2,1,0:T(8,128)(2,1)} %get-tuple-element.125), channel_id=1, source_target_pairs={{0,4},{4,0},{8,12},{12,8},{16,20},{20,16},{24,28},{28,24},{1,5},{5... | collective-permute-start | bytes 4718600 | tf_op jit(solution)/shard_map/ppermute | solution.py:960
  174.4 85.9 %collective-permute-start.19 = (bf16[2,4,192,1024]{3,2,1,0:T(8,128)(2,1)}, bf16[2,4,192,1024]{3,2,1,0:T(8,128)(2,1)}, u32[]{:S(2)}, u32[]{:S(2)}) collective-permute-start(bf16[2,4,192,1024]{3,2,1,0:T(8,128)(2,1)} %get-tuple-element.145), channel_id=1, source_target_pairs={{0,4},{4,0},{8,12},{12,8},{16,20},{20,16},{24,28},{28,24},{1,5},{5... | collective-permute-start | bytes 9437192 | tf_op jit(solution)/shard_map/ppermute | solution.py:960
  182.9 120.1 %reduce-scatter.11.cloned.1.call-start = ((), (), s32[]{:S(2)}) async-start(), calls=%async_computation.8 | async-start | bytes 3932160 | tf_op jit(solution)/shard_map/reduce_scatter | solution.py:921
  229.5 251.0 %reduce-scatter.13.cloned.1.call-start = ((), (), s32[]{:S(2)}) async-start(), calls=%async_computation.9 | async-start | bytes 3932160 | tf_op jit(solution)/shard_map/reduce_scatter | solution.py:921
  265.7 25.6 %collective-permute-start.23 = (f32[2,8,320]{2,1,0:T(8,128)S(1)}, f32[2,8,320]{2,1,0:T(8,128)S(1)}, u32[]{:S(2)}, u32[]{:S(2)}) collective-permute-start(f32[2,8,320]{2,1,0:T(8,128)S(1)} %get-tuple-element.211), channel_id=1, source_target_pairs={{3,0},{2,1},{1,2},{0,3},{7,4},{6,5},{5,6},{4,7},{11,8},{10,9},{9,1... | collective-permute-start | bytes 61448 | tf_op jit(solution)/shard_map/ppermute | solution.py:409
  265.7 25.6 %collective-permute-start.22 = (f32[2,8,320]{2,1,0:T(8,128)S(1)}, f32[2,8,320]{2,1,0:T(8,128)S(1)}, u32[]{:S(2)}, u32[]{:S(2)}) collective-permute-start(f32[2,8,320]{2,1,0:T(8,128)S(1)} %get-tuple-element.212), channel_id=1, source_target_pairs={{2,0},{3,1},{0,2},{1,3},{6,4},{7,5},{4,6},{5,7},{10,8},{11,9},{8,1... | collective-permute-start | bytes 61448 | tf_op jit(solution)/shard_map/ppermute | solution.py:409
  266.3 25.0 %collective-permute-start.21 = (f32[2,8,320]{2,1,0:T(8,128)S(1)}, f32[2,8,320]{2,1,0:T(8,128)S(1)}, u32[]{:S(2)}, u32[]{:S(2)}) collective-permute-start(f32[2,8,320]{2,1,0:T(8,128)S(1)} %get-tuple-element.213), channel_id=1, source_target_pairs={{1,0},{0,1},{3,2},{2,3},{5,4},{4,5},{7,6},{6,7},{9,8},{8,9},{11,10... | collective-permute-start | bytes 61448 | tf_op jit(solution)/shard_map/ppermute | solution.py:409
  272.9 18.5 %collective-permute-start.24 = (bf16[2,320,1024]{2,1,0:T(8,128)(2,1)}, bf16[2,320,1024]{2,1,0:T(8,128)(2,1)}, u32[]{:S(2)}, u32[]{:S(2)}) collective-permute-start(bf16[2,320,1024]{2,1,0:T(8,128)(2,1)} %get-tuple-element.193), channel_id=1, source_target_pairs={{0,1},{1,0},{2,3},{3,2},{4,5},{5,4},{6,7},{7,6},{8,9},{9,8},{10,11... | collective-permute-start | bytes 3932168 | tf_op jit(solution)/shard_map/ppermute | solution.py:351
  294.6 32.0 %collective-permute-start.25 = (bf16[2,320,1024]{2,1,0:T(8,128)(2,1)}, bf16[2,320,1024]{2,1,0:T(8,128)(2,1)}, u32[]{:S(2)}, u32[]{:S(2)}) collective-permute-start(bf16[2,320,1024]{2,1,0:T(8,128)(2,1)} %add_convert_fusion.7), channel_id=1, source_target_pairs={{0,2},{1,3},{2,0},{3,1},{4,6},{5,7},{6,4},{7,5},{8,10},{9,11},{10,... | collective-permute-start | bytes 3932168 | tf_op jit(solution)/shard_map/ppermute | solution.py:363
  296.1 70.6 %collective-permute-start.31 = (bf16[2,4,192,1024]{3,2,1,0:T(8,128)(2,1)}, bf16[2,4,192,1024]{3,2,1,0:T(8,128)(2,1)}, u32[]{:S(2)}, u32[]{:S(2)}) collective-permute-start(bf16[2,4,192,1024]{3,2,1,0:T(8,128)(2,1)} %get-tuple-element.167), channel_id=1, source_target_pairs={{0,4},{4,0},{8,12},{12,8},{16,20},{20,16},{24,28},{28,24},{1,5},{5... | collective-permute-start | bytes 9437192 | tf_op jit(solution)/shard_map/ppermute | solution.py:960
  297.6 69.1 %collective-permute-start.26 = (bf16[2,320,1024]{2,1,0:T(8,128)(2,1)}, bf16[2,320,1024]{2,1,0:T(8,128)(2,1)}, u32[]{:S(2)}, u32[]{:S(2)}) collective-permute-start(bf16[2,320,1024]{2,1,0:T(8,128)(2,1)} %get-tuple-element.191), channel_id=1, source_target_pairs={{0,1},{1,0},{2,3},{3,2},{4,5},{5,4},{6,7},{7,6},{8,9},{9,8},{10,11... | collective-permute-start | bytes 3932168 | tf_op jit(solution)/shard_map/ppermute | solution.py:351
  297.6 182.9 %reduce-scatter.15.cloned.1.call-start = ((), (), s32[]{:S(2)}) async-start(), calls=%async_computation.10 | async-start | bytes 3932160 | tf_op jit(solution)/shard_map/reduce_scatter | solution.py:921
  301.7 65.0 %collective-permute-start.28 = (bf16[2,320,1024]{2,1,0:T(8,128)(2,1)}, bf16[2,320,1024]{2,1,0:T(8,128)(2,1)}, u32[]{:S(2)}, u32[]{:S(2)}) collective-permute-start(bf16[2,320,1024]{2,1,0:T(8,128)(2,1)} %add_convert_fusion.6), channel_id=1, source_target_pairs={{0,2},{1,3},{2,0},{3,1},{4,6},{5,7},{6,4},{7,5},{8,10},{9,11},{10,... | collective-permute-start | bytes 3932168 | tf_op jit(solution)/shard_map/ppermute | solution.py:363
  339.3 37.4 %collective-permute-start.29 = (bf16[512,1024]{1,0:T(8,128)(2,1)}, bf16[512,1024]{1,0:T(8,128)(2,1)}, u32[]{:S(2)}, u32[]{:S(2)}) collective-permute-start(bf16[512,1024]{1,0:T(8,128)(2,1)} %constant_dynamic-slice_fusion.3), channel_id=1, source_target_pairs={{0,1},{1,0},{2,3},{3,2},{4,5},{5,4},{6,7},{7,6},{8,9},{9,8},{10,11... | collective-permute-start | bytes 3145736 | tf_op jit(solution)/shard_map/ppermute | solution.py:783
  368.5 15.1 %collective-permute-start.33 = (bf16[2,64,512]{2,1,0:T(8,128)(2,1)S(1)}, bf16[2,64,512]{2,1,0:T(8,128)(2,1)S(1)}, u32[]{:S(2)}, u32[]{:S(2)}) collective-permute-start(bf16[2,64,512]{2,1,0:T(8,128)(2,1)S(1)} %get-tuple-element.205), channel_id=1, source_target_pairs={{0,1},{1,0},{2,3},{3,2},{4,5},{5,4},{6,7},{7,6},{8,9},{9,8},{10,11... | collective-permute-start | bytes 393224 | tf_op jit(solution)/shard_map/ppermute | solution.py:351
  368.5 25.9 %collective-permute-start.32 = (bf16[2,64,512]{2,1,0:T(8,128)(2,1)S(1)}, bf16[2,64,512]{2,1,0:T(8,128)(2,1)S(1)}, u32[]{:S(2)}, u32[]{:S(2)}) collective-permute-start(bf16[2,64,512]{2,1,0:T(8,128)(2,1)S(1)} %get-tuple-element.206), channel_id=1, source_target_pairs={{0,1},{1,0},{2,3},{3,2},{4,5},{5,4},{6,7},{7,6},{8,9},{9,8},{10,11... | collective-permute-start | bytes 393224 | tf_op jit(solution)/shard_map/ppermute | solution.py:351
  370.8 13.7 %collective-permute-start.36 = (bf16[2,64,512]{2,1,0:T(8,128)(2,1)S(1)}, bf16[2,64,512]{2,1,0:T(8,128)(2,1)S(1)}, u32[]{:S(2)}, u32[]{:S(2)}) collective-permute-start(bf16[2,64,512]{2,1,0:T(8,128)(2,1)S(1)} %get-tuple-element.201), channel_id=1, source_target_pairs={{0,1},{1,0},{2,3},{3,2},{4,5},{5,4},{6,7},{7,6},{8,9},{9,8},{10,11... | collective-permute-start | bytes 393224 | tf_op jit(solution)/shard_map/ppermute | solution.py:351
  370.8 23.6 %collective-permute-start.35 = (bf16[2,64,512]{2,1,0:T(8,128)(2,1)S(1)}, bf16[2,64,512]{2,1,0:T(8,128)(2,1)S(1)}, u32[]{:S(2)}, u32[]{:S(2)}) collective-permute-start(bf16[2,64,512]{2,1,0:T(8,128)(2,1)S(1)} %get-tuple-element.202), channel_id=1, source_target_pairs={{0,1},{1,0},{2,3},{3,2},{4,5},{5,4},{6,7},{7,6},{8,9},{9,8},{10,11... | collective-permute-start | bytes 393224 | tf_op jit(solution)/shard_map/ppermute | solution.py:351
  378.6 14.9 %collective-permute-start.30 = (bf16[256,1024]{1,0:T(8,128)(2,1)S(1)}, bf16[256,1024]{1,0:T(8,128)(2,1)S(1)}, u32[]{:S(2)}, u32[]{:S(2)}) collective-permute-start(bf16[256,1024]{1,0:T(8,128)(2,1)S(1)} %constant_dynamic-slice_fusion.2), channel_id=1, source_target_pairs={{0,2},{1,3},{2,0},{3,1},{4,6},{5,7},{6,4},{7,5},{8,10},{9,11},{10,... | collective-permute-start | bytes 1572872 | tf_op jit(solution)/shard_map/ppermute | solution.py:783
  383.6 12.6 %collective-permute-start.34 = (bf16[2,64,512]{2,1,0:T(8,128)(2,1)S(1)}, bf16[2,64,512]{2,1,0:T(8,128)(2,1)S(1)}, u32[]{:S(2)}, u32[]{:S(2)}) collective-permute-start(bf16[2,64,512]{2,1,0:T(8,128)(2,1)S(1)} %add_convert_fusion.14), channel_id=1, source_target_pairs={{0,2},{1,3},{2,0},{3,1},{4,6},{5,7},{6,4},{7,5},{8,10},{9,11},{10,... | collective-permute-start | bytes 393224 | tf_op jit(solution)/shard_map/ppermute | solution.py:363
  384.6 13.5 %collective-permute-start.37 = (bf16[2,64,512]{2,1,0:T(8,128)(2,1)S(1)}, bf16[2,64,512]{2,1,0:T(8,128)(2,1)S(1)}, u32[]{:S(2)}, u32[]{:S(2)}) collective-permute-start(bf16[2,64,512]{2,1,0:T(8,128)(2,1)S(1)} %add_convert_fusion.13), channel_id=1, source_target_pairs={{0,2},{1,3},{2,0},{3,1},{4,6},{5,7},{6,4},{7,5},{8,10},{9,11},{10,... | collective-permute-start | bytes 393224 | tf_op jit(solution)/shard_map/ppermute | solution.py:363
  411.9 117.4 %all-reduce.2.cloned.1.call-start = ((), (), s32[]{:S(2)}) async-start(), calls=%async_computation.11 | async-start | bytes 1769472 | tf_op jit(solution)/shard_map/psum | solution.py:1066
  412.0 37.1 %collective-permute-start.41 = (bf16[1,4,192,1024]{3,2,1,0:T(8,128)(2,1)}, bf16[1,4,192,1024]{3,2,1,0:T(8,128)(2,1)}, u32[]{:S(2)}, u32[]{:S(2)}) collective-permute-start(bf16[1,4,192,1024]{3,2,1,0:T(8,128)(2,1)} %get-tuple-element.182), channel_id=1, source_target_pairs={{0,4},{4,0},{8,12},{12,8},{16,20},{20,16},{24,28},{28,24},{1,5},{5... | collective-permute-start | bytes 4718600 | tf_op jit(solution)/shard_map/ppermute | solution.py:960
  420.2 33.0 %collective-permute-start.39 = (bf16[256,2048]{1,0:T(8,128)(2,1)}, bf16[256,2048]{1,0:T(8,128)(2,1)}, u32[]{:S(2)}, u32[]{:S(2)}) collective-permute-start(bf16[256,2048]{1,0:T(8,128)(2,1)} %constant_dynamic-slice_fusion), channel_id=1, source_target_pairs={{0,2},{1,3},{2,0},{3,1},{4,6},{5,7},{6,4},{7,5},{8,10},{9,11},{10,... | collective-permute-start | bytes 3145736 | tf_op jit(solution)/shard_map/ppermute | solution.py:783
  455.0 25.3 %collective-permute-start.40 = (bf16[128,3072]{1,0:T(8,128)(2,1)S(1)}, bf16[128,3072]{1,0:T(8,128)(2,1)S(1)}, u32[]{:S(2)}, u32[]{:S(2)}) collective-permute-start(bf16[128,3072]{1,0:T(8,128)(2,1)S(1)} %fusion.10), channel_id=1, source_target_pairs={{0,4},{4,0},{8,12},{12,8},{16,20},{20,16},{24,28},{28,24},{1,5},{5... | collective-permute-start | bytes 2359304 | tf_op jit(solution)/shard_map/ppermute | solution.py:783
  463.6 15.6 %collective-permute-start.44 = (f32[48,1024]{1,0:T(8,128)S(1)}, f32[48,1024]{1,0:T(8,128)}, u32[]{:S(2)}, u32[]{:S(2)}) collective-permute-start(f32[48,1024]{1,0:T(8,128)S(1)} %add.308), channel_id=1, source_target_pairs={{0,4},{4,0},{8,12},{12,8},{16,20},{20,16},{24,28},{28,24},{1,5},{5... | collective-permute-start | bytes 589832 | tf_op jit(solution)/shard_map/ppermute | solution.py:1061
  481.5 85.1 %reduce-scatter.17.cloned.1.call-start = ((), (), s32[]{:S(2)}) async-start(), calls=%async_computation.12 | async-start | bytes 1966080 | tf_op jit(solution)/shard_map/reduce_scatter | solution.py:921
  482.8 19.1 %collective-permute-start.59 = (bf16[2,192,1024]{2,1,0:T(8,128)(2,1)S(1)}, bf16[2,192,1024]{2,1,0:T(8,128)(2,1)S(1)}, u32[]{:S(2)}, u32[]{:S(2)}) collective-permute-start(bf16[2,192,1024]{2,1,0:T(8,128)(2,1)S(1)} %slice.166), channel_id=1, source_target_pairs={{0,4},{4,0},{8,12},{12,8},{16,20},{20,16},{24,28},{28,24},{1,5},{5... | collective-permute-start | bytes 2359304 | tf_op jit(solution)/shard_map/ppermute | solution.py:1038
  531.3 40.5 %collective-permute-start.55 = (bf16[128,1536]{1,0:T(8,128)(2,1)S(1)}, bf16[128,1536]{1,0:T(8,128)(2,1)}, u32[]{:S(2)}, u32[]{:S(2)}) collective-permute-start(bf16[128,1536]{1,0:T(8,128)(2,1)S(1)} %get-tuple-element.198.refs_8_), channel_id=1, source_target_pairs={{0,1},{1,0},{2,3},{3,2},{4,5},{5,4},{6,7},{7,6},{8,9},{9,8},{10,11... | collective-permute-start | bytes 1179656 | tf_op jit(solution)/shard_map/ppermute | solution.py:351
  531.3 41.9 %collective-permute-start.53 = (bf16[128,1536]{1,0:T(8,128)(2,1)S(1)}, bf16[128,1536]{1,0:T(8,128)(2,1)}, u32[]{:S(2)}, u32[]{:S(2)}) collective-permute-start(bf16[128,1536]{1,0:T(8,128)(2,1)S(1)} %get-tuple-element.198.refs_8_), channel_id=1, source_target_pairs={{0,2},{1,3},{2,0},{3,1},{4,6},{5,7},{6,4},{7,5},{8,10},{9,11},{10,... | collective-permute-start | bytes 1179656 | tf_op jit(solution)/shard_map/ppermute | solution.py:1075
  532.7 40.7 %collective-permute-start.52 = (bf16[128,1536]{1,0:T(8,128)(2,1)S(1)}, bf16[128,1536]{1,0:T(8,128)(2,1)}, u32[]{:S(2)}, u32[]{:S(2)}) collective-permute-start(bf16[128,1536]{1,0:T(8,128)(2,1)S(1)} %get-tuple-element.198.refs_8_), channel_id=1, source_target_pairs={{0,4},{4,0},{8,12},{12,8},{16,20},{20,16},{24,28},{28,24},{1,5},{5... | collective-permute-start | bytes 1179656 | tf_op jit(solution)/shard_map/ppermute | solution.py:1079
  534.2 40.7 %collective-permute-start.45 = (bf16[128,1536]{1,0:T(8,128)(2,1)}, bf16[128,1536]{1,0:T(8,128)(2,1)}, u32[]{:S(2)}, u32[]{:S(2)}) collective-permute-start(bf16[128,1536]{1,0:T(8,128)(2,1)} %get-tuple-element.199.refs_0_), channel_id=1, source_target_pairs={{0,4},{4,0},{8,12},{12,8},{16,20},{20,16},{24,28},{28,24},{1,5},{5... | collective-permute-start | bytes 1179656 | tf_op jit(solution)/shard_map/ppermute | solution.py:1074
  574.9 17.0 %collective-permute-start.47 = (bf16[128,1536]{1,0:T(8,128)(2,1)}, bf16[128,1536]{1,0:T(8,128)(2,1)S(1)}, u32[]{:S(2)}, u32[]{:S(2)}) collective-permute-start(bf16[128,1536]{1,0:T(8,128)(2,1)} %collective-permute-done.45.refs_1_), channel_id=1, source_target_pairs={{0,2},{1,3},{2,0},{3,1},{4,6},{5,7},{6,4},{7,5},{8,10},{9,11},{10,... | collective-permute-start | bytes 1179656 | tf_op jit(solution)/shard_map/ppermute | solution.py:1077
  576.4 16.8 %collective-permute-start.49 = (bf16[128,1536]{1,0:T(8,128)(2,1)}, bf16[128,1536]{1,0:T(8,128)(2,1)S(1)}, u32[]{:S(2)}, u32[]{:S(2)}) collective-permute-start(bf16[128,1536]{1,0:T(8,128)(2,1)} %collective-permute-done.45.refs_1_), channel_id=1, source_target_pairs={{0,1},{1,0},{2,3},{3,2},{4,5},{5,4},{6,7},{7,6},{8,9},{9,8},{10,11... | collective-permute-start | bytes 1179656 | tf_op jit(solution)/shard_map/ppermute | solution.py:351
  (72 other events, 580.5 us)
Sparse Core Ops, SparseCore 0:
  124.1 60.7 reduce-scatter.6
  187.2 35.3 reduce-scatter.8
  229.6 60.7 reduce-scatter.10
  297.8 60.5 reduce-scatter.12
  412.0 61.2 reduce-scatter.14
  481.6 47.5 all-reduce.1
  532.1 34.4 reduce-scatter.16

commit v4 on v3

--- a/solution.py
+++ b/solution.py
@@ -186,16 +186,24 @@
     refs = refs[1 + chunks :]
     if with_dots:
         dot_refs, refs = refs[:chunks], refs[chunks:]
-        out_ref, back_ref, onehot_ref, flat_ref = refs
+        back_ref, onehot_ref, flat_ref = refs[-3:]
+        out_refs = refs[:-3]
     else:
-        out_ref, onehot_ref, flat_ref = refs
+        onehot_ref, flat_ref = refs[-2:]
+        out_refs = refs[:-2]
     fill_one_hot(slot_ref[0], onehot_ref)
     e = 0
     for ref in row_refs:
         for i in range(ref.shape[0]):
             flat_ref[e * SLOTS : (e + 1) * SLOTS, :] = ref[i, 0]
             e += 1
-    out_ref[0] = mm(onehot_ref[...], flat_ref[...], ((0,), (0,))).astype(bf16)
+    total = mm(onehot_ref[...], flat_ref[...], ((0,), (0,))).astype(bf16)
+    for j, out_ref in enumerate(out_refs):
+
+        @pl.when(pl.program_id(0) // MICRO == j)
+        def _(out_ref=out_ref):
+            out_ref[0] = total
+
     if with_dots:
         place = lax.broadcasted_iota(jnp.int32, (SLOTS, slot_ref.shape[2]), 0)
         e = 0
@@ -217,8 +225,15 @@
     in_specs = [pl.BlockSpec((1, experts, tok), lambda b: (b, 0, 0))]
     in_specs += [chunk_spec(chunk) for chunk in rows]
     args = [slots] + rows
-    out_shape = [jax.ShapeDtypeStruct((blocks, tok, D), bf16)]
-    out_specs = [pl.BlockSpec((1, tok, D), lambda b: (b, 0, 0))]
+    members = blocks // MICRO
+
+    def member_spec(j):
+        return pl.BlockSpec(
+            (1, tok, D), lambda b: (jnp.clip(b - j * MICRO, 0, MICRO - 1), 0, 0)
+        )
+
+    out_shape = [jax.ShapeDtypeStruct((MICRO, tok, D), bf16)] * members
+    out_specs = [member_spec(j) for j in range(members)]
     if dots is not None:
         in_specs += [chunk_spec(chunk) for chunk in dots]
         args += dots
@@ -385,12 +400,13 @@
 
 def return_members(pieces, groups, *before):
     swapped = [core_swap(pieces[2 * s + 1], groups) for s in range(groups // 2)]
-    terms = [pieces[0], swapped[0]]
+    terms, sent = [pieces[0], swapped[0]], []
     for s in range(1, groups // 2):
         mine = after(pieces[2 * s], *before)
         both = (mine.astype(f32) + swapped[s].astype(f32)).astype(bf16)
+        sent.append(both)
         terms.append(to_row(both, groups, s))
-    return terms
+    return terms, sent
 
 
 def exchange_members(pieces, groups):
@@ -872,7 +888,9 @@
     ids_all = lax.rem(jnp.concatenate(ids_t, axis=0) + (EXPERTS - first_expert), EXPERTS)
     cot_pieces = [gather_members(cot_rows[:1], groups)]
     normed, queries, key_value = project(token_rows, attn_gain, w_qkv, cosine, sine)
-    prompt_pieces = gather_members(key_value[:, :PROMPT_DEV], groups)
+    prompt_pieces = gather_members(
+        after(key_value[:, :PROMPT_DEV], cot_pieces[0][2]), groups
+    )
     prompt = jnp.concatenate(prompt_pieces, axis=1)
     cot_pieces += [
         gather_members(after(cot_rows[m : m + 1], prompt_pieces[2]), groups)
@@ -884,7 +902,7 @@
 
     attended, lse, hidden, moe_pieces, moe_low = [], [], [], [], []
     for m in range(MICRO):
-        mask = after(bias, cot_pieces[0][2] if m == 0 else moe_low[-1])
+        mask = bias if m == 0 else after(bias, moe_low[-1])
         att, log_total, hid, low = attend(
             m, queries, key_value, prompt, mask, token_rows, w_out, moe_gain
         )
@@ -931,11 +949,16 @@
         plan = tuple((1, e == 0) for e in range(local_experts))
     outs, backs, dots, halves, parts = [], [], [], {}, {}
 
-    def add_x(i, *before):
+    held = {}
+
+    def add_x(i, *before, hold=False):
         keep, got = halves.pop(i)
         got = after(got, *before)
         half = (keep.astype(f32) + got.astype(f32)).astype(bf16)
-        parts[i] = sum_z(half)
+        if hold:
+            held[i] = half
+        else:
+            parts[i] = sum_z(half)
         return half
 
     first = 0
@@ -960,19 +983,19 @@
             halves[i] = (sums[0], lax.ppermute(sums[1], "dp", swap_x))
         first += count
 
-    def left(i, *before):
-        return [add_x(i, *before)] if i in halves else []
+    def left(i, *before, hold=False):
+        return [add_x(i, *before, hold=hold)] if i in halves else []
 
     def sent(i):
         return [parts[i]] if i in parts else []
 
-    back_sum, back_dots = sum_rows(slots, backs, dots)
+    *back_sum, back_dots = sum_rows(slots, backs, dots)
 
     def pieces_of(value):
         return [value[j * MICRO : (j + 1) * MICRO] for j in range(groups)]
 
     dot_pieces = exchange_members(pieces_of(back_dots), groups)
-    back_terms = return_members(pieces_of(back_sum), groups, *dot_pieces)
+    back_terms, back_sent = return_members(back_sum, groups, *dot_pieces)
     token_dots = jnp.zeros((MICRO, EXPERTS, tok_rows), f32)
     for s in range(groups // 2):
         for c in range(2):
@@ -986,21 +1009,25 @@
     own_gates = gates[:MICRO]
     centre = jnp.sum(own_gates * token_dots, axis=1, keepdims=True)
     grad_logits = (own_gates * (token_dots - centre)).astype(bf16)
-    (mixed,) = sum_rows(after(slots, back_sum, *sent(1), *left(2, back_sum)), outs)
-    mix_terms = return_members(pieces_of(mixed), groups)
+    mixed = sum_rows(
+        after(slots, *back_sent, *sent(1), *left(2, back_sum[0], hold=True)), outs
+    )
+    mix_terms, _ = return_members(mixed, groups)
 
     grad_hidden, grad_branch, grad_attended, grad_norm_moe = middle_back(
-        back_terms, grad_logits, router, hidden, moe_gain, after(cot_rows, mixed, *sent(4)), w_out
+        back_terms, grad_logits, router, hidden, moe_gain, after(cot_rows, *mixed, *sent(4)), w_out
     )
     grad_router = jnp.einsum("bet,btd->ed", grad_logits, moe_low, preferred_element_type=f32)
     grad_out = jnp.einsum(
         "brd,bre->de", attended, grad_branch, preferred_element_type=f32
     ).astype(bf16)
+    core_bit, row_bit = lax.rem(member, 2), lax.rem(member // 2, 2)
+    grad_out = halve(grad_out, "expert", swap_core, core_bit)
     gq, gpk, gpv, gok, gov = attend_back(
         queries,
         key_value,
         prompt,
-        after(bias, grad_out),
+        after(bias, grad_out, *left(3, grad_branch)),
         lse,
         grad_attended,
         cosine,
@@ -1010,14 +1037,13 @@
     def prompt_terms(value):
         return return_members(
             [value[:, j * PROMPT_DEV : (j + 1) * PROMPT_DEV] for j in range(groups)], groups
-        )
+        )[0]
 
     mixture = sum(after(term, gq).astype(f32) for term in mix_terms)
     output = (hidden + branch_scale * mixture).astype(bf16)
-    core_bit, row_bit = lax.rem(member, 2), lax.rem(member // 2, 2)
-    grad_out = halve(halve(grad_out, "expert", swap_core, core_bit), "expert", swap_y, row_bit)
+    grad_out = halve(grad_out, "expert", swap_y, row_bit)
     gp, grad_qkv = weight_back(
-        after(normed, output, grad_out, *left(3, gq)),
+        after(normed, grad_out, *mix_terms[2:], *left(5, gq)),
         gq,
         gok,
         gov,
@@ -1027,9 +1053,9 @@
         sine,
     )
     grad_tokens, grad_norm_attn = token_back(
-        after(gp, grad_qkv), w_qkv, token_rows, attn_gain, grad_hidden
-    )
-    last = [add_x(i, grad_norm_attn) for i in list(halves)]
+        after(gp, grad_qkv, output), w_qkv, token_rows, attn_gain, grad_hidden
+    )
+    last = [add_x(i, grad_norm_attn) for i in list(halves)] + sent(2) + sent(3)
     grad_qkv = halve(grad_qkv, "expert", swap_core, core_bit)
     grad_qkv = halve(grad_qkv, "expert", swap_y, row_bit)
 
@@ -1039,7 +1065,7 @@
     whole_sums = (whole_sums[:, :piece].astype(f32) + swapped.astype(f32)).astype(bf16)
     pieces, at = [], 0
     for i, (count, whole) in enumerate(plan):
-        pieces.append(whole_sums[at : at + count] if whole else parts[i])
+        pieces.append(whole_sums[at : at + count] if whole else parts.get(i))
         at += count if whole else 0
 
     small = jnp.concatenate(
@@ -1057,10 +1083,13 @@
         axis=0,
     )
     small = after(small, *last)
-    for axis, swap in (("expert", swap_core), ("expert", swap_y), ("dp", swap_x)):
+    for axis, swap in (("expert", swap_core), ("dp", swap_x), ("expert", swap_y)):
         small = small + lax.ppermute(small, axis, swap)
     dense = jnp.concatenate([grad_qkv, grad_out], axis=1)
-    dense = after(halve(dense, "dp", swap_x, parity), *sent(2), *sent(3))
+    dense = after(halve(dense, "dp", swap_x, parity), *sent(5))
+    for i in list(held):
+        parts[i] = sum_z(after(held.pop(i), dense))
+        pieces[i] = parts[i]
     dense_rows = dense.shape[0]
     dense = jnp.concatenate([dense, small.reshape(-1, 3 * D).astype(bf16)], axis=0)
     dense = lax.psum(dense, "dp", axis_index_groups=z_groups)
@@ -1078,6 +1107,7 @@
     ]
     right_x = [lax.ppermute(value, "dp", swap_x) for value in (right_own, right_y)]
     right_four = [right_own, right_x[0], right_y, right_x[1]]
+    pieces[2] = after(pieces[2], left_four[3], right_four[3])
     left_all = left_four + [core_swap(value, groups) for value in left_four]
     right_all = right_four + [core_swap(value, groups) for value in right_four]
     base = core_bit * 4 + row_bit * 2 + parity

time: 620 us -> 589 us (0.950)
  waiting for transfers between devices: 197 us -> 174 us
    ppermute x4, waiting for transfers between devices: 29.6 us -> 6.04 us  [local(): halves[i] = (sums[0], lax.ppermute(sums[1], 'dp', swap_x))]
    ppermute x5, waiting for transfers between devices: 8.8 us -> 31.1 us  [halve(): got = lax.ppermute(send, axis, swap)]
    psum x1, waiting for transfers between devices: 25 us -> 43.9 us  [local(): dense = lax.psum(dense, 'dp', axis_index_groups=z_groups)]
    ppermute x1, waiting for transfers between devices: 16.9 us -> 0.01 us  [local(): swapped = lax.ppermute(after(whole_sums[:, piece:], *last), 'dp', swap_x)]
    reduce_scatter x6, waiting for transfers between devices: 31.8 us -> 19.4 us  [sum_z(): lax.psum_scatter(value.reshape(count, pairs * height, D), 'dp', scatter_d...]
    ppermute x2, waiting for transfers between devices: 14.3 us -> 2.28 us  [local(): lax.ppermute(value, 'expert', swap_y)]
    ppermute x4, waiting for transfers between devices: 27.1 us -> 16.1 us  [to_row(): return lax.ppermute(value, 'expert', pairs)]
    slice x3 -> x1, local copies, waits for them, and re-layouts: 11.7 us -> 0.97 us  [local(): key_value[:, :PROMPT_DEV]]
  transfers between devices with their start and end apart: 67 -> 67, of which waited for: 23 -> 24; matrix products, arithmetic and copies ran while one was open for 13% -> 11% of each run, Pallas kernels for 38% -> 42%
where the time goes in v4:
time: 589 us; the launch traced here: 579 us
  Pallas kernels  276 us (47%)
  waiting for transfers between devices  174 us (30%)
  other arithmetic  40.9 us (7%)
  starting transfers between devices  34.6 us (6%)
  local copies, waits for them, and re-layouts  33.4 us (6%)
  between operations  15.4 us (3%)
    pallas_call x6, Pallas kernels, expert_chunk(): pl.pallas_call(functools.partial(expert_body, tile=tile), grid_spec=grid_...  127 us
    psum x1, waiting for transfers between devices, local(): dense = lax.psum(dense, 'dp', axis_index_groups=z_groups)  43.9 us
    ppermute x5, waiting for transfers between devices, halve(): got = lax.ppermute(send, axis, swap)  31.1 us
    pallas_call x2, Pallas kernels, sum_rows(): pl.pallas_call(functools.partial(sum_rows_body, chunks=len(rows), with_do...  28.1 us
    pallas_call x1, Pallas kernels, attend_back(): pl.pallas_call(attend_back_body, grid=(micro, steps), in_specs=[wide, pro...  22.9 us
    pallas_call x2, Pallas kernels, attend(): pl.pallas_call(attend_body, grid=(steps,), in_specs=[pl.BlockSpec((1, row...  22.4 us
    reduce_scatter x6, waiting for transfers between devices, sum_z(): lax.psum_scatter(value.reshape(count, pairs * height, D), 'dp', scatter_d...  19.4 us
    ppermute x6, waiting for transfers between devices, from_row(): return lax.ppermute(value, 'expert', pairs)  17.2 us
  transfers between devices with their start and end apart: 67, of which 24 were waited for; matrix products, arithmetic and copies ran while one was open for 11% of the time, Pallas kernels for 42%

profile of v4, /device:TPU:0, one launch (start us, length us, event | category | flops | bytes accessed | tf_op | source)
XLA Modules:
  0.0 579.4 jit_solution(1439653119245505188)
XLA Ops:
  8.0 3.1 collective-permute-start.5
  15.1 6.7 %shard_map.169 = (bf16[2,320,1024]{2,1,0:T(8,128)(2,1)}, bf16[2,320,1024]{2,1,0:T(8,128)(2,1)}, bf16[2,320,1024]{2,1,0:T(8,128)(2,1)}) custom-call(bf16[2,320,1024]{2,1,0:T(8,128)(2,1)} %bitcast.74, f32[1,1024]{1,0:T(1,128)} %bitcast.81, bf16[1024,2048]{1,0:T(8,128)(2,1)} %w_ref.7, f32[320,128]{1,0:T(8,128)} %copy.24.cos_ref.refs_10_, ...), custom_call_target="tpu_custom_call" | custom-call | flops 8049999872 | tf_op jit(solution)/shard_map/pallas_call | solution.py:468
  22.7 7.2 %collective-permute-done.refs_5_ = bf16[1,320,1024]{2,1,0:T(8,128)(2,1)} collective-permute-done((bf16[1,320,1024]{2,1,0:T(8,128)(2,1)S(1)}, bf16[1,320,1024]{2,1,0:T(8,128)(2,1)}, u32[]{:S(2)}, u32[]{:S(2)}) %collective-permute-start) | collective-permute-done | bytes 655392 | tf_op jit(solution)/shard_map/ppermute | solution.py:372
  30.9 6.4 %collective-permute-done.2 = bf16[2,64,1024]{2,1,0:T(8,128)(2,1)S(1)} collective-permute-done((bf16[2,64,1024]{2,1,0:T(8,128)(2,1)S(1)}, bf16[2,64,1024]{2,1,0:T(8,128)(2,1)S(1)}, u32[]{:S(2)}, u32[]{:S(2)}) %collective-permute-start.2) | collective-permute-done | bytes 262176 | tf_op jit(solution)/shard_map/ppermute | solution.py:372
  41.9 11.2 %shard_map.170 = (bf16[1,320,1024]{2,1,0:T(8,128)(2,1)}, f32[4,1,1280]{2,1,0:T(1,128)}, f32[1,320,1024]{2,1,0:T(8,128)}, bf16[1,320,1024]{2,1,0:T(8,128)(2,1)}) custom-call(bf16[2,320,1024]{2,1,0:T(8,128)(2,1)} %get-tuple-element.108.q_ref, bf16[2,256,1024]{2,1,0:T(8,128)(2,1)} %pad_maximum_fusion.pk_ref.pv_ref, ...), custom_call_target="tpu_custom_call" | custom-call | flops 13799999488 | tf_op jit(solution)/shard_map/pallas_call | solution.py:544
  54.7 2.7 collective-permute-done.9.refs_6_
  57.4 11.2 %shard_map.171 = (bf16[1,320,1024]{2,1,0:T(8,128)(2,1)}, f32[4,1,1280]{2,1,0:T(1,128)}, f32[1,320,1024]{2,1,0:T(8,128)}, bf16[1,320,1024]{2,1,0:T(8,128)(2,1)}) custom-call(bf16[2,320,1024]{2,1,0:T(8,128)(2,1)} %get-tuple-element.108.q_ref, bf16[2,256,1024]{2,1,0:T(8,128)(2,1)} %pad_maximum_fusion.pk_ref.pv_ref, ...), custom_call_target="tpu_custom_call" | custom-call | flops 13799999488 | tf_op jit(solution)/shard_map/pallas_call | solution.py:544
  70.4 15.1 %shard_map.172 = (bf16[8,8,112,1024]{3,2,1,0:T(8,128)(2,1)}, s32[8,8,320]{2,1,0:T(8,128)}) custom-call(s32[8,8,320]{2,1,0:T(8,128)} %negate_select_fusion.1.refs_0_, bf16[1,320,1024]{2,1,0:T(8,128)(2,1)} %copy-done.19, bf16[1,320,1024]{2,1,0:T(8,128)(2,1)} %copy-done.18, bf16[1,320,1024]{2,1,0:T(8,128)(2,1)} %copy-done.31, ...), custom_call_target="tpu_custom_call" | custom-call | flops 17250000896 | tf_op jit(solution)/shard_map/pallas_call | solution.py:112
  89.7 16.8 %shard_map.173 = (bf16[8,8,112,1024]{3,2,1,0:T(8,128)(2,1)}, f32[8,8,112,128]{3,2,1,0:T(8,128)}, f32[8,32,320]{2,1,0:T(8,128)}) custom-call(s32[8,8,320]{2,1,0:T(8,128)} %negate_select_fusion.1.refs_0_, s32[8,8,320]{2,1,0:T(8,128)} %get-tuple-element.160.refs_1_.refs_0_, bf16[1024,32]{1,0:T(8,128)(2,1)} %dynamic-slice_maximum_fusion.refs_2_.refs_4_, ...), custom_call_target="tpu_custom_call" | custom-call | flops 19549999104 | tf_op jit(solution)/shard_map/pallas_call | solution.py:158
  106.4 17.0 %shard_map.174 = (bf16[1,896,1024]{2,1,0:T(8,128)(2,1)}, bf16[1,896,1024]{2,1,0:T(8,128)(2,1)}, f32[1,896,128]{2,1,0:T(8,128)}, bf16[1,4,384,1024]{3,2,1,0:T(8,128)(2,1)}) custom-call(s32[1]{0:T(128)} %bitcast.8.parity_ref, bf16[8,896,1024]{2,1,0:T(8,128)(2,1)} %bitcast.89, bf16[8,896,1024]{2,1,0:T(8,128)(2,1)} %bitcast.83, f32[8,896,128]{2,1,0:T(8,128)} %bitcast.95, ...), custom_call_target="tpu_custom_call" | custom-call | flops 17250000896 | tf_op jit(solution)/shard_map/pallas_call | solution.py:351
  127.1 17.1 %shard_map.175 = (bf16[1,896,1024]{2,1,0:T(8,128)(2,1)}, bf16[1,896,1024]{2,1,0:T(8,128)(2,1)}, f32[1,896,128]{2,1,0:T(8,128)}, bf16[1,4,192,1024]{3,2,1,0:T(8,128)(2,1)}, bf16[1,4,192,1024]{3,2,1,0:T(8,128)(2,1)}) custom-call(s32[1]{0:T(128)} %bitcast.8.parity_ref, bf16[8,896,1024]{2,1,0:T(8,128)(2,1)} %bitcast.90, bf16[8,896,1024]{2,1,0:T(8,128)(2,1)} %bitcast.84, ...), custom_call_target="tpu_custom_call" | custom-call | flops 17250000896 | tf_op jit(solution)/shard_map/pallas_call | solution.py:351
  145.7 29.4 %shard_map.176 = (bf16[2,896,1024]{2,1,0:T(8,128)(2,1)}, bf16[2,896,1024]{2,1,0:T(8,128)(2,1)}, f32[2,896,128]{2,1,0:T(8,128)}, bf16[2,4,192,1024]{3,2,1,0:T(8,128)(2,1)}, bf16[2,4,192,1024]{3,2,1,0:T(8,128)(2,1)}) custom-call(s32[1]{0:T(128)} %bitcast.8.parity_ref, bf16[8,896,1024]{2,1,0:T(8,128)(2,1)} %bitcast.91, bf16[8,896,1024]{2,1,0:T(8,128)(2,1)} %bitcast.85, ...), custom_call_target="tpu_custom_call" | custom-call | flops 34500001792 | tf_op jit(solution)/shard_map/pallas_call | solution.py:351
  175.6 6.0 %collective-permute-done.18 = bf16[1,4,192,1024]{3,2,1,0:T(8,128)(2,1)S(1)} collective-permute-done((bf16[1,4,192,1024]{3,2,1,0:T(8,128)(2,1)}, bf16[1,4,192,1024]{3,2,1,0:T(8,128)(2,1)S(1)}, u32[]{:S(2)}, u32[]{:S(2)}) %collective-permute-start.18) | collective-permute-done | bytes 1572896 | tf_op jit(solution)/shard_map/ppermute | solution.py:983
  181.7 1.8 add_convert_fusion.4
  183.6 29.7 %shard_map.177 = (bf16[2,896,1024]{2,1,0:T(8,128)(2,1)}, bf16[2,896,1024]{2,1,0:T(8,128)(2,1)}, f32[2,896,128]{2,1,0:T(8,128)}, bf16[2,4,192,1024]{3,2,1,0:T(8,128)(2,1)}, bf16[2,4,192,1024]{3,2,1,0:T(8,128)(2,1)}) custom-call(s32[1]{0:T(128)} %bitcast.8.parity_ref, bf16[8,896,1024]{2,1,0:T(8,128)(2,1)} %bitcast.92, bf16[8,896,1024]{2,1,0:T(8,128)(2,1)} %bitcast.86, ...), custom_call_target="tpu_custom_call" | custom-call | flops 34500001792 | tf_op jit(solution)/shard_map/pallas_call | solution.py:351
  214.8 16.9 %shard_map.178 = (bf16[1,896,1024]{2,1,0:T(8,128)(2,1)}, bf16[1,896,1024]{2,1,0:T(8,128)(2,1)}, f32[1,896,128]{2,1,0:T(8,128)}, bf16[1,4,384,1024]{3,2,1,0:T(8,128)(2,1)}) custom-call(s32[1]{0:T(128)} %bitcast.8.parity_ref, bf16[8,896,1024]{2,1,0:T(8,128)(2,1)} %bitcast.93, bf16[8,896,1024]{2,1,0:T(8,128)(2,1)} %bitcast.87, f32[8,896,128]{2,1,0:T(8,128)} %bitcast.99, ...), custom_call_target="tpu_custom_call" | custom-call | flops 17250000896 | tf_op jit(solution)/shard_map/pallas_call | solution.py:351
  231.7 17.3 %shard_map.179 = (bf16[1,896,1024]{2,1,0:T(8,128)(2,1)}, bf16[1,896,1024]{2,1,0:T(8,128)(2,1)}, f32[1,896,128]{2,1,0:T(8,128)}, bf16[1,4,192,1024]{3,2,1,0:T(8,128)(2,1)}, bf16[1,4,192,1024]{3,2,1,0:T(8,128)(2,1)}) custom-call(s32[1]{0:T(128)} %bitcast.8.parity_ref, bf16[8,896,1024]{2,1,0:T(8,128)(2,1)} %bitcast.94, bf16[8,896,1024]{2,1,0:T(8,128)(2,1)} %bitcast.88, ...), custom_call_target="tpu_custom_call" | custom-call | flops 17250000896 | tf_op jit(solution)/shard_map/pallas_call | solution.py:351
  249.0 14.7 %shard_map.180 = (bf16[2,320,1024]{2,1,0:T(8,128)(2,1)}, bf16[2,320,1024]{2,1,0:T(8,128)(2,1)}, bf16[2,320,1024]{2,1,0:T(8,128)(2,1)}, bf16[2,320,1024]{2,1,0:T(8,128)(2,1)}, f32[8,8,320]{2,1,0:T(8,128)}) custom-call(s32[8,8,320]{2,1,0:T(8,128)} %get-tuple-element.160.refs_1_.refs_0_, bf16[1,8,112,1024]{3,2,1,0:T(8,128)(2,1)} %bitcast.106, ...), custom_call_target="tpu_custom_call" | custom-call | flops 17250000896 | tf_op jit(solution)/shard_map/pallas_call | solution.py:242
  266.9 5.4 add_convert_fusion.1
  275.3 13.4 %shard_map.181 = (bf16[2,320,1024]{2,1,0:T(8,128)(2,1)}, bf16[2,320,1024]{2,1,0:T(8,128)(2,1)}, bf16[2,320,1024]{2,1,0:T(8,128)(2,1)}, bf16[2,320,1024]{2,1,0:T(8,128)(2,1)}) custom-call(s32[8,8,320]{2,1,0:T(8,128)} %get-tuple-element.160.refs_1_.refs_0_, bf16[1,8,112,1024]{3,2,1,0:T(8,128)(2,1)} %bitcast.105, bf16[1,8,112,1024]{3,2,1,0:T(8,128)(2,1)} %bitcast.107, ...), custom_call_target="tpu_custom_call" | custom-call | flops 17250000896 | tf_op jit(solution)/shard_map/pallas_call | solution.py:242
  288.7 3.3 reduce-scatter.11.cloned.1.call-done
  292.1 12.9 %collective-permute-done.25.refs_2_ = bf16[2,320,1024]{2,1,0:T(8,128)(2,1)} collective-permute-done((bf16[2,320,1024]{2,1,0:T(8,128)(2,1)S(1)}, bf16[2,320,1024]{2,1,0:T(8,128)(2,1)}, u32[]{:S(2)}, u32[]{:S(2)}) %collective-permute-start.25) | collective-permute-done | bytes 1310752 | tf_op jit(solution)/shard_map/ppermute | solution.py:378
  304.9 8.3 %shard_map.182 = (f32[2,320,1024]{2,1,0:T(8,128)}, bf16[2,320,1024]{2,1,0:T(8,128)(2,1)}, bf16[2,320,1024]{2,1,0:T(8,128)(2,1)}, f32[1,1024]{1,0:T(1,128)}) custom-call(bf16[2,320,1024]{2,1,0:T(8,128)(2,1)} %get-tuple-element.158.refs_0_, bf16[2,320,1024]{2,1,0:T(8,128)(2,1)} %copy-done.29, bf16[2,320,1024]{2,1,0:T(8,128)(2,1)} %collective-permute-done.25.refs_2_, ...), custom_call_target="tpu_custom_call" | custom-call | flops 9200000000 | tf_op jit(solution)/shard_map/pallas_call | solution.py:611
  313.2 3.4 bitcast_convert_fusion
  320.1 3.3 add_convert_fusion.6
  324.5 5.1 add_convert_fusion
  332.9 22.9 %shard_map.183 = (bf16[2,320,1024]{2,1,0:T(8,128)(2,1)}, bf16[2,256,512]{2,1,0:T(8,128)(2,1)}, bf16[2,256,512]{2,1,0:T(8,128)(2,1)}, bf16[2,256,512]{2,1,0:T(8,128)(2,1)}, bf16[2,256,512]{2,1,0:T(8,128)(2,1)}) custom-call(bf16[2,320,1024]{2,1,0:T(8,128)(2,1)} %get-tuple-element.108.q_ref, bf16[2,256,1024]{2,1,0:T(8,128)(2,1)} %pad_maximum_fusion.pk_ref.pv_ref, ...), custom_call_target="tpu_custom_call" | custom-call | flops 26449999872 | tf_op jit(solution)/shard_map/pallas_call | solution.py:672
  355.7 1.9 fusion.20
  361.0 3.2 add_convert_fusion.3
  365.7 9.2 %collective-permute-done.31 = bf16[256,1024]{1,0:T(8,128)(2,1)S(1)} collective-permute-done((bf16[256,1024]{1,0:T(8,128)(2,1)S(1)}, bf16[256,1024]{1,0:T(8,128)(2,1)S(1)}, u32[]{:S(2)}, u32[]{:S(2)}) %collective-permute-start.31) | collective-permute-done | bytes 524320 | tf_op jit(solution)/shard_map/ppermute | solution.py:799
  377.7 2.4 collective-permute-done.38.refs_9_
  380.7 11.1 %shard_map.184 = (bf16[2,320,2048]{2,1,0:T(8,128)(2,1)}, bf16[1024,2048]{1,0:T(8,128)(2,1)}) custom-call(bf16[2,320,1024]{2,1,0:T(8,128)(2,1)} %get-tuple-element.188.refs_0_, bf16[2,320,1024]{2,1,0:T(8,128)(2,1)} %get-tuple-element.180.refs_1_, bf16[2,256,512]{2,1,0:T(8,128)(2,1)} %get-tuple-element.189.refs_2_, ...), custom_call_target="tpu_custom_call" | custom-call | flops 12650000384 | tf_op jit(solution)/shard_map/pallas_call | solution.py:739
  391.8 1.9 constant_dynamic-slice_fusion.1
  394.2 3.6 collective-permute-done.39
  402.5 4.5 add_convert_fusion.5
  407.1 18.3 %collective-permute-done.40 = bf16[256,2048]{1,0:T(8,128)(2,1)} collective-permute-done((bf16[256,2048]{1,0:T(8,128)(2,1)}, bf16[256,2048]{1,0:T(8,128)(2,1)}, u32[]{:S(2)}, u32[]{:S(2)}) %collective-permute-start.40) | collective-permute-done | bytes 1048608 | tf_op jit(solution)/shard_map/ppermute | solution.py:799
  428.8 8.4 %shard_map.185 = (bf16[2,320,1024]{2,1,0:T(8,128)(2,1)}, f32[1,1024]{1,0:T(1,128)}) custom-call(bf16[2,320,2048]{2,1,0:T(8,128)(2,1)} %get-tuple-element.195.gp_ref, bf16[1024,2048]{1,0:T(8,128)(2,1)} %w_ref.7, bf16[2,320,1024]{2,1,0:T(8,128)(2,1)} %bitcast.77, f32[1,1024]{1,0:T(1,128)} %bitcast.82, f32[2,320,1024]{2,1,0:T(8,128)} %get-tuple-element.196.hidden_ref), custom_call_target="tpu_custom_call" | custom-call | flops 9200000000 | tf_op jit(solution)/shard_map/pallas_call | solution.py:775
  440.0 10.1 %collective-permute-done.43 = f32[48,1024]{1,0:T(8,128)S(1)} collective-permute-done((f32[48,1024]{1,0:T(8,128)S(1)}, f32[48,1024]{1,0:T(8,128)S(1)}, u32[]{:S(2)}, u32[]{:S(2)}) %collective-permute-start.43) | collective-permute-done | bytes 196640 | tf_op jit(solution)/shard_map/ppermute | solution.py:1087
  452.4 3.5 collective-permute-done.44
  460.6 43.9 %all-reduce.2.cloned.1.call-done = bf16[144,3072]{1,0:T(8,128)(2,1)} async-done(((bf16[144,3072]{1,0:T(8,128)(2,1)}), bf16[144,3072]{1,0:T(8,128)(2,1)}) %all-reduce.2.cloned.1.call-update) | async-done | bytes 884752 | tf_op jit(solution)/shard_map/psum | solution.py:1095
  504.5 1.9 fusion.18
  511.7 6.8 %collective-permute-done.53.refs_10_ = bf16[128,1536]{1,0:T(8,128)(2,1)} collective-permute-done((bf16[128,1536]{1,0:T(8,128)(2,1)S(1)}, bf16[128,1536]{1,0:T(8,128)(2,1)}, u32[]{:S(2)}, u32[]{:S(2)}) %collective-permute-start.53) | collective-permute-done | bytes 393248 | tf_op jit(solution)/shard_map/ppermute | solution.py:1104
  521.3 7.1 %collective-permute-done.45.refs_1_ = bf16[128,1536]{1,0:T(8,128)(2,1)} collective-permute-done((bf16[128,1536]{1,0:T(8,128)(2,1)}, bf16[128,1536]{1,0:T(8,128)(2,1)}, u32[]{:S(2)}, u32[]{:S(2)}) %collective-permute-start.45) | collective-permute-done | bytes 393248 | tf_op jit(solution)/shard_map/ppermute | solution.py:1103
  530.6 5.5 collective-permute-done.54.refs_11_
  536.1 2.3 collective-permute-done.47.refs_3_
  541.3 9.0 %shard_map.186 = (f32[1024,2048]{1,0:T(8,128)}, f32[1024,1024]{1,0:T(8,128)}) custom-call(s32[8]{0:T(128)} %iota_xor_fusion.table_ref, bf16[128,1536]{1,0:T(8,128)(2,1)} %get-tuple-element.210.refs_0_, bf16[128,1536]{1,0:T(8,128)(2,1)} %collective-permute-done.45.refs_1_, bf16[128,1536]{1,0:T(8,128)(2,1)} %collective-permute-done.46.refs_2_, ...), custom_call_target="tpu_custom_call" | custom-call | flops 10350000128 | tf_op jit(solution)/shard_map/pallas_call | solution.py:829
  550.3 16.0 %reduce-scatter.17.cloned.1.call-done = bf16[2,192,1024]{2,1,0:T(8,128)(2,1)} async-done(((bf16[2,768,1024]{2,1,0:T(8,128)(2,1)}), bf16[2,192,1024]{2,1,0:T(8,128)(2,1)}) %reduce-scatter.17.cloned.1.call-update) | async-done | bytes 786448 | tf_op jit(solution)/shard_map/reduce_scatter | solution.py:939
  569.6 2.5 slice.133
  (289 shorter events, 82.9 us)
Async XLA Ops:
  7.2 207.6 %reduce-scatter.7.cloned.1.call-start = ((), (), s32[]{:S(2)}) async-start(), calls=%async_computation.6 | async-start | bytes 3932160 | tf_op jit(solution)/shard_map/reduce_scatter | solution.py:939
  8.0 22.3 %collective-permute-start.5 = (s32[2,8,320]{2,1,0:T(8,128)S(1)}, s32[2,8,320]{2,1,0:T(8,128)S(1)}, u32[]{:S(2)}, u32[]{:S(2)}) collective-permute-start(s32[2,8,320]{2,1,0:T(8,128)S(1)} %bitcast.67), channel_id=1, source_target_pairs={{2,0},{3,1},{0,2},{1,3},{6,4},{7,5},{4,6},{5,7},{10,8},{11,9},{8,1... | collective-permute-start | bytes 61448 | tf_op jit(solution)/shard_map/ppermute | solution.py:372
  11.1 28.0 %collective-permute-start.4 = (s32[2,8,320]{2,1,0:T(8,128)S(1)}, s32[2,8,320]{2,1,0:T(8,128)S(1)}, u32[]{:S(2)}, u32[]{:S(2)}) collective-permute-start(s32[2,8,320]{2,1,0:T(8,128)S(1)} %bitcast.68), channel_id=1, source_target_pairs={{0,1},{1,0},{2,3},{3,2},{4,5},{5,4},{6,7},{7,6},{8,9},{9,8},{10,11... | collective-permute-start | bytes 61448 | tf_op jit(solution)/shard_map/ppermute | solution.py:366
  12.5 56.1 %collective-permute-start.7 = (bf16[1,320,1024]{2,1,0:T(8,128)(2,1)S(1)}, bf16[1,320,1024]{2,1,0:T(8,128)(2,1)S(1)}, u32[]{:S(2)}, u32[]{:S(2)}) collective-permute-start(bf16[1,320,1024]{2,1,0:T(8,128)(2,1)S(1)} %get-tuple-element.208.refs_1_), channel_id=1, source_target_pairs={{0,1},{1,0},{2,3},{3,2},{4,5},{5,4},{6,7},{7,6},{8,9},{9,8},{10,11... | collective-permute-start | bytes 1966088 | tf_op jit(solution)/shard_map/ppermute | solution.py:366
  13.1 16.8 %collective-permute-start = (bf16[1,320,1024]{2,1,0:T(8,128)(2,1)S(1)}, bf16[1,320,1024]{2,1,0:T(8,128)(2,1)}, u32[]{:S(2)}, u32[]{:S(2)}) collective-permute-start(bf16[1,320,1024]{2,1,0:T(8,128)(2,1)S(1)} %get-tuple-element.208.refs_1_), channel_id=1, source_target_pairs={{2,0},{3,1},{0,2},{1,3},{6,4},{7,5},{4,6},{5,7},{10,8},{11,9},{8,1... | collective-permute-start | bytes 1966088 | tf_op jit(solution)/shard_map/ppermute | solution.py:372
  30.4 10.4 %collective-permute-start.1 = (bf16[2,64,1024]{2,1,0:T(8,128)(2,1)S(1)}, bf16[2,64,1024]{2,1,0:T(8,128)(2,1)S(1)}, u32[]{:S(2)}, u32[]{:S(2)}) collective-permute-start(bf16[2,64,1024]{2,1,0:T(8,128)(2,1)S(1)} %slice.93), channel_id=1, source_target_pairs={{0,1},{1,0},{2,3},{3,2},{4,5},{5,4},{6,7},{7,6},{8,9},{9,8},{10,11... | collective-permute-start | bytes 786440 | tf_op jit(solution)/shard_map/ppermute | solution.py:366
  39.8 29.5 %collective-permute-start.10 = (bf16[1,320,1024]{2,1,0:T(8,128)(2,1)}, bf16[1,320,1024]{2,1,0:T(8,128)(2,1)}, u32[]{:S(2)}, u32[]{:S(2)}) collective-permute-start(bf16[1,320,1024]{2,1,0:T(8,128)(2,1)} %collective-permute-done.refs_5_), channel_id=1, source_target_pairs={{0,1},{1,0},{2,3},{3,2},{4,5},{5,4},{6,7},{7,6},{8,9},{9,8},{10,11... | collective-permute-start | bytes 1966088 | tf_op jit(solution)/shard_map/ppermute | solution.py:366
  40.3 17.2 %collective-permute-start.9 = (bf16[1,320,1024]{2,1,0:T(8,128)(2,1)S(1)}, bf16[1,320,1024]{2,1,0:T(8,128)(2,1)}, u32[]{:S(2)}, u32[]{:S(2)}) collective-permute-start(bf16[1,320,1024]{2,1,0:T(8,128)(2,1)S(1)} %get-tuple-element.117.refs_2_), channel_id=1, source_target_pairs={{2,0},{3,1},{0,2},{1,3},{6,4},{7,5},{4,6},{5,7},{10,8},{11,9},{8,1... | collective-permute-start | bytes 1966088 | tf_op jit(solution)/shard_map/ppermute | solution.py:372
  40.8 28.5 %collective-permute-start.8 = (bf16[1,320,1024]{2,1,0:T(8,128)(2,1)S(1)}, bf16[1,320,1024]{2,1,0:T(8,128)(2,1)}, u32[]{:S(2)}, u32[]{:S(2)}) collective-permute-start(bf16[1,320,1024]{2,1,0:T(8,128)(2,1)S(1)} %get-tuple-element.117.refs_2_), channel_id=1, source_target_pairs={{0,1},{1,0},{2,3},{3,2},{4,5},{5,4},{6,7},{7,6},{8,9},{9,8},{10,11... | collective-permute-start | bytes 1966088 | tf_op jit(solution)/shard_map/ppermute | solution.py:366
  53.1 33.2 %collective-permute-start.14 = (bf16[1,320,1024]{2,1,0:T(8,128)(2,1)}, bf16[1,320,1024]{2,1,0:T(8,128)(2,1)}, u32[]{:S(2)}, u32[]{:S(2)}) collective-permute-start(bf16[1,320,1024]{2,1,0:T(8,128)(2,1)} %get-tuple-element.112.refs_3_), channel_id=1, source_target_pairs={{2,0},{3,1},{0,2},{1,3},{6,4},{7,5},{4,6},{5,7},{10,8},{11,9},{8,1... | collective-permute-start | bytes 1966088 | tf_op jit(solution)/shard_map/ppermute | solution.py:372
  57.4 12.0 %collective-permute-start.11 = (bf16[1,320,1024]{2,1,0:T(8,128)(2,1)}, bf16[1,320,1024]{2,1,0:T(8,128)(2,1)S(1)}, u32[]{:S(2)}, u32[]{:S(2)}) collective-permute-start(bf16[1,320,1024]{2,1,0:T(8,128)(2,1)} %collective-permute-done.9.refs_6_), channel_id=1, source_target_pairs={{0,1},{1,0},{2,3},{3,2},{4,5},{5,4},{6,7},{7,6},{8,9},{9,8},{10,11... | collective-permute-start | bytes 1966088 | tf_op jit(solution)/shard_map/ppermute | solution.py:366
  68.7 19.3 %collective-permute-start.12 = (bf16[1,320,1024]{2,1,0:T(8,128)(2,1)S(1)}, bf16[1,320,1024]{2,1,0:T(8,128)(2,1)S(1)}, u32[]{:S(2)}, u32[]{:S(2)}) collective-permute-start(bf16[1,320,1024]{2,1,0:T(8,128)(2,1)S(1)} %copy-done.30), channel_id=1, source_target_pairs={{0,1},{1,0},{2,3},{3,2},{4,5},{5,4},{6,7},{7,6},{8,9},{9,8},{10,11... | collective-permute-start | bytes 1966088 | tf_op jit(solution)/shard_map/ppermute | solution.py:366
  69.2 17.0 %collective-permute-start.15 = (bf16[1,320,1024]{2,1,0:T(8,128)(2,1)}, bf16[1,320,1024]{2,1,0:T(8,128)(2,1)}, u32[]{:S(2)}, u32[]{:S(2)}) collective-permute-start(bf16[1,320,1024]{2,1,0:T(8,128)(2,1)} %get-tuple-element.115.refs_4_), channel_id=1, source_target_pairs={{2,0},{3,1},{0,2},{1,3},{6,4},{7,5},{4,6},{5,7},{10,8},{11,9},{8,1... | collective-permute-start | bytes 1966088 | tf_op jit(solution)/shard_map/ppermute | solution.py:372
  69.3 18.7 %collective-permute-start.13 = (bf16[1,320,1024]{2,1,0:T(8,128)(2,1)}, bf16[1,320,1024]{2,1,0:T(8,128)(2,1)S(1)}, u32[]{:S(2)}, u32[]{:S(2)}) collective-permute-start(bf16[1,320,1024]{2,1,0:T(8,128)(2,1)} %get-tuple-element.115.refs_4_), channel_id=1, source_target_pairs={{0,1},{1,0},{2,3},{3,2},{4,5},{5,4},{6,7},{7,6},{8,9},{9,8},{10,11... | collective-permute-start | bytes 1966088 | tf_op jit(solution)/shard_map/ppermute | solution.py:366
  123.5 151.8 %reduce-scatter.9.cloned.1.call-start = ((), (), s32[]{:S(2)}) async-start(), calls=%async_computation.7 | async-start | bytes 1966080 | tf_op jit(solution)/shard_map/reduce_scatter | solution.py:939
  144.2 37.5 %collective-permute-start.18 = (bf16[1,4,192,1024]{3,2,1,0:T(8,128)(2,1)}, bf16[1,4,192,1024]{3,2,1,0:T(8,128)(2,1)S(1)}, u32[]{:S(2)}, u32[]{:S(2)}) collective-permute-start(bf16[1,4,192,1024]{3,2,1,0:T(8,128)(2,1)} %get-tuple-element.134), channel_id=1, source_target_pairs={{0,4},{4,0},{8,12},{12,8},{16,20},{20,16},{24,28},{28,24},{1,5},{5... | collective-permute-start | bytes 4718600 | tf_op jit(solution)/shard_map/ppermute | solution.py:983
  175.1 88.7 %collective-permute-start.23 = (bf16[2,4,192,1024]{3,2,1,0:T(8,128)(2,1)}, bf16[2,4,192,1024]{3,2,1,0:T(8,128)(2,1)}, u32[]{:S(2)}, u32[]{:S(2)}) collective-permute-start(bf16[2,4,192,1024]{3,2,1,0:T(8,128)(2,1)} %get-tuple-element.157), channel_id=1, source_target_pairs={{0,4},{4,0},{8,12},{12,8},{16,20},{20,16},{24,28},{28,24},{1,5},{5... | collective-permute-start | bytes 9437192 | tf_op jit(solution)/shard_map/ppermute | solution.py:983
  183.5 108.5 %reduce-scatter.11.cloned.1.call-start = ((), (), s32[]{:S(2)}) async-start(), calls=%async_computation.8 | async-start | bytes 3932160 | tf_op jit(solution)/shard_map/reduce_scatter | solution.py:939
  213.3 111.2 %collective-permute-start.27 = (bf16[2,4,192,1024]{3,2,1,0:T(8,128)(2,1)}, bf16[2,4,192,1024]{3,2,1,0:T(8,128)(2,1)}, u32[]{:S(2)}, u32[]{:S(2)}) collective-permute-start(bf16[2,4,192,1024]{3,2,1,0:T(8,128)(2,1)} %get-tuple-element.174), channel_id=1, source_target_pairs={{0,4},{4,0},{8,12},{12,8},{16,20},{20,16},{24,28},{28,24},{1,5},{5... | collective-permute-start | bytes 9437192 | tf_op jit(solution)/shard_map/ppermute | solution.py:983
  231.7 206.3 %reduce-scatter.15.cloned.1.call-start = ((), (), s32[]{:S(2)}) async-start(), calls=%async_computation.10 | async-start | bytes 3932160 | tf_op jit(solution)/shard_map/reduce_scatter | solution.py:939
  263.8 9.7 %collective-permute-start.22 = (bf16[2,320,1024]{2,1,0:T(8,128)(2,1)}, bf16[2,320,1024]{2,1,0:T(8,128)(2,1)S(1)}, u32[]{:S(2)}, u32[]{:S(2)}) collective-permute-start(bf16[2,320,1024]{2,1,0:T(8,128)(2,1)} %get-tuple-element.155), channel_id=1, source_target_pairs={{0,1},{1,0},{2,3},{3,2},{4,5},{5,4},{6,7},{7,6},{8,9},{9,8},{10,11... | collective-permute-start | bytes 3932168 | tf_op jit(solution)/shard_map/ppermute | solution.py:366
  272.3 19.8 %collective-permute-start.24 = (bf16[2,320,1024]{2,1,0:T(8,128)(2,1)}, bf16[2,320,1024]{2,1,0:T(8,128)(2,1)S(1)}, u32[]{:S(2)}, u32[]{:S(2)}) collective-permute-start(bf16[2,320,1024]{2,1,0:T(8,128)(2,1)} %get-tuple-element.165), channel_id=1, source_target_pairs={{0,1},{1,0},{2,3},{3,2},{4,5},{5,4},{6,7},{7,6},{8,9},{9,8},{10,11... | collective-permute-start | bytes 3932168 | tf_op jit(solution)/shard_map/ppermute | solution.py:366
  274.1 30.9 %collective-permute-start.25 = (bf16[2,320,1024]{2,1,0:T(8,128)(2,1)S(1)}, bf16[2,320,1024]{2,1,0:T(8,128)(2,1)}, u32[]{:S(2)}, u32[]{:S(2)}) collective-permute-start(bf16[2,320,1024]{2,1,0:T(8,128)(2,1)S(1)} %add_convert_fusion.7), channel_id=1, source_target_pairs={{0,2},{1,3},{2,0},{3,1},{4,6},{5,7},{6,4},{7,5},{8,10},{9,11},{10,... | collective-permute-start | bytes 3932168 | tf_op jit(solution)/shard_map/ppermute | solution.py:378
  288.7 31.4 %collective-permute-start.29 = (bf16[2,320,1024]{2,1,0:T(8,128)(2,1)}, bf16[2,320,1024]{2,1,0:T(8,128)(2,1)}, u32[]{:S(2)}, u32[]{:S(2)}) collective-permute-start(bf16[2,320,1024]{2,1,0:T(8,128)(2,1)} %get-tuple-element.169), channel_id=1, source_target_pairs={{0,1},{1,0},{2,3},{3,2},{4,5},{5,4},{6,7},{7,6},{8,9},{9,8},{10,11... | collective-permute-start | bytes 3932168 | tf_op jit(solution)/shard_map/ppermute | solution.py:366
  319.0 10.7 %collective-permute-start.26 = (bf16[512,1024]{1,0:T(8,128)(2,1)}, bf16[512,1024]{1,0:T(8,128)(2,1)}, u32[]{:S(2)}, u32[]{:S(2)}) collective-permute-start(bf16[512,1024]{1,0:T(8,128)(2,1)} %constant_dynamic-slice_fusion.3), channel_id=1, source_target_pairs={{0,1},{1,0},{2,3},{3,2},{4,5},{5,4},{6,7},{7,6},{8,9},{9,8},{10,11... | collective-permute-start | bytes 3145736 | tf_op jit(solution)/shard_map/ppermute | solution.py:799
  319.6 40.4 %collective-permute-start.32 = (bf16[1,4,192,1024]{3,2,1,0:T(8,128)(2,1)}, bf16[1,4,192,1024]{3,2,1,0:T(8,128)(2,1)}, u32[]{:S(2)}, u32[]{:S(2)}) collective-permute-start(bf16[1,4,192,1024]{3,2,1,0:T(8,128)(2,1)} %get-tuple-element.186), channel_id=1, source_target_pairs={{0,4},{4,0},{8,12},{12,8},{16,20},{20,16},{24,28},{28,24},{1,5},{5... | collective-permute-start | bytes 4718600 | tf_op jit(solution)/shard_map/ppermute | solution.py:983
  323.4 53.4 %collective-permute-start.30 = (bf16[2,320,1024]{2,1,0:T(8,128)(2,1)}, bf16[2,320,1024]{2,1,0:T(8,128)(2,1)}, u32[]{:S(2)}, u32[]{:S(2)}) collective-permute-start(bf16[2,320,1024]{2,1,0:T(8,128)(2,1)} %add_convert_fusion.6), channel_id=1, source_target_pairs={{0,2},{1,3},{2,0},{3,1},{4,6},{5,7},{6,4},{7,5},{8,10},{9,11},{10,... | collective-permute-start | bytes 3932168 | tf_op jit(solution)/shard_map/ppermute | solution.py:378
  329.7 122.7 %reduce-scatter.13.cloned.1.call-start = ((), (), s32[]{:S(2)}) async-start(), calls=%async_computation.9 | async-start | bytes 1966080 | tf_op jit(solution)/shard_map/reduce_scatter | solution.py:939
  357.6 19.1 %collective-permute-start.33 = (bf16[2,64,512]{2,1,0:T(8,128)(2,1)S(1)}, bf16[2,64,512]{2,1,0:T(8,128)(2,1)S(1)}, u32[]{:S(2)}, u32[]{:S(2)}) collective-permute-start(bf16[2,64,512]{2,1,0:T(8,128)(2,1)S(1)} %get-tuple-element.217), channel_id=1, source_target_pairs={{0,1},{1,0},{2,3},{3,2},{4,5},{5,4},{6,7},{7,6},{8,9},{9,8},{10,11... | collective-permute-start | bytes 393224 | tf_op jit(solution)/shard_map/ppermute | solution.py:366
  360.0 14.9 %collective-permute-start.31 = (bf16[256,1024]{1,0:T(8,128)(2,1)S(1)}, bf16[256,1024]{1,0:T(8,128)(2,1)S(1)}, u32[]{:S(2)}, u32[]{:S(2)}) collective-permute-start(bf16[256,1024]{1,0:T(8,128)(2,1)S(1)} %constant_dynamic-slice_fusion.2), channel_id=1, source_target_pairs={{0,2},{1,3},{2,0},{3,1},{4,6},{5,7},{6,4},{7,5},{8,10},{9,11},{10,... | collective-permute-start | bytes 1572872 | tf_op jit(solution)/shard_map/ppermute | solution.py:799
  364.2 12.6 %collective-permute-start.36 = (bf16[2,64,512]{2,1,0:T(8,128)(2,1)S(1)}, bf16[2,64,512]{2,1,0:T(8,128)(2,1)S(1)}, u32[]{:S(2)}, u32[]{:S(2)}) collective-permute-start(bf16[2,64,512]{2,1,0:T(8,128)(2,1)S(1)} %get-tuple-element.213), channel_id=1, source_target_pairs={{0,1},{1,0},{2,3},{3,2},{4,5},{5,4},{6,7},{7,6},{8,9},{9,8},{10,11... | collective-permute-start | bytes 393224 | tf_op jit(solution)/shard_map/ppermute | solution.py:366
  364.5 13.2 %collective-permute-start.35 = (bf16[2,64,512]{2,1,0:T(8,128)(2,1)S(1)}, bf16[2,64,512]{2,1,0:T(8,128)(2,1)S(1)}, u32[]{:S(2)}, u32[]{:S(2)}) collective-permute-start(bf16[2,64,512]{2,1,0:T(8,128)(2,1)S(1)} %add_convert_fusion.14), channel_id=1, source_target_pairs={{0,2},{1,3},{2,0},{3,1},{4,6},{5,7},{6,4},{7,5},{8,10},{9,11},{10,... | collective-permute-start | bytes 393224 | tf_op jit(solution)/shard_map/ppermute | solution.py:378
  399.9 25.5 %collective-permute-start.40 = (bf16[256,2048]{1,0:T(8,128)(2,1)}, bf16[256,2048]{1,0:T(8,128)(2,1)}, u32[]{:S(2)}, u32[]{:S(2)}) collective-permute-start(bf16[256,2048]{1,0:T(8,128)(2,1)} %constant_dynamic-slice_fusion), channel_id=1, source_target_pairs={{0,2},{1,3},{2,0},{3,1},{4,6},{5,7},{6,4},{7,5},{8,10},{9,11},{10,... | collective-permute-start | bytes 3145736 | tf_op jit(solution)/shard_map/ppermute | solution.py:799
  402.4 102.0 %all-reduce.2.cloned.1.call-start = ((), (), s32[]{:S(2)}) async-start(), calls=%async_computation.11 | async-start | bytes 1769472 | tf_op jit(solution)/shard_map/psum | solution.py:1095
  427.1 23.9 %collective-permute-start.41 = (bf16[128,3072]{1,0:T(8,128)(2,1)S(1)}, bf16[128,3072]{1,0:T(8,128)(2,1)}, u32[]{:S(2)}, u32[]{:S(2)}) collective-permute-start(bf16[128,3072]{1,0:T(8,128)(2,1)S(1)} %fusion.10), channel_id=1, source_target_pairs={{0,4},{4,0},{8,12},{12,8},{16,20},{20,16},{24,28},{28,24},{1,5},{5... | collective-permute-start | bytes 2359304 | tf_op jit(solution)/shard_map/ppermute | solution.py:799
  439.5 10.6 %collective-permute-start.43 = (f32[48,1024]{1,0:T(8,128)S(1)}, f32[48,1024]{1,0:T(8,128)S(1)}, u32[]{:S(2)}, u32[]{:S(2)}) collective-permute-start(f32[48,1024]{1,0:T(8,128)S(1)} %add.307), channel_id=1, source_target_pairs={{0,4},{4,0},{8,12},{12,8},{16,20},{20,16},{24,28},{28,24},{1,5},{5... | collective-permute-start | bytes 589832 | tf_op jit(solution)/shard_map/ppermute | solution.py:1087
  456.9 109.4 %reduce-scatter.17.cloned.1.call-start = ((), (), s32[]{:S(2)}) async-start(), calls=%async_computation.12 | async-start | bytes 3932160 | tf_op jit(solution)/shard_map/reduce_scatter | solution.py:939
  458.4 51.5 %collective-permute-start.59 = (bf16[2,192,1024]{2,1,0:T(8,128)(2,1)S(1)}, bf16[2,192,1024]{2,1,0:T(8,128)(2,1)S(1)}, u32[]{:S(2)}, u32[]{:S(2)}) collective-permute-start(bf16[2,192,1024]{2,1,0:T(8,128)(2,1)S(1)} %slice.130), channel_id=1, source_target_pairs={{0,4},{4,0},{8,12},{12,8},{16,20},{20,16},{24,28},{28,24},{1,5},{5... | collective-permute-start | bytes 2359304 | tf_op jit(solution)/shard_map/ppermute | solution.py:1064
  506.4 12.1 %collective-permute-start.53 = (bf16[128,1536]{1,0:T(8,128)(2,1)S(1)}, bf16[128,1536]{1,0:T(8,128)(2,1)}, u32[]{:S(2)}, u32[]{:S(2)}) collective-permute-start(bf16[128,1536]{1,0:T(8,128)(2,1)S(1)} %get-tuple-element.209.refs_8_), channel_id=1, source_target_pairs={{0,2},{1,3},{2,0},{3,1},{4,6},{5,7},{6,4},{7,5},{8,10},{9,11},{10,... | collective-permute-start | bytes 1179656 | tf_op jit(solution)/shard_map/ppermute | solution.py:1104
  507.9 12.0 %collective-permute-start.52 = (bf16[128,1536]{1,0:T(8,128)(2,1)S(1)}, bf16[128,1536]{1,0:T(8,128)(2,1)S(1)}, u32[]{:S(2)}, u32[]{:S(2)}) collective-permute-start(bf16[128,1536]{1,0:T(8,128)(2,1)S(1)} %get-tuple-element.209.refs_8_), channel_id=1, source_target_pairs={{0,4},{4,0},{8,12},{12,8},{16,20},{20,16},{24,28},{28,24},{1,5},{5... | collective-permute-start | bytes 1179656 | tf_op jit(solution)/shard_map/ppermute | solution.py:1108
  509.4 19.1 %collective-permute-start.45 = (bf16[128,1536]{1,0:T(8,128)(2,1)}, bf16[128,1536]{1,0:T(8,128)(2,1)}, u32[]{:S(2)}, u32[]{:S(2)}) collective-permute-start(bf16[128,1536]{1,0:T(8,128)(2,1)} %get-tuple-element.210.refs_0_), channel_id=1, source_target_pairs={{0,4},{4,0},{8,12},{12,8},{16,20},{20,16},{24,28},{28,24},{1,5},{5... | collective-permute-start | bytes 1179656 | tf_op jit(solution)/shard_map/ppermute | solution.py:1103
  511.1 18.8 %collective-permute-start.48 = (bf16[128,1536]{1,0:T(8,128)(2,1)}, bf16[128,1536]{1,0:T(8,128)(2,1)}, u32[]{:S(2)}, u32[]{:S(2)}) collective-permute-start(bf16[128,1536]{1,0:T(8,128)(2,1)} %get-tuple-element.210.refs_0_), channel_id=1, source_target_pairs={{0,1},{1,0},{2,3},{3,2},{4,5},{5,4},{6,7},{7,6},{8,9},{9,8},{10,11... | collective-permute-start | bytes 1179656 | tf_op jit(solution)/shard_map/ppermute | solution.py:366
  511.1 18.9 %collective-permute-start.46 = (bf16[128,1536]{1,0:T(8,128)(2,1)}, bf16[128,1536]{1,0:T(8,128)(2,1)}, u32[]{:S(2)}, u32[]{:S(2)}) collective-permute-start(bf16[128,1536]{1,0:T(8,128)(2,1)} %get-tuple-element.210.refs_0_), channel_id=1, source_target_pairs={{0,2},{1,3},{2,0},{3,1},{4,6},{5,7},{6,4},{7,5},{8,10},{9,11},{10,... | collective-permute-start | bytes 1179656 | tf_op jit(solution)/shard_map/ppermute | solution.py:1106
  518.5 12.0 %collective-permute-start.57 = (bf16[128,1536]{1,0:T(8,128)(2,1)}, bf16[128,1536]{1,0:T(8,128)(2,1)}, u32[]{:S(2)}, u32[]{:S(2)}) collective-permute-start(bf16[128,1536]{1,0:T(8,128)(2,1)} %collective-permute-done.53.refs_10_), channel_id=1, source_target_pairs={{0,1},{1,0},{2,3},{3,2},{4,5},{5,4},{6,7},{7,6},{8,9},{9,8},{10,11... | collective-permute-start | bytes 1179656 | tf_op jit(solution)/shard_map/ppermute | solution.py:366
  519.9 16.2 %collective-permute-start.54 = (bf16[128,1536]{1,0:T(8,128)(2,1)}, bf16[128,1536]{1,0:T(8,128)(2,1)}, u32[]{:S(2)}, u32[]{:S(2)}) collective-permute-start(bf16[128,1536]{1,0:T(8,128)(2,1)} %collective-permute-done.53.refs_10_), channel_id=1, source_target_pairs={{0,4},{4,0},{8,12},{12,8},{16,20},{20,16},{24,28},{28,24},{1,5},{5... | collective-permute-start | bytes 1179656 | tf_op jit(solution)/shard_map/ppermute | solution.py:1108
  528.4 10.0 %collective-permute-start.47 = (bf16[128,1536]{1,0:T(8,128)(2,1)}, bf16[128,1536]{1,0:T(8,128)(2,1)}, u32[]{:S(2)}, u32[]{:S(2)}) collective-permute-start(bf16[128,1536]{1,0:T(8,128)(2,1)} %collective-permute-done.45.refs_1_), channel_id=1, source_target_pairs={{0,2},{1,3},{2,0},{3,1},{4,6},{5,7},{6,4},{7,5},{8,10},{9,11},{10,... | collective-permute-start | bytes 1179656 | tf_op jit(solution)/shard_map/ppermute | solution.py:1106
  529.9 9.7 %collective-permute-start.49 = (bf16[128,1536]{1,0:T(8,128)(2,1)}, bf16[128,1536]{1,0:T(8,128)(2,1)S(1)}, u32[]{:S(2)}, u32[]{:S(2)}) collective-permute-start(bf16[128,1536]{1,0:T(8,128)(2,1)} %collective-permute-done.45.refs_1_), channel_id=1, source_target_pairs={{0,1},{1,0},{2,3},{3,2},{4,5},{5,4},{6,7},{7,6},{8,9},{9,8},{10,11... | collective-permute-start | bytes 1179656 | tf_op jit(solution)/shard_map/ppermute | solution.py:366
  530.0 9.6 %collective-permute-start.56 = (bf16[128,1536]{1,0:T(8,128)(2,1)}, bf16[128,1536]{1,0:T(8,128)(2,1)S(1)}, u32[]{:S(2)}, u32[]{:S(2)}) collective-permute-start(bf16[128,1536]{1,0:T(8,128)(2,1)} %copy-done.37), channel_id=1, source_target_pairs={{0,1},{1,0},{2,3},{3,2},{4,5},{5,4},{6,7},{7,6},{8,9},{9,8},{10,11... | collective-permute-start | bytes 1179656 | tf_op jit(solution)/shard_map/ppermute | solution.py:366
  (66 other events, 483.4 us)
Sparse Core Ops, SparseCore 0:
  123.6 61.2 reduce-scatter.6
  187.2 35.3 reduce-scatter.8
  231.8 60.2 reduce-scatter.10
  329.8 60.9 reduce-scatter.14
  402.6 36.3 reduce-scatter.12
  457.0 47.4 all-reduce.1
  506.8 59.4 reduce-scatter.16

commit v5 on v4

--- a/solution.py
+++ b/solution.py
@@ -792,11 +792,11 @@
     )(gp, w_qkv, tokens, gain, grad_hidden)
 
 
-def halve(value, axis, swap, bit):
+def halve(value, axis, swap, bit, *before):
     rows = value.shape[0] // 2
     keep = lax.dynamic_slice_in_dim(value, bit * rows, rows, 0)
     send = lax.dynamic_slice_in_dim(value, (1 - bit) * rows, rows, 0)
-    got = lax.ppermute(send, axis, swap)
+    got = after(lax.ppermute(send, axis, swap), *before)
     return (keep.astype(f32) + got.astype(f32)).astype(bf16)
 
 
@@ -1034,6 +1034,9 @@
         sine,
     )
 
+    for i in list(held):
+        parts[i] = sum_z(after(held.pop(i), gq))
+
     def prompt_terms(value):
         return return_members(
             [value[:, j * PROMPT_DEV : (j + 1) * PROMPT_DEV] for j in range(groups)], groups
@@ -1041,23 +1044,24 @@
 
     mixture = sum(after(term, gq).astype(f32) for term in mix_terms)
     output = (hidden + branch_scale * mixture).astype(bf16)
-    grad_out = halve(grad_out, "expert", swap_y, row_bit)
+    k_terms, v_terms = prompt_terms(gpk), prompt_terms(gpv)
+    grad_out = halve(after(grad_out, k_terms[2], v_terms[2]), "expert", swap_y, row_bit)
     gp, grad_qkv = weight_back(
-        after(normed, grad_out, *mix_terms[2:], *left(5, gq)),
+        after(normed, *mix_terms[2:], *left(5, gq, hold=True)),
         gq,
         gok,
         gov,
-        prompt_terms(gpk),
-        prompt_terms(gpv),
+        k_terms,
+        v_terms,
         cosine,
         sine,
     )
     grad_tokens, grad_norm_attn = token_back(
         after(gp, grad_qkv, output), w_qkv, token_rows, attn_gain, grad_hidden
     )
-    last = [add_x(i, grad_norm_attn) for i in list(halves)] + sent(2) + sent(3)
-    grad_qkv = halve(grad_qkv, "expert", swap_core, core_bit)
-    grad_qkv = halve(grad_qkv, "expert", swap_y, row_bit)
+    last = [add_x(i, grad_norm_attn) for i in list(halves)]
+    grad_qkv = after(halve(grad_qkv, "expert", swap_core, core_bit), grad_out)
+    grad_qkv = halve(grad_qkv, "expert", swap_y, row_bit, grad_norm_attn)
 
     whole_sums = [parts[i] for i, (_, whole) in enumerate(plan) if whole]
     whole_sums = jnp.concatenate(whole_sums, axis=0)
@@ -1086,7 +1090,7 @@
     for axis, swap in (("expert", swap_core), ("dp", swap_x), ("expert", swap_y)):
         small = small + lax.ppermute(small, axis, swap)
     dense = jnp.concatenate([grad_qkv, grad_out], axis=1)
-    dense = after(halve(dense, "dp", swap_x, parity), *sent(5))
+    dense = after(halve(dense, "dp", swap_x, parity), *sent(2), *sent(3))
     for i in list(held):
         parts[i] = sum_z(after(held.pop(i), dense))
         pieces[i] = parts[i]
@@ -1107,7 +1111,8 @@
     ]
     right_x = [lax.ppermute(value, "dp", swap_x) for value in (right_own, right_y)]
     right_four = [right_own, right_x[0], right_y, right_x[1]]
-    pieces[2] = after(pieces[2], left_four[3], right_four[3])
+    if 5 in parts:
+        pieces[5] = after(pieces[5], left_four[3], right_four[3])
     left_all = left_four + [core_swap(value, groups) for value in left_four]
     right_all = right_four + [core_swap(value, groups) for value in right_four]
     base = core_bit * 4 + row_bit * 2 + parity

time: 589 us -> 581 us (0.986)
  waiting for transfers between devices: 174 us -> 156 us
    reduce_scatter x6, waiting for transfers between devices: 19.4 us -> 1.6 us  [sum_z(): lax.psum_scatter(value.reshape(count, pairs * height, D), 'dp', scatter_d...]
    ppermute x5, waiting for transfers between devices: 31.1 us -> 19.3 us  [halve(): got = after(lax.ppermute(send, axis, swap), *before)]
    ppermute x1, waiting for transfers between devices: 0.01 us -> 10.6 us  [local(): swapped = lax.ppermute(after(whole_sums[:, piece:], *last), 'dp', swap_x)]
    psum x1, waiting for transfers between devices: 43.9 us -> 33.7 us  [local(): dense = lax.psum(dense, 'dp', axis_index_groups=z_groups)]
    unnamed x102 -> x90, local copies, waits for them, and re-layouts: 11.8 us -> 11.1 us
  transfers between devices with their start and end apart: 67 -> 67, of which waited for: 24 -> 24; matrix products, arithmetic and copies ran while one was open for 11% -> 13% of each run, Pallas kernels for 42% -> 42%
where the time goes in v5:
time: 581 us; the launch traced here: 571 us
  Pallas kernels  276 us (48%)
  waiting for transfers between devices  156 us (27%)
  other arithmetic  46.4 us (8%)
  starting transfers between devices  37.2 us (6%)
  local copies, waits for them, and re-layouts  34.7 us (6%)
  between operations  15.4 us (3%)
    pallas_call x6, Pallas kernels, expert_chunk(): pl.pallas_call(functools.partial(expert_body, tile=tile), grid_spec=grid_...  127 us
    psum x1, waiting for transfers between devices, local(): dense = lax.psum(dense, 'dp', axis_index_groups=z_groups)  33.7 us
    pallas_call x2, Pallas kernels, sum_rows(): pl.pallas_call(functools.partial(sum_rows_body, chunks=len(rows), with_do...  28 us
    pallas_call x1, Pallas kernels, attend_back(): pl.pallas_call(attend_back_body, grid=(micro, steps), in_specs=[wide, pro...  22.8 us
    pallas_call x2, Pallas kernels, attend(): pl.pallas_call(attend_body, grid=(steps,), in_specs=[pl.BlockSpec((1, row...  22.4 us
    ppermute x3, waiting for transfers between devices, local(): small = small + lax.ppermute(small, axis, swap)  20.2 us
    ppermute x5, waiting for transfers between devices, halve(): got = after(lax.ppermute(send, axis, swap), *before)  19.3 us
    ppermute x4, waiting for transfers between devices, to_row(): return lax.ppermute(value, 'expert', pairs)  18.1 us
  transfers between devices with their start and end apart: 67, of which 24 were waited for; matrix products, arithmetic and copies ran while one was open for 13% of the time, Pallas kernels for 42%

profile of v5, /device:TPU:0, one launch (start us, length us, event | category | flops | bytes accessed | tf_op | source)
XLA Modules:
  0.0 571.1 jit_solution(4139188361652946935)
XLA Ops:
  8.0 3.1 collective-permute-start.5
  15.1 6.6 %shard_map.169 = (bf16[2,320,1024]{2,1,0:T(8,128)(2,1)}, bf16[2,320,1024]{2,1,0:T(8,128)(2,1)}, bf16[2,320,1024]{2,1,0:T(8,128)(2,1)}) custom-call(bf16[2,320,1024]{2,1,0:T(8,128)(2,1)} %bitcast.74, f32[1,1024]{1,0:T(1,128)} %bitcast.81, bf16[1024,2048]{1,0:T(8,128)(2,1)} %w_ref.7, f32[320,128]{1,0:T(8,128)} %copy.23.cos_ref.refs_10_, ...), custom_call_target="tpu_custom_call" | custom-call | flops 8049999872 | tf_op jit(solution)/shard_map/pallas_call | solution.py:468
  22.7 7.2 %collective-permute-done.refs_5_ = bf16[1,320,1024]{2,1,0:T(8,128)(2,1)} collective-permute-done((bf16[1,320,1024]{2,1,0:T(8,128)(2,1)S(1)}, bf16[1,320,1024]{2,1,0:T(8,128)(2,1)}, u32[]{:S(2)}, u32[]{:S(2)}) %collective-permute-start) | collective-permute-done | bytes 655392 | tf_op jit(solution)/shard_map/ppermute | solution.py:372
  30.9 6.4 %collective-permute-done.2 = bf16[2,64,1024]{2,1,0:T(8,128)(2,1)S(1)} collective-permute-done((bf16[2,64,1024]{2,1,0:T(8,128)(2,1)S(1)}, bf16[2,64,1024]{2,1,0:T(8,128)(2,1)S(1)}, u32[]{:S(2)}, u32[]{:S(2)}) %collective-permute-start.2) | collective-permute-done | bytes 262176 | tf_op jit(solution)/shard_map/ppermute | solution.py:372
  41.9 11.2 %shard_map.170 = (bf16[1,320,1024]{2,1,0:T(8,128)(2,1)}, f32[4,1,1280]{2,1,0:T(1,128)}, f32[1,320,1024]{2,1,0:T(8,128)}, bf16[1,320,1024]{2,1,0:T(8,128)(2,1)}) custom-call(bf16[2,320,1024]{2,1,0:T(8,128)(2,1)} %get-tuple-element.110.q_ref, bf16[2,256,1024]{2,1,0:T(8,128)(2,1)} %pad_maximum_fusion.pk_ref.pv_ref, ...), custom_call_target="tpu_custom_call" | custom-call | flops 13799999488 | tf_op jit(solution)/shard_map/pallas_call | solution.py:544
  54.7 2.8 collective-permute-done.9.refs_6_
  57.5 11.2 %shard_map.171 = (bf16[1,320,1024]{2,1,0:T(8,128)(2,1)}, f32[4,1,1280]{2,1,0:T(1,128)}, f32[1,320,1024]{2,1,0:T(8,128)}, bf16[1,320,1024]{2,1,0:T(8,128)(2,1)}) custom-call(bf16[2,320,1024]{2,1,0:T(8,128)(2,1)} %get-tuple-element.110.q_ref, bf16[2,256,1024]{2,1,0:T(8,128)(2,1)} %pad_maximum_fusion.pk_ref.pv_ref, ...), custom_call_target="tpu_custom_call" | custom-call | flops 13799999488 | tf_op jit(solution)/shard_map/pallas_call | solution.py:544
  70.4 15.1 %shard_map.172 = (bf16[8,8,112,1024]{3,2,1,0:T(8,128)(2,1)}, s32[8,8,320]{2,1,0:T(8,128)}) custom-call(s32[8,8,320]{2,1,0:T(8,128)} %negate_select_fusion.1.refs_0_, bf16[1,320,1024]{2,1,0:T(8,128)(2,1)} %copy-done.16, bf16[1,320,1024]{2,1,0:T(8,128)(2,1)} %copy-done.15, bf16[1,320,1024]{2,1,0:T(8,128)(2,1)} %copy-done.26, ...), custom_call_target="tpu_custom_call" | custom-call | flops 17250000896 | tf_op jit(solution)/shard_map/pallas_call | solution.py:112
  89.7 16.8 %shard_map.173 = (bf16[8,8,112,1024]{3,2,1,0:T(8,128)(2,1)}, f32[8,8,112,128]{3,2,1,0:T(8,128)}, f32[8,32,320]{2,1,0:T(8,128)}) custom-call(s32[8,8,320]{2,1,0:T(8,128)} %negate_select_fusion.1.refs_0_, s32[8,8,320]{2,1,0:T(8,128)} %get-tuple-element.162.refs_1_.refs_0_, bf16[1024,32]{1,0:T(8,128)(2,1)} %dynamic-slice_maximum_fusion.refs_2_.refs_4_, ...), custom_call_target="tpu_custom_call" | custom-call | flops 19549999104 | tf_op jit(solution)/shard_map/pallas_call | solution.py:158
  106.5 17.1 %shard_map.174 = (bf16[1,896,1024]{2,1,0:T(8,128)(2,1)}, bf16[1,896,1024]{2,1,0:T(8,128)(2,1)}, f32[1,896,128]{2,1,0:T(8,128)}, bf16[1,4,384,1024]{3,2,1,0:T(8,128)(2,1)}) custom-call(s32[1]{0:T(128)} %bitcast.8.parity_ref, bf16[8,896,1024]{2,1,0:T(8,128)(2,1)} %bitcast.89, bf16[8,896,1024]{2,1,0:T(8,128)(2,1)} %bitcast.83, f32[8,896,128]{2,1,0:T(8,128)} %bitcast.95, ...), custom_call_target="tpu_custom_call" | custom-call | flops 17250000896 | tf_op jit(solution)/shard_map/pallas_call | solution.py:351
  127.3 17.0 %shard_map.175 = (bf16[1,896,1024]{2,1,0:T(8,128)(2,1)}, bf16[1,896,1024]{2,1,0:T(8,128)(2,1)}, f32[1,896,128]{2,1,0:T(8,128)}, bf16[1,4,192,1024]{3,2,1,0:T(8,128)(2,1)}, bf16[1,4,192,1024]{3,2,1,0:T(8,128)(2,1)}) custom-call(s32[1]{0:T(128)} %bitcast.8.parity_ref, bf16[8,896,1024]{2,1,0:T(8,128)(2,1)} %bitcast.90, bf16[8,896,1024]{2,1,0:T(8,128)(2,1)} %bitcast.84, ...), custom_call_target="tpu_custom_call" | custom-call | flops 17250000896 | tf_op jit(solution)/shard_map/pallas_call | solution.py:351
  145.8 29.4 %shard_map.176 = (bf16[2,896,1024]{2,1,0:T(8,128)(2,1)}, bf16[2,896,1024]{2,1,0:T(8,128)(2,1)}, f32[2,896,128]{2,1,0:T(8,128)}, bf16[2,4,192,1024]{3,2,1,0:T(8,128)(2,1)}, bf16[2,4,192,1024]{3,2,1,0:T(8,128)(2,1)}) custom-call(s32[1]{0:T(128)} %bitcast.8.parity_ref, bf16[8,896,1024]{2,1,0:T(8,128)(2,1)} %bitcast.91, bf16[8,896,1024]{2,1,0:T(8,128)(2,1)} %bitcast.85, ...), custom_call_target="tpu_custom_call" | custom-call | flops 34500001792 | tf_op jit(solution)/shard_map/pallas_call | solution.py:351
  175.7 6.0 %collective-permute-done.18 = bf16[1,4,192,1024]{3,2,1,0:T(8,128)(2,1)S(1)} collective-permute-done((bf16[1,4,192,1024]{3,2,1,0:T(8,128)(2,1)}, bf16[1,4,192,1024]{3,2,1,0:T(8,128)(2,1)S(1)}, u32[]{:S(2)}, u32[]{:S(2)}) %collective-permute-start.18) | collective-permute-done | bytes 1572896 | tf_op jit(solution)/shard_map/ppermute | solution.py:983
  181.8 2.0 add_convert_fusion.4
  183.8 29.8 %shard_map.177 = (bf16[2,896,1024]{2,1,0:T(8,128)(2,1)}, bf16[2,896,1024]{2,1,0:T(8,128)(2,1)}, f32[2,896,128]{2,1,0:T(8,128)}, bf16[2,4,192,1024]{3,2,1,0:T(8,128)(2,1)}, bf16[2,4,192,1024]{3,2,1,0:T(8,128)(2,1)}) custom-call(s32[1]{0:T(128)} %bitcast.8.parity_ref, bf16[8,896,1024]{2,1,0:T(8,128)(2,1)} %bitcast.92, bf16[8,896,1024]{2,1,0:T(8,128)(2,1)} %bitcast.86, ...), custom_call_target="tpu_custom_call" | custom-call | flops 34500001792 | tf_op jit(solution)/shard_map/pallas_call | solution.py:351
  215.1 17.0 %shard_map.178 = (bf16[1,896,1024]{2,1,0:T(8,128)(2,1)}, bf16[1,896,1024]{2,1,0:T(8,128)(2,1)}, f32[1,896,128]{2,1,0:T(8,128)}, bf16[1,4,384,1024]{3,2,1,0:T(8,128)(2,1)}) custom-call(s32[1]{0:T(128)} %bitcast.8.parity_ref, bf16[8,896,1024]{2,1,0:T(8,128)(2,1)} %bitcast.93, bf16[8,896,1024]{2,1,0:T(8,128)(2,1)} %bitcast.87, f32[8,896,128]{2,1,0:T(8,128)} %bitcast.99, ...), custom_call_target="tpu_custom_call" | custom-call | flops 17250000896 | tf_op jit(solution)/shard_map/pallas_call | solution.py:351
  232.1 17.2 %shard_map.179 = (bf16[1,896,1024]{2,1,0:T(8,128)(2,1)}, bf16[1,896,1024]{2,1,0:T(8,128)(2,1)}, f32[1,896,128]{2,1,0:T(8,128)}, bf16[1,4,192,1024]{3,2,1,0:T(8,128)(2,1)}, bf16[1,4,192,1024]{3,2,1,0:T(8,128)(2,1)}) custom-call(s32[1]{0:T(128)} %bitcast.8.parity_ref, bf16[8,896,1024]{2,1,0:T(8,128)(2,1)} %bitcast.94, bf16[8,896,1024]{2,1,0:T(8,128)(2,1)} %bitcast.88, ...), custom_call_target="tpu_custom_call" | custom-call | flops 17250000896 | tf_op jit(solution)/shard_map/pallas_call | solution.py:351
  249.3 14.6 %shard_map.180 = (bf16[2,320,1024]{2,1,0:T(8,128)(2,1)}, bf16[2,320,1024]{2,1,0:T(8,128)(2,1)}, bf16[2,320,1024]{2,1,0:T(8,128)(2,1)}, bf16[2,320,1024]{2,1,0:T(8,128)(2,1)}, f32[8,8,320]{2,1,0:T(8,128)}) custom-call(s32[8,8,320]{2,1,0:T(8,128)} %get-tuple-element.162.refs_1_.refs_0_, bf16[1,8,112,1024]{3,2,1,0:T(8,128)(2,1)} %bitcast.106, ...), custom_call_target="tpu_custom_call" | custom-call | flops 17250000896 | tf_op jit(solution)/shard_map/pallas_call | solution.py:242
  267.0 6.4 %add_convert_fusion.1 = bf16[2,4,192,1024]{3,2,1,0:T(8,128)(2,1)} fusion(bf16[2,4,192,1024]{3,2,1,0:T(8,128)(2,1)} %collective-permute-done.23, bf16[2,4,192,1024]{3,2,1,0:T(8,128)(2,1)} %get-tuple-element.158), kind=kLoop, calls=%fused_computation.1 | loop fusion | flops 6291456 | bytes 9437184 | tf_op jit(solution)/shard_map/convert_element_type | solution.py:957
  277.4 13.4 %shard_map.181 = (bf16[2,320,1024]{2,1,0:T(8,128)(2,1)}, bf16[2,320,1024]{2,1,0:T(8,128)(2,1)}, bf16[2,320,1024]{2,1,0:T(8,128)(2,1)}, bf16[2,320,1024]{2,1,0:T(8,128)(2,1)}) custom-call(s32[8,8,320]{2,1,0:T(8,128)} %get-tuple-element.162.refs_1_.refs_0_, bf16[1,8,112,1024]{3,2,1,0:T(8,128)(2,1)} %bitcast.105, bf16[1,8,112,1024]{3,2,1,0:T(8,128)(2,1)} %bitcast.107, ...), custom_call_target="tpu_custom_call" | custom-call | flops 17250000896 | tf_op jit(solution)/shard_map/pallas_call | solution.py:242
  292.4 14.8 %collective-permute-done.25.refs_2_ = bf16[2,320,1024]{2,1,0:T(8,128)(2,1)} collective-permute-done((bf16[2,320,1024]{2,1,0:T(8,128)(2,1)}, bf16[2,320,1024]{2,1,0:T(8,128)(2,1)}, u32[]{:S(2)}, u32[]{:S(2)}) %collective-permute-start.25) | collective-permute-done | bytes 1310752 | tf_op jit(solution)/shard_map/ppermute | solution.py:378
  307.2 8.3 %shard_map.182 = (f32[2,320,1024]{2,1,0:T(8,128)}, bf16[2,320,1024]{2,1,0:T(8,128)(2,1)}, bf16[2,320,1024]{2,1,0:T(8,128)(2,1)}, f32[1,1024]{1,0:T(1,128)}) custom-call(bf16[2,320,1024]{2,1,0:T(8,128)(2,1)} %get-tuple-element.160.refs_0_, bf16[2,320,1024]{2,1,0:T(8,128)(2,1)} %collective-permute-done.24.refs_1_, ...), custom_call_target="tpu_custom_call" | custom-call | flops 9200000000 | tf_op jit(solution)/shard_map/pallas_call | solution.py:611
  315.7 3.7 bitcast_convert_fusion
  321.8 3.2 add_convert_fusion
  327.9 3.3 add_convert_fusion.6
  334.3 22.8 %shard_map.183 = (bf16[2,320,1024]{2,1,0:T(8,128)(2,1)}, bf16[2,256,512]{2,1,0:T(8,128)(2,1)}, bf16[2,256,512]{2,1,0:T(8,128)(2,1)}, bf16[2,256,512]{2,1,0:T(8,128)(2,1)}, bf16[2,256,512]{2,1,0:T(8,128)(2,1)}) custom-call(bf16[2,320,1024]{2,1,0:T(8,128)(2,1)} %get-tuple-element.110.q_ref, bf16[2,256,1024]{2,1,0:T(8,128)(2,1)} %pad_maximum_fusion.pk_ref.pv_ref, ...), custom_call_target="tpu_custom_call" | custom-call | flops 26449999872 | tf_op jit(solution)/shard_map/pallas_call | solution.py:672
  361.4 2.1 collective-permute-done.31
  365.8 3.2 add_convert_fusion.3
  370.0 2.3 collective-permute-done.37.refs_9_
  373.0 11.1 %shard_map.184 = (bf16[2,320,2048]{2,1,0:T(8,128)(2,1)}, bf16[1024,2048]{1,0:T(8,128)(2,1)}) custom-call(bf16[2,320,1024]{2,1,0:T(8,128)(2,1)} %get-tuple-element.190.refs_0_, bf16[2,320,1024]{2,1,0:T(8,128)(2,1)} %get-tuple-element.182.refs_1_, bf16[2,256,512]{2,1,0:T(8,128)(2,1)} %get-tuple-element.191.refs_2_, ...), custom_call_target="tpu_custom_call" | custom-call | flops 12650000384 | tf_op jit(solution)/shard_map/pallas_call | solution.py:739
  389.9 2.2 collective-permute-done.28
  392.1 4.7 add_convert_fusion.5
  396.8 5.5 collective-permute-done.39
  402.6 2.6 add_convert_fusion.2
  406.7 8.4 %shard_map.185 = (bf16[2,320,1024]{2,1,0:T(8,128)(2,1)}, f32[1,1024]{1,0:T(1,128)}) custom-call(bf16[2,320,2048]{2,1,0:T(8,128)(2,1)} %get-tuple-element.197.gp_ref, bf16[1024,2048]{1,0:T(8,128)(2,1)} %w_ref.7, bf16[2,320,1024]{2,1,0:T(8,128)(2,1)} %bitcast.77, f32[1,1024]{1,0:T(1,128)} %bitcast.82, f32[2,320,1024]{2,1,0:T(8,128)} %get-tuple-element.198.hidden_ref), custom_call_target="tpu_custom_call" | custom-call | flops 9200000000 | tf_op jit(solution)/shard_map/pallas_call | solution.py:775
  416.0 13.8 %collective-permute-done.40 = bf16[256,2048]{1,0:T(8,128)(2,1)} collective-permute-done((bf16[256,2048]{1,0:T(8,128)(2,1)S(1)}, bf16[256,2048]{1,0:T(8,128)(2,1)}, u32[]{:S(2)}, u32[]{:S(2)}) %collective-permute-start.40) | collective-permute-done | bytes 1048608 | tf_op jit(solution)/shard_map/ppermute | solution.py:799
  434.5 20.1 %collective-permute-done.43 = f32[48,1024]{1,0:T(8,128)S(1)} collective-permute-done((f32[48,1024]{1,0:T(8,128)S(1)}, f32[48,1024]{1,0:T(8,128)S(1)}, u32[]{:S(2)}, u32[]{:S(2)}) %collective-permute-start.43) | collective-permute-done | bytes 196640 | tf_op jit(solution)/shard_map/ppermute | solution.py:1091
  461.1 2.2 add_convert_fusion.11
  463.3 2.1 pad_maximum_fusion.1
  466.0 10.6 %collective-permute-done.59 = bf16[2,192,1024]{2,1,0:T(8,128)(2,1)} collective-permute-done((bf16[2,192,1024]{2,1,0:T(8,128)(2,1)}, bf16[2,192,1024]{2,1,0:T(8,128)(2,1)}, u32[]{:S(2)}, u32[]{:S(2)}) %collective-permute-start.59) | collective-permute-done | bytes 786464 | tf_op jit(solution)/shard_map/ppermute | solution.py:1068
  479.1 33.7 %all-reduce.2.cloned.1.call-done = bf16[144,3072]{1,0:T(8,128)(2,1)} async-done(((bf16[144,3072]{1,0:T(8,128)(2,1)}), bf16[144,3072]{1,0:T(8,128)(2,1)}) %all-reduce.2.cloned.1.call-update) | async-done | bytes 884752 | tf_op jit(solution)/shard_map/psum | solution.py:1099
  512.8 2.0 fusion.18
  520.4 6.6 %collective-permute-done.53.refs_10_ = bf16[128,1536]{1,0:T(8,128)(2,1)} collective-permute-done((bf16[128,1536]{1,0:T(8,128)(2,1)S(1)}, bf16[128,1536]{1,0:T(8,128)(2,1)}, u32[]{:S(2)}, u32[]{:S(2)}) %collective-permute-start.53) | collective-permute-done | bytes 393248 | tf_op jit(solution)/shard_map/ppermute | solution.py:1108
  529.8 7.1 %collective-permute-done.45.refs_1_ = bf16[128,1536]{1,0:T(8,128)(2,1)} collective-permute-done((bf16[128,1536]{1,0:T(8,128)(2,1)}, bf16[128,1536]{1,0:T(8,128)(2,1)}, u32[]{:S(2)}, u32[]{:S(2)}) %collective-permute-start.45) | collective-permute-done | bytes 393248 | tf_op jit(solution)/shard_map/ppermute | solution.py:1107
  539.1 5.5 collective-permute-done.54.refs_11_
  544.5 2.3 collective-permute-done.47.refs_3_
  549.8 9.0 %shard_map.186 = (f32[1024,2048]{1,0:T(8,128)}, f32[1024,1024]{1,0:T(8,128)}) custom-call(s32[8]{0:T(128)} %iota_xor_fusion.table_ref, bf16[128,1536]{1,0:T(8,128)(2,1)} %get-tuple-element.214.refs_0_, bf16[128,1536]{1,0:T(8,128)(2,1)} %collective-permute-done.45.refs_1_, bf16[128,1536]{1,0:T(8,128)(2,1)} %collective-permute-done.46.refs_2_, ...), custom_call_target="tpu_custom_call" | custom-call | flops 10350000128 | tf_op jit(solution)/shard_map/pallas_call | solution.py:829
  561.3 2.5 slice.133
  (277 shorter events, 89.5 us)
Async XLA Ops:
  7.2 207.9 %reduce-scatter.7.cloned.1.call-start = ((), (), s32[]{:S(2)}) async-start(), calls=%async_computation.6 | async-start | bytes 3932160 | tf_op jit(solution)/shard_map/reduce_scatter | solution.py:939
  8.0 22.3 %collective-permute-start.5 = (s32[2,8,320]{2,1,0:T(8,128)S(1)}, s32[2,8,320]{2,1,0:T(8,128)S(1)}, u32[]{:S(2)}, u32[]{:S(2)}) collective-permute-start(s32[2,8,320]{2,1,0:T(8,128)S(1)} %bitcast.67), channel_id=1, source_target_pairs={{2,0},{3,1},{0,2},{1,3},{6,4},{7,5},{4,6},{5,7},{10,8},{11,9},{8,1... | collective-permute-start | bytes 61448 | tf_op jit(solution)/shard_map/ppermute | solution.py:372
  11.1 28.0 %collective-permute-start.4 = (s32[2,8,320]{2,1,0:T(8,128)S(1)}, s32[2,8,320]{2,1,0:T(8,128)S(1)}, u32[]{:S(2)}, u32[]{:S(2)}) collective-permute-start(s32[2,8,320]{2,1,0:T(8,128)S(1)} %bitcast.68), channel_id=1, source_target_pairs={{0,1},{1,0},{2,3},{3,2},{4,5},{5,4},{6,7},{7,6},{8,9},{9,8},{10,11... | collective-permute-start | bytes 61448 | tf_op jit(solution)/shard_map/ppermute | solution.py:366
  12.5 56.2 %collective-permute-start.7 = (bf16[1,320,1024]{2,1,0:T(8,128)(2,1)S(1)}, bf16[1,320,1024]{2,1,0:T(8,128)(2,1)S(1)}, u32[]{:S(2)}, u32[]{:S(2)}) collective-permute-start(bf16[1,320,1024]{2,1,0:T(8,128)(2,1)S(1)} %get-tuple-element.212.refs_1_), channel_id=1, source_target_pairs={{0,1},{1,0},{2,3},{3,2},{4,5},{5,4},{6,7},{7,6},{8,9},{9,8},{10,11... | collective-permute-start | bytes 1966088 | tf_op jit(solution)/shard_map/ppermute | solution.py:366
  13.1 16.8 %collective-permute-start = (bf16[1,320,1024]{2,1,0:T(8,128)(2,1)S(1)}, bf16[1,320,1024]{2,1,0:T(8,128)(2,1)}, u32[]{:S(2)}, u32[]{:S(2)}) collective-permute-start(bf16[1,320,1024]{2,1,0:T(8,128)(2,1)S(1)} %get-tuple-element.212.refs_1_), channel_id=1, source_target_pairs={{2,0},{3,1},{0,2},{1,3},{6,4},{7,5},{4,6},{5,7},{10,8},{11,9},{8,1... | collective-permute-start | bytes 1966088 | tf_op jit(solution)/shard_map/ppermute | solution.py:372
  30.4 10.4 %collective-permute-start.1 = (bf16[2,64,1024]{2,1,0:T(8,128)(2,1)S(1)}, bf16[2,64,1024]{2,1,0:T(8,128)(2,1)S(1)}, u32[]{:S(2)}, u32[]{:S(2)}) collective-permute-start(bf16[2,64,1024]{2,1,0:T(8,128)(2,1)S(1)} %slice.93), channel_id=1, source_target_pairs={{0,1},{1,0},{2,3},{3,2},{4,5},{5,4},{6,7},{7,6},{8,9},{9,8},{10,11... | collective-permute-start | bytes 786440 | tf_op jit(solution)/shard_map/ppermute | solution.py:366
  39.8 29.5 %collective-permute-start.10 = (bf16[1,320,1024]{2,1,0:T(8,128)(2,1)}, bf16[1,320,1024]{2,1,0:T(8,128)(2,1)}, u32[]{:S(2)}, u32[]{:S(2)}) collective-permute-start(bf16[1,320,1024]{2,1,0:T(8,128)(2,1)} %collective-permute-done.refs_5_), channel_id=1, source_target_pairs={{0,1},{1,0},{2,3},{3,2},{4,5},{5,4},{6,7},{7,6},{8,9},{9,8},{10,11... | collective-permute-start | bytes 1966088 | tf_op jit(solution)/shard_map/ppermute | solution.py:366
  40.3 17.2 %collective-permute-start.9 = (bf16[1,320,1024]{2,1,0:T(8,128)(2,1)S(1)}, bf16[1,320,1024]{2,1,0:T(8,128)(2,1)}, u32[]{:S(2)}, u32[]{:S(2)}) collective-permute-start(bf16[1,320,1024]{2,1,0:T(8,128)(2,1)S(1)} %get-tuple-element.119.refs_2_), channel_id=1, source_target_pairs={{2,0},{3,1},{0,2},{1,3},{6,4},{7,5},{4,6},{5,7},{10,8},{11,9},{8,1... | collective-permute-start | bytes 1966088 | tf_op jit(solution)/shard_map/ppermute | solution.py:372
  40.8 28.6 %collective-permute-start.8 = (bf16[1,320,1024]{2,1,0:T(8,128)(2,1)S(1)}, bf16[1,320,1024]{2,1,0:T(8,128)(2,1)}, u32[]{:S(2)}, u32[]{:S(2)}) collective-permute-start(bf16[1,320,1024]{2,1,0:T(8,128)(2,1)S(1)} %get-tuple-element.119.refs_2_), channel_id=1, source_target_pairs={{0,1},{1,0},{2,3},{3,2},{4,5},{5,4},{6,7},{7,6},{8,9},{9,8},{10,11... | collective-permute-start | bytes 1966088 | tf_op jit(solution)/shard_map/ppermute | solution.py:366
  53.1 33.2 %collective-permute-start.14 = (bf16[1,320,1024]{2,1,0:T(8,128)(2,1)}, bf16[1,320,1024]{2,1,0:T(8,128)(2,1)}, u32[]{:S(2)}, u32[]{:S(2)}) collective-permute-start(bf16[1,320,1024]{2,1,0:T(8,128)(2,1)} %get-tuple-element.114.refs_3_), channel_id=1, source_target_pairs={{2,0},{3,1},{0,2},{1,3},{6,4},{7,5},{4,6},{5,7},{10,8},{11,9},{8,1... | collective-permute-start | bytes 1966088 | tf_op jit(solution)/shard_map/ppermute | solution.py:372
  57.5 12.0 %collective-permute-start.11 = (bf16[1,320,1024]{2,1,0:T(8,128)(2,1)}, bf16[1,320,1024]{2,1,0:T(8,128)(2,1)S(1)}, u32[]{:S(2)}, u32[]{:S(2)}) collective-permute-start(bf16[1,320,1024]{2,1,0:T(8,128)(2,1)} %collective-permute-done.9.refs_6_), channel_id=1, source_target_pairs={{0,1},{1,0},{2,3},{3,2},{4,5},{5,4},{6,7},{7,6},{8,9},{9,8},{10,11... | collective-permute-start | bytes 1966088 | tf_op jit(solution)/shard_map/ppermute | solution.py:366
  68.7 19.3 %collective-permute-start.12 = (bf16[1,320,1024]{2,1,0:T(8,128)(2,1)S(1)}, bf16[1,320,1024]{2,1,0:T(8,128)(2,1)S(1)}, u32[]{:S(2)}, u32[]{:S(2)}) collective-permute-start(bf16[1,320,1024]{2,1,0:T(8,128)(2,1)S(1)} %copy-done.25), channel_id=1, source_target_pairs={{0,1},{1,0},{2,3},{3,2},{4,5},{5,4},{6,7},{7,6},{8,9},{9,8},{10,11... | collective-permute-start | bytes 1966088 | tf_op jit(solution)/shard_map/ppermute | solution.py:366
  69.3 17.0 %collective-permute-start.15 = (bf16[1,320,1024]{2,1,0:T(8,128)(2,1)}, bf16[1,320,1024]{2,1,0:T(8,128)(2,1)}, u32[]{:S(2)}, u32[]{:S(2)}) collective-permute-start(bf16[1,320,1024]{2,1,0:T(8,128)(2,1)} %get-tuple-element.117.refs_4_), channel_id=1, source_target_pairs={{2,0},{3,1},{0,2},{1,3},{6,4},{7,5},{4,6},{5,7},{10,8},{11,9},{8,1... | collective-permute-start | bytes 1966088 | tf_op jit(solution)/shard_map/ppermute | solution.py:372
  69.3 18.7 %collective-permute-start.13 = (bf16[1,320,1024]{2,1,0:T(8,128)(2,1)}, bf16[1,320,1024]{2,1,0:T(8,128)(2,1)S(1)}, u32[]{:S(2)}, u32[]{:S(2)}) collective-permute-start(bf16[1,320,1024]{2,1,0:T(8,128)(2,1)} %get-tuple-element.117.refs_4_), channel_id=1, source_target_pairs={{0,1},{1,0},{2,3},{3,2},{4,5},{5,4},{6,7},{7,6},{8,9},{9,8},{10,11... | collective-permute-start | bytes 1966088 | tf_op jit(solution)/shard_map/ppermute | solution.py:366
  123.7 153.7 %reduce-scatter.9.cloned.1.call-start = ((), (), s32[]{:S(2)}) async-start(), calls=%async_computation.7 | async-start | bytes 1966080 | tf_op jit(solution)/shard_map/reduce_scatter | solution.py:939
  144.3 37.5 %collective-permute-start.18 = (bf16[1,4,192,1024]{3,2,1,0:T(8,128)(2,1)}, bf16[1,4,192,1024]{3,2,1,0:T(8,128)(2,1)S(1)}, u32[]{:S(2)}, u32[]{:S(2)}) collective-permute-start(bf16[1,4,192,1024]{3,2,1,0:T(8,128)(2,1)} %get-tuple-element.136), channel_id=1, source_target_pairs={{0,4},{4,0},{8,12},{12,8},{16,20},{20,16},{24,28},{28,24},{1,5},{5... | collective-permute-start | bytes 4718600 | tf_op jit(solution)/shard_map/ppermute | solution.py:983
  175.2 88.7 %collective-permute-start.23 = (bf16[2,4,192,1024]{3,2,1,0:T(8,128)(2,1)}, bf16[2,4,192,1024]{3,2,1,0:T(8,128)(2,1)}, u32[]{:S(2)}, u32[]{:S(2)}) collective-permute-start(bf16[2,4,192,1024]{3,2,1,0:T(8,128)(2,1)} %get-tuple-element.159), channel_id=1, source_target_pairs={{0,4},{4,0},{8,12},{12,8},{16,20},{20,16},{24,28},{28,24},{1,5},{5... | collective-permute-start | bytes 9437192 | tf_op jit(solution)/shard_map/ppermute | solution.py:983
  183.7 108.7 %reduce-scatter.11.cloned.1.call-start = ((), (), s32[]{:S(2)}) async-start(), calls=%async_computation.8 | async-start | bytes 3932160 | tf_op jit(solution)/shard_map/reduce_scatter | solution.py:939
  213.6 102.1 %collective-permute-start.27 = (bf16[2,4,192,1024]{3,2,1,0:T(8,128)(2,1)}, bf16[2,4,192,1024]{3,2,1,0:T(8,128)(2,1)S(1)}, u32[]{:S(2)}, u32[]{:S(2)}) collective-permute-start(bf16[2,4,192,1024]{3,2,1,0:T(8,128)(2,1)} %get-tuple-element.176), channel_id=1, source_target_pairs={{0,4},{4,0},{8,12},{12,8},{16,20},{20,16},{24,28},{28,24},{1,5},{5... | collective-permute-start | bytes 9437192 | tf_op jit(solution)/shard_map/ppermute | solution.py:983
  232.0 231.3 %reduce-scatter.15.cloned.1.call-start = ((), (), s32[]{:S(2)}) async-start(), calls=%async_computation.10 | async-start | bytes 3932160 | tf_op jit(solution)/shard_map/reduce_scatter | solution.py:939
  263.9 10.7 %collective-permute-start.22 = (bf16[2,320,1024]{2,1,0:T(8,128)(2,1)}, bf16[2,320,1024]{2,1,0:T(8,128)(2,1)S(1)}, u32[]{:S(2)}, u32[]{:S(2)}) collective-permute-start(bf16[2,320,1024]{2,1,0:T(8,128)(2,1)} %get-tuple-element.157), channel_id=1, source_target_pairs={{0,1},{1,0},{2,3},{3,2},{4,5},{5,4},{6,7},{7,6},{8,9},{9,8},{10,11... | collective-permute-start | bytes 3932168 | tf_op jit(solution)/shard_map/ppermute | solution.py:366
  273.3 19.1 %collective-permute-start.24 = (bf16[2,320,1024]{2,1,0:T(8,128)(2,1)}, bf16[2,320,1024]{2,1,0:T(8,128)(2,1)}, u32[]{:S(2)}, u32[]{:S(2)}) collective-permute-start(bf16[2,320,1024]{2,1,0:T(8,128)(2,1)} %get-tuple-element.167), channel_id=1, source_target_pairs={{0,1},{1,0},{2,3},{3,2},{4,5},{5,4},{6,7},{7,6},{8,9},{9,8},{10,11... | collective-permute-start | bytes 3932168 | tf_op jit(solution)/shard_map/ppermute | solution.py:366
  276.2 31.0 %collective-permute-start.25 = (bf16[2,320,1024]{2,1,0:T(8,128)(2,1)}, bf16[2,320,1024]{2,1,0:T(8,128)(2,1)}, u32[]{:S(2)}, u32[]{:S(2)}) collective-permute-start(bf16[2,320,1024]{2,1,0:T(8,128)(2,1)} %add_convert_fusion.7), channel_id=1, source_target_pairs={{0,2},{1,3},{2,0},{3,1},{4,6},{5,7},{6,4},{7,5},{8,10},{9,11},{10,... | collective-permute-start | bytes 3932168 | tf_op jit(solution)/shard_map/ppermute | solution.py:378
  290.8 37.1 %collective-permute-start.29 = (bf16[2,320,1024]{2,1,0:T(8,128)(2,1)}, bf16[2,320,1024]{2,1,0:T(8,128)(2,1)}, u32[]{:S(2)}, u32[]{:S(2)}) collective-permute-start(bf16[2,320,1024]{2,1,0:T(8,128)(2,1)} %get-tuple-element.171), channel_id=1, source_target_pairs={{0,1},{1,0},{2,3},{3,2},{4,5},{5,4},{6,7},{7,6},{8,9},{9,8},{10,11... | collective-permute-start | bytes 3932168 | tf_op jit(solution)/shard_map/ppermute | solution.py:366
  321.8 10.8 %collective-permute-start.26 = (bf16[512,1024]{1,0:T(8,128)(2,1)}, bf16[512,1024]{1,0:T(8,128)(2,1)}, u32[]{:S(2)}, u32[]{:S(2)}) collective-permute-start(bf16[512,1024]{1,0:T(8,128)(2,1)} %constant_dynamic-slice_fusion.3), channel_id=1, source_target_pairs={{0,1},{1,0},{2,3},{3,2},{4,5},{5,4},{6,7},{7,6},{8,9},{9,8},{10,11... | collective-permute-start | bytes 3145736 | tf_op jit(solution)/shard_map/ppermute | solution.py:799
  325.0 138.3 %reduce-scatter.13.cloned.1.call-start = ((), (), s32[]{:S(2)}) async-start(), calls=%async_computation.9 | async-start | bytes 3932160 | tf_op jit(solution)/shard_map/reduce_scatter | solution.py:939
  326.4 37.1 %collective-permute-start.31 = (bf16[1,4,192,1024]{3,2,1,0:T(8,128)(2,1)}, bf16[1,4,192,1024]{3,2,1,0:T(8,128)(2,1)}, u32[]{:S(2)}, u32[]{:S(2)}) collective-permute-start(bf16[1,4,192,1024]{3,2,1,0:T(8,128)(2,1)} %get-tuple-element.188), channel_id=1, source_target_pairs={{0,4},{4,0},{8,12},{12,8},{16,20},{20,16},{24,28},{28,24},{1,5},{5... | collective-permute-start | bytes 4718600 | tf_op jit(solution)/shard_map/ppermute | solution.py:983
  331.2 37.8 %collective-permute-start.30 = (bf16[2,320,1024]{2,1,0:T(8,128)(2,1)}, bf16[2,320,1024]{2,1,0:T(8,128)(2,1)}, u32[]{:S(2)}, u32[]{:S(2)}) collective-permute-start(bf16[2,320,1024]{2,1,0:T(8,128)(2,1)} %add_convert_fusion.6), channel_id=1, source_target_pairs={{0,2},{1,3},{2,0},{3,1},{4,6},{5,7},{6,4},{7,5},{8,10},{9,11},{10,... | collective-permute-start | bytes 3932168 | tf_op jit(solution)/shard_map/ppermute | solution.py:378
  359.1 9.9 %collective-permute-start.32 = (bf16[2,64,512]{2,1,0:T(8,128)(2,1)S(1)}, bf16[2,64,512]{2,1,0:T(8,128)(2,1)S(1)}, u32[]{:S(2)}, u32[]{:S(2)}) collective-permute-start(bf16[2,64,512]{2,1,0:T(8,128)(2,1)S(1)} %get-tuple-element.221), channel_id=1, source_target_pairs={{0,1},{1,0},{2,3},{3,2},{4,5},{5,4},{6,7},{7,6},{8,9},{9,8},{10,11... | collective-permute-start | bytes 393224 | tf_op jit(solution)/shard_map/ppermute | solution.py:366
  385.8 16.7 %collective-permute-start.38 = (bf16[512,2048]{1,0:T(8,128)(2,1)S(1)}, bf16[512,2048]{1,0:T(8,128)(2,1)}, u32[]{:S(2)}, u32[]{:S(2)}) collective-permute-start(bf16[512,2048]{1,0:T(8,128)(2,1)S(1)} %constant_dynamic-slice_fusion.2), channel_id=1, source_target_pairs={{0,1},{1,0},{2,3},{3,2},{4,5},{5,4},{6,7},{7,6},{8,9},{9,8},{10,11... | collective-permute-start | bytes 6291464 | tf_op jit(solution)/shard_map/ppermute | solution.py:799
  386.0 126.9 %all-reduce.2.cloned.1.call-start = ((), (), s32[]{:S(2)}) async-start(), calls=%async_computation.11 | async-start | bytes 1769472 | tf_op jit(solution)/shard_map/psum | solution.py:1099
  388.4 13.9 %collective-permute-start.39 = (bf16[256,1024]{1,0:T(8,128)(2,1)S(1)}, bf16[256,1024]{1,0:T(8,128)(2,1)S(1)}, u32[]{:S(2)}, u32[]{:S(2)}) collective-permute-start(bf16[256,1024]{1,0:T(8,128)(2,1)S(1)} %constant_dynamic-slice_fusion.1), channel_id=1, source_target_pairs={{0,2},{1,3},{2,0},{3,1},{4,6},{5,7},{6,4},{7,5},{8,10},{9,11},{10,... | collective-permute-start | bytes 1572872 | tf_op jit(solution)/shard_map/ppermute | solution.py:799
  405.2 24.5 %collective-permute-start.40 = (bf16[256,2048]{1,0:T(8,128)(2,1)S(1)}, bf16[256,2048]{1,0:T(8,128)(2,1)}, u32[]{:S(2)}, u32[]{:S(2)}) collective-permute-start(bf16[256,2048]{1,0:T(8,128)(2,1)S(1)} %constant_dynamic-slice_fusion), channel_id=1, source_target_pairs={{0,2},{1,3},{2,0},{3,1},{4,6},{5,7},{6,4},{7,5},{8,10},{9,11},{10,... | collective-permute-start | bytes 3145736 | tf_op jit(solution)/shard_map/ppermute | solution.py:799
  415.9 17.9 %collective-permute-start.42 = (f32[48,1024]{1,0:T(8,128)S(1)}, f32[48,1024]{1,0:T(8,128)S(1)}, u32[]{:S(2)}, u32[]{:S(2)}) collective-permute-start(f32[48,1024]{1,0:T(8,128)S(1)} %maximum_maximum_fusion), channel_id=1, source_target_pairs={{0,1},{1,0},{2,3},{3,2},{4,5},{5,4},{6,7},{7,6},{8,9},{9,8},{10,11... | collective-permute-start | bytes 589832 | tf_op jit(solution)/shard_map/ppermute | solution.py:1091
  432.4 28.7 %collective-permute-start.41 = (bf16[128,3072]{1,0:T(8,128)(2,1)}, bf16[128,3072]{1,0:T(8,128)(2,1)}, u32[]{:S(2)}, u32[]{:S(2)}) collective-permute-start(bf16[128,3072]{1,0:T(8,128)(2,1)} %fusion.10), channel_id=1, source_target_pairs={{0,4},{4,0},{8,12},{12,8},{16,20},{20,16},{24,28},{28,24},{1,5},{5... | collective-permute-start | bytes 2359304 | tf_op jit(solution)/shard_map/ppermute | solution.py:799
  433.9 20.7 %collective-permute-start.43 = (f32[48,1024]{1,0:T(8,128)S(1)}, f32[48,1024]{1,0:T(8,128)S(1)}, u32[]{:S(2)}, u32[]{:S(2)}) collective-permute-start(f32[48,1024]{1,0:T(8,128)S(1)} %add.307), channel_id=1, source_target_pairs={{0,4},{4,0},{8,12},{12,8},{16,20},{20,16},{24,28},{28,24},{1,5},{5... | collective-permute-start | bytes 589832 | tf_op jit(solution)/shard_map/ppermute | solution.py:1091
  459.5 17.1 %collective-permute-start.59 = (bf16[2,192,1024]{2,1,0:T(8,128)(2,1)}, bf16[2,192,1024]{2,1,0:T(8,128)(2,1)}, u32[]{:S(2)}, u32[]{:S(2)}) collective-permute-start(bf16[2,192,1024]{2,1,0:T(8,128)(2,1)} %slice.130), channel_id=1, source_target_pairs={{0,4},{4,0},{8,12},{12,8},{16,20},{20,16},{24,28},{28,24},{1,5},{5... | collective-permute-start | bytes 2359304 | tf_op jit(solution)/shard_map/ppermute | solution.py:1068
  465.5 93.3 %reduce-scatter.17.cloned.1.call-start = ((), (), s32[]{:S(2)}) async-start(), calls=%async_computation.12 | async-start | bytes 1966080 | tf_op jit(solution)/shard_map/reduce_scatter | solution.py:939
  514.9 12.1 %collective-permute-start.53 = (bf16[128,1536]{1,0:T(8,128)(2,1)S(1)}, bf16[128,1536]{1,0:T(8,128)(2,1)}, u32[]{:S(2)}, u32[]{:S(2)}) collective-permute-start(bf16[128,1536]{1,0:T(8,128)(2,1)S(1)} %get-tuple-element.213.refs_8_), channel_id=1, source_target_pairs={{0,2},{1,3},{2,0},{3,1},{4,6},{5,7},{6,4},{7,5},{8,10},{9,11},{10,... | collective-permute-start | bytes 1179656 | tf_op jit(solution)/shard_map/ppermute | solution.py:1108
  516.3 12.0 %collective-permute-start.52 = (bf16[128,1536]{1,0:T(8,128)(2,1)S(1)}, bf16[128,1536]{1,0:T(8,128)(2,1)S(1)}, u32[]{:S(2)}, u32[]{:S(2)}) collective-permute-start(bf16[128,1536]{1,0:T(8,128)(2,1)S(1)} %get-tuple-element.213.refs_8_), channel_id=1, source_target_pairs={{0,4},{4,0},{8,12},{12,8},{16,20},{20,16},{24,28},{28,24},{1,5},{5... | collective-permute-start | bytes 1179656 | tf_op jit(solution)/shard_map/ppermute | solution.py:1112
  517.8 19.1 %collective-permute-start.45 = (bf16[128,1536]{1,0:T(8,128)(2,1)}, bf16[128,1536]{1,0:T(8,128)(2,1)}, u32[]{:S(2)}, u32[]{:S(2)}) collective-permute-start(bf16[128,1536]{1,0:T(8,128)(2,1)} %get-tuple-element.214.refs_0_), channel_id=1, source_target_pairs={{0,4},{4,0},{8,12},{12,8},{16,20},{20,16},{24,28},{28,24},{1,5},{5... | collective-permute-start | bytes 1179656 | tf_op jit(solution)/shard_map/ppermute | solution.py:1107
  519.7 18.7 %collective-permute-start.48 = (bf16[128,1536]{1,0:T(8,128)(2,1)}, bf16[128,1536]{1,0:T(8,128)(2,1)}, u32[]{:S(2)}, u32[]{:S(2)}) collective-permute-start(bf16[128,1536]{1,0:T(8,128)(2,1)} %get-tuple-element.214.refs_0_), channel_id=1, source_target_pairs={{0,1},{1,0},{2,3},{3,2},{4,5},{5,4},{6,7},{7,6},{8,9},{9,8},{10,11... | collective-permute-start | bytes 1179656 | tf_op jit(solution)/shard_map/ppermute | solution.py:366
  519.8 18.7 %collective-permute-start.46 = (bf16[128,1536]{1,0:T(8,128)(2,1)}, bf16[128,1536]{1,0:T(8,128)(2,1)}, u32[]{:S(2)}, u32[]{:S(2)}) collective-permute-start(bf16[128,1536]{1,0:T(8,128)(2,1)} %get-tuple-element.214.refs_0_), channel_id=1, source_target_pairs={{0,2},{1,3},{2,0},{3,1},{4,6},{5,7},{6,4},{7,5},{8,10},{9,11},{10,... | collective-permute-start | bytes 1179656 | tf_op jit(solution)/shard_map/ppermute | solution.py:1110
  526.9 12.0 %collective-permute-start.57 = (bf16[128,1536]{1,0:T(8,128)(2,1)}, bf16[128,1536]{1,0:T(8,128)(2,1)}, u32[]{:S(2)}, u32[]{:S(2)}) collective-permute-start(bf16[128,1536]{1,0:T(8,128)(2,1)} %collective-permute-done.53.refs_10_), channel_id=1, source_target_pairs={{0,1},{1,0},{2,3},{3,2},{4,5},{5,4},{6,7},{7,6},{8,9},{9,8},{10,11... | collective-permute-start | bytes 1179656 | tf_op jit(solution)/shard_map/ppermute | solution.py:366
  528.3 16.2 %collective-permute-start.54 = (bf16[128,1536]{1,0:T(8,128)(2,1)}, bf16[128,1536]{1,0:T(8,128)(2,1)}, u32[]{:S(2)}, u32[]{:S(2)}) collective-permute-start(bf16[128,1536]{1,0:T(8,128)(2,1)} %collective-permute-done.53.refs_10_), channel_id=1, source_target_pairs={{0,4},{4,0},{8,12},{12,8},{16,20},{20,16},{24,28},{28,24},{1,5},{5... | collective-permute-start | bytes 1179656 | tf_op jit(solution)/shard_map/ppermute | solution.py:1112
  536.9 10.0 %collective-permute-start.47 = (bf16[128,1536]{1,0:T(8,128)(2,1)}, bf16[128,1536]{1,0:T(8,128)(2,1)}, u32[]{:S(2)}, u32[]{:S(2)}) collective-permute-start(bf16[128,1536]{1,0:T(8,128)(2,1)} %collective-permute-done.45.refs_1_), channel_id=1, source_target_pairs={{0,2},{1,3},{2,0},{3,1},{4,6},{5,7},{6,4},{7,5},{8,10},{9,11},{10,... | collective-permute-start | bytes 1179656 | tf_op jit(solution)/shard_map/ppermute | solution.py:1110
  538.4 9.7 %collective-permute-start.49 = (bf16[128,1536]{1,0:T(8,128)(2,1)}, bf16[128,1536]{1,0:T(8,128)(2,1)S(1)}, u32[]{:S(2)}, u32[]{:S(2)}) collective-permute-start(bf16[128,1536]{1,0:T(8,128)(2,1)} %collective-permute-done.45.refs_1_), channel_id=1, source_target_pairs={{0,1},{1,0},{2,3},{3,2},{4,5},{5,4},{6,7},{7,6},{8,9},{9,8},{10,11... | collective-permute-start | bytes 1179656 | tf_op jit(solution)/shard_map/ppermute | solution.py:366
  538.5 9.6 %collective-permute-start.56 = (bf16[128,1536]{1,0:T(8,128)(2,1)}, bf16[128,1536]{1,0:T(8,128)(2,1)S(1)}, u32[]{:S(2)}, u32[]{:S(2)}) collective-permute-start(bf16[128,1536]{1,0:T(8,128)(2,1)} %copy-done.32), channel_id=1, source_target_pairs={{0,1},{1,0},{2,3},{3,2},{4,5},{5,4},{6,7},{7,6},{8,9},{9,8},{10,11... | collective-permute-start | bytes 1179656 | tf_op jit(solution)/shard_map/ppermute | solution.py:366
  (60 other events, 415.6 us)
Sparse Core Ops, SparseCore 0:
  123.8 61.2 reduce-scatter.6
  187.4 35.3 reduce-scatter.8
  232.2 60.1 reduce-scatter.10
  325.2 61.6 reduce-scatter.14
  389.6 60.3 reduce-scatter.12
  465.6 47.1 all-reduce.1
  515.7 34.4 reduce-scatter.16

commit v6 on v5

--- a/solution.py
+++ b/solution.py
@@ -1060,8 +1060,7 @@
         after(gp, grad_qkv, output), w_qkv, token_rows, attn_gain, grad_hidden
     )
     last = [add_x(i, grad_norm_attn) for i in list(halves)]
-    grad_qkv = after(halve(grad_qkv, "expert", swap_core, core_bit), grad_out)
-    grad_qkv = halve(grad_qkv, "expert", swap_y, row_bit, grad_norm_attn)
+    grad_qkv = halve(after(grad_qkv, grad_out), "expert", swap_core, core_bit)
 
     whole_sums = [parts[i] for i, (_, whole) in enumerate(plan) if whole]
     whole_sums = jnp.concatenate(whole_sums, axis=0)
@@ -1087,8 +1086,10 @@
         axis=0,
     )
     small = after(small, *last)
-    for axis, swap in (("expert", swap_core), ("dp", swap_x), ("expert", swap_y)):
+    for axis, swap in (("expert", swap_core), ("dp", swap_x)):
         small = small + lax.ppermute(small, axis, swap)
+    grad_qkv = halve(grad_qkv, "expert", swap_y, row_bit, small)
+    small = small + lax.ppermute(small, "expert", swap_y)
     dense = jnp.concatenate([grad_qkv, grad_out], axis=1)
     dense = after(halve(dense, "dp", swap_x, parity), *sent(2), *sent(3))
     for i in list(held):

time: 581 us -> 572 us (0.985)
  waiting for transfers between devices: 156 us -> 146 us
    ppermute x3 -> x2, waiting for transfers between devices: 20.2 us -> 6.72 us  [local(): small = small + lax.ppermute(small, axis, swap)]
    unnamed x90 -> x94, local copies, waits for them, and re-layouts: 11.1 us -> 12.2 us
  transfers between devices with their start and end apart: 67 -> 67, of which waited for: 24 -> 26; matrix products, arithmetic and copies ran while one was open for 13% -> 13% of each run, Pallas kernels for 42% -> 43%
where the time goes in v6:
time: 572 us; the launch traced here: 562 us
  Pallas kernels  276 us (48%)
  waiting for transfers between devices  146 us (26%)
  other arithmetic  48.4 us (8%)
  local copies, waits for them, and re-layouts  35.8 us (6%)
  starting transfers between devices  35 us (6%)
  between operations  15.4 us (3%)
    pallas_call x6, Pallas kernels, expert_chunk(): pl.pallas_call(functools.partial(expert_body, tile=tile), grid_spec=grid_...  127 us
    psum x1, waiting for transfers between devices, local(): dense = lax.psum(dense, 'dp', axis_index_groups=z_groups)  38.1 us
    pallas_call x2, Pallas kernels, sum_rows(): pl.pallas_call(functools.partial(sum_rows_body, chunks=len(rows), with_do...  28.1 us
    pallas_call x1, Pallas kernels, attend_back(): pl.pallas_call(attend_back_body, grid=(micro, steps), in_specs=[wide, pro...  22.8 us
    pallas_call x2, Pallas kernels, attend(): pl.pallas_call(attend_body, grid=(steps,), in_specs=[pl.BlockSpec((1, row...  22.4 us
    ppermute x5, waiting for transfers between devices, halve(): got = after(lax.ppermute(send, axis, swap), *before)  19.2 us
    ppermute x6, waiting for transfers between devices, from_row(): return lax.ppermute(value, 'expert', pairs)  17.2 us
    pallas_call x1, Pallas kernels, pick_tokens(): pl.pallas_call(functools.partial(pick_token_body, pieces=len(pieces)), gr...  16.8 us
  transfers between devices with their start and end apart: 67, of which 26 were waited for; matrix products, arithmetic and copies ran while one was open for 13% of the time, Pallas kernels for 43%

profile of v6, /device:TPU:0, one launch (start us, length us, event | category | flops | bytes accessed | tf_op | source)
XLA Modules:
  0.0 561.7 jit_solution(10086723805818282520)
XLA Ops:
  8.0 3.1 collective-permute-start.5
  15.1 6.7 %shard_map.169 = (bf16[2,320,1024]{2,1,0:T(8,128)(2,1)}, bf16[2,320,1024]{2,1,0:T(8,128)(2,1)}, bf16[2,320,1024]{2,1,0:T(8,128)(2,1)}) custom-call(bf16[2,320,1024]{2,1,0:T(8,128)(2,1)} %bitcast.74, f32[1,1024]{1,0:T(1,128)} %bitcast.81, bf16[1024,2048]{1,0:T(8,128)(2,1)} %w_ref.7, f32[320,128]{1,0:T(8,128)} %copy.23.cos_ref.refs_10_, ...), custom_call_target="tpu_custom_call" | custom-call | flops 8049999872 | tf_op jit(solution)/shard_map/pallas_call | solution.py:468
  22.7 7.2 %collective-permute-done.refs_5_ = bf16[1,320,1024]{2,1,0:T(8,128)(2,1)} collective-permute-done((bf16[1,320,1024]{2,1,0:T(8,128)(2,1)S(1)}, bf16[1,320,1024]{2,1,0:T(8,128)(2,1)}, u32[]{:S(2)}, u32[]{:S(2)}) %collective-permute-start) | collective-permute-done | bytes 655392 | tf_op jit(solution)/shard_map/ppermute | solution.py:372
  30.9 6.4 %collective-permute-done.2 = bf16[2,64,1024]{2,1,0:T(8,128)(2,1)S(1)} collective-permute-done((bf16[2,64,1024]{2,1,0:T(8,128)(2,1)S(1)}, bf16[2,64,1024]{2,1,0:T(8,128)(2,1)S(1)}, u32[]{:S(2)}, u32[]{:S(2)}) %collective-permute-start.2) | collective-permute-done | bytes 262176 | tf_op jit(solution)/shard_map/ppermute | solution.py:372
  41.9 11.2 %shard_map.170 = (bf16[1,320,1024]{2,1,0:T(8,128)(2,1)}, f32[4,1,1280]{2,1,0:T(1,128)}, f32[1,320,1024]{2,1,0:T(8,128)}, bf16[1,320,1024]{2,1,0:T(8,128)(2,1)}) custom-call(bf16[2,320,1024]{2,1,0:T(8,128)(2,1)} %get-tuple-element.110.q_ref, bf16[2,256,1024]{2,1,0:T(8,128)(2,1)} %pad_maximum_fusion.pk_ref.pv_ref, ...), custom_call_target="tpu_custom_call" | custom-call | flops 13799999488 | tf_op jit(solution)/shard_map/pallas_call | solution.py:544
  54.7 2.7 collective-permute-done.9.refs_6_
  57.4 11.2 %shard_map.171 = (bf16[1,320,1024]{2,1,0:T(8,128)(2,1)}, f32[4,1,1280]{2,1,0:T(1,128)}, f32[1,320,1024]{2,1,0:T(8,128)}, bf16[1,320,1024]{2,1,0:T(8,128)(2,1)}) custom-call(bf16[2,320,1024]{2,1,0:T(8,128)(2,1)} %get-tuple-element.110.q_ref, bf16[2,256,1024]{2,1,0:T(8,128)(2,1)} %pad_maximum_fusion.pk_ref.pv_ref, ...), custom_call_target="tpu_custom_call" | custom-call | flops 13799999488 | tf_op jit(solution)/shard_map/pallas_call | solution.py:544
  70.4 15.1 %shard_map.172 = (bf16[8,8,112,1024]{3,2,1,0:T(8,128)(2,1)}, s32[8,8,320]{2,1,0:T(8,128)}) custom-call(s32[8,8,320]{2,1,0:T(8,128)} %negate_select_fusion.1.refs_0_, bf16[1,320,1024]{2,1,0:T(8,128)(2,1)} %copy-done.16, bf16[1,320,1024]{2,1,0:T(8,128)(2,1)} %copy-done.15, bf16[1,320,1024]{2,1,0:T(8,128)(2,1)} %copy-done.27, ...), custom_call_target="tpu_custom_call" | custom-call | flops 17250000896 | tf_op jit(solution)/shard_map/pallas_call | solution.py:112
  89.7 16.8 %shard_map.173 = (bf16[8,8,112,1024]{3,2,1,0:T(8,128)(2,1)}, f32[8,8,112,128]{3,2,1,0:T(8,128)}, f32[8,32,320]{2,1,0:T(8,128)}) custom-call(s32[8,8,320]{2,1,0:T(8,128)} %negate_select_fusion.1.refs_0_, s32[8,8,320]{2,1,0:T(8,128)} %get-tuple-element.162.refs_1_.refs_0_, bf16[1024,32]{1,0:T(8,128)(2,1)} %dynamic-slice_maximum_fusion.refs_2_.refs_4_, ...), custom_call_target="tpu_custom_call" | custom-call | flops 19549999104 | tf_op jit(solution)/shard_map/pallas_call | solution.py:158
  106.5 17.0 %shard_map.174 = (bf16[1,896,1024]{2,1,0:T(8,128)(2,1)}, bf16[1,896,1024]{2,1,0:T(8,128)(2,1)}, f32[1,896,128]{2,1,0:T(8,128)}, bf16[1,4,384,1024]{3,2,1,0:T(8,128)(2,1)}) custom-call(s32[1]{0:T(128)} %bitcast.8.parity_ref, bf16[8,896,1024]{2,1,0:T(8,128)(2,1)} %bitcast.89, bf16[8,896,1024]{2,1,0:T(8,128)(2,1)} %bitcast.83, f32[8,896,128]{2,1,0:T(8,128)} %bitcast.95, ...), custom_call_target="tpu_custom_call" | custom-call | flops 17250000896 | tf_op jit(solution)/shard_map/pallas_call | solution.py:351
  127.1 17.0 %shard_map.175 = (bf16[1,896,1024]{2,1,0:T(8,128)(2,1)}, bf16[1,896,1024]{2,1,0:T(8,128)(2,1)}, f32[1,896,128]{2,1,0:T(8,128)}, bf16[1,4,192,1024]{3,2,1,0:T(8,128)(2,1)}, bf16[1,4,192,1024]{3,2,1,0:T(8,128)(2,1)}) custom-call(s32[1]{0:T(128)} %bitcast.8.parity_ref, bf16[8,896,1024]{2,1,0:T(8,128)(2,1)} %bitcast.90, bf16[8,896,1024]{2,1,0:T(8,128)(2,1)} %bitcast.84, ...), custom_call_target="tpu_custom_call" | custom-call | flops 17250000896 | tf_op jit(solution)/shard_map/pallas_call | solution.py:351
  145.7 29.4 %shard_map.176 = (bf16[2,896,1024]{2,1,0:T(8,128)(2,1)}, bf16[2,896,1024]{2,1,0:T(8,128)(2,1)}, f32[2,896,128]{2,1,0:T(8,128)}, bf16[2,4,192,1024]{3,2,1,0:T(8,128)(2,1)}, bf16[2,4,192,1024]{3,2,1,0:T(8,128)(2,1)}) custom-call(s32[1]{0:T(128)} %bitcast.8.parity_ref, bf16[8,896,1024]{2,1,0:T(8,128)(2,1)} %bitcast.91, bf16[8,896,1024]{2,1,0:T(8,128)(2,1)} %bitcast.85, ...), custom_call_target="tpu_custom_call" | custom-call | flops 34500001792 | tf_op jit(solution)/shard_map/pallas_call | solution.py:351
  175.6 6.0 %collective-permute-done.18 = bf16[1,4,192,1024]{3,2,1,0:T(8,128)(2,1)S(1)} collective-permute-done((bf16[1,4,192,1024]{3,2,1,0:T(8,128)(2,1)}, bf16[1,4,192,1024]{3,2,1,0:T(8,128)(2,1)S(1)}, u32[]{:S(2)}, u32[]{:S(2)}) %collective-permute-start.18) | collective-permute-done | bytes 1572896 | tf_op jit(solution)/shard_map/ppermute | solution.py:983
  183.6 29.7 %shard_map.177 = (bf16[2,896,1024]{2,1,0:T(8,128)(2,1)}, bf16[2,896,1024]{2,1,0:T(8,128)(2,1)}, f32[2,896,128]{2,1,0:T(8,128)}, bf16[2,4,192,1024]{3,2,1,0:T(8,128)(2,1)}, bf16[2,4,192,1024]{3,2,1,0:T(8,128)(2,1)}) custom-call(s32[1]{0:T(128)} %bitcast.8.parity_ref, bf16[8,896,1024]{2,1,0:T(8,128)(2,1)} %bitcast.92, bf16[8,896,1024]{2,1,0:T(8,128)(2,1)} %bitcast.86, ...), custom_call_target="tpu_custom_call" | custom-call | flops 34500001792 | tf_op jit(solution)/shard_map/pallas_call | solution.py:351
  214.8 16.9 %shard_map.178 = (bf16[1,896,1024]{2,1,0:T(8,128)(2,1)}, bf16[1,896,1024]{2,1,0:T(8,128)(2,1)}, f32[1,896,128]{2,1,0:T(8,128)}, bf16[1,4,384,1024]{3,2,1,0:T(8,128)(2,1)}) custom-call(s32[1]{0:T(128)} %bitcast.8.parity_ref, bf16[8,896,1024]{2,1,0:T(8,128)(2,1)} %bitcast.93, bf16[8,896,1024]{2,1,0:T(8,128)(2,1)} %bitcast.87, f32[8,896,128]{2,1,0:T(8,128)} %bitcast.99, ...), custom_call_target="tpu_custom_call" | custom-call | flops 17250000896 | tf_op jit(solution)/shard_map/pallas_call | solution.py:351
  231.7 17.3 %shard_map.179 = (bf16[1,896,1024]{2,1,0:T(8,128)(2,1)}, bf16[1,896,1024]{2,1,0:T(8,128)(2,1)}, f32[1,896,128]{2,1,0:T(8,128)}, bf16[1,4,192,1024]{3,2,1,0:T(8,128)(2,1)}, bf16[1,4,192,1024]{3,2,1,0:T(8,128)(2,1)}) custom-call(s32[1]{0:T(128)} %bitcast.8.parity_ref, bf16[8,896,1024]{2,1,0:T(8,128)(2,1)} %bitcast.94, bf16[8,896,1024]{2,1,0:T(8,128)(2,1)} %bitcast.88, ...), custom_call_target="tpu_custom_call" | custom-call | flops 17250000896 | tf_op jit(solution)/shard_map/pallas_call | solution.py:351
  249.0 14.7 %shard_map.180 = (bf16[2,320,1024]{2,1,0:T(8,128)(2,1)}, bf16[2,320,1024]{2,1,0:T(8,128)(2,1)}, bf16[2,320,1024]{2,1,0:T(8,128)(2,1)}, bf16[2,320,1024]{2,1,0:T(8,128)(2,1)}, f32[8,8,320]{2,1,0:T(8,128)}) custom-call(s32[8,8,320]{2,1,0:T(8,128)} %get-tuple-element.162.refs_1_.refs_0_, bf16[1,8,112,1024]{3,2,1,0:T(8,128)(2,1)} %bitcast.106, ...), custom_call_target="tpu_custom_call" | custom-call | flops 17250000896 | tf_op jit(solution)/shard_map/pallas_call | solution.py:242
  266.9 5.4 add_convert_fusion.1
  275.3 13.4 %shard_map.181 = (bf16[2,320,1024]{2,1,0:T(8,128)(2,1)}, bf16[2,320,1024]{2,1,0:T(8,128)(2,1)}, bf16[2,320,1024]{2,1,0:T(8,128)(2,1)}, bf16[2,320,1024]{2,1,0:T(8,128)(2,1)}) custom-call(s32[8,8,320]{2,1,0:T(8,128)} %get-tuple-element.162.refs_1_.refs_0_, bf16[1,8,112,1024]{3,2,1,0:T(8,128)(2,1)} %bitcast.105, bf16[1,8,112,1024]{3,2,1,0:T(8,128)(2,1)} %bitcast.107, ...), custom_call_target="tpu_custom_call" | custom-call | flops 17250000896 | tf_op jit(solution)/shard_map/pallas_call | solution.py:242
  288.7 3.3 reduce-scatter.11.cloned.1.call-done
  292.0 12.9 %collective-permute-done.25.refs_2_ = bf16[2,320,1024]{2,1,0:T(8,128)(2,1)} collective-permute-done((bf16[2,320,1024]{2,1,0:T(8,128)(2,1)S(1)}, bf16[2,320,1024]{2,1,0:T(8,128)(2,1)}, u32[]{:S(2)}, u32[]{:S(2)}) %collective-permute-start.25) | collective-permute-done | bytes 1310752 | tf_op jit(solution)/shard_map/ppermute | solution.py:378
  304.9 8.2 %shard_map.182 = (f32[2,320,1024]{2,1,0:T(8,128)}, bf16[2,320,1024]{2,1,0:T(8,128)(2,1)}, bf16[2,320,1024]{2,1,0:T(8,128)(2,1)}, f32[1,1024]{1,0:T(1,128)}) custom-call(bf16[2,320,1024]{2,1,0:T(8,128)(2,1)} %get-tuple-element.160.refs_0_, bf16[2,320,1024]{2,1,0:T(8,128)(2,1)} %copy-done.25, bf16[2,320,1024]{2,1,0:T(8,128)(2,1)} %collective-permute-done.25.refs_2_, ...), custom_call_target="tpu_custom_call" | custom-call | flops 9200000000 | tf_op jit(solution)/shard_map/pallas_call | solution.py:611
  313.2 3.4 bitcast_convert_fusion
  320.1 3.3 add_convert_fusion.6
  324.5 5.1 add_convert_fusion
  332.8 22.8 %shard_map.183 = (bf16[2,320,1024]{2,1,0:T(8,128)(2,1)}, bf16[2,256,512]{2,1,0:T(8,128)(2,1)}, bf16[2,256,512]{2,1,0:T(8,128)(2,1)}, bf16[2,256,512]{2,1,0:T(8,128)(2,1)}, bf16[2,256,512]{2,1,0:T(8,128)(2,1)}) custom-call(bf16[2,320,1024]{2,1,0:T(8,128)(2,1)} %get-tuple-element.110.q_ref, bf16[2,256,1024]{2,1,0:T(8,128)(2,1)} %pad_maximum_fusion.pk_ref.pv_ref, ...), custom_call_target="tpu_custom_call" | custom-call | flops 26449999872 | tf_op jit(solution)/shard_map/pallas_call | solution.py:672
  355.7 1.9 fusion.20
  362.7 3.2 add_convert_fusion.3
  370.5 11.1 %shard_map.184 = (bf16[2,320,2048]{2,1,0:T(8,128)(2,1)}, bf16[1024,2048]{1,0:T(8,128)(2,1)}) custom-call(bf16[2,320,1024]{2,1,0:T(8,128)(2,1)} %get-tuple-element.190.refs_0_, bf16[2,320,1024]{2,1,0:T(8,128)(2,1)} %get-tuple-element.182.refs_1_, bf16[2,256,512]{2,1,0:T(8,128)(2,1)} %get-tuple-element.191.refs_2_, ...), custom_call_target="tpu_custom_call" | custom-call | flops 12650000384 | tf_op jit(solution)/shard_map/pallas_call | solution.py:739
  387.4 3.6 collective-permute-done.28
  391.0 4.5 add_convert_fusion.5
  395.6 2.4 add_convert_fusion.2
  399.0 8.6 %shard_map.185 = (bf16[2,320,1024]{2,1,0:T(8,128)(2,1)}, f32[1,1024]{1,0:T(1,128)}) custom-call(bf16[2,320,2048]{2,1,0:T(8,128)(2,1)} %get-tuple-element.197.gp_ref, bf16[1024,2048]{1,0:T(8,128)(2,1)} %w_ref.7, bf16[2,320,1024]{2,1,0:T(8,128)(2,1)} %bitcast.77, f32[1,1024]{1,0:T(1,128)} %bitcast.82, f32[2,320,1024]{2,1,0:T(8,128)} %get-tuple-element.198.hidden_ref), custom_call_target="tpu_custom_call" | custom-call | flops 9200000000 | tf_op jit(solution)/shard_map/pallas_call | solution.py:775
  411.7 5.3 collective-permute-done.42
  418.0 5.5 collective-permute-done.40
  434.5 13.2 %collective-permute-done.43 = bf16[128,3072]{1,0:T(8,128)(2,1)} collective-permute-done((bf16[128,3072]{1,0:T(8,128)(2,1)}, bf16[128,3072]{1,0:T(8,128)(2,1)}, u32[]{:S(2)}, u32[]{:S(2)}) %collective-permute-start.43) | collective-permute-done | bytes 786464 | tf_op jit(solution)/shard_map/ppermute | solution.py:799
  447.7 2.2 add_convert_fusion.11
  449.9 3.9 reduce-scatter.13.cloned.1.call-done
  453.9 2.1 pad_maximum_fusion.1
  456.6 6.2 %collective-permute-done.59 = bf16[2,192,1024]{2,1,0:T(8,128)(2,1)} collective-permute-done((bf16[2,192,1024]{2,1,0:T(8,128)(2,1)}, bf16[2,192,1024]{2,1,0:T(8,128)(2,1)}, u32[]{:S(2)}, u32[]{:S(2)}) %collective-permute-start.59) | collective-permute-done | bytes 786464 | tf_op jit(solution)/shard_map/ppermute | solution.py:1067
  465.3 38.1 %all-reduce.2.cloned.1.call-done = bf16[144,3072]{1,0:T(8,128)(2,1)} async-done(((bf16[144,3072]{1,0:T(8,128)(2,1)}), bf16[144,3072]{1,0:T(8,128)(2,1)}) %all-reduce.2.cloned.1.call-update) | async-done | bytes 884752 | tf_op jit(solution)/shard_map/psum | solution.py:1100
  503.4 2.0 fusion.18
  511.0 6.6 %collective-permute-done.53.refs_10_ = bf16[128,1536]{1,0:T(8,128)(2,1)} collective-permute-done((bf16[128,1536]{1,0:T(8,128)(2,1)S(1)}, bf16[128,1536]{1,0:T(8,128)(2,1)}, u32[]{:S(2)}, u32[]{:S(2)}) %collective-permute-start.53) | collective-permute-done | bytes 393248 | tf_op jit(solution)/shard_map/ppermute | solution.py:1109
  520.4 7.1 %collective-permute-done.45.refs_1_ = bf16[128,1536]{1,0:T(8,128)(2,1)} collective-permute-done((bf16[128,1536]{1,0:T(8,128)(2,1)}, bf16[128,1536]{1,0:T(8,128)(2,1)}, u32[]{:S(2)}, u32[]{:S(2)}) %collective-permute-start.45) | collective-permute-done | bytes 393248 | tf_op jit(solution)/shard_map/ppermute | solution.py:1108
  529.6 5.5 collective-permute-done.54.refs_11_
  535.1 2.3 collective-permute-done.47.refs_3_
  540.4 9.0 %shard_map.186 = (f32[1024,2048]{1,0:T(8,128)}, f32[1024,1024]{1,0:T(8,128)}) custom-call(s32[8]{0:T(128)} %iota_xor_fusion.table_ref, bf16[128,1536]{1,0:T(8,128)(2,1)} %get-tuple-element.214.refs_0_, bf16[128,1536]{1,0:T(8,128)(2,1)} %collective-permute-done.45.refs_1_, bf16[128,1536]{1,0:T(8,128)(2,1)} %collective-permute-done.46.refs_2_, ...), custom_call_target="tpu_custom_call" | custom-call | flops 10350000128 | tf_op jit(solution)/shard_map/pallas_call | solution.py:829
  551.9 2.5 slice.133
  (281 shorter events, 93.1 us)
Async XLA Ops:
  7.2 207.6 %reduce-scatter.7.cloned.1.call-start = ((), (), s32[]{:S(2)}) async-start(), calls=%async_computation.6 | async-start | bytes 3932160 | tf_op jit(solution)/shard_map/reduce_scatter | solution.py:939
  8.0 22.3 %collective-permute-start.5 = (s32[2,8,320]{2,1,0:T(8,128)S(1)}, s32[2,8,320]{2,1,0:T(8,128)S(1)}, u32[]{:S(2)}, u32[]{:S(2)}) collective-permute-start(s32[2,8,320]{2,1,0:T(8,128)S(1)} %bitcast.67), channel_id=1, source_target_pairs={{2,0},{3,1},{0,2},{1,3},{6,4},{7,5},{4,6},{5,7},{10,8},{11,9},{8,1... | collective-permute-start | bytes 61448 | tf_op jit(solution)/shard_map/ppermute | solution.py:372
  11.1 28.0 %collective-permute-start.4 = (s32[2,8,320]{2,1,0:T(8,128)S(1)}, s32[2,8,320]{2,1,0:T(8,128)S(1)}, u32[]{:S(2)}, u32[]{:S(2)}) collective-permute-start(s32[2,8,320]{2,1,0:T(8,128)S(1)} %bitcast.68), channel_id=1, source_target_pairs={{0,1},{1,0},{2,3},{3,2},{4,5},{5,4},{6,7},{7,6},{8,9},{9,8},{10,11... | collective-permute-start | bytes 61448 | tf_op jit(solution)/shard_map/ppermute | solution.py:366
  12.5 56.1 %collective-permute-start.7 = (bf16[1,320,1024]{2,1,0:T(8,128)(2,1)S(1)}, bf16[1,320,1024]{2,1,0:T(8,128)(2,1)S(1)}, u32[]{:S(2)}, u32[]{:S(2)}) collective-permute-start(bf16[1,320,1024]{2,1,0:T(8,128)(2,1)S(1)} %get-tuple-element.212.refs_1_), channel_id=1, source_target_pairs={{0,1},{1,0},{2,3},{3,2},{4,5},{5,4},{6,7},{7,6},{8,9},{9,8},{10,11... | collective-permute-start | bytes 1966088 | tf_op jit(solution)/shard_map/ppermute | solution.py:366
  13.1 16.8 %collective-permute-start = (bf16[1,320,1024]{2,1,0:T(8,128)(2,1)S(1)}, bf16[1,320,1024]{2,1,0:T(8,128)(2,1)}, u32[]{:S(2)}, u32[]{:S(2)}) collective-permute-start(bf16[1,320,1024]{2,1,0:T(8,128)(2,1)S(1)} %get-tuple-element.212.refs_1_), channel_id=1, source_target_pairs={{2,0},{3,1},{0,2},{1,3},{6,4},{7,5},{4,6},{5,7},{10,8},{11,9},{8,1... | collective-permute-start | bytes 1966088 | tf_op jit(solution)/shard_map/ppermute | solution.py:372
  30.4 10.4 %collective-permute-start.1 = (bf16[2,64,1024]{2,1,0:T(8,128)(2,1)S(1)}, bf16[2,64,1024]{2,1,0:T(8,128)(2,1)S(1)}, u32[]{:S(2)}, u32[]{:S(2)}) collective-permute-start(bf16[2,64,1024]{2,1,0:T(8,128)(2,1)S(1)} %slice.93), channel_id=1, source_target_pairs={{0,1},{1,0},{2,3},{3,2},{4,5},{5,4},{6,7},{7,6},{8,9},{9,8},{10,11... | collective-permute-start | bytes 786440 | tf_op jit(solution)/shard_map/ppermute | solution.py:366
  39.8 29.5 %collective-permute-start.10 = (bf16[1,320,1024]{2,1,0:T(8,128)(2,1)}, bf16[1,320,1024]{2,1,0:T(8,128)(2,1)}, u32[]{:S(2)}, u32[]{:S(2)}) collective-permute-start(bf16[1,320,1024]{2,1,0:T(8,128)(2,1)} %collective-permute-done.refs_5_), channel_id=1, source_target_pairs={{0,1},{1,0},{2,3},{3,2},{4,5},{5,4},{6,7},{7,6},{8,9},{9,8},{10,11... | collective-permute-start | bytes 1966088 | tf_op jit(solution)/shard_map/ppermute | solution.py:366
  40.3 17.2 %collective-permute-start.9 = (bf16[1,320,1024]{2,1,0:T(8,128)(2,1)S(1)}, bf16[1,320,1024]{2,1,0:T(8,128)(2,1)}, u32[]{:S(2)}, u32[]{:S(2)}) collective-permute-start(bf16[1,320,1024]{2,1,0:T(8,128)(2,1)S(1)} %get-tuple-element.119.refs_2_), channel_id=1, source_target_pairs={{2,0},{3,1},{0,2},{1,3},{6,4},{7,5},{4,6},{5,7},{10,8},{11,9},{8,1... | collective-permute-start | bytes 1966088 | tf_op jit(solution)/shard_map/ppermute | solution.py:372
  40.8 28.6 %collective-permute-start.8 = (bf16[1,320,1024]{2,1,0:T(8,128)(2,1)S(1)}, bf16[1,320,1024]{2,1,0:T(8,128)(2,1)}, u32[]{:S(2)}, u32[]{:S(2)}) collective-permute-start(bf16[1,320,1024]{2,1,0:T(8,128)(2,1)S(1)} %get-tuple-element.119.refs_2_), channel_id=1, source_target_pairs={{0,1},{1,0},{2,3},{3,2},{4,5},{5,4},{6,7},{7,6},{8,9},{9,8},{10,11... | collective-permute-start | bytes 1966088 | tf_op jit(solution)/shard_map/ppermute | solution.py:366
  53.1 33.2 %collective-permute-start.14 = (bf16[1,320,1024]{2,1,0:T(8,128)(2,1)}, bf16[1,320,1024]{2,1,0:T(8,128)(2,1)}, u32[]{:S(2)}, u32[]{:S(2)}) collective-permute-start(bf16[1,320,1024]{2,1,0:T(8,128)(2,1)} %get-tuple-element.114.refs_3_), channel_id=1, source_target_pairs={{2,0},{3,1},{0,2},{1,3},{6,4},{7,5},{4,6},{5,7},{10,8},{11,9},{8,1... | collective-permute-start | bytes 1966088 | tf_op jit(solution)/shard_map/ppermute | solution.py:372
  57.4 12.0 %collective-permute-start.11 = (bf16[1,320,1024]{2,1,0:T(8,128)(2,1)}, bf16[1,320,1024]{2,1,0:T(8,128)(2,1)S(1)}, u32[]{:S(2)}, u32[]{:S(2)}) collective-permute-start(bf16[1,320,1024]{2,1,0:T(8,128)(2,1)} %collective-permute-done.9.refs_6_), channel_id=1, source_target_pairs={{0,1},{1,0},{2,3},{3,2},{4,5},{5,4},{6,7},{7,6},{8,9},{9,8},{10,11... | collective-permute-start | bytes 1966088 | tf_op jit(solution)/shard_map/ppermute | solution.py:366
  68.7 19.3 %collective-permute-start.12 = (bf16[1,320,1024]{2,1,0:T(8,128)(2,1)S(1)}, bf16[1,320,1024]{2,1,0:T(8,128)(2,1)S(1)}, u32[]{:S(2)}, u32[]{:S(2)}) collective-permute-start(bf16[1,320,1024]{2,1,0:T(8,128)(2,1)S(1)} %copy-done.26), channel_id=1, source_target_pairs={{0,1},{1,0},{2,3},{3,2},{4,5},{5,4},{6,7},{7,6},{8,9},{9,8},{10,11... | collective-permute-start | bytes 1966088 | tf_op jit(solution)/shard_map/ppermute | solution.py:366
  69.2 17.0 %collective-permute-start.15 = (bf16[1,320,1024]{2,1,0:T(8,128)(2,1)}, bf16[1,320,1024]{2,1,0:T(8,128)(2,1)}, u32[]{:S(2)}, u32[]{:S(2)}) collective-permute-start(bf16[1,320,1024]{2,1,0:T(8,128)(2,1)} %get-tuple-element.117.refs_4_), channel_id=1, source_target_pairs={{2,0},{3,1},{0,2},{1,3},{6,4},{7,5},{4,6},{5,7},{10,8},{11,9},{8,1... | collective-permute-start | bytes 1966088 | tf_op jit(solution)/shard_map/ppermute | solution.py:372
  69.3 18.7 %collective-permute-start.13 = (bf16[1,320,1024]{2,1,0:T(8,128)(2,1)}, bf16[1,320,1024]{2,1,0:T(8,128)(2,1)S(1)}, u32[]{:S(2)}, u32[]{:S(2)}) collective-permute-start(bf16[1,320,1024]{2,1,0:T(8,128)(2,1)} %get-tuple-element.117.refs_4_), channel_id=1, source_target_pairs={{0,1},{1,0},{2,3},{3,2},{4,5},{5,4},{6,7},{7,6},{8,9},{9,8},{10,11... | collective-permute-start | bytes 1966088 | tf_op jit(solution)/shard_map/ppermute | solution.py:366
  123.5 151.8 %reduce-scatter.9.cloned.1.call-start = ((), (), s32[]{:S(2)}) async-start(), calls=%async_computation.7 | async-start | bytes 1966080 | tf_op jit(solution)/shard_map/reduce_scatter | solution.py:939
  144.2 37.5 %collective-permute-start.18 = (bf16[1,4,192,1024]{3,2,1,0:T(8,128)(2,1)}, bf16[1,4,192,1024]{3,2,1,0:T(8,128)(2,1)S(1)}, u32[]{:S(2)}, u32[]{:S(2)}) collective-permute-start(bf16[1,4,192,1024]{3,2,1,0:T(8,128)(2,1)} %get-tuple-element.136), channel_id=1, source_target_pairs={{0,4},{4,0},{8,12},{12,8},{16,20},{20,16},{24,28},{28,24},{1,5},{5... | collective-permute-start | bytes 4718600 | tf_op jit(solution)/shard_map/ppermute | solution.py:983
  175.1 88.7 %collective-permute-start.23 = (bf16[2,4,192,1024]{3,2,1,0:T(8,128)(2,1)}, bf16[2,4,192,1024]{3,2,1,0:T(8,128)(2,1)}, u32[]{:S(2)}, u32[]{:S(2)}) collective-permute-start(bf16[2,4,192,1024]{3,2,1,0:T(8,128)(2,1)} %get-tuple-element.159), channel_id=1, source_target_pairs={{0,4},{4,0},{8,12},{12,8},{16,20},{20,16},{24,28},{28,24},{1,5},{5... | collective-permute-start | bytes 9437192 | tf_op jit(solution)/shard_map/ppermute | solution.py:983
  183.5 108.5 %reduce-scatter.11.cloned.1.call-start = ((), (), s32[]{:S(2)}) async-start(), calls=%async_computation.8 | async-start | bytes 3932160 | tf_op jit(solution)/shard_map/reduce_scatter | solution.py:939
  213.3 111.2 %collective-permute-start.27 = (bf16[2,4,192,1024]{3,2,1,0:T(8,128)(2,1)}, bf16[2,4,192,1024]{3,2,1,0:T(8,128)(2,1)}, u32[]{:S(2)}, u32[]{:S(2)}) collective-permute-start(bf16[2,4,192,1024]{3,2,1,0:T(8,128)(2,1)} %get-tuple-element.176), channel_id=1, source_target_pairs={{0,4},{4,0},{8,12},{12,8},{16,20},{20,16},{24,28},{28,24},{1,5},{5... | collective-permute-start | bytes 9437192 | tf_op jit(solution)/shard_map/ppermute | solution.py:983
  231.7 218.2 %reduce-scatter.15.cloned.1.call-start = ((), (), s32[]{:S(2)}) async-start(), calls=%async_computation.10 | async-start | bytes 3932160 | tf_op jit(solution)/shard_map/reduce_scatter | solution.py:939
  263.8 9.7 %collective-permute-start.22 = (bf16[2,320,1024]{2,1,0:T(8,128)(2,1)}, bf16[2,320,1024]{2,1,0:T(8,128)(2,1)S(1)}, u32[]{:S(2)}, u32[]{:S(2)}) collective-permute-start(bf16[2,320,1024]{2,1,0:T(8,128)(2,1)} %get-tuple-element.157), channel_id=1, source_target_pairs={{0,1},{1,0},{2,3},{3,2},{4,5},{5,4},{6,7},{7,6},{8,9},{9,8},{10,11... | collective-permute-start | bytes 3932168 | tf_op jit(solution)/shard_map/ppermute | solution.py:366
  272.3 19.7 %collective-permute-start.24 = (bf16[2,320,1024]{2,1,0:T(8,128)(2,1)}, bf16[2,320,1024]{2,1,0:T(8,128)(2,1)S(1)}, u32[]{:S(2)}, u32[]{:S(2)}) collective-permute-start(bf16[2,320,1024]{2,1,0:T(8,128)(2,1)} %get-tuple-element.167), channel_id=1, source_target_pairs={{0,1},{1,0},{2,3},{3,2},{4,5},{5,4},{6,7},{7,6},{8,9},{9,8},{10,11... | collective-permute-start | bytes 3932168 | tf_op jit(solution)/shard_map/ppermute | solution.py:366
  274.1 30.9 %collective-permute-start.25 = (bf16[2,320,1024]{2,1,0:T(8,128)(2,1)S(1)}, bf16[2,320,1024]{2,1,0:T(8,128)(2,1)}, u32[]{:S(2)}, u32[]{:S(2)}) collective-permute-start(bf16[2,320,1024]{2,1,0:T(8,128)(2,1)S(1)} %add_convert_fusion.7), channel_id=1, source_target_pairs={{0,2},{1,3},{2,0},{3,1},{4,6},{5,7},{6,4},{7,5},{8,10},{9,11},{10,... | collective-permute-start | bytes 3932168 | tf_op jit(solution)/shard_map/ppermute | solution.py:378
  288.7 31.4 %collective-permute-start.29 = (bf16[2,320,1024]{2,1,0:T(8,128)(2,1)}, bf16[2,320,1024]{2,1,0:T(8,128)(2,1)}, u32[]{:S(2)}, u32[]{:S(2)}) collective-permute-start(bf16[2,320,1024]{2,1,0:T(8,128)(2,1)} %get-tuple-element.171), channel_id=1, source_target_pairs={{0,1},{1,0},{2,3},{3,2},{4,5},{5,4},{6,7},{7,6},{8,9},{9,8},{10,11... | collective-permute-start | bytes 3932168 | tf_op jit(solution)/shard_map/ppermute | solution.py:366
  319.0 10.7 %collective-permute-start.26 = (bf16[512,1024]{1,0:T(8,128)(2,1)}, bf16[512,1024]{1,0:T(8,128)(2,1)}, u32[]{:S(2)}, u32[]{:S(2)}) collective-permute-start(bf16[512,1024]{1,0:T(8,128)(2,1)} %constant_dynamic-slice_fusion.3), channel_id=1, source_target_pairs={{0,1},{1,0},{2,3},{3,2},{4,5},{5,4},{6,7},{7,6},{8,9},{9,8},{10,11... | collective-permute-start | bytes 3145736 | tf_op jit(solution)/shard_map/ppermute | solution.py:799
  319.6 40.3 %collective-permute-start.31 = (bf16[1,4,192,1024]{3,2,1,0:T(8,128)(2,1)}, bf16[1,4,192,1024]{3,2,1,0:T(8,128)(2,1)}, u32[]{:S(2)}, u32[]{:S(2)}) collective-permute-start(bf16[1,4,192,1024]{3,2,1,0:T(8,128)(2,1)} %get-tuple-element.188), channel_id=1, source_target_pairs={{0,4},{4,0},{8,12},{12,8},{16,20},{20,16},{24,28},{28,24},{1,5},{5... | collective-permute-start | bytes 4718600 | tf_op jit(solution)/shard_map/ppermute | solution.py:983
  323.4 42.5 %collective-permute-start.30 = (bf16[2,320,1024]{2,1,0:T(8,128)(2,1)}, bf16[2,320,1024]{2,1,0:T(8,128)(2,1)}, u32[]{:S(2)}, u32[]{:S(2)}) collective-permute-start(bf16[2,320,1024]{2,1,0:T(8,128)(2,1)} %add_convert_fusion.6), channel_id=1, source_target_pairs={{0,2},{1,3},{2,0},{3,1},{4,6},{5,7},{6,4},{7,5},{8,10},{9,11},{10,... | collective-permute-start | bytes 3932168 | tf_op jit(solution)/shard_map/ppermute | solution.py:378
  329.6 124.2 %reduce-scatter.13.cloned.1.call-start = ((), (), s32[]{:S(2)}) async-start(), calls=%async_computation.9 | async-start | bytes 3932160 | tf_op jit(solution)/shard_map/reduce_scatter | solution.py:939
  357.6 12.2 %collective-permute-start.32 = (bf16[2,64,512]{2,1,0:T(8,128)(2,1)S(1)}, bf16[2,64,512]{2,1,0:T(8,128)(2,1)S(1)}, u32[]{:S(2)}, u32[]{:S(2)}) collective-permute-start(bf16[2,64,512]{2,1,0:T(8,128)(2,1)S(1)} %get-tuple-element.221), channel_id=1, source_target_pairs={{0,1},{1,0},{2,3},{3,2},{4,5},{5,4},{6,7},{7,6},{8,9},{9,8},{10,11... | collective-permute-start | bytes 393224 | tf_op jit(solution)/shard_map/ppermute | solution.py:366
  359.9 9.9 %collective-permute-start.35 = (bf16[2,64,512]{2,1,0:T(8,128)(2,1)S(1)}, bf16[2,64,512]{2,1,0:T(8,128)(2,1)S(1)}, u32[]{:S(2)}, u32[]{:S(2)}) collective-permute-start(bf16[2,64,512]{2,1,0:T(8,128)(2,1)S(1)} %get-tuple-element.217), channel_id=1, source_target_pairs={{0,1},{1,0},{2,3},{3,2},{4,5},{5,4},{6,7},{7,6},{8,9},{9,8},{10,11... | collective-permute-start | bytes 393224 | tf_op jit(solution)/shard_map/ppermute | solution.py:366
  368.8 13.2 %collective-permute-start.38 = (bf16[256,1024]{1,0:T(8,128)(2,1)S(1)}, bf16[256,1024]{1,0:T(8,128)(2,1)S(1)}, u32[]{:S(2)}, u32[]{:S(2)}) collective-permute-start(bf16[256,1024]{1,0:T(8,128)(2,1)S(1)} %constant_dynamic-slice_fusion.2), channel_id=1, source_target_pairs={{0,2},{1,3},{2,0},{3,1},{4,6},{5,7},{6,4},{7,5},{8,10},{9,11},{10,... | collective-permute-start | bytes 1572872 | tf_op jit(solution)/shard_map/ppermute | solution.py:799
  384.8 10.8 %collective-permute-start.39 = (bf16[512,2048]{1,0:T(8,128)(2,1)S(1)}, bf16[512,2048]{1,0:T(8,128)(2,1)}, u32[]{:S(2)}, u32[]{:S(2)}) collective-permute-start(bf16[512,2048]{1,0:T(8,128)(2,1)S(1)} %constant_dynamic-slice_fusion.1), channel_id=1, source_target_pairs={{0,1},{1,0},{2,3},{3,2},{4,5},{5,4},{6,7},{7,6},{8,9},{9,8},{10,11... | collective-permute-start | bytes 6291464 | tf_op jit(solution)/shard_map/ppermute | solution.py:799
  385.4 118.0 %all-reduce.2.cloned.1.call-start = ((), (), s32[]{:S(2)}) async-start(), calls=%async_computation.11 | async-start | bytes 1769472 | tf_op jit(solution)/shard_map/psum | solution.py:1100
  398.1 25.4 %collective-permute-start.40 = (bf16[256,2048]{1,0:T(8,128)(2,1)S(1)}, bf16[256,2048]{1,0:T(8,128)(2,1)}, u32[]{:S(2)}, u32[]{:S(2)}) collective-permute-start(bf16[256,2048]{1,0:T(8,128)(2,1)S(1)} %constant_dynamic-slice_fusion), channel_id=1, source_target_pairs={{0,2},{1,3},{2,0},{3,1},{4,6},{5,7},{6,4},{7,5},{8,10},{9,11},{10,... | collective-permute-start | bytes 3145736 | tf_op jit(solution)/shard_map/ppermute | solution.py:799
  427.0 20.7 %collective-permute-start.43 = (bf16[128,3072]{1,0:T(8,128)(2,1)}, bf16[128,3072]{1,0:T(8,128)(2,1)}, u32[]{:S(2)}, u32[]{:S(2)}) collective-permute-start(bf16[128,3072]{1,0:T(8,128)(2,1)} %fusion.10), channel_id=1, source_target_pairs={{0,4},{4,0},{8,12},{12,8},{16,20},{20,16},{24,28},{28,24},{1,5},{5... | collective-permute-start | bytes 2359304 | tf_op jit(solution)/shard_map/ppermute | solution.py:799
  432.9 30.0 %collective-permute-start.59 = (bf16[2,192,1024]{2,1,0:T(8,128)(2,1)}, bf16[2,192,1024]{2,1,0:T(8,128)(2,1)}, u32[]{:S(2)}, u32[]{:S(2)}) collective-permute-start(bf16[2,192,1024]{2,1,0:T(8,128)(2,1)} %slice.130), channel_id=1, source_target_pairs={{0,4},{4,0},{8,12},{12,8},{16,20},{20,16},{24,28},{28,24},{1,5},{5... | collective-permute-start | bytes 2359304 | tf_op jit(solution)/shard_map/ppermute | solution.py:1067
  456.0 93.3 %reduce-scatter.17.cloned.1.call-start = ((), (), s32[]{:S(2)}) async-start(), calls=%async_computation.12 | async-start | bytes 1966080 | tf_op jit(solution)/shard_map/reduce_scatter | solution.py:939
  505.4 12.1 %collective-permute-start.53 = (bf16[128,1536]{1,0:T(8,128)(2,1)S(1)}, bf16[128,1536]{1,0:T(8,128)(2,1)}, u32[]{:S(2)}, u32[]{:S(2)}) collective-permute-start(bf16[128,1536]{1,0:T(8,128)(2,1)S(1)} %get-tuple-element.213.refs_8_), channel_id=1, source_target_pairs={{0,2},{1,3},{2,0},{3,1},{4,6},{5,7},{6,4},{7,5},{8,10},{9,11},{10,... | collective-permute-start | bytes 1179656 | tf_op jit(solution)/shard_map/ppermute | solution.py:1109
  506.9 12.0 %collective-permute-start.52 = (bf16[128,1536]{1,0:T(8,128)(2,1)S(1)}, bf16[128,1536]{1,0:T(8,128)(2,1)S(1)}, u32[]{:S(2)}, u32[]{:S(2)}) collective-permute-start(bf16[128,1536]{1,0:T(8,128)(2,1)S(1)} %get-tuple-element.213.refs_8_), channel_id=1, source_target_pairs={{0,4},{4,0},{8,12},{12,8},{16,20},{20,16},{24,28},{28,24},{1,5},{5... | collective-permute-start | bytes 1179656 | tf_op jit(solution)/shard_map/ppermute | solution.py:1113
  508.4 19.1 %collective-permute-start.45 = (bf16[128,1536]{1,0:T(8,128)(2,1)}, bf16[128,1536]{1,0:T(8,128)(2,1)}, u32[]{:S(2)}, u32[]{:S(2)}) collective-permute-start(bf16[128,1536]{1,0:T(8,128)(2,1)} %get-tuple-element.214.refs_0_), channel_id=1, source_target_pairs={{0,4},{4,0},{8,12},{12,8},{16,20},{20,16},{24,28},{28,24},{1,5},{5... | collective-permute-start | bytes 1179656 | tf_op jit(solution)/shard_map/ppermute | solution.py:1108
  510.2 18.7 %collective-permute-start.48 = (bf16[128,1536]{1,0:T(8,128)(2,1)}, bf16[128,1536]{1,0:T(8,128)(2,1)}, u32[]{:S(2)}, u32[]{:S(2)}) collective-permute-start(bf16[128,1536]{1,0:T(8,128)(2,1)} %get-tuple-element.214.refs_0_), channel_id=1, source_target_pairs={{0,1},{1,0},{2,3},{3,2},{4,5},{5,4},{6,7},{7,6},{8,9},{9,8},{10,11... | collective-permute-start | bytes 1179656 | tf_op jit(solution)/shard_map/ppermute | solution.py:366
  510.3 18.7 %collective-permute-start.46 = (bf16[128,1536]{1,0:T(8,128)(2,1)}, bf16[128,1536]{1,0:T(8,128)(2,1)}, u32[]{:S(2)}, u32[]{:S(2)}) collective-permute-start(bf16[128,1536]{1,0:T(8,128)(2,1)} %get-tuple-element.214.refs_0_), channel_id=1, source_target_pairs={{0,2},{1,3},{2,0},{3,1},{4,6},{5,7},{6,4},{7,5},{8,10},{9,11},{10,... | collective-permute-start | bytes 1179656 | tf_op jit(solution)/shard_map/ppermute | solution.py:1111
  517.5 12.0 %collective-permute-start.57 = (bf16[128,1536]{1,0:T(8,128)(2,1)}, bf16[128,1536]{1,0:T(8,128)(2,1)}, u32[]{:S(2)}, u32[]{:S(2)}) collective-permute-start(bf16[128,1536]{1,0:T(8,128)(2,1)} %collective-permute-done.53.refs_10_), channel_id=1, source_target_pairs={{0,1},{1,0},{2,3},{3,2},{4,5},{5,4},{6,7},{7,6},{8,9},{9,8},{10,11... | collective-permute-start | bytes 1179656 | tf_op jit(solution)/shard_map/ppermute | solution.py:366
  518.9 16.2 %collective-permute-start.54 = (bf16[128,1536]{1,0:T(8,128)(2,1)}, bf16[128,1536]{1,0:T(8,128)(2,1)}, u32[]{:S(2)}, u32[]{:S(2)}) collective-permute-start(bf16[128,1536]{1,0:T(8,128)(2,1)} %collective-permute-done.53.refs_10_), channel_id=1, source_target_pairs={{0,4},{4,0},{8,12},{12,8},{16,20},{20,16},{24,28},{28,24},{1,5},{5... | collective-permute-start | bytes 1179656 | tf_op jit(solution)/shard_map/ppermute | solution.py:1113
  527.4 10.0 %collective-permute-start.47 = (bf16[128,1536]{1,0:T(8,128)(2,1)}, bf16[128,1536]{1,0:T(8,128)(2,1)}, u32[]{:S(2)}, u32[]{:S(2)}) collective-permute-start(bf16[128,1536]{1,0:T(8,128)(2,1)} %collective-permute-done.45.refs_1_), channel_id=1, source_target_pairs={{0,2},{1,3},{2,0},{3,1},{4,6},{5,7},{6,4},{7,5},{8,10},{9,11},{10,... | collective-permute-start | bytes 1179656 | tf_op jit(solution)/shard_map/ppermute | solution.py:1111
  529.0 9.7 %collective-permute-start.49 = (bf16[128,1536]{1,0:T(8,128)(2,1)}, bf16[128,1536]{1,0:T(8,128)(2,1)S(1)}, u32[]{:S(2)}, u32[]{:S(2)}) collective-permute-start(bf16[128,1536]{1,0:T(8,128)(2,1)} %collective-permute-done.45.refs_1_), channel_id=1, source_target_pairs={{0,1},{1,0},{2,3},{3,2},{4,5},{5,4},{6,7},{7,6},{8,9},{9,8},{10,11... | collective-permute-start | bytes 1179656 | tf_op jit(solution)/shard_map/ppermute | solution.py:366
  529.0 9.6 %collective-permute-start.56 = (bf16[128,1536]{1,0:T(8,128)(2,1)}, bf16[128,1536]{1,0:T(8,128)(2,1)S(1)}, u32[]{:S(2)}, u32[]{:S(2)}) collective-permute-start(bf16[128,1536]{1,0:T(8,128)(2,1)} %copy-done.33), channel_id=1, source_target_pairs={{0,1},{1,0},{2,3},{3,2},{4,5},{5,4},{6,7},{7,6},{8,9},{9,8},{10,11... | collective-permute-start | bytes 1179656 | tf_op jit(solution)/shard_map/ppermute | solution.py:366
  529.5 9.1 %collective-permute-start.50 = (bf16[128,1536]{1,0:T(8,128)(2,1)}, bf16[128,1536]{1,0:T(8,128)(2,1)S(1)}, u32[]{:S(2)}, u32[]{:S(2)}) collective-permute-start(bf16[128,1536]{1,0:T(8,128)(2,1)} %collective-permute-done.46.refs_2_), channel_id=1, source_target_pairs={{0,1},{1,0},{2,3},{3,2},{4,5},{5,4},{6,7},{7,6},{8,9},{9,8},{10,11... | collective-permute-start | bytes 1179656 | tf_op jit(solution)/shard_map/ppermute | solution.py:366
  (62 other events, 418.5 us)
Sparse Core Ops, SparseCore 0:
  123.6 61.2 reduce-scatter.6
  187.2 35.3 reduce-scatter.8
  231.8 60.1 reduce-scatter.10
  329.7 61.0 reduce-scatter.14
  393.5 60.3 reduce-scatter.12
  456.7 46.6 all-reduce.1
  506.3 34.4 reduce-scatter.16
